TPU v7x, 32 devices: a whole 2x2x4 slice. The times are simulated.
32 devices in a mesh: rows: 16 (over z, y, x), samp: 2 (over core).
Axes of the slice: x: 2, y: 2, z: 4, core: 2. Of those that a mesh axis runs over, the one named last changes fastest.
Arguments:
- samples: float32 [12288, 1024], P('rows', 'samp'), may hold values from -6 to 6
- probes: float32 [12288, 1024], P('rows', 'samp'), may hold values from -6 to 6
- near_blocks: float32 [48, 3, 256, 256], P('rows'), may hold values from -0.375 to 0.375
- near_cols: int32 [48, 3], P('rows'), may hold values from 0 to 47, as said below
- near_count: int32 [48], P('rows'), may hold values from 1 to 3, as said below
- sketch: float32 [1024, 256], P('samp'), may hold values from -0.1875 to 0.1875
Outputs:
- leaf_basis: float32 [12288, 256], P('rows')
- reduced: float32 [4, 16, 256, 1024], P(None, 'rows', None, 'samp')
Inputs may be any that keep to these rules, and one draw needn't show every extreme that they name: `near_cols`: slot 0 of block row b names b itself; every slot names a column block within 3 blocks of b; the slots of a row are distinct except near the first and last 3 block rows, where two may repeat. `near_count`: every fourth block row, starting with block row 0, has all 3 slots valid.
All inputs are finite; a program needn't handle non-finite values.
Results may differ from a plain program's by a relative error of at most 0.0003.
Values sent between devices are 32-bit elements; how exact they have to be, the bound alone decides.
No kernel may reach another device: no remote copies, remote signals or barrier semaphores. Data moves between devices by JAX's collectives and lax.ppermute only.
A program may use at most 64 MiB of HBM per device.

v0:
```python
import jax
import jax.numpy as jnp
from jax import lax
from jax.sharding import PartitionSpec as P

LEVELS = 4


PRECISE = lax.Precision.HIGHEST


def extended(block, sides, width):
    for axis, dim in sides:
        count = lax.axis_size(axis)
        forward = [(i, i + 1) for i in range(count - 1)]
        backward = [(target, source) for source, target in forward]
        low = lax.ppermute(
            lax.slice_in_dim(block, block.shape[dim] - width, None, axis=dim), axis, forward
        )
        high = lax.ppermute(lax.slice_in_dim(block, 0, width, axis=dim), axis, backward)
        block = jnp.concatenate([low, block, high], axis=dim)
    return block


def from_partner(value, axis, bit):
    return lax.ppermute(value, axis, [(i, i ^ 1 << bit) for i in range(lax.axis_size(axis))])


def factor_and_rows(sketched):
    gram_matrix = jnp.einsum("rk,rl->kl", sketched, sketched, precision=PRECISE)
    lower_factor = jnp.linalg.cholesky(gram_matrix)
    project_t = jax.scipy.linalg.solve_triangular(lower_factor, sketched.T, lower=True)
    return (lower_factor, project_t)


def shards(samples, probes, near_blocks, near_cols, near_count, sketch):
    rows_dev, samp_dev = samples.shape
    block_size = near_blocks.shape[2]
    slot_count = near_blocks.shape[1]
    block_count = rows_dev // block_size
    padded = extended(probes, (("rows", 0),), rows_dev)
    probe_blocks = padded.reshape(3 * block_count, block_size, samp_dev)
    position = lax.axis_index("rows")
    first_block = position * block_count - block_count
    pieces = jnp.take(probe_blocks, near_cols - first_block, axis=0)
    live_slots = (jnp.arange(slot_count)[None, :] < near_count[:, None]).astype(jnp.float32)
    pieces = pieces * live_slots[:, :, None, None]
    near_part = jnp.einsum("bjrc,bjcs->brs", near_blocks, pieces, precision=PRECISE)
    far_samples = samples - near_part.reshape(rows_dev, samp_dev)
    partial_value = jnp.dot(far_samples, sketch, precision=PRECISE)
    sketched = lax.psum(partial_value, "samp")
    lower_factor, basis_t = factor_and_rows(sketched)
    leaf_basis = basis_t.T
    reduced = jnp.dot(basis_t, far_samples, precision=PRECISE)
    outputs = []
    for height in range(LEVELS):
        upper_half = position >> height & 1 == 1
        own_factor = lower_factor.T
        peer_reduced, peer_factor = from_partner((reduced, own_factor), "rows", height)
        first_red = jnp.where(upper_half, peer_reduced, reduced)
        second_red = jnp.where(upper_half, reduced, peer_reduced)
        stacked = jnp.concatenate([first_red, second_red], axis=0)
        first_fac = jnp.where(upper_half, peer_factor, own_factor)
        second_fac = jnp.where(upper_half, own_factor, peer_factor)
        node_sketch = jnp.concatenate([first_fac, second_fac], axis=0)
        lower_factor, project_t = factor_and_rows(node_sketch)
        reduced = jnp.dot(project_t, stacked, precision=PRECISE)
        outputs.append(reduced)
    return (leaf_basis, jnp.stack(outputs)[:, None, :, :])


def solution(mesh):
    return jax.shard_map(
        shards,
        mesh=mesh,
        in_specs=(
            P("rows", "samp"),
            P("rows", "samp"),
            P("rows", None, None, None),
            P("rows", None),
            P("rows"),
            P("samp", None),
        ),
        out_specs=(P("rows", None), P(None, "rows", None, "samp")),
        check_vma=False,
    )
```

profile of v0, /device:TPU:0, one launch (start us, length us, event | category | flops | bytes accessed | tf_op | source)
XLA Modules:
  0.0 547.7 jit_solution(1213517043680876175)
XLA Ops:
  7.2 6.2 %collective-permute-start = (f32[768,512]{1,0:T(8,128)}, f32[768,512]{1,0:T(8,128)}, u32[]{:S(2)}, u32[]{:S(2)}) collective-permute-start(f32[768,512]{1,0:T(8,128)} %param.10), channel_id=1, source_target_pairs={{0,2},{2,4},{4,6},{6,8},{8,10},{10,12},{12,14},{14,16},{16,18},{18... | collective-permute-start | bytes 4718600 | tf_op jit(solution)/shard_map/ppermute | solution.py:17
  15.5 64.4 %collective-permute-done = f32[768,512]{1,0:T(8,128)} collective-permute-done((f32[768,512]{1,0:T(8,128)}, f32[768,512]{1,0:T(8,128)}, u32[]{:S(2)}, u32[]{:S(2)}) %collective-permute-start) | collective-permute-done | bytes 1572896 | tf_op jit(solution)/shard_map/ppermute | solution.py:17
  79.9 1.9 collective-permute-done.1
  81.8 5.0 pad_maximum_fusion
  86.8 5.4 gather_fusion
  92.2 7.5 %fusion = f32[3,512,256,1]{1,2,3,0:T(8,128)S(1)} fusion(f32[3,3,256,256]{3,2,1,0:T(8,128)S(1)} %copy-done, f32[3,3,256,512]{3,2,1,0:T(8,128)} %bitcast.186, f32[3,3]{1,0:T(4,128)S(1)} %get-tuple-element.142, pred[3,3]{1,0:T(4,128)(4,1)S(1)} %get-tuple-element.84), kind=kOutput, calls=%fused_computation.12 | convolution fusion | flops 3626237952 | bytes 8650797 | tf_op jit(solution)/shard_map/bjrc,bjcs->brs/dot_general | solution.py:48
  101.3 2.3 fusion.111
  103.6 19.4 %all-reduce.3.cloned.1.call-done = f32[768,256]{1,0:T(8,128)} async-done(((f32[768,256]{1,0:T(8,128)}), f32[768,256]{1,0:T(8,128)}) %all-reduce.3.cloned.1.call-update) | async-done | bytes 786448 | tf_op jit(solution)/shard_map/psum | solution.py:51
  123.0 2.8 fusion.112
  128.4 11.7 %cholesky.256 = f32[128,128]{1,0:T(8,128)S(1)} custom-call(f32[128,128]{1,0:T(8,128)S(1)} %cholesky.422), custom_call_target="Cholesky" | custom-call | tf_op jit(solution)/shard_map/jit(cholesky)/cholesky | solution.py:31
  140.1 9.8 %custom-call.23 = f32[1,128,128]{1,2,0:T(8,128)S(1)} custom-call(f32[1,128,128]{2,1,0:T(8,128)S(1)} %get-tuple-element.139), custom_call_target="InvertDiagBlocksLowerTriangular" | custom-call | tf_op jit(solution)/shard_map/jit(cholesky)/cholesky | solution.py:31
  152.9 12.9 %cholesky.273 = f32[128,128]{1,0:T(8,128)S(1)} custom-call(f32[128,128]{1,0:T(8,128)} %convolution_subtract_fusion.5), custom_call_target="Cholesky" | custom-call | tf_op jit(solution)/shard_map/jit(cholesky)/cholesky | solution.py:31
  170.3 1.8 collective-permute-start.2
  172.2 4.0 while.9
  176.1 20.3 %custom-call.15 = f32[2,128,128]{1,2,0:T(8,128)} custom-call(f32[2,128,128]{2,1,0:T(8,128)S(1)} %get-tuple-element.19), custom_call_target="InvertDiagBlocksLowerTriangular" | custom-call | tf_op jit(solution)/shard_map/jit(_solve_triangular)/triangular_solve | solution.py:32
  199.3 2.3 fusion.21
  205.6 11.7 %cholesky.290 = f32[128,128]{1,0:T(8,128)S(1)} custom-call(f32[128,128]{1,0:T(8,128)S(1)} %cholesky.425), custom_call_target="Cholesky" | custom-call | tf_op jit(solution)/shard_map/jit(cholesky)/cholesky | solution.py:31
  217.4 9.8 %custom-call.24 = f32[1,128,128]{1,2,0:T(8,128)S(1)} custom-call(f32[1,128,128]{2,1,0:T(8,128)S(1)} %get-tuple-element.135), custom_call_target="InvertDiagBlocksLowerTriangular" | custom-call | tf_op jit(solution)/shard_map/jit(cholesky)/cholesky | solution.py:31
  231.1 12.8 %cholesky.307 = f32[128,128]{1,0:T(8,128)S(1)} custom-call(f32[128,128]{1,0:T(8,128)} %convolution_subtract_fusion.4), custom_call_target="Cholesky" | custom-call | tf_op jit(solution)/shard_map/jit(cholesky)/cholesky | solution.py:31
  248.9 3.8 while.10
  252.6 19.7 %custom-call.25 = f32[2,128,128]{1,2,0:T(8,128)S(1)} custom-call(f32[2,128,128]{2,1,0:T(8,128)S(1)} %get-tuple-element.38), custom_call_target="InvertDiagBlocksLowerTriangular" | custom-call | tf_op jit(solution)/shard_map/jit(_solve_triangular)/triangular_solve | solution.py:32
  278.5 11.7 %cholesky.324 = f32[128,128]{1,0:T(8,128)S(1)} custom-call(f32[128,128]{1,0:T(8,128)S(1)} %cholesky.428), custom_call_target="Cholesky" | custom-call | tf_op jit(solution)/shard_map/jit(cholesky)/cholesky | solution.py:31
  290.3 9.8 %custom-call.26 = f32[1,128,128]{1,2,0:T(8,128)S(1)} custom-call(f32[1,128,128]{2,1,0:T(8,128)S(1)} %get-tuple-element.131), custom_call_target="InvertDiagBlocksLowerTriangular" | custom-call | tf_op jit(solution)/shard_map/jit(cholesky)/cholesky | solution.py:31
  303.9 12.6 %cholesky.341 = f32[128,128]{1,0:T(8,128)S(1)} custom-call(f32[128,128]{1,0:T(8,128)} %convolution_subtract_fusion.3), custom_call_target="Cholesky" | custom-call | tf_op jit(solution)/shard_map/jit(cholesky)/cholesky | solution.py:31
  319.1 2.1 fusion.68
  322.7 3.8 while.11
  326.5 20.3 %custom-call.27 = f32[2,128,128]{1,2,0:T(8,128)} custom-call(f32[2,128,128]{2,1,0:T(8,128)S(1)} %get-tuple-element.39), custom_call_target="InvertDiagBlocksLowerTriangular" | custom-call | tf_op jit(solution)/shard_map/jit(_solve_triangular)/triangular_solve | solution.py:32
  349.2 2.0 fusion.51
  359.1 11.7 %cholesky.358 = f32[128,128]{1,0:T(8,128)S(1)} custom-call(f32[128,128]{1,0:T(8,128)S(1)} %cholesky.431), custom_call_target="Cholesky" | custom-call | tf_op jit(solution)/shard_map/jit(cholesky)/cholesky | solution.py:31
  370.8 9.8 %custom-call.28 = f32[1,128,128]{1,2,0:T(8,128)S(1)} custom-call(f32[1,128,128]{2,1,0:T(8,128)S(1)} %get-tuple-element.127), custom_call_target="InvertDiagBlocksLowerTriangular" | custom-call | tf_op jit(solution)/shard_map/jit(cholesky)/cholesky | solution.py:31
  383.7 1.8 fusion.37
  386.2 12.7 %cholesky.375 = f32[128,128]{1,0:T(8,128)S(1)} custom-call(f32[128,128]{1,0:T(8,128)} %convolution_subtract_fusion.2), custom_call_target="Cholesky" | custom-call | tf_op jit(solution)/shard_map/jit(cholesky)/cholesky | solution.py:31
  402.7 1.8 fusion.69
  404.5 2.4 collective-permute-start.8
  407.0 5.7 %while.12 = (s32[]{:T(128)}, f32[256,256]{1,0:T(8,128)}, s32[2,2]{1,0:T(2,128)S(1)}, f32[2,128,128]{2,1,0:T(8,128)S(1)}, s32[]{:T(128)}) while((s32[]{:T(128)}, f32[256,256]{1,0:T(8,128)}, s32[2,2]{1,0:T(2,128)S(1)}, f32[2,128,128]{2,1,0:T(8,128)S(1)}, s32[]{:T(128)}) %tuple.127), condition=%wide.while_cond.clone.1, body=%wide.while_body.clone.1.sunk | while | flops 2 | bytes 131181 | solution.py:32
  407.6 2.2 bitcast_dynamic-update-slice_fusion.13
  410.5 2.2 bitcast_dynamic-update-slice_fusion.13
  412.7 20.3 %custom-call.29 = f32[2,128,128]{1,2,0:T(8,128)} custom-call(f32[2,128,128]{2,1,0:T(8,128)S(1)} %get-tuple-element.40), custom_call_target="InvertDiagBlocksLowerTriangular" | custom-call | tf_op jit(solution)/shard_map/jit(_solve_triangular)/triangular_solve | solution.py:32
  435.5 2.0 fusion.48
  440.9 11.7 %cholesky.392 = f32[128,128]{1,0:T(8,128)S(1)} custom-call(f32[128,128]{1,0:T(8,128)S(1)} %cholesky.434), custom_call_target="Cholesky" | custom-call | tf_op jit(solution)/shard_map/jit(cholesky)/cholesky | solution.py:31
  452.7 9.8 %custom-call.30 = f32[1,128,128]{1,2,0:T(8,128)S(1)} custom-call(f32[1,128,128]{2,1,0:T(8,128)S(1)} %get-tuple-element.123), custom_call_target="InvertDiagBlocksLowerTriangular" | custom-call | tf_op jit(solution)/shard_map/jit(cholesky)/cholesky | solution.py:31
  464.6 11.7 %cholesky.409 = f32[128,128]{1,0:T(8,128)S(1)} custom-call(f32[128,128]{1,0:T(8,128)S(1)} %convolution_subtract_fusion.1), custom_call_target="Cholesky" | custom-call | tf_op jit(solution)/shard_map/jit(cholesky)/cholesky | solution.py:31
  478.8 2.2 fusion.10
  484.5 5.3 while.13
  485.1 2.1 bitcast_dynamic-update-slice_fusion.14
  487.8 2.0 bitcast_dynamic-update-slice_fusion.14
  489.8 20.3 %custom-call.31 = f32[2,128,128]{1,2,0:T(8,128)} custom-call(f32[2,128,128]{2,1,0:T(8,128)S(1)} %get-tuple-element.41), custom_call_target="InvertDiagBlocksLowerTriangular" | custom-call | tf_op jit(solution)/shard_map/jit(_solve_triangular)/triangular_solve | solution.py:32
  515.9 22.0 %collective-permute-done.9 = f32[256,512]{1,0:T(8,128)S(1)} collective-permute-done((f32[256,512]{1,0:T(8,128)S(1)}, f32[256,512]{1,0:T(8,128)S(1)}, u32[]{:S(2)}, u32[]{:S(2)}) %collective-permute-start.9) | collective-permute-done | bytes 524320 | tf_op jit(solution)/shard_map/ppermute | solution.py:26
  (204 shorter events, 91.4 us)
Async XLA Ops:
  7.2 85.0 %copy-start = (f32[3,3,256,256]{3,2,1,0:T(8,128)S(1)}, f32[3,3,256,256]{3,2,1,0:T(8,128)}, u32[]{:S(2)}) copy-start(f32[3,3,256,256]{3,2,1,0:T(8,128)} %param.11) | copy-start | bytes 7077892
  7.2 115.8 %all-reduce.3.cloned.1.call-start = ((), (), s32[]{:S(2)}) async-start(), calls=%async_computation | async-start | bytes 1572864 | tf_op jit(solution)/shard_map/psum | solution.py:51
  7.2 72.7 %collective-permute-start = (f32[768,512]{1,0:T(8,128)}, f32[768,512]{1,0:T(8,128)}, u32[]{:S(2)}, u32[]{:S(2)}) collective-permute-start(f32[768,512]{1,0:T(8,128)} %param.10), channel_id=1, source_target_pairs={{0,2},{2,4},{4,6},{6,8},{8,10},{10,12},{12,14},{14,16},{16,18},{18... | collective-permute-start | bytes 4718600 | tf_op jit(solution)/shard_map/ppermute | solution.py:17
  13.4 68.5 %collective-permute-start.1 = (f32[768,512]{1,0:T(8,128)}, f32[768,512]{1,0:T(8,128)}, u32[]{:S(2)}, u32[]{:S(2)}) collective-permute-start(f32[768,512]{1,0:T(8,128)} %param.10), channel_id=1, source_target_pairs={{2,0},{4,2},{6,4},{8,6},{10,8},{12,10},{14,12},{16,14},{18,16},{20... | collective-permute-start | bytes 4718600 | tf_op jit(solution)/shard_map/ppermute | solution.py:20
  92.2 7.5 %copy-start.13 = (f32[768,512]{1,0:T(8,128)S(1)}, f32[768,512]{1,0:T(8,128)}, u32[]{:S(2)}) copy-start(f32[768,512]{1,0:T(8,128)} %param.9) | copy-start | bytes 4718596
  99.7 1.5 copy-start.25
  100.1 1.1 copy-start.1
  126.6 69.9 %copy-start.3 = (f32[768,256]{1,0:T(8,128)S(1)}, f32[768,256]{1,0:T(8,128)}, u32[]{:S(2)}) copy-start(f32[768,256]{1,0:T(8,128)} %all-reduce.3.cloned.1.call-done) | copy-start | bytes 2359300
  127.7 0.7 copy-start.20
  165.9 2.7 copy-start.15
  170.3 32.7 %collective-permute-start.2 = (f32[256,256]{0,1:T(8,128)}, f32[256,256]{0,1:T(8,128)}, u32[]{:S(2)}, u32[]{:S(2)}) collective-permute-start(f32[256,256]{0,1:T(8,128)} %get-tuple-element.118), channel_id=1, source_target_pairs={{0,2},{2,0},{4,6},{6,4},{8,10},{10,8},{12,14},{14,12},{16,18},{18,... | collective-permute-start | bytes 786440 | tf_op jit(solution)/shard_map/ppermute | solution.py:26
  196.4 2.3 copy-start.27
  196.4 2.8 copy-start.2
  201.6 149.6 %collective-permute-start.3 = (f32[256,512]{1,0:T(8,128)}, f32[256,512]{1,0:T(8,128)}, u32[]{:S(2)}, u32[]{:S(2)}) collective-permute-start(f32[256,512]{1,0:T(8,128)} %fusion.21), channel_id=1, source_target_pairs={{0,2},{2,0},{4,6},{6,4},{8,10},{10,8},{12,14},{14,12},{16,18},{18,... | collective-permute-start | bytes 1572872 | tf_op jit(solution)/shard_map/ppermute | solution.py:26
  204.9 0.7 copy-start.21
  231.0 41.3 %copy-start.10 = (f32[256,512]{1,0:T(8,128)S(1)}, f32[256,512]{1,0:T(8,128)}, u32[]{:S(2)}) copy-start(f32[256,512]{1,0:T(8,128)} %fusion.41) | copy-start | bytes 1572868
  247.1 27.2 %collective-permute-start.4 = (f32[256,256]{0,1:T(8,128)}, f32[256,256]{0,1:T(8,128)}, u32[]{:S(2)}, u32[]{:S(2)}) collective-permute-start(f32[256,256]{0,1:T(8,128)} %get-tuple-element.116), channel_id=1, source_target_pairs={{0,4},{2,6},{4,0},{6,2},{8,12},{10,14},{12,8},{14,10},{16,20},{18,... | collective-permute-start | bytes 786440 | tf_op jit(solution)/shard_map/ppermute | solution.py:26
  277.8 0.7 copy-start.22
  303.9 42.9 %copy-start.11 = (f32[256,512]{1,0:T(8,128)S(1)}, f32[256,512]{1,0:T(8,128)}, u32[]{:S(2)}) copy-start(f32[256,512]{1,0:T(8,128)} %fusion.39) | copy-start | bytes 1572868
  316.6 2.5 copy-start.16
  321.2 33.0 %collective-permute-start.6 = (f32[256,256]{0,1:T(8,128)}, f32[256,256]{0,1:T(8,128)}, u32[]{:S(2)}, u32[]{:S(2)}) collective-permute-start(f32[256,256]{0,1:T(8,128)} %get-tuple-element.114), channel_id=1, source_target_pairs={{0,8},{2,10},{4,12},{6,14},{8,0},{10,2},{12,4},{14,6},{16,24},{18,... | collective-permute-start | bytes 786440 | tf_op jit(solution)/shard_map/ppermute | solution.py:26
  346.8 5.7 %copy-start.19 = (f32[128,512]{1,0:T(8,128)S(1)}, f32[128,512]{1,0:T(8,128)}, u32[]{:S(2)}) copy-start(f32[128,512]{1,0:T(8,128)} %fusion.54) | copy-start | bytes 786436
  348.1 0.7 copy-start.7
  353.5 124.1 %collective-permute-start.5 = (f32[256,512]{1,0:T(8,128)S(1)}, f32[256,512]{1,0:T(8,128)}, u32[]{:S(2)}, u32[]{:S(2)}) collective-permute-start(f32[256,512]{1,0:T(8,128)S(1)} %fusion.6), channel_id=1, source_target_pairs={{0,4},{2,6},{4,0},{6,2},{8,12},{10,14},{12,8},{14,10},{16,20},{18,... | collective-permute-start | bytes 1572872 | tf_op jit(solution)/shard_map/ppermute | solution.py:26
  355.2 0.7 copy-start.6
  358.4 0.7 copy-start.23
  385.4 47.5 %copy-start.12 = (f32[256,512]{1,0:T(8,128)S(1)}, f32[256,512]{1,0:T(8,128)}, u32[]{:S(2)}) copy-start(f32[256,512]{1,0:T(8,128)} %fusion.37) | copy-start | bytes 1572868
  404.5 33.0 %collective-permute-start.8 = (f32[256,256]{0,1:T(8,128)}, f32[256,256]{0,1:T(8,128)}, u32[]{:S(2)}, u32[]{:S(2)}) collective-permute-start(f32[256,256]{0,1:T(8,128)} %get-tuple-element.112), channel_id=1, source_target_pairs={{0,16},{2,18},{4,20},{6,22},{8,24},{10,26},{12,28},{14,30},{16,0},... | collective-permute-start | bytes 786440 | tf_op jit(solution)/shard_map/ppermute | solution.py:26
  434.2 3.3 copy-start.8
  438.6 0.7 copy-start.4
  438.6 0.8 copy-start.5
  440.1 0.7 copy-start.24
  476.3 2.5 copy-start.17
  476.4 2.4 copy-start.14
  481.0 30.2 %collective-permute-start.7 = (f32[256,512]{1,0:T(8,128)S(1)}, f32[256,512]{1,0:T(8,128)}, u32[]{:S(2)}, u32[]{:S(2)}) collective-permute-start(f32[256,512]{1,0:T(8,128)S(1)} %fusion.10), channel_id=1, source_target_pairs={{0,8},{2,10},{4,12},{6,14},{8,0},{10,2},{12,4},{14,6},{16,24},{18,... | collective-permute-start | bytes 1572872 | tf_op jit(solution)/shard_map/ppermute | solution.py:26
  510.1 2.3 copy-start.9
  510.1 2.4 copy-start.18
  511.3 2.6 copy-start.26
  513.6 24.4 %collective-permute-start.9 = (f32[256,512]{1,0:T(8,128)S(1)}, f32[256,512]{1,0:T(8,128)S(1)}, u32[]{:S(2)}, u32[]{:S(2)}) collective-permute-start(f32[256,512]{1,0:T(8,128)S(1)} %fusion.14), channel_id=1, source_target_pairs={{0,16},{2,18},{4,20},{6,22},{8,24},{10,26},{12,28},{14,30},{16,0},... | collective-permute-start | bytes 1572872 | tf_op jit(solution)/shard_map/ppermute | solution.py:26
Sparse Core Ops, SparseCore 0:
  103.7 19.2 all-reduce.2
where the time goes:
time: 553 us; the launch traced here: 548 us
  other arithmetic  310 us (56%)
  waiting for transfers between devices  108 us (20%)
  matrix products  51.3 us (9%)
  local copies, waits for them, and re-layouts  40.5 us (7%)
  between operations  21.2 us (4%)
  starting transfers between devices  16.7 us (3%)
    another operation x35, other arithmetic, factor_and_rows(): lower_factor = jnp.linalg.cholesky(gram_matrix)  178 us
    another operation x7, other arithmetic, factor_and_rows(): jax.scipy.linalg.solve_triangular(lower_factor, sketched.T, lower=True)  103 us
    ppermute x1, waiting for transfers between devices, extended(): lax.ppermute(lax.slice_in_dim(block, block.shape[dim] - width, None, axis...  64.4 us
    ppermute x8, waiting for transfers between devices, from_partner(): lax.ppermute(value, axis, [(i, i ^ 1 << bit) for i in range(lax.axis_size...  22 us
    psum x1, waiting for transfers between devices, shards(): sketched = lax.psum(partial_value, 'samp')  19.4 us
    another operation x25, local copies, waits for them, and re-layouts, factor_and_rows(): jax.scipy.linalg.solve_triangular(lower_factor, sketched.T, lower=True)  18.4 us
    another operation x15, matrix products, factor_and_rows(): jax.scipy.linalg.solve_triangular(lower_factor, sketched.T, lower=True)  14.9 us
    another operation x10, matrix products, factor_and_rows(): lower_factor = jnp.linalg.cholesky(gram_matrix)  13.7 us
  transfers between devices with their start and end apart: 11, of which 4 were waited for; matrix products, arithmetic and copies ran while one was open for 59% of the time, Pallas kernels for 0%

commit v1 on v0

v1 whole, which is shorter than its diff:
```python
import functools

import jax
import jax.numpy as jnp
from jax import lax
from jax.experimental import pallas as pl
from jax.experimental.pallas import tpu as pltpu
from jax.sharding import PartitionSpec as P

LEVELS = 4
LANES = 128
BASE = 32
NN = ((1,), (0,))
NT = ((1,), (1,))
TN = ((0,), (0,))
HIGH = lax.Precision.HIGH


def split(value):
    high = value.astype(jnp.bfloat16)
    return high, (value - high.astype(jnp.float32)).astype(jnp.bfloat16)


def dot3(left, right, dims):
    lh, ll = split(left)
    rh, rl = split(right)

    def product(a, b):
        return lax.dot_general(a, b, (dims, ((), ())), preferred_element_type=jnp.float32)

    return product(lh, rh) + (product(lh, rl) + product(ll, rh))


def pad_rows(block, start, total):
    parts = []
    if start:
        parts.append(jnp.zeros((start, block.shape[1]), block.dtype))
    parts.append(block)
    rest = total - start - block.shape[0]
    if rest:
        parts.append(jnp.zeros((rest, block.shape[1]), block.dtype))
    return jnp.concatenate(parts, axis=0) if len(parts) > 1 else block


def leaf_factor(work, out, start, base):
    tile = start // LANES * LANES
    off = start - tile
    lane = lax.broadcasted_iota(jnp.int32, (base, LANES), 1)
    row = lax.broadcasted_iota(jnp.int32, (base, LANES), 0)
    col = lane % base
    seg = lane // base
    packed = jnp.where(col == row, 1.0, 0.0)
    for k in range(len(work)):
        block = work[k][start : start + base, tile : tile + LANES]
        shift = (base * k - off) % LANES
        if shift:
            block = pltpu.roll(block, shift, 1)
        packed = jnp.where(seg == k, block, packed)
    pivots = jnp.ones((base, LANES), jnp.float32)
    for j in range(base):
        column = jnp.take_along_axis(packed, seg * base + j, axis=1)
        pivot = column[j : j + 1, :]
        pivots = jnp.where(row == j, pivot, pivots)
        if j == base - 1:
            break
        low = j // 8 * 8
        below = row[low:] > j
        mult = jnp.where(below, column[low:] * (1.0 / pivot), 0.0)
        pivot_row = jnp.where(col[:1] == j, 1.0, packed[j : j + 1, :])
        kept = jnp.where(below & (col[low:] == j), 0.0, packed[low:])
        new = kept - mult * pivot_row
        packed = new if low == 0 else jnp.concatenate([packed[:low], new], axis=0)
    unit = jnp.where(col < row, packed, jnp.where(col == row, 1.0, 0.0))
    unit = unit * lax.rsqrt(pivots)
    inside = (lane >= off) & (lane < off + base)
    for k in range(len(work)):
        shift = (off - base * k) % LANES
        block = pltpu.roll(unit, shift, 1) if shift else unit
        out[k][start : start + base, tile : tile + LANES] = jnp.where(inside, block, 0.0)


def node_factor(work, out, start, size, base):
    if size == base:
        leaf_factor(work, out, start, base)
        return
    half = size // 2
    mid = start + half
    end = start + size
    node_factor(work, out, start, half, base)
    t1 = start // LANES * LANES
    t2 = mid // LANES * LANES
    width = max(LANES, half)
    kept = []
    for k in range(len(work)):
        x1 = out[k][start:mid, t1 : t1 + width]
        l21 = dot3(work[k][mid:end, t1 : t1 + width], x1, NT)
        work[k][mid:end, t2 : t2 + width] -= dot3(l21, pad_rows(l21, mid - t2, width), NT)
        kept.append(dot3(l21, x1, NN))
    node_factor(work, out, mid, half, base)
    for k in range(len(work)):
        x2 = out[k][mid:end, t2 : t2 + width]
        m21 = dot3(x2, pad_rows(kept[k], mid - t2, width), NN)
        out[k][mid:end, t1 : t1 + width] = x2 - m21 if t1 == t2 else -m21


def inverse_kernel(count, size, *refs):
    ins, outs, work = refs[:count], refs[count : 2 * count], refs[2 * count :]
    for k in range(count):
        work[k][...] = ins[k][...]
        for t in range(0, size, LANES):
            outs[k][:, t : t + LANES] = jnp.zeros((size, LANES), jnp.float32)
    node_factor(work, outs, 0, size, BASE)


def factor_inverse(grams):
    count, size = len(grams), grams[0].shape[0]
    spec = pl.BlockSpec(memory_space=pltpu.VMEM)
    return pl.pallas_call(
        functools.partial(inverse_kernel, count, size),
        out_shape=[jax.ShapeDtypeStruct((size, size), jnp.float32)] * count,
        in_specs=[spec] * count,
        out_specs=[spec] * count,
        scratch_shapes=[pltpu.VMEM((size, size), jnp.float32)] * count,
        cost_estimate=pl.CostEstimate(flops=30 * 10**9, bytes_accessed=8 * count * size**2, transcendentals=0),
        name="factor_inverse",
    )(*grams)


def near_kernel(groups, block_count, slot_count, index_ref, count_ref, *refs):
    blocks_ref, base_ref = refs[0], refs[1]
    pieces = refs[2 : 2 + groups]
    out_ref, ext, sems = refs[2 + groups :]
    copies = []
    at = 0
    for g in range(groups):
        depth = pieces[g].shape[0]
        copies.append(pltpu.make_async_copy(pieces[g], ext.at[pl.ds(at, depth)], sems.at[g]))
        at += depth
    for copy in copies:
        copy.start()
    for copy in copies:
        copy.wait()
    size = blocks_ref.shape[2]
    for b in range(block_count):
        rows = pl.ds(b * size, size)
        out_ref[rows, :] = base_ref[rows, :]
        for j in range(slot_count):

            @pl.when(j < count_ref[b])
            def _(b=b, j=j, rows=rows):
                start = pl.multiple_of(index_ref[b, j] * size, size)
                piece = ext[pl.ds(start, size), :]
                out_ref[rows, :] -= dot3(blocks_ref[b, j], piece, NN)


def near_apply(blocks, base, pieces, index, count):
    block_count, slot_count, size, _ = blocks.shape
    rows, width = base.shape
    total = sum(piece.shape[0] for piece in pieces)
    vmem = pl.BlockSpec(memory_space=pltpu.VMEM)
    smem = pl.BlockSpec(memory_space=pltpu.SMEM)
    hbm = pl.BlockSpec(memory_space=pl.ANY)
    return pl.pallas_call(
        functools.partial(near_kernel, len(pieces), block_count, slot_count),
        out_shape=jax.ShapeDtypeStruct((rows, width), jnp.float32),
        in_specs=[smem, smem, vmem, vmem] + [hbm] * len(pieces),
        out_specs=vmem,
        scratch_shapes=[
            pltpu.VMEM((total, width), jnp.float32),
            pltpu.SemaphoreType.DMA((len(pieces),)),
        ],
        cost_estimate=pl.CostEstimate(
            flops=6 * block_count * slot_count * size * size * width,
            bytes_accessed=4 * (total * width + 2 * rows * width + blocks.size),
            transcendentals=0,
        ),
        name="near_apply",
    )(index, count, blocks, base, *pieces)


def across(value, axis, bit):
    return lax.ppermute(value, axis, [(i, i ^ 1 << bit) for i in range(lax.axis_size(axis))])


def relayed(value, axis):
    count = lax.axis_size(axis)
    steps = [(i, i + 2 if i % 2 == 0 else i - 2) for i in range(count)]
    return lax.ppermute(value, axis, [(i, t) for i, t in steps if 0 <= t < count])


def halo(own, parts):
    rows = own.shape[0] // parts
    peer = [across(own[i * rows : (i + 1) * rows], "rows", 0) for i in range(parts)]
    far = [relayed(piece, "rows") for piece in peer]
    return far + [own] + peer


def pick(flag, first, second):
    return jnp.where(flag, second, first)


def shards(samples, probes, near_blocks, near_cols, near_count, sketch):
    rows_dev, samp_dev = samples.shape
    block_size = near_blocks.shape[2]
    block_count = rows_dev // block_size
    rank = sketch.shape[1]
    position = lax.axis_index("rows")
    bits = [position >> h & 1 == 1 for h in range(LEVELS)]
    halves = 2 if lax.axis_size("samp") == 2 else 1
    core = lax.axis_index("samp") % 2 == 1

    index = near_cols - (position * block_count - block_count)
    swapped = jnp.where(index < block_count, index + 2 * block_count, jnp.where(index >= 2 * block_count, index - 2 * block_count, index))
    index = jnp.where(bits[0], swapped, index)

    probe_pieces = halo(probes, block_count)

    if halves == 2:
        width = rank // 2
        turned = pick(core, sketch, jnp.concatenate([sketch[:, width:], sketch[:, :width]], axis=1))
        probe_part = jnp.dot(probes, turned, precision=HIGH)
        sample_part = jnp.dot(samples, turned, precision=HIGH)
        got_probe = across(probe_part[:, width:], "samp", 0)
        got_sample = across(sample_part[:, width:], "samp", 0)
        probe_sketch = probe_part[:, :width] + got_probe
        sample_sketch = sample_part[:, :width] + got_sample
    else:
        width = rank
        probe_sketch = lax.psum(jnp.dot(probes, sketch, precision=HIGH), "samp")
        sample_sketch = lax.psum(jnp.dot(samples, sketch, precision=HIGH), "samp")
    mine = near_apply(near_blocks, sample_sketch, halo(probe_sketch, 1), index, near_count)
    if halves == 2:
        other = across(mine, "samp", 0)
        leaf_sketch = jnp.concatenate([pick(core, mine, other), pick(core, other, mine)], axis=1)
    else:
        leaf_sketch = mine

    gram = jnp.einsum("rk,rl->kl", leaf_sketch, leaf_sketch, precision=HIGH)
    part = pick(core, gram[:, :width], gram[:, rank - width :])
    sums = []
    for h in range(LEVELS):
        part = part + across(part, "rows", h)
        sums.append(part)
    sums = jnp.stack(sums)
    if halves == 2:
        other = across(sums, "samp", 0)
        sums = jnp.concatenate([pick(core, sums, other), pick(core, other, sums)], axis=2)
    (leaf_inverse,) = factor_inverse([gram])
    inverses = factor_inverse([sums[h] for h in range(LEVELS)])
    leaf_basis = lax.dot_general(leaf_sketch, leaf_inverse, (NT, ((), ())), precision=HIGH)

    far_samples = near_apply(near_blocks, samples, probe_pieces, index, near_count)
    product = jnp.einsum("rk,rs->ks", leaf_sketch, far_samples, precision=HIGH)

    def keep_send(value, bit):
        half = value.shape[0] // 2
        return pick(bit, value[:half], value[half:]), pick(bit, value[half:], value[:half])

    def joined(value, bit, level):
        other = across(value, "rows", level)
        return jnp.concatenate([pick(bit, value, other), pick(bit, other, value)], axis=-2)

    keep, send = keep_send(product, bits[0])
    first = keep + across(send, "rows", 0)
    keep, send = keep_send(first, bits[1])
    quarter = keep + across(send, "rows", 1)
    quarters = [quarter]
    for h in range(2, LEVELS):
        quarter = quarter + across(quarter, "rows", h)
        quarters.append(quarter)
    outputs = [joined(first, bits[0], 0)]
    early = joined(joined(jnp.stack(quarters[:2]), bits[1], 1), bits[0], 0)
    outputs += [early[0], early[1]]
    outputs += [joined(joined(value, bits[1], 1), bits[0], 0) for value in quarters[2:]]
    reduced = [jnp.dot(inverse, value, precision=HIGH) for inverse, value in zip(inverses, outputs)]
    return (leaf_basis, jnp.stack(reduced)[:, None, :, :])


def solution(mesh):
    return jax.shard_map(
        shards,
        mesh=mesh,
        in_specs=(
            P("rows", "samp"),
            P("rows", "samp"),
            P("rows", None, None, None),
            P("rows", None),
            P("rows"),
            P("samp", None),
        ),
        out_specs=(P("rows", None), P(None, "rows", None, "samp")),
        check_vma=False,
    )
```

time: 553 us -> 187 us (0.34)
  other arithmetic: 310 us -> 6.77 us
  Pallas kernels: 0 us -> 71.2 us
  waiting for transfers between devices: 108 us -> 45.8 us
  matrix products: 51.3 us -> 8.85 us
  local copies, waits for them, and re-layouts: 40.5 us -> 4.98 us
  starting transfers between devices: 16.7 us -> 47.2 us
  between operations: 21.2 us -> 1.13 us
    another operation x42 -> x3, other arithmetic: 280 us -> 0.07 us  [the longest x2 0.05 us: shards(): sums = jnp.stack(sums)]
    pallas_call x0 -> x4, Pallas kernels: none -> 71.2 us  [the longest x2 58.4 us: factor_inverse(): pl.pallas_call(functools.partial(inverse_kernel, count, size), out_shape=...]
    ppermute x10 -> x25, waiting for transfers between devices: 88.3 us -> 45.8 us  [the longest x21 37.1 us: across(): lax.ppermute(value, axis, [(i, i ^ 1 << bit) for i in range(lax.axis_size...]
    ppermute x10 -> x25, starting transfers between devices: 16.6 us -> 47.2 us  [the longest x21 30 us: across(): lax.ppermute(value, axis, [(i, i ^ 1 << bit) for i in range(lax.axis_size...]
    another operation x25 -> x0, matrix products: 28.6 us -> none  [the longest x15 14.9 us: factor_and_rows(): jax.scipy.linalg.solve_triangular(lower_factor, sketched.T, lower=True)]
    another operation x49 -> x0, local copies, waits for them, and re-layouts: 24.2 us -> none  [the longest x25 18.4 us: factor_and_rows(): jax.scipy.linalg.solve_triangular(lower_factor, sketched.T, lower=True)]
    psum x1 -> x0, waiting for transfers between devices: 19.4 us -> none  [shards(): sketched = lax.psum(partial_value, 'samp')]
    dot_general x12 -> x9, matrix products: 22.7 us -> 8.85 us  [the longest x4 2.52 us: shards(): jnp.dot(inverse, value, precision=HIGH)]
  transfers between devices with their start and end apart: 11 -> 25, of which waited for: 4 -> 11; matrix products, arithmetic and copies ran while one was open for 59% -> 5% of each run, Pallas kernels for 0% -> 38%
where the time goes in v1:
time: 187 us; the launch traced here: 186 us
  Pallas kernels  71.2 us (38%)
  starting transfers between devices  47.2 us (25%)
  waiting for transfers between devices  45.8 us (24%)
  matrix products  8.85 us (5%)
  other arithmetic  6.77 us (4%)
  local copies, waits for them, and re-layouts  4.98 us (3%)
    pallas_call x2, Pallas kernels, factor_inverse(): pl.pallas_call(functools.partial(inverse_kernel, count, size), out_shape=...  58.4 us
    ppermute x21, waiting for transfers between devices, across(): lax.ppermute(value, axis, [(i, i ^ 1 << bit) for i in range(lax.axis_size...  37.1 us
    ppermute x21, starting transfers between devices, across(): lax.ppermute(value, axis, [(i, i ^ 1 << bit) for i in range(lax.axis_size...  30 us
    ppermute x4, starting transfers between devices, relayed(): lax.ppermute(value, axis, [(i, t) for i, t in steps if 0 <= t < count])  17.2 us
    pallas_call x2, Pallas kernels, near_apply(): pl.pallas_call(functools.partial(near_kernel, len(pieces), block_count, s...  12.9 us
    ppermute x4, waiting for transfers between devices, relayed(): lax.ppermute(value, axis, [(i, t) for i, t in steps if 0 <= t < count])  8.68 us
  transfers between devices with their start and end apart: 25, of which 11 were waited for; matrix products, arithmetic and copies ran while one was open for 5% of the time, Pallas kernels for 38%

profile of v1, /device:TPU:0, one launch (start us, length us, event | category | flops | bytes accessed | tf_op | source)
XLA Modules:
  0.0 185.9 jit_solution(4047046533367278785)
XLA Ops:
  0.6 1.1 fusion.34
  1.7 2.5 %convolution_bitcast_fusion = f32[768,256]{1,0:T(8,128)S(1)} fusion(f32[768,512]{1,0:T(8,128)} %refs_5_.1, f32[512,256]{1,0:T(8,128)} %param.11, f32[512,128]{1,0:T(8,128)S(1)} %get-tuple-element.32, f32[512,128]{1,0:T(8,128)S(1)} %get-tuple-element.31, pred[]{:T(512)S(6)} %eq.11), kind=kOutput, calls=%fused_computation.7 | convolution fusion | flops 604241920 | bytes 3407873 | tf_op jit(solution)/shard_map/dot_general | solution.py:221
  4.7 1.1 fusion.33
  5.8 2.6 %collective-permute-start.10 = (f32[256,512]{1,0:T(8,128)S(1)}, f32[256,512]{1,0:T(8,128)S(1)}, u32[]{:S(2)}, u32[]{:S(2)}) collective-permute-start(f32[256,512]{1,0:T(8,128)S(1)} %get-tuple-element.14), channel_id=1, source_target_pairs={{0,2},{2,0},{4,6},{6,4},{8,10},{10,8},{12,14},{14,12},{16,18},{18,... | collective-permute-start | bytes 1572872 | tf_op jit(solution)/shard_map/ppermute | solution.py:182
  8.5 2.0 %collective-permute-start.14 = (f32[256,512]{1,0:T(8,128)}, f32[256,512]{1,0:T(8,128)S(1)}, u32[]{:S(2)}, u32[]{:S(2)}) collective-permute-start(f32[256,512]{1,0:T(8,128)} %get-tuple-element.12), channel_id=1, source_target_pairs={{0,2},{2,0},{4,6},{6,4},{8,10},{10,8},{12,14},{14,12},{16,18},{18,... | collective-permute-start | bytes 1572872 | tf_op jit(solution)/shard_map/ppermute | solution.py:182
  10.7 0.8 convolution_bitcast_fusion.1
  11.5 0.8 slice.89
  12.3 9.0 %collective-permute-done.10.refs_6_ = f32[256,512]{1,0:T(8,128)S(1)} collective-permute-done((f32[256,512]{1,0:T(8,128)S(1)}, f32[256,512]{1,0:T(8,128)S(1)}, u32[]{:S(2)}, u32[]{:S(2)}) %collective-permute-start.10) | collective-permute-done | bytes 524320 | tf_op jit(solution)/shard_map/ppermute | solution.py:182
  21.2 4.0 %collective-permute-start.11 = (f32[256,512]{1,0:T(8,128)S(1)}, f32[256,512]{1,0:T(8,128)S(1)}, u32[]{:S(2)}, u32[]{:S(2)}) collective-permute-start(f32[256,512]{1,0:T(8,128)S(1)} %collective-permute-done.10.refs_6_), channel_id=1, source_target_pairs={{0,4},{4,8},{6,2},{8,12},{10,6},{12,16},{14,10},{16,20},{18,14},{2... | collective-permute-start | bytes 1572872 | tf_op jit(solution)/shard_map/ppermute | solution.py:188
  25.2 7.2 %collective-permute-done.12.refs_7_ = f32[256,512]{1,0:T(8,128)S(1)} collective-permute-done((f32[256,512]{1,0:T(8,128)}, f32[256,512]{1,0:T(8,128)S(1)}, u32[]{:S(2)}, u32[]{:S(2)}) %collective-permute-start.12) | collective-permute-done | bytes 524320 | tf_op jit(solution)/shard_map/ppermute | solution.py:182
  32.5 4.7 %collective-permute-start.13 = (f32[256,512]{1,0:T(8,128)S(1)}, f32[256,512]{1,0:T(8,128)}, u32[]{:S(2)}, u32[]{:S(2)}) collective-permute-start(f32[256,512]{1,0:T(8,128)S(1)} %collective-permute-done.12.refs_7_), channel_id=1, source_target_pairs={{0,4},{4,8},{6,2},{8,12},{10,6},{12,16},{14,10},{16,20},{18,14},{2... | collective-permute-start | bytes 1572872 | tf_op jit(solution)/shard_map/ppermute | solution.py:188
  37.2 6.5 %collective-permute-done.14.refs_8_ = f32[256,512]{1,0:T(8,128)S(1)} collective-permute-done((f32[256,512]{1,0:T(8,128)}, f32[256,512]{1,0:T(8,128)S(1)}, u32[]{:S(2)}, u32[]{:S(2)}) %collective-permute-start.14) | collective-permute-done | bytes 524320 | tf_op jit(solution)/shard_map/ppermute | solution.py:182
  43.7 4.8 %collective-permute-start.15 = (f32[256,512]{1,0:T(8,128)S(1)}, f32[256,512]{1,0:T(8,128)}, u32[]{:S(2)}, u32[]{:S(2)}) collective-permute-start(f32[256,512]{1,0:T(8,128)S(1)} %collective-permute-done.14.refs_8_), channel_id=1, source_target_pairs={{0,4},{4,8},{6,2},{8,12},{10,6},{12,16},{14,10},{16,20},{18,14},{2... | collective-permute-start | bytes 1572872 | tf_op jit(solution)/shard_map/ppermute | solution.py:188
  48.5 3.6 %collective-permute-done.2.refs_4_ = f32[768,128]{1,0:T(8,128)} collective-permute-done((f32[768,128]{1,0:T(8,128)S(1)}, f32[768,128]{1,0:T(8,128)}, u32[]{:S(2)}, u32[]{:S(2)}) %collective-permute-start.2) | collective-permute-done | bytes 393248 | tf_op jit(solution)/shard_map/ppermute | solution.py:182
  52.0 3.7 %collective-permute-start.3 = (f32[768,128]{1,0:T(8,128)}, f32[768,128]{1,0:T(8,128)S(1)}, u32[]{:S(2)}, u32[]{:S(2)}) collective-permute-start(f32[768,128]{1,0:T(8,128)} %collective-permute-done.2.refs_4_), channel_id=1, source_target_pairs={{0,4},{4,8},{6,2},{8,12},{10,6},{12,16},{14,10},{16,20},{18,14},{2... | collective-permute-start | bytes 1179656 | tf_op jit(solution)/shard_map/ppermute | solution.py:188
  55.8 0.6 fusion.23.index_ref
  56.3 1.8 slice_add_fusion.1.refs_1_
  58.1 8.7 %collective-permute-done.3.refs_2_ = f32[768,128]{1,0:T(8,128)S(1)} collective-permute-done((f32[768,128]{1,0:T(8,128)}, f32[768,128]{1,0:T(8,128)S(1)}, u32[]{:S(2)}, u32[]{:S(2)}) %collective-permute-start.3) | collective-permute-done | bytes 393248 | tf_op jit(solution)/shard_map/ppermute | solution.py:188
  66.8 0.7 copy-done.12
  67.5 5.0 %near_apply.2 = f32[768,128]{1,0:T(8,128)} custom-call(s32[3,3]{1,0:T(4,128)} %fusion.23.index_ref, s32[3]{0:T(128)} %count_ref.3, f32[3,3,256,256]{3,2,1,0:T(8,128)} %refs_0_.3, f32[768,128]{1,0:T(8,128)} %slice_add_fusion.1.refs_1_, f32[768,128]{1,0:T(8,128)} %copy-done.12, f32[768,128]{1,0:T(8,128)} %copy-done.6, f32[768,128]{1,0:T(8,128)} %collective-permute-done.2.refs_4_), custom_call_target="tpu_custom_call" | custom-call | flops 452984832 | bytes 4325376 | tf_op jit(solution)/shard_map/near_apply/pallas_call | solution.py:163
  72.7 0.8 copy-done.11
  73.5 7.8 %near_apply.3 = f32[768,512]{1,0:T(8,128)} custom-call(s32[3,3]{1,0:T(4,128)} %fusion.23.index_ref, s32[3]{0:T(128)} %count_ref.3, f32[3,3,256,256]{3,2,1,0:T(8,128)} %refs_0_.3, f32[768,512]{1,0:T(8,128)} %refs_1_.1, f32[256,512]{1,0:T(8,128)} %copy-done.11, f32[256,512]{1,0:T(8,128)} %collective-permute-done.13.refs_3_, ...), custom_call_target="tpu_custom_call" | custom-call | flops 1811939328 | bytes 10223616 | tf_op jit(solution)/shard_map/near_apply/pallas_call | solution.py:163
  81.4 1.2 broadcast_select_fusion.5
  82.6 0.8 fusion.14.refs_0_
  83.4 0.8 fusion.12
  84.3 4.9 %collective-permute-start.16 = (f32[128,512]{1,0:T(8,128)S(1)}, f32[128,512]{1,0:T(8,128)S(1)}, u32[]{:S(2)}, u32[]{:S(2)}) collective-permute-start(f32[128,512]{1,0:T(8,128)S(1)} %slice_select_fusion), channel_id=1, source_target_pairs={{0,2},{2,0},{4,6},{6,4},{8,10},{10,8},{12,14},{14,12},{16,18},{18,... | collective-permute-start | bytes 786440 | tf_op jit(solution)/shard_map/ppermute | solution.py:182
  89.3 26.7 %factor_inverse.2 = f32[256,256]{1,0:T(8,128)} custom-call(f32[256,256]{1,0:T(8,128)} %copy-done.4), custom_call_target="tpu_custom_call" | custom-call | flops 30000001024 | bytes 524288 | tf_op jit(solution)/shard_map/factor_inverse/pallas_call | solution.py:118
  116.0 1.2 collective-permute-start.6
  117.3 2.1 %collective-permute-start.17 = (f32[128,512]{1,0:T(8,128)S(1)}, f32[128,512]{1,0:T(8,128)S(1)}, u32[]{:S(2)}, u32[]{:S(2)}) collective-permute-start(f32[128,512]{1,0:T(8,128)S(1)} %select_add_fusion), channel_id=1, source_target_pairs={{0,2},{2,0},{4,6},{6,4},{8,10},{10,8},{12,14},{14,12},{16,18},{18,... | collective-permute-start | bytes 786440 | tf_op jit(solution)/shard_map/ppermute | solution.py:182
  119.4 2.3 %collective-permute-done.6 = f32[256,128]{1,0:T(8,128)S(1)} collective-permute-done((f32[256,128]{1,0:T(8,128)S(1)}, f32[256,128]{1,0:T(8,128)S(1)}, u32[]{:S(2)}, u32[]{:S(2)}) %collective-permute-start.6) | collective-permute-done | bytes 131104 | tf_op jit(solution)/shard_map/ppermute | solution.py:182
  121.7 1.7 collective-permute-start.7
  123.4 1.8 collective-permute-start.18
  125.3 1.4 fusion.13
  126.8 2.1 %collective-permute-start.8 = (f32[256,128]{1,0:T(8,128)S(1)}, f32[256,128]{1,0:T(8,128)S(1)}, u32[]{:S(2)}, u32[]{:S(2)}) collective-permute-start(f32[256,128]{1,0:T(8,128)S(1)} %add.45), channel_id=1, source_target_pairs={{0,16},{2,18},{4,20},{6,22},{8,24},{10,26},{12,28},{14,30},{16,0},... | collective-permute-start | bytes 393224 | tf_op jit(solution)/shard_map/ppermute | solution.py:182
  128.9 2.1 %collective-permute-start.19 = (f32[64,512]{1,0:T(8,128)S(1)}, f32[64,512]{1,0:T(8,128)S(1)}, u32[]{:S(2)}, u32[]{:S(2)}) collective-permute-start(f32[64,512]{1,0:T(8,128)S(1)} %select_add_fusion.1), channel_id=1, source_target_pairs={{0,8},{2,10},{4,12},{6,14},{8,0},{10,2},{12,4},{14,6},{16,24},{18,... | collective-permute-start | bytes 393224 | tf_op jit(solution)/shard_map/ppermute | solution.py:182
  131.0 3.2 %collective-permute-done.19 = f32[64,512]{1,0:T(8,128)S(1)} collective-permute-done((f32[64,512]{1,0:T(8,128)S(1)}, f32[64,512]{1,0:T(8,128)S(1)}, u32[]{:S(2)}, u32[]{:S(2)}) %collective-permute-start.19) | collective-permute-done | bytes 131104 | tf_op jit(solution)/shard_map/ppermute | solution.py:182
  134.3 1.9 %collective-permute-start.22 = (f32[64,512]{1,0:T(8,128)S(1)}, f32[64,512]{1,0:T(8,128)S(1)}, u32[]{:S(2)}, u32[]{:S(2)}) collective-permute-start(f32[64,512]{1,0:T(8,128)S(1)} %add.49), channel_id=1, source_target_pairs={{0,16},{2,18},{4,20},{6,22},{8,24},{10,26},{12,28},{14,30},{16,0},... | collective-permute-start | bytes 393224 | tf_op jit(solution)/shard_map/ppermute | solution.py:182
  136.2 1.6 collective-permute-start.20
  137.9 3.7 %collective-permute-done.22 = f32[64,512]{1,0:T(8,128)S(1)} collective-permute-done((f32[64,512]{1,0:T(8,128)S(1)}, f32[64,512]{1,0:T(8,128)S(1)}, u32[]{:S(2)}, u32[]{:S(2)}) %collective-permute-start.22) | collective-permute-done | bytes 131104 | tf_op jit(solution)/shard_map/ppermute | solution.py:182
  141.6 1.5 collective-permute-start.23
  143.1 0.9 collective-permute-done.20
  144.1 2.0 %collective-permute-start.21 = (f32[2,128,512]{2,1,0:T(8,128)S(1)}, f32[2,128,512]{2,1,0:T(8,128)S(1)}, u32[]{:S(2)}, u32[]{:S(2)}) collective-permute-start(f32[2,128,512]{2,1,0:T(8,128)S(1)} %pad_maximum_fusion.3), channel_id=1, source_target_pairs={{0,2},{2,0},{4,6},{6,4},{8,10},{10,8},{12,14},{14,12},{16,18},{18,... | collective-permute-start | bytes 1572872 | tf_op jit(solution)/shard_map/ppermute | solution.py:182
  146.1 0.6 collective-permute-done.23
  146.7 1.8 collective-permute-start.24
  148.6 1.0 fusion.21
  149.6 31.7 %factor_inverse.3 = (f32[256,256]{1,0:T(8,128)}, f32[256,256]{1,0:T(8,128)}, f32[256,256]{1,0:T(8,128)}, f32[256,256]{1,0:T(8,128)}) custom-call(f32[256,256]{1,0:T(8,128)} %get-tuple-element.18.refs_0_, f32[256,256]{1,0:T(8,128)} %get-tuple-element.19.refs_1_, f32[256,256]{1,0:T(8,128)} %get-tuple-element.20.refs_2_, f32[256,256]{1,0:T(8,128)} %get-tuple-element.17.refs_3_), custom_call_target="tpu_custom_call" | custom-call | flops 30000001024 | bytes 2097152 | tf_op jit(solution)/shard_map/factor_inverse/pallas_call | solution.py:118
  181.2 1.4 convolution_bitcast_fusion.5
  184.4 1.5 maximum_bitcast_fusion
  (82 shorter events, 3.4 us)
Async XLA Ops:
  1.7 3.0 %copy-start = (f32[768,512]{1,0:T(8,128)S(1)}, f32[768,512]{1,0:T(8,128)}, u32[]{:S(2)}) copy-start(f32[768,512]{1,0:T(8,128)} %refs_5_.1) | copy-start | bytes 4718596
  4.3 6.4 %copy-start.1 = (f32[768,512]{1,0:T(8,128)S(1)}, f32[768,512]{1,0:T(8,128)}, u32[]{:S(2)}) copy-start(f32[768,512]{1,0:T(8,128)} %refs_1_.1) | copy-start | bytes 4718596
  4.3 6.4 %copy-start.3 = (f32[512,256]{1,0:T(8,128)S(1)}, f32[512,256]{1,0:T(8,128)}, u32[]{:S(2)}) copy-start(f32[512,256]{1,0:T(8,128)} %param.11) | copy-start | bytes 1572868
  4.3 6.2 %collective-permute-start.1 = (f32[768,128]{1,0:T(8,128)S(1)}, f32[768,128]{1,0:T(8,128)S(1)}, u32[]{:S(2)}, u32[]{:S(2)}) collective-permute-start(f32[768,128]{1,0:T(8,128)S(1)} %slice.91), channel_id=1, source_target_pairs={{0,1},{1,0},{2,3},{3,2},{4,5},{5,4},{6,7},{7,6},{8,9},{9,8},{10,11... | collective-permute-start | bytes 1179656 | tf_op jit(solution)/shard_map/ppermute | solution.py:182
  5.8 15.4 %collective-permute-start.10 = (f32[256,512]{1,0:T(8,128)S(1)}, f32[256,512]{1,0:T(8,128)S(1)}, u32[]{:S(2)}, u32[]{:S(2)}) collective-permute-start(f32[256,512]{1,0:T(8,128)S(1)} %get-tuple-element.14), channel_id=1, source_target_pairs={{0,2},{2,0},{4,6},{6,4},{8,10},{10,8},{12,14},{14,12},{16,18},{18,... | collective-permute-start | bytes 1572872 | tf_op jit(solution)/shard_map/ppermute | solution.py:182
  8.5 24.0 %collective-permute-start.12 = (f32[256,512]{1,0:T(8,128)}, f32[256,512]{1,0:T(8,128)S(1)}, u32[]{:S(2)}, u32[]{:S(2)}) collective-permute-start(f32[256,512]{1,0:T(8,128)} %get-tuple-element.13), channel_id=1, source_target_pairs={{0,2},{2,0},{4,6},{6,4},{8,10},{10,8},{12,14},{14,12},{16,18},{18,... | collective-permute-start | bytes 1572872 | tf_op jit(solution)/shard_map/ppermute | solution.py:182
  8.5 35.2 %collective-permute-start.14 = (f32[256,512]{1,0:T(8,128)}, f32[256,512]{1,0:T(8,128)S(1)}, u32[]{:S(2)}, u32[]{:S(2)}) collective-permute-start(f32[256,512]{1,0:T(8,128)} %get-tuple-element.12), channel_id=1, source_target_pairs={{0,2},{2,0},{4,6},{6,4},{8,10},{10,8},{12,14},{14,12},{16,18},{18,... | collective-permute-start | bytes 1572872 | tf_op jit(solution)/shard_map/ppermute | solution.py:182
  10.5 0.9 copy-start.6
  10.6 45.2 %copy-start.17 = (s32[3,3]{1,0:T(4,128)S(1)}, s32[3,3]{1,0:T(4,128)}, u32[]{:S(2)}) copy-start(s32[3,3]{1,0:T(4,128)} %param.9) | copy-start | bytes 112
  10.6 41.5 %collective-permute-start.2 = (f32[768,128]{1,0:T(8,128)S(1)}, f32[768,128]{1,0:T(8,128)}, u32[]{:S(2)}, u32[]{:S(2)}) collective-permute-start(f32[768,128]{1,0:T(8,128)S(1)} %slice_add_fusion.refs_3_), channel_id=1, source_target_pairs={{0,2},{2,0},{4,6},{6,4},{8,10},{10,8},{12,14},{14,12},{16,18},{18,... | collective-permute-start | bytes 1179656 | tf_op jit(solution)/shard_map/ppermute | solution.py:182
  12.3 44.1 %collective-permute-start = (f32[768,128]{1,0:T(8,128)}, f32[768,128]{1,0:T(8,128)}, u32[]{:S(2)}, u32[]{:S(2)}) collective-permute-start(f32[768,128]{1,0:T(8,128)} %slice.89), channel_id=1, source_target_pairs={{0,1},{1,0},{2,3},{3,2},{4,5},{5,4},{6,7},{7,6},{8,9},{9,8},{10,11... | collective-permute-start | bytes 1179656 | tf_op jit(solution)/shard_map/ppermute | solution.py:182
  21.2 51.3 %copy-start.8 = (f32[256,512]{1,0:T(8,128)}, f32[256,512]{1,0:T(8,128)S(1)}, u32[]{:S(2)}) copy-start(f32[256,512]{1,0:T(8,128)S(1)} %collective-permute-done.10.refs_6_) | copy-start | bytes 1572868
  21.2 51.5 %collective-permute-start.11 = (f32[256,512]{1,0:T(8,128)S(1)}, f32[256,512]{1,0:T(8,128)S(1)}, u32[]{:S(2)}, u32[]{:S(2)}) collective-permute-start(f32[256,512]{1,0:T(8,128)S(1)} %collective-permute-done.10.refs_6_), channel_id=1, source_target_pairs={{0,4},{4,8},{6,2},{8,12},{10,6},{12,16},{14,10},{16,20},{18,14},{2... | collective-permute-start | bytes 1572872 | tf_op jit(solution)/shard_map/ppermute | solution.py:188
  32.5 40.1 %copy-start.9 = (f32[256,512]{1,0:T(8,128)}, f32[256,512]{1,0:T(8,128)S(1)}, u32[]{:S(2)}) copy-start(f32[256,512]{1,0:T(8,128)S(1)} %collective-permute-done.12.refs_7_) | copy-start | bytes 1572868
  32.5 40.3 %collective-permute-start.13 = (f32[256,512]{1,0:T(8,128)S(1)}, f32[256,512]{1,0:T(8,128)}, u32[]{:S(2)}, u32[]{:S(2)}) collective-permute-start(f32[256,512]{1,0:T(8,128)S(1)} %collective-permute-done.12.refs_7_), channel_id=1, source_target_pairs={{0,4},{4,8},{6,2},{8,12},{10,6},{12,16},{14,10},{16,20},{18,14},{2... | collective-permute-start | bytes 1572872 | tf_op jit(solution)/shard_map/ppermute | solution.py:188
  43.7 28.9 %copy-start.10 = (f32[256,512]{1,0:T(8,128)}, f32[256,512]{1,0:T(8,128)S(1)}, u32[]{:S(2)}) copy-start(f32[256,512]{1,0:T(8,128)S(1)} %collective-permute-done.14.refs_8_) | copy-start | bytes 1572868
  43.7 29.0 %collective-permute-start.15 = (f32[256,512]{1,0:T(8,128)S(1)}, f32[256,512]{1,0:T(8,128)}, u32[]{:S(2)}, u32[]{:S(2)}) collective-permute-start(f32[256,512]{1,0:T(8,128)S(1)} %collective-permute-done.14.refs_8_), channel_id=1, source_target_pairs={{0,4},{4,8},{6,2},{8,12},{10,6},{12,16},{14,10},{16,20},{18,14},{2... | collective-permute-start | bytes 1572872 | tf_op jit(solution)/shard_map/ppermute | solution.py:188
  52.0 14.7 %collective-permute-start.3 = (f32[768,128]{1,0:T(8,128)}, f32[768,128]{1,0:T(8,128)S(1)}, u32[]{:S(2)}, u32[]{:S(2)}) collective-permute-start(f32[768,128]{1,0:T(8,128)} %collective-permute-done.2.refs_4_), channel_id=1, source_target_pairs={{0,4},{4,8},{6,2},{8,12},{10,6},{12,16},{14,10},{16,20},{18,14},{2... | collective-permute-start | bytes 1179656 | tf_op jit(solution)/shard_map/ppermute | solution.py:188
  66.8 0.7 copy-start.12
  72.6 8.8 %collective-permute-start.4 = (f32[768,128]{1,0:T(8,128)}, f32[768,128]{1,0:T(8,128)}, u32[]{:S(2)}, u32[]{:S(2)}) collective-permute-start(f32[768,128]{1,0:T(8,128)} %near_apply.2), channel_id=1, source_target_pairs={{0,1},{1,0},{2,3},{3,2},{4,5},{5,4},{6,7},{7,6},{8,9},{9,8},{10,11... | collective-permute-start | bytes 1179656 | tf_op jit(solution)/shard_map/ppermute | solution.py:182
  72.7 8.7 %copy-start.7 = (f32[768,128]{1,0:T(8,128)S(1)}, f32[768,128]{1,0:T(8,128)}, u32[]{:S(2)}) copy-start(f32[768,128]{1,0:T(8,128)} %near_apply.2) | copy-start | bytes 1179652
  72.7 0.8 copy-start.11
  81.4 2.0 %copy-start.2 = (f32[768,512]{1,0:T(8,128)S(1)}, f32[768,512]{1,0:T(8,128)}, u32[]{:S(2)}) copy-start(f32[768,512]{1,0:T(8,128)} %near_apply.3) | copy-start | bytes 4718596
  83.4 5.8 %copy-start.4 = (f32[256,256]{1,0:T(8,128)}, f32[256,256]{1,0:T(8,128)S(1)}, u32[]{:S(2)}) copy-start(f32[256,256]{1,0:T(8,128)S(1)} %fusion.14.refs_0_) | copy-start | bytes 786436
  84.3 33.0 %collective-permute-start.16 = (f32[128,512]{1,0:T(8,128)S(1)}, f32[128,512]{1,0:T(8,128)S(1)}, u32[]{:S(2)}, u32[]{:S(2)}) collective-permute-start(f32[128,512]{1,0:T(8,128)S(1)} %slice_select_fusion), channel_id=1, source_target_pairs={{0,2},{2,0},{4,6},{6,4},{8,10},{10,8},{12,14},{14,12},{16,18},{18,... | collective-permute-start | bytes 786440 | tf_op jit(solution)/shard_map/ppermute | solution.py:182
  89.2 26.8 %copy-start.5 = (f32[256,256]{1,0:T(8,128)S(1)}, f32[256,256]{1,0:T(8,128)}, u32[]{:S(2)}) copy-start(f32[256,256]{1,0:T(8,128)} %copy-done.4) | copy-start | bytes 786436
  89.2 26.8 %collective-permute-start.5 = (f32[256,128]{1,0:T(8,128)S(1)}, f32[256,128]{1,0:T(8,128)S(1)}, u32[]{:S(2)}, u32[]{:S(2)}) collective-permute-start(f32[256,128]{1,0:T(8,128)S(1)} %slice_select_fusion.1), channel_id=1, source_target_pairs={{0,2},{2,0},{4,6},{6,4},{8,10},{10,8},{12,14},{14,12},{16,18},{18,... | collective-permute-start | bytes 393224 | tf_op jit(solution)/shard_map/ppermute | solution.py:182
  116.0 9.3 %copy-start.14 = (f32[256,256]{1,0:T(8,128)S(1)}, f32[256,256]{1,0:T(8,128)}, u32[]{:S(2)}) copy-start(f32[256,256]{1,0:T(8,128)} %factor_inverse.2) | copy-start | bytes 786436
  116.0 5.7 %collective-permute-start.6 = (f32[256,128]{1,0:T(8,128)S(1)}, f32[256,128]{1,0:T(8,128)S(1)}, u32[]{:S(2)}, u32[]{:S(2)}) collective-permute-start(f32[256,128]{1,0:T(8,128)S(1)} %fusion.43), channel_id=1, source_target_pairs={{0,4},{2,6},{4,0},{6,2},{8,12},{10,14},{12,8},{14,10},{16,20},{18,... | collective-permute-start | bytes 393224 | tf_op jit(solution)/shard_map/ppermute | solution.py:182
  117.3 13.7 %collective-permute-start.17 = (f32[128,512]{1,0:T(8,128)S(1)}, f32[128,512]{1,0:T(8,128)S(1)}, u32[]{:S(2)}, u32[]{:S(2)}) collective-permute-start(f32[128,512]{1,0:T(8,128)S(1)} %select_add_fusion), channel_id=1, source_target_pairs={{0,2},{2,0},{4,6},{6,4},{8,10},{10,8},{12,14},{14,12},{16,18},{18,... | collective-permute-start | bytes 786440 | tf_op jit(solution)/shard_map/ppermute | solution.py:182
  121.7 5.0 %collective-permute-start.7 = (f32[256,128]{1,0:T(8,128)S(1)}, f32[256,128]{1,0:T(8,128)S(1)}, u32[]{:S(2)}, u32[]{:S(2)}) collective-permute-start(f32[256,128]{1,0:T(8,128)S(1)} %add.44), channel_id=1, source_target_pairs={{0,8},{2,10},{4,12},{6,14},{8,0},{10,2},{12,4},{14,6},{16,24},{18,... | collective-permute-start | bytes 393224 | tf_op jit(solution)/shard_map/ppermute | solution.py:182
  123.4 5.4 %collective-permute-start.18 = (f32[64,512]{1,0:T(8,128)S(1)}, f32[64,512]{1,0:T(8,128)S(1)}, u32[]{:S(2)}, u32[]{:S(2)}) collective-permute-start(f32[64,512]{1,0:T(8,128)S(1)} %slice_select_fusion.2), channel_id=1, source_target_pairs={{0,4},{2,6},{4,0},{6,2},{8,12},{10,14},{12,8},{14,10},{16,20},{18,... | collective-permute-start | bytes 393224 | tf_op jit(solution)/shard_map/ppermute | solution.py:182
  126.8 11.0 %collective-permute-start.8 = (f32[256,128]{1,0:T(8,128)S(1)}, f32[256,128]{1,0:T(8,128)S(1)}, u32[]{:S(2)}, u32[]{:S(2)}) collective-permute-start(f32[256,128]{1,0:T(8,128)S(1)} %add.45), channel_id=1, source_target_pairs={{0,16},{2,18},{4,20},{6,22},{8,24},{10,26},{12,28},{14,30},{16,0},... | collective-permute-start | bytes 393224 | tf_op jit(solution)/shard_map/ppermute | solution.py:182
  128.9 5.3 %collective-permute-start.19 = (f32[64,512]{1,0:T(8,128)S(1)}, f32[64,512]{1,0:T(8,128)S(1)}, u32[]{:S(2)}, u32[]{:S(2)}) collective-permute-start(f32[64,512]{1,0:T(8,128)S(1)} %select_add_fusion.1), channel_id=1, source_target_pairs={{0,8},{2,10},{4,12},{6,14},{8,0},{10,2},{12,4},{14,6},{16,24},{18,... | collective-permute-start | bytes 393224 | tf_op jit(solution)/shard_map/ppermute | solution.py:182
  134.3 7.3 %collective-permute-start.22 = (f32[64,512]{1,0:T(8,128)S(1)}, f32[64,512]{1,0:T(8,128)S(1)}, u32[]{:S(2)}, u32[]{:S(2)}) collective-permute-start(f32[64,512]{1,0:T(8,128)S(1)} %add.49), channel_id=1, source_target_pairs={{0,16},{2,18},{4,20},{6,22},{8,24},{10,26},{12,28},{14,30},{16,0},... | collective-permute-start | bytes 393224 | tf_op jit(solution)/shard_map/ppermute | solution.py:182
  136.2 7.8 %collective-permute-start.20 = (f32[2,64,512]{2,1,0:T(8,128)S(1)}, f32[2,64,512]{2,1,0:T(8,128)S(1)}, u32[]{:S(2)}, u32[]{:S(2)}) collective-permute-start(f32[2,64,512]{2,1,0:T(8,128)S(1)} %pad_maximum_fusion.8), channel_id=1, source_target_pairs={{0,4},{2,6},{4,0},{6,2},{8,12},{10,14},{12,8},{14,10},{16,20},{18,... | collective-permute-start | bytes 786440 | tf_op jit(solution)/shard_map/ppermute | solution.py:182
  137.8 10.7 %collective-permute-start.9 = (f32[4,256,128]{2,1,0:T(8,128)S(1)}, f32[4,256,128]{2,1,0:T(8,128)S(1)}, u32[]{:S(2)}, u32[]{:S(2)}) collective-permute-start(f32[4,256,128]{2,1,0:T(8,128)S(1)} %pad_maximum_fusion.2), channel_id=1, source_target_pairs={{0,1},{1,0},{2,3},{3,2},{4,5},{5,4},{6,7},{7,6},{8,9},{9,8},{10,11... | collective-permute-start | bytes 1572872 | tf_op jit(solution)/shard_map/ppermute | solution.py:182
  141.6 5.0 %collective-permute-start.23 = (f32[64,512]{1,0:T(8,128)S(1)}, f32[64,512]{1,0:T(8,128)S(1)}, u32[]{:S(2)}, u32[]{:S(2)}) collective-permute-start(f32[64,512]{1,0:T(8,128)S(1)} %add.50), channel_id=1, source_target_pairs={{0,4},{2,6},{4,0},{6,2},{8,12},{10,14},{12,8},{14,10},{16,20},{18,... | collective-permute-start | bytes 393224 | tf_op jit(solution)/shard_map/ppermute | solution.py:182
  144.1 39.0 %collective-permute-start.21 = (f32[2,128,512]{2,1,0:T(8,128)S(1)}, f32[2,128,512]{2,1,0:T(8,128)S(1)}, u32[]{:S(2)}, u32[]{:S(2)}) collective-permute-start(f32[2,128,512]{2,1,0:T(8,128)S(1)} %pad_maximum_fusion.3), channel_id=1, source_target_pairs={{0,2},{2,0},{4,6},{6,4},{8,10},{10,8},{12,14},{14,12},{16,18},{18,... | collective-permute-start | bytes 1572872 | tf_op jit(solution)/shard_map/ppermute | solution.py:182
  146.7 35.9 %collective-permute-start.24 = (f32[128,512]{1,0:T(8,128)S(1)}, f32[128,512]{1,0:T(8,128)S(1)}, u32[]{:S(2)}, u32[]{:S(2)}) collective-permute-start(f32[128,512]{1,0:T(8,128)S(1)} %pad_maximum_fusion.9), channel_id=1, source_target_pairs={{0,2},{2,0},{4,6},{6,4},{8,10},{10,8},{12,14},{14,12},{16,18},{18,... | collective-permute-start | bytes 786440 | tf_op jit(solution)/shard_map/ppermute | solution.py:182
  181.2 1.4 copy-start.16
  182.7 1.0 copy-start.15
  183.1 1.0 copy-start.13

commit v2 on v1

--- a/solution.py
+++ b/solution.py
@@ -9,7 +9,8 @@
 
 LEVELS = 4
 LANES = 128
-BASE = 32
+BASE = 64
+WIDE = 16
 NN = ((1,), (0,))
 NT = ((1,), (1,))
 TN = ((0,), (0,))
@@ -43,40 +44,54 @@
 
 
 def leaf_factor(work, out, start, base):
+    fit = LANES // base
     tile = start // LANES * LANES
     off = start - tile
     lane = lax.broadcasted_iota(jnp.int32, (base, LANES), 1)
     row = lax.broadcasted_iota(jnp.int32, (base, LANES), 0)
     col = lane % base
     seg = lane // base
-    packed = jnp.where(col == row, 1.0, 0.0)
-    for k in range(len(work)):
-        block = work[k][start : start + base, tile : tile + LANES]
-        shift = (base * k - off) % LANES
-        if shift:
-            block = pltpu.roll(block, shift, 1)
-        packed = jnp.where(seg == k, block, packed)
-    pivots = jnp.ones((base, LANES), jnp.float32)
-    for j in range(base):
-        column = jnp.take_along_axis(packed, seg * base + j, axis=1)
-        pivot = column[j : j + 1, :]
-        pivots = jnp.where(row == j, pivot, pivots)
-        if j == base - 1:
-            break
-        low = j // 8 * 8
-        below = row[low:] > j
-        mult = jnp.where(below, column[low:] * (1.0 / pivot), 0.0)
-        pivot_row = jnp.where(col[:1] == j, 1.0, packed[j : j + 1, :])
-        kept = jnp.where(below & (col[low:] == j), 0.0, packed[low:])
-        new = kept - mult * pivot_row
-        packed = new if low == 0 else jnp.concatenate([packed[:low], new], axis=0)
-    unit = jnp.where(col < row, packed, jnp.where(col == row, 1.0, 0.0))
-    unit = unit * lax.rsqrt(pivots)
+    groups = [range(g, min(g + fit, len(work))) for g in range(0, len(work), fit)]
+    packs, pivots = [], []
+    for group in groups:
+        packed = jnp.where(col == row, 1.0, 0.0)
+        for k in group:
+            block = work[k][start:start + base, tile:tile + LANES]
+            shift = (base * (k % fit) - off) % LANES
+            if shift:
+                block = pltpu.roll(block, shift, 1)
+            packed = jnp.where(seg == k % fit, block, packed)
+        packs.append(packed)
+        pivots.append(jnp.ones((base, LANES), jnp.float32))
+    for first in range(0, base, WIDE):
+        low = first // 8 * 8
+        rows = row[low:]
+        cols = col[low:]
+        for g in range(len(groups)):
+            active = packs[g][low:]
+            columns = [jnp.take_along_axis(active, (seg * base + first + t)[low:], axis=1) for t in range(WIDE)]
+            for t in range(WIDE):
+                j = first + t
+                at = j - low
+                pivot = columns[t][at:at + 1, :]
+                pivots[g] = jnp.where(row == j, pivot, pivots[g])
+                if j == base - 1:
+                    break
+                mult = jnp.where(rows > j, columns[t] * (1.0 / pivot), 0.0)
+                for s in range(t + 1, WIDE):
+                    columns[s] = columns[s] - mult * columns[s][at:at + 1, :]
+                pivot_row = jnp.where(col[:1] == j, 1.0, active[at:at + 1, :])
+                kept = jnp.where((rows > j) & (cols == j), 0.0, active)
+                active = kept - mult * pivot_row
+            packs[g] = active if low == 0 else jnp.concatenate([packs[g][:low], active], axis=0)
     inside = (lane >= off) & (lane < off + base)
-    for k in range(len(work)):
-        shift = (off - base * k) % LANES
-        block = pltpu.roll(unit, shift, 1) if shift else unit
-        out[k][start : start + base, tile : tile + LANES] = jnp.where(inside, block, 0.0)
+    for g, group in enumerate(groups):
+        unit = jnp.where(col < row, packs[g], jnp.where(col == row, 1.0, 0.0))
+        unit = unit * lax.rsqrt(pivots[g])
+        for k in group:
+            shift = (off - base * (k % fit)) % LANES
+            block = pltpu.roll(unit, shift, 1) if shift else unit
+            out[k][start:start + base, tile:tile + LANES] = jnp.where(inside, block, 0.0)
 
 
 def node_factor(work, out, start, size, base):
@@ -121,7 +136,7 @@
         in_specs=[spec] * count,
         out_specs=[spec] * count,
         scratch_shapes=[pltpu.VMEM((size, size), jnp.float32)] * count,
-        cost_estimate=pl.CostEstimate(flops=30 * 10**9, bytes_accessed=8 * count * size**2, transcendentals=0),
+        cost_estimate=pl.CostEstimate(flops=15 * 10**9, bytes_accessed=8 * count * size**2, transcendentals=0),
         name="factor_inverse",
     )(*grams)
 
@@ -178,6 +193,38 @@
     )(index, count, blocks, base, *pieces)
 
 
+def fold_kernel(index_ref, count_ref, blocks_ref, sketch_ref, out_ref):
+    block_count, slot_count, size, _ = blocks_ref.shape
+    out_ref[...] = jnp.zeros(out_ref.shape, jnp.float32)
+    for b in range(block_count):
+        for j in range(slot_count):
+
+            @pl.when(j < count_ref[b])
+            def _(b=b, j=j):
+                target = pl.ds(pl.multiple_of(index_ref[b, j] * size, size), size)
+                rows = pl.ds(b * size, size)
+                out_ref[target, :] += dot3(blocks_ref[b, j], sketch_ref[rows, :], TN)
+
+
+def near_fold(blocks, sketch, index, count, total):
+    block_count, slot_count, size, _ = blocks.shape
+    rank = sketch.shape[1]
+    vmem = pl.BlockSpec(memory_space=pltpu.VMEM)
+    smem = pl.BlockSpec(memory_space=pltpu.SMEM)
+    return pl.pallas_call(
+        fold_kernel,
+        out_shape=jax.ShapeDtypeStruct((total, rank), jnp.float32),
+        in_specs=[smem, smem, vmem, vmem],
+        out_specs=vmem,
+        cost_estimate=pl.CostEstimate(
+            flops=6 * block_count * slot_count * size * size * rank,
+            bytes_accessed=4 * (total * rank + sketch.size + blocks.size),
+            transcendentals=0,
+        ),
+        name="near_fold",
+    )(index, count, blocks, sketch)
+
+
 def across(value, axis, bit):
     return lax.ppermute(value, axis, [(i, i ^ 1 << bit) for i in range(lax.axis_size(axis))])
 
@@ -212,8 +259,6 @@
     index = near_cols - (position * block_count - block_count)
     swapped = jnp.where(index < block_count, index + 2 * block_count, jnp.where(index >= 2 * block_count, index - 2 * block_count, index))
     index = jnp.where(bits[0], swapped, index)
-
-    probe_pieces = halo(probes, block_count)
 
     if halves == 2:
         width = rank // 2
@@ -245,12 +290,25 @@
     if halves == 2:
         other = across(sums, "samp", 0)
         sums = jnp.concatenate([pick(core, sums, other), pick(core, other, sums)], axis=2)
-    (leaf_inverse,) = factor_inverse([gram])
-    inverses = factor_inverse([sums[h] for h in range(LEVELS)])
+    leaf_inverse, *inverses = factor_inverse([gram] + [sums[h] for h in range(LEVELS)])
     leaf_basis = lax.dot_general(leaf_sketch, leaf_inverse, (NT, ((), ())), precision=HIGH)
 
-    far_samples = near_apply(near_blocks, samples, probe_pieces, index, near_count)
-    product = jnp.einsum("rk,rs->ks", leaf_sketch, far_samples, precision=HIGH)
+    folded = near_fold(near_blocks, leaf_sketch, index, near_count, 3 * rows_dev)
+
+    def transposed(left, right):
+        return lax.dot_general(left, right, (TN, ((), ())), precision=HIGH)
+
+    pieces = halo(probes, block_count)
+    product = transposed(leaf_sketch, samples)
+    at = 0
+    terms = []
+    for piece in pieces:
+        depth = piece.shape[0]
+        terms.append(transposed(folded[at : at + depth], piece))
+        at += depth
+    parts = len(terms) // 2
+    for i in [parts] + [i for p in range(parts) for i in (parts + 1 + p, p)]:
+        product = product - terms[i]
 
     def keep_send(value, bit):
         half = value.shape[0] // 2

time: 187 us -> 144 us (0.77)
  Pallas kernels: 71.2 us -> 27.9 us
  waiting for transfers between devices: 45.8 us -> 26.2 us
  matrix products: 8.85 us -> 21.4 us
  other arithmetic: 6.77 us -> 13.1 us
    pallas_call x2 -> x1, Pallas kernels: 58.4 us -> 17.6 us  [factor_inverse(): pl.pallas_call(functools.partial(inverse_kernel, count, size), out_shape=...]
    ppermute x21, waiting for transfers between devices: 37.1 us -> 21.4 us  [across(): lax.ppermute(value, axis, [(i, i ^ 1 << bit) for i in range(lax.axis_size...]
    dot_general x1 -> x8, matrix products: 0.82 us -> 11.7 us  [transposed(): return lax.dot_general(left, right, (TN, ((), ())), precision=HIGH)]
    pallas_call x2 -> x1, Pallas kernels: 12.9 us -> 5.05 us  [near_apply(): pl.pallas_call(functools.partial(near_kernel, len(pieces), block_count, s...]
    pallas_call x0 -> x1, Pallas kernels: none -> 5.23 us  [near_fold(): pl.pallas_call(fold_kernel, out_shape=jax.ShapeDtypeStruct((total, rank),...]
    ppermute x4, waiting for transfers between devices: 8.68 us -> 4.73 us  [relayed(): lax.ppermute(value, axis, [(i, t) for i, t in steps if 0 <= t < count])]
    select_n x10, other arithmetic: 1.59 us -> 4.34 us  [pick(): return jnp.where(flag, second, first)]
  transfers between devices with their start and end apart: 25 -> 25, of which waited for: 11 -> 10; matrix products, arithmetic and copies ran while one was open for 5% -> 22% of each run, Pallas kernels for 38% -> 19%
where the time goes in v2:
time: 144 us; the launch traced here: 143 us
  starting transfers between devices  48.7 us (34%)
  Pallas kernels  27.9 us (19%)
  waiting for transfers between devices  26.2 us (18%)
  matrix products  21.4 us (15%)
  other arithmetic  13.1 us (9%)
  local copies, waits for them, and re-layouts  5.02 us (3%)
    ppermute x21, starting transfers between devices, across(): lax.ppermute(value, axis, [(i, i ^ 1 << bit) for i in range(lax.axis_size...  30.2 us
    ppermute x21, waiting for transfers between devices, across(): lax.ppermute(value, axis, [(i, i ^ 1 << bit) for i in range(lax.axis_size...  21.4 us
    ppermute x4, starting transfers between devices, relayed(): lax.ppermute(value, axis, [(i, t) for i, t in steps if 0 <= t < count])  18.5 us
    pallas_call x1, Pallas kernels, factor_inverse(): pl.pallas_call(functools.partial(inverse_kernel, count, size), out_shape=...  17.6 us
    dot_general x8, matrix products, transposed(): return lax.dot_general(left, right, (TN, ((), ())), precision=HIGH)  11.7 us
    pallas_call x1, Pallas kernels, near_fold(): pl.pallas_call(fold_kernel, out_shape=jax.ShapeDtypeStruct((total, rank),...  5.23 us
    pallas_call x1, Pallas kernels, near_apply(): pl.pallas_call(functools.partial(near_kernel, len(pieces), block_count, s...  5.05 us
    ppermute x4, waiting for transfers between devices, relayed(): lax.ppermute(value, axis, [(i, t) for i, t in steps if 0 <= t < count])  4.73 us
  transfers between devices with their start and end apart: 25, of which 10 were waited for; matrix products, arithmetic and copies ran while one was open for 22% of the time, Pallas kernels for 19%

profile of v2, /device:TPU:0, one launch (start us, length us, event | category | flops | bytes accessed | tf_op | source)
XLA Modules:
  0.0 143.4 jit_solution(12720557424142640503)
XLA Ops:
  0.7 1.2 fusion.44
  1.9 2.4 %convolution_bitcast_fusion = f32[768,256]{1,0:T(8,128)S(1)} fusion(f32[768,512]{1,0:T(8,128)} %param.7, f32[512,256]{1,0:T(8,128)} %param.11, f32[512,128]{1,0:T(8,128)S(1)} %get-tuple-element.34, f32[512,128]{1,0:T(8,128)S(1)} %get-tuple-element.33, pred[]{:T(512)S(6)} %eq.11), kind=kOutput, calls=%fused_computation.7 | convolution fusion | flops 604241920 | bytes 3407873 | tf_op jit(solution)/shard_map/dot_general | solution.py:266
  4.7 1.4 collective-permute-done.1
  6.2 3.0 %collective-permute-start.2 = (f32[768,128]{1,0:T(8,128)S(1)}, f32[768,128]{1,0:T(8,128)}, u32[]{:S(2)}, u32[]{:S(2)}) collective-permute-start(f32[768,128]{1,0:T(8,128)S(1)} %slice_add_fusion.refs_3_), channel_id=1, source_target_pairs={{0,2},{2,0},{4,6},{6,4},{8,10},{10,8},{12,14},{14,12},{16,18},{18,... | collective-permute-start | bytes 1179656 | tf_op jit(solution)/shard_map/ppermute | solution.py:229
  9.2 1.7 %convolution_bitcast_fusion.1 = f32[768,256]{1,0:T(8,128)} fusion(f32[768,512]{1,0:T(8,128)S(1)} %copy-done, f32[512,256]{1,0:T(8,128)S(1)} %copy-done.5, f32[512,128]{1,0:T(8,128)S(1)} %get-tuple-element.34, f32[512,128]{1,0:T(8,128)S(1)} %get-tuple-element.33, pred[]{:T(512)S(6)} %eq.11), kind=kOutput, calls=%fused_computation.8 | convolution fusion | flops 604241920 | bytes 3407873 | tf_op jit(solution)/shard_map/dot_general | solution.py:267
  10.9 1.8 %slice.117 = f32[768,128]{1,0:T(8,128)} slice(f32[768,256]{1,0:T(8,128)} %convolution_bitcast_fusion.1), slice={[0:768], [128:256]} | slice | bytes 786432 | tf_op jit(solution)/shard_map/slice | solution.py:269
  12.7 1.2 fusion.43
  14.1 1.9 %collective-permute-start.12 = (f32[256,512]{1,0:T(8,128)}, f32[256,512]{1,0:T(8,128)}, u32[]{:S(2)}, u32[]{:S(2)}) collective-permute-start(f32[256,512]{1,0:T(8,128)} %get-tuple-element.16), channel_id=1, source_target_pairs={{0,2},{2,0},{4,6},{6,4},{8,10},{10,8},{12,14},{14,12},{16,18},{18,... | collective-permute-start | bytes 1572872 | tf_op jit(solution)/shard_map/ppermute | solution.py:229
  16.1 3.2 %collective-permute-done.2.refs_4_ = f32[768,128]{1,0:T(8,128)} collective-permute-done((f32[768,128]{1,0:T(8,128)S(1)}, f32[768,128]{1,0:T(8,128)}, u32[]{:S(2)}, u32[]{:S(2)}) %collective-permute-start.2) | collective-permute-done | bytes 393248 | tf_op jit(solution)/shard_map/ppermute | solution.py:229
  19.3 4.0 %collective-permute-start.3 = (f32[768,128]{1,0:T(8,128)}, f32[768,128]{1,0:T(8,128)S(1)}, u32[]{:S(2)}, u32[]{:S(2)}) collective-permute-start(f32[768,128]{1,0:T(8,128)} %collective-permute-done.2.refs_4_), channel_id=1, source_target_pairs={{0,4},{4,8},{6,2},{8,12},{10,6},{12,16},{14,10},{16,20},{18,14},{2... | collective-permute-start | bytes 1179656 | tf_op jit(solution)/shard_map/ppermute | solution.py:235
  23.9 1.9 %slice_add_fusion.1.refs_1_ = f32[768,128]{1,0:T(8,128)} fusion(f32[768,128]{1,0:T(8,128)} %collective-permute-done, f32[768,256]{1,0:T(8,128)} %convolution_bitcast_fusion.1), kind=kLoop, calls=%fused_computation.40 | loop fusion | flops 98304 | bytes 1179648 | tf_op jit(solution)/shard_map/add | solution.py:271
  25.8 4.7 %collective-permute-done.3.refs_2_ = f32[768,128]{1,0:T(8,128)S(1)} collective-permute-done((f32[768,128]{1,0:T(8,128)}, f32[768,128]{1,0:T(8,128)S(1)}, u32[]{:S(2)}, u32[]{:S(2)}) %collective-permute-start.3) | collective-permute-done | bytes 393248 | tf_op jit(solution)/shard_map/ppermute | solution.py:235
  31.3 5.0 %near_apply.1 = f32[768,128]{1,0:T(8,128)} custom-call(s32[3,3]{1,0:T(4,128)} %fusion.34.index_ref, s32[3]{0:T(128)} %count_ref.3, f32[3,3,256,256]{3,2,1,0:T(8,128)} %blocks_ref.1, f32[768,128]{1,0:T(8,128)} %slice_add_fusion.1.refs_1_, f32[768,128]{1,0:T(8,128)} %copy-done.12, f32[768,128]{1,0:T(8,128)} %copy-done.7, f32[768,128]{1,0:T(8,128)} %collective-permute-done.2.refs_4_), custom_call_target="tpu_custom_call" | custom-call | flops 452984832 | bytes 4325376 | tf_op jit(solution)/shard_map/near_apply/pallas_call | solution.py:178
  36.4 5.6 %collective-permute-start.11 = (f32[256,512]{1,0:T(8,128)}, f32[256,512]{1,0:T(8,128)}, u32[]{:S(2)}, u32[]{:S(2)}) collective-permute-start(f32[256,512]{1,0:T(8,128)} %collective-permute-done.10), channel_id=1, source_target_pairs={{0,4},{4,8},{6,2},{8,12},{10,6},{12,16},{14,10},{16,20},{18,14},{2... | collective-permute-start | bytes 1572872 | tf_op jit(solution)/shard_map/ppermute | solution.py:235
  42.0 4.5 %collective-permute-start.13 = (f32[256,512]{1,0:T(8,128)}, f32[256,512]{1,0:T(8,128)}, u32[]{:S(2)}, u32[]{:S(2)}) collective-permute-start(f32[256,512]{1,0:T(8,128)} %collective-permute-done.12), channel_id=1, source_target_pairs={{0,4},{4,8},{6,2},{8,12},{10,6},{12,16},{14,10},{16,20},{18,14},{2... | collective-permute-start | bytes 1572872 | tf_op jit(solution)/shard_map/ppermute | solution.py:235
  46.5 5.9 %collective-permute-done.14 = f32[256,512]{1,0:T(8,128)} collective-permute-done((f32[256,512]{1,0:T(8,128)}, f32[256,512]{1,0:T(8,128)}, u32[]{:S(2)}, u32[]{:S(2)}) %collective-permute-start.14) | collective-permute-done | bytes 524320 | tf_op jit(solution)/shard_map/ppermute | solution.py:229
  52.5 4.4 %collective-permute-start.15 = (f32[256,512]{1,0:T(8,128)}, f32[256,512]{1,0:T(8,128)}, u32[]{:S(2)}, u32[]{:S(2)}) collective-permute-start(f32[256,512]{1,0:T(8,128)} %collective-permute-done.14), channel_id=1, source_target_pairs={{0,4},{4,8},{6,2},{8,12},{10,6},{12,16},{14,10},{16,20},{18,14},{2... | collective-permute-start | bytes 1572872 | tf_op jit(solution)/shard_map/ppermute | solution.py:235
  56.9 1.0 broadcast_select_fusion.5
  59.0 1.5 %fusion.42.refs_0_ = f32[256,256]{1,0:T(8,128)} fusion(f32[768,128]{1,0:T(8,128)S(1)} %get-tuple-element.26, f32[768,128]{1,0:T(8,128)S(1)} %get-tuple-element.25), kind=kOutput, calls=%fused_computation.90 | convolution fusion | flops 302186496 | bytes 1048576 | tf_op jit(solution)/shard_map/rk,rl->kl/dot_general | solution.py:283
  60.5 5.2 %near_fold.1 = f32[2304,256]{1,0:T(8,128)} custom-call(s32[3,3]{1,0:T(4,128)} %fusion.34.index_ref, s32[3]{0:T(128)} %count_ref.3, f32[3,3,256,256]{3,2,1,0:T(8,128)} %blocks_ref.1, f32[768,256]{1,0:T(8,128)} %pad_maximum_fusion.sketch_ref), custom_call_target="tpu_custom_call" | custom-call | flops 905969664 | bytes 5505024 | tf_op jit(solution)/shard_map/near_fold/pallas_call | solution.py:214
  65.7 2.1 %fusion.3 = f32[256,512]{1,0:T(8,128)S(1)} fusion(f32[768,512]{1,0:T(8,128)S(1)} %copy-done.1, f32[2304,256]{1,0:T(8,128)} %near_fold.1), kind=kOutput, calls=%fused_computation.22 | convolution fusion | flops 603979776 | bytes 2883584 | tf_op jit(solution)/shard_map/dot_general | solution.py:299
  67.9 1.5 %fusion.30 = f32[256,512]{1,0:T(8,128)S(1)} fusion(f32[256,512]{1,0:T(8,128)} %collective-permute-done.10, f32[2304,256]{1,0:T(8,128)S(1)} %copy-done.4), kind=kOutput, calls=%fused_computation.54 | convolution fusion | flops 201326592 | bytes 1310720 | tf_op jit(solution)/shard_map/dot_general | solution.py:299
  69.4 1.5 %fusion.27 = f32[256,512]{1,0:T(8,128)S(1)} fusion(f32[256,512]{1,0:T(8,128)} %collective-permute-done.12, f32[2304,256]{1,0:T(8,128)S(1)} %copy-done.4), kind=kOutput, calls=%fused_computation.51 | convolution fusion | flops 201326592 | bytes 1310720 | tf_op jit(solution)/shard_map/dot_general | solution.py:299
  71.7 1.5 %fusion.2 = f32[256,512]{1,0:T(8,128)S(1)} fusion(f32[256,512]{1,0:T(8,128)S(1)} %fusion.27, f32[256,512]{1,0:T(8,128)S(1)} %fusion, f32[256,512]{1,0:T(8,128)} %collective-permute-done.11, f32[2304,256]{1,0:T(8,128)S(1)} %copy-done.4), kind=kOutput, calls=%fused_computation.19 | convolution fusion | flops 201588736 | bytes 2359296 | tf_op jit(solution)/shard_map/dot_general | solution.py:299
  73.2 1.5 %fusion.24 = f32[256,512]{1,0:T(8,128)S(1)} fusion(f32[256,512]{1,0:T(8,128)} %collective-permute-done.14, f32[2304,256]{1,0:T(8,128)S(1)} %copy-done.4), kind=kOutput, calls=%fused_computation.48 | convolution fusion | flops 201326592 | bytes 1310720 | tf_op jit(solution)/shard_map/dot_general | solution.py:299
  74.7 1.5 %fusion.1 = f32[256,512]{1,0:T(8,128)S(1)} fusion(f32[256,512]{1,0:T(8,128)S(1)} %fusion.24, f32[256,512]{1,0:T(8,128)S(1)} %fusion.2, f32[256,512]{1,0:T(8,128)} %collective-permute-done.13, f32[2304,256]{1,0:T(8,128)S(1)} %copy-done.4), kind=kOutput, calls=%fused_computation.17 | convolution fusion | flops 201588736 | bytes 2359296 | tf_op jit(solution)/shard_map/dot_general | solution.py:299
  76.2 1.5 %convolution_subtract_fusion.1 = f32[256,512]{1,0:T(8,128)S(1)} fusion(f32[256,512]{1,0:T(8,128)S(1)} %fusion.1, f32[256,512]{1,0:T(8,128)} %collective-permute-done.15, f32[2304,256]{1,0:T(8,128)S(1)} %copy-done.4), kind=kOutput, calls=%fused_computation.15 | convolution fusion | flops 201457664 | bytes 1835008 | tf_op jit(solution)/shard_map/dot_general | solution.py:299
  77.7 2.1 %collective-permute-start.16 = (f32[128,512]{1,0:T(8,128)S(1)}, f32[128,512]{1,0:T(8,128)S(1)}, u32[]{:S(2)}, u32[]{:S(2)}) collective-permute-start(f32[128,512]{1,0:T(8,128)S(1)} %slice_select_fusion), channel_id=1, source_target_pairs={{0,2},{2,0},{4,6},{6,4},{8,10},{10,8},{12,14},{14,12},{16,18},{18,... | collective-permute-start | bytes 786440 | tf_op jit(solution)/shard_map/ppermute | solution.py:229
  79.8 2.7 %collective-permute-start.6 = (f32[256,128]{1,0:T(8,128)S(1)}, f32[256,128]{1,0:T(8,128)}, u32[]{:S(2)}, u32[]{:S(2)}) collective-permute-start(f32[256,128]{1,0:T(8,128)S(1)} %fusion.60), channel_id=1, source_target_pairs={{0,4},{2,6},{4,0},{6,2},{8,12},{10,14},{12,8},{14,10},{16,20},{18,... | collective-permute-start | bytes 393224 | tf_op jit(solution)/shard_map/ppermute | solution.py:229
  82.5 3.1 %collective-permute-done.6 = f32[256,128]{1,0:T(8,128)} collective-permute-done((f32[256,128]{1,0:T(8,128)S(1)}, f32[256,128]{1,0:T(8,128)}, u32[]{:S(2)}, u32[]{:S(2)}) %collective-permute-start.6) | collective-permute-done | bytes 131104 | tf_op jit(solution)/shard_map/ppermute | solution.py:229
  86.5 2.2 %collective-permute-start.7 = (f32[256,128]{1,0:T(8,128)S(1)}, f32[256,128]{1,0:T(8,128)S(1)}, u32[]{:S(2)}, u32[]{:S(2)}) collective-permute-start(f32[256,128]{1,0:T(8,128)S(1)} %add.44), channel_id=1, source_target_pairs={{0,8},{2,10},{4,12},{6,14},{8,0},{10,2},{12,4},{14,6},{16,24},{18,... | collective-permute-start | bytes 393224 | tf_op jit(solution)/shard_map/ppermute | solution.py:229
  88.8 2.0 %collective-permute-start.18 = (f32[64,512]{1,0:T(8,128)S(1)}, f32[64,512]{1,0:T(8,128)S(1)}, u32[]{:S(2)}, u32[]{:S(2)}) collective-permute-start(f32[64,512]{1,0:T(8,128)S(1)} %slice_select_fusion.2), channel_id=1, source_target_pairs={{0,4},{2,6},{4,0},{6,2},{8,12},{10,14},{12,8},{14,10},{16,20},{18,... | collective-permute-start | bytes 393224 | tf_op jit(solution)/shard_map/ppermute | solution.py:229
  91.7 2.8 %collective-permute-start.8 = (f32[256,128]{1,0:T(8,128)S(1)}, f32[256,128]{1,0:T(8,128)S(1)}, u32[]{:S(2)}, u32[]{:S(2)}) collective-permute-start(f32[256,128]{1,0:T(8,128)S(1)} %add.45), channel_id=1, source_target_pairs={{0,16},{2,18},{4,20},{6,22},{8,24},{10,26},{12,28},{14,30},{16,0},... | collective-permute-start | bytes 393224 | tf_op jit(solution)/shard_map/ppermute | solution.py:229
  94.5 1.2 collective-permute-start.19
  95.7 1.5 %collective-permute-done.17 = f32[128,512]{1,0:T(8,128)S(1)} collective-permute-done((f32[128,512]{1,0:T(8,128)S(1)}, f32[128,512]{1,0:T(8,128)S(1)}, u32[]{:S(2)}, u32[]{:S(2)}) %collective-permute-start.17) | collective-permute-done | bytes 262176 | tf_op jit(solution)/shard_map/ppermute | solution.py:229
  98.0 1.5 %collective-permute-done.19 = f32[64,512]{1,0:T(8,128)S(1)} collective-permute-done((f32[64,512]{1,0:T(8,128)S(1)}, f32[64,512]{1,0:T(8,128)S(1)}, u32[]{:S(2)}, u32[]{:S(2)}) %collective-permute-start.19) | collective-permute-done | bytes 131104 | tf_op jit(solution)/shard_map/ppermute | solution.py:229
  99.6 1.5 %collective-permute-start.22 = (f32[64,512]{1,0:T(8,128)S(1)}, f32[64,512]{1,0:T(8,128)S(1)}, u32[]{:S(2)}, u32[]{:S(2)}) collective-permute-start(f32[64,512]{1,0:T(8,128)S(1)} %add.49), channel_id=1, source_target_pairs={{0,16},{2,18},{4,20},{6,22},{8,24},{10,26},{12,28},{14,30},{16,0},... | collective-permute-start | bytes 393224 | tf_op jit(solution)/shard_map/ppermute | solution.py:229
  101.1 2.5 %collective-permute-start.20 = (f32[2,64,512]{2,1,0:T(8,128)S(1)}, f32[2,64,512]{2,1,0:T(8,128)S(1)}, u32[]{:S(2)}, u32[]{:S(2)}) collective-permute-start(f32[2,64,512]{2,1,0:T(8,128)S(1)} %pad_maximum_fusion.5), channel_id=1, source_target_pairs={{0,4},{2,6},{4,0},{6,2},{8,12},{10,14},{12,8},{14,10},{16,20},{18,... | collective-permute-start | bytes 786440 | tf_op jit(solution)/shard_map/ppermute | solution.py:229
  103.7 3.2 %collective-permute-done.22 = f32[64,512]{1,0:T(8,128)S(1)} collective-permute-done((f32[64,512]{1,0:T(8,128)S(1)}, f32[64,512]{1,0:T(8,128)S(1)}, u32[]{:S(2)}, u32[]{:S(2)}) %collective-permute-start.22) | collective-permute-done | bytes 131104 | tf_op jit(solution)/shard_map/ppermute | solution.py:229
  106.9 3.4 %collective-permute-start.23 = (f32[64,512]{1,0:T(8,128)S(1)}, f32[64,512]{1,0:T(8,128)S(1)}, u32[]{:S(2)}, u32[]{:S(2)}) collective-permute-start(f32[64,512]{1,0:T(8,128)S(1)} %add.50), channel_id=1, source_target_pairs={{0,4},{2,6},{4,0},{6,2},{8,12},{10,14},{12,8},{14,10},{16,20},{18,... | collective-permute-start | bytes 393224 | tf_op jit(solution)/shard_map/ppermute | solution.py:229
  111.2 1.2 collective-permute-start.21
  114.1 2.7 %collective-permute-start.24 = (f32[128,512]{1,0:T(8,128)}, f32[128,512]{1,0:T(8,128)}, u32[]{:S(2)}, u32[]{:S(2)}) collective-permute-start(f32[128,512]{1,0:T(8,128)} %pad_maximum_fusion.6), channel_id=1, source_target_pairs={{0,2},{2,0},{4,6},{6,4},{8,10},{10,8},{12,14},{14,12},{16,18},{18,... | collective-permute-start | bytes 786440 | tf_op jit(solution)/shard_map/ppermute | solution.py:229
  117.9 17.6 %factor_inverse.1 = (f32[256,256]{1,0:T(8,128)}, f32[256,256]{1,0:T(8,128)}, f32[256,256]{1,0:T(8,128)}, f32[256,256]{1,0:T(8,128)}, f32[256,256]{1,0:T(8,128)}) custom-call(f32[256,256]{1,0:T(8,128)} %fusion.42.refs_0_, f32[256,256]{1,0:T(8,128)} %get-tuple-element.20.refs_1_, f32[256,256]{1,0:T(8,128)} %get-tuple-element.21.refs_2_, ...), custom_call_target="tpu_custom_call" | custom-call | flops 15000000512 | bytes 2621440 | tf_op jit(solution)/shard_map/factor_inverse/pallas_call | solution.py:133
  135.5 1.0 broadcast_select_fusion.9
  136.5 1.5 %convolution_bitcast_fusion.5 = f32[1,256,512]{2,1,0:T(8,128)S(1)} fusion(f32[256,256]{1,0:T(8,128)} %get-tuple-element.8, f32[128,512]{1,0:T(8,128)} %get-tuple-element.28, f32[128,512]{1,0:T(8,128)} %get-tuple-element.27), kind=kOutput, calls=%fused_computation.12 | convolution fusion | flops 201457664 | bytes 1310720 | tf_op jit(solution)/shard_map/dot_general | solution.py:333
  138.5 1.4 fusion.41
  139.9 1.2 broadcast_select_fusion.1
  141.9 1.5 %maximum_bitcast_fusion = f32[4,1,256,512]{3,2,1,0:T(8,128)} fusion(f32[1,256,512]{2,1,0:T(8,128)S(1)} %convolution_bitcast_fusion.2, f32[1,256,512]{2,1,0:T(8,128)S(1)} %convolution_bitcast_fusion.3, f32[1,256,512]{2,1,0:T(8,128)S(1)} %convolution_bitcast_fusion.4, f32[1,256,512]{2,1,0:T(8,128)S(1)} %convolution_bitcast_fusion.5), kind=kLoop, calls=%fused_computation | loop fusion | flops 1572864 | bytes 4194304
  (89 shorter events, 11.9 us)
Async XLA Ops:
  0.6 8.6 %copy-start = (f32[768,512]{1,0:T(8,128)S(1)}, f32[768,512]{1,0:T(8,128)}, u32[]{:S(2)}) copy-start(f32[768,512]{1,0:T(8,128)} %param.6) | copy-start | bytes 4718596
  1.8 7.4 %copy-start.5 = (f32[512,256]{1,0:T(8,128)S(1)}, f32[512,256]{1,0:T(8,128)}, u32[]{:S(2)}) copy-start(f32[512,256]{1,0:T(8,128)} %param.11) | copy-start | bytes 1572868
  4.3 1.8 %collective-permute-start.1 = (f32[768,128]{1,0:T(8,128)S(1)}, f32[768,128]{1,0:T(8,128)S(1)}, u32[]{:S(2)}, u32[]{:S(2)}) collective-permute-start(f32[768,128]{1,0:T(8,128)S(1)} %slice.119), channel_id=1, source_target_pairs={{0,1},{1,0},{2,3},{3,2},{4,5},{5,4},{6,7},{7,6},{8,9},{9,8},{10,11... | collective-permute-start | bytes 1179656 | tf_op jit(solution)/shard_map/ppermute | solution.py:229
  6.2 6.6 %copy-start.7 = (f32[768,128]{1,0:T(8,128)}, f32[768,128]{1,0:T(8,128)S(1)}, u32[]{:S(2)}) copy-start(f32[768,128]{1,0:T(8,128)S(1)} %slice_add_fusion.refs_3_) | copy-start | bytes 1179652
  6.2 6.6 %copy-start.1 = (f32[768,512]{1,0:T(8,128)S(1)}, f32[768,512]{1,0:T(8,128)}, u32[]{:S(2)}) copy-start(f32[768,512]{1,0:T(8,128)} %param.7) | copy-start | bytes 4718596
  6.2 13.1 %collective-permute-start.2 = (f32[768,128]{1,0:T(8,128)S(1)}, f32[768,128]{1,0:T(8,128)}, u32[]{:S(2)}, u32[]{:S(2)}) collective-permute-start(f32[768,128]{1,0:T(8,128)S(1)} %slice_add_fusion.refs_3_), channel_id=1, source_target_pairs={{0,2},{2,0},{4,6},{6,4},{8,10},{10,8},{12,14},{14,12},{16,18},{18,... | collective-permute-start | bytes 1179656 | tf_op jit(solution)/shard_map/ppermute | solution.py:229
  10.9 12.3 %copy-start.17 = (s32[3,3]{1,0:T(4,128)S(1)}, s32[3,3]{1,0:T(4,128)}, u32[]{:S(2)}) copy-start(s32[3,3]{1,0:T(4,128)} %param.9) | copy-start | bytes 112
  12.7 11.1 %collective-permute-start = (f32[768,128]{1,0:T(8,128)}, f32[768,128]{1,0:T(8,128)}, u32[]{:S(2)}, u32[]{:S(2)}) collective-permute-start(f32[768,128]{1,0:T(8,128)} %slice.117), channel_id=1, source_target_pairs={{0,1},{1,0},{2,3},{3,2},{4,5},{5,4},{6,7},{7,6},{8,9},{9,8},{10,11... | collective-permute-start | bytes 1179656 | tf_op jit(solution)/shard_map/ppermute | solution.py:229
  13.9 22.5 %collective-permute-start.10 = (f32[256,512]{1,0:T(8,128)}, f32[256,512]{1,0:T(8,128)}, u32[]{:S(2)}, u32[]{:S(2)}) collective-permute-start(f32[256,512]{1,0:T(8,128)} %get-tuple-element.14), channel_id=1, source_target_pairs={{0,2},{2,0},{4,6},{6,4},{8,10},{10,8},{12,14},{14,12},{16,18},{18,... | collective-permute-start | bytes 1572872 | tf_op jit(solution)/shard_map/ppermute | solution.py:229
  14.1 27.9 %collective-permute-start.12 = (f32[256,512]{1,0:T(8,128)}, f32[256,512]{1,0:T(8,128)}, u32[]{:S(2)}, u32[]{:S(2)}) collective-permute-start(f32[256,512]{1,0:T(8,128)} %get-tuple-element.16), channel_id=1, source_target_pairs={{0,2},{2,0},{4,6},{6,4},{8,10},{10,8},{12,14},{14,12},{16,18},{18,... | collective-permute-start | bytes 1572872 | tf_op jit(solution)/shard_map/ppermute | solution.py:229
  16.0 36.5 %collective-permute-start.14 = (f32[256,512]{1,0:T(8,128)}, f32[256,512]{1,0:T(8,128)}, u32[]{:S(2)}, u32[]{:S(2)}) collective-permute-start(f32[256,512]{1,0:T(8,128)} %get-tuple-element.15), channel_id=1, source_target_pairs={{0,2},{2,0},{4,6},{6,4},{8,10},{10,8},{12,14},{14,12},{16,18},{18,... | collective-permute-start | bytes 1572872 | tf_op jit(solution)/shard_map/ppermute | solution.py:229
  19.3 11.2 %collective-permute-start.3 = (f32[768,128]{1,0:T(8,128)}, f32[768,128]{1,0:T(8,128)S(1)}, u32[]{:S(2)}, u32[]{:S(2)}) collective-permute-start(f32[768,128]{1,0:T(8,128)} %collective-permute-done.2.refs_4_), channel_id=1, source_target_pairs={{0,4},{4,8},{6,2},{8,12},{10,6},{12,16},{14,10},{16,20},{18,14},{2... | collective-permute-start | bytes 1179656 | tf_op jit(solution)/shard_map/ppermute | solution.py:235
  30.5 0.7 copy-start.12
  36.3 20.6 %collective-permute-start.4 = (f32[768,128]{1,0:T(8,128)}, f32[768,128]{1,0:T(8,128)S(1)}, u32[]{:S(2)}, u32[]{:S(2)}) collective-permute-start(f32[768,128]{1,0:T(8,128)} %near_apply.1), channel_id=1, source_target_pairs={{0,1},{1,0},{2,3},{3,2},{4,5},{5,4},{6,7},{7,6},{8,9},{9,8},{10,11... | collective-permute-start | bytes 1179656 | tf_op jit(solution)/shard_map/ppermute | solution.py:229
  36.4 35.3 %collective-permute-start.11 = (f32[256,512]{1,0:T(8,128)}, f32[256,512]{1,0:T(8,128)}, u32[]{:S(2)}, u32[]{:S(2)}) collective-permute-start(f32[256,512]{1,0:T(8,128)} %collective-permute-done.10), channel_id=1, source_target_pairs={{0,4},{4,8},{6,2},{8,12},{10,6},{12,16},{14,10},{16,20},{18,14},{2... | collective-permute-start | bytes 1572872 | tf_op jit(solution)/shard_map/ppermute | solution.py:235
  42.0 32.7 %collective-permute-start.13 = (f32[256,512]{1,0:T(8,128)}, f32[256,512]{1,0:T(8,128)}, u32[]{:S(2)}, u32[]{:S(2)}) collective-permute-start(f32[256,512]{1,0:T(8,128)} %collective-permute-done.12), channel_id=1, source_target_pairs={{0,4},{4,8},{6,2},{8,12},{10,6},{12,16},{14,10},{16,20},{18,14},{2... | collective-permute-start | bytes 1572872 | tf_op jit(solution)/shard_map/ppermute | solution.py:235
  52.5 23.7 %collective-permute-start.15 = (f32[256,512]{1,0:T(8,128)}, f32[256,512]{1,0:T(8,128)}, u32[]{:S(2)}, u32[]{:S(2)}) collective-permute-start(f32[256,512]{1,0:T(8,128)} %collective-permute-done.14), channel_id=1, source_target_pairs={{0,4},{4,8},{6,2},{8,12},{10,6},{12,16},{14,10},{16,20},{18,14},{2... | collective-permute-start | bytes 1572872 | tf_op jit(solution)/shard_map/ppermute | solution.py:235
  58.0 1.0 copy-start.2
  65.7 2.1 %copy-start.6 = (f32[256,256]{1,0:T(8,128)S(1)}, f32[256,256]{1,0:T(8,128)}, u32[]{:S(2)}) copy-start(f32[256,256]{1,0:T(8,128)} %fusion.42.refs_0_) | copy-start | bytes 786436
  65.7 2.2 %copy-start.4 = (f32[2304,256]{1,0:T(8,128)S(1)}, f32[2304,256]{1,0:T(8,128)}, u32[]{:S(2)}) copy-start(f32[2304,256]{1,0:T(8,128)} %near_fold.1) | copy-start | bytes 7077892
  67.8 3.1 %copy-start.3 = (f32[768,128]{1,0:T(8,128)S(1)}, f32[768,128]{1,0:T(8,128)}, u32[]{:S(2)}) copy-start(f32[768,128]{1,0:T(8,128)} %copy-done.2) | copy-start | bytes 1179652
  67.9 11.9 %collective-permute-start.5 = (f32[256,128]{1,0:T(8,128)S(1)}, f32[256,128]{1,0:T(8,128)S(1)}, u32[]{:S(2)}, u32[]{:S(2)}) collective-permute-start(f32[256,128]{1,0:T(8,128)S(1)} %slice_select_fusion.1), channel_id=1, source_target_pairs={{0,2},{2,0},{4,6},{6,4},{8,10},{10,8},{12,14},{14,12},{16,18},{18,... | collective-permute-start | bytes 393224 | tf_op jit(solution)/shard_map/ppermute | solution.py:229
  77.7 11.0 %collective-permute-start.16 = (f32[128,512]{1,0:T(8,128)S(1)}, f32[128,512]{1,0:T(8,128)S(1)}, u32[]{:S(2)}, u32[]{:S(2)}) collective-permute-start(f32[128,512]{1,0:T(8,128)S(1)} %slice_select_fusion), channel_id=1, source_target_pairs={{0,2},{2,0},{4,6},{6,4},{8,10},{10,8},{12,14},{14,12},{16,18},{18,... | collective-permute-start | bytes 786440 | tf_op jit(solution)/shard_map/ppermute | solution.py:229
  79.8 5.8 %collective-permute-start.6 = (f32[256,128]{1,0:T(8,128)S(1)}, f32[256,128]{1,0:T(8,128)}, u32[]{:S(2)}, u32[]{:S(2)}) collective-permute-start(f32[256,128]{1,0:T(8,128)S(1)} %fusion.60), channel_id=1, source_target_pairs={{0,4},{2,6},{4,0},{6,2},{8,12},{10,14},{12,8},{14,10},{16,20},{18,... | collective-permute-start | bytes 393224 | tf_op jit(solution)/shard_map/ppermute | solution.py:229
  86.5 5.1 %collective-permute-start.7 = (f32[256,128]{1,0:T(8,128)S(1)}, f32[256,128]{1,0:T(8,128)S(1)}, u32[]{:S(2)}, u32[]{:S(2)}) collective-permute-start(f32[256,128]{1,0:T(8,128)S(1)} %add.44), channel_id=1, source_target_pairs={{0,8},{2,10},{4,12},{6,14},{8,0},{10,2},{12,4},{14,6},{16,24},{18,... | collective-permute-start | bytes 393224 | tf_op jit(solution)/shard_map/ppermute | solution.py:229
  88.8 5.7 %collective-permute-start.18 = (f32[64,512]{1,0:T(8,128)S(1)}, f32[64,512]{1,0:T(8,128)S(1)}, u32[]{:S(2)}, u32[]{:S(2)}) collective-permute-start(f32[64,512]{1,0:T(8,128)S(1)} %slice_select_fusion.2), channel_id=1, source_target_pairs={{0,4},{2,6},{4,0},{6,2},{8,12},{10,14},{12,8},{14,10},{16,20},{18,... | collective-permute-start | bytes 393224 | tf_op jit(solution)/shard_map/ppermute | solution.py:229
  90.8 6.4 %collective-permute-start.17 = (f32[128,512]{1,0:T(8,128)S(1)}, f32[128,512]{1,0:T(8,128)S(1)}, u32[]{:S(2)}, u32[]{:S(2)}) collective-permute-start(f32[128,512]{1,0:T(8,128)S(1)} %select_add_fusion), channel_id=1, source_target_pairs={{0,2},{2,0},{4,6},{6,4},{8,10},{10,8},{12,14},{14,12},{16,18},{18,... | collective-permute-start | bytes 786440 | tf_op jit(solution)/shard_map/ppermute | solution.py:229
  91.7 11.9 %collective-permute-start.8 = (f32[256,128]{1,0:T(8,128)S(1)}, f32[256,128]{1,0:T(8,128)S(1)}, u32[]{:S(2)}, u32[]{:S(2)}) collective-permute-start(f32[256,128]{1,0:T(8,128)S(1)} %add.45), channel_id=1, source_target_pairs={{0,16},{2,18},{4,20},{6,22},{8,24},{10,26},{12,28},{14,30},{16,0},... | collective-permute-start | bytes 393224 | tf_op jit(solution)/shard_map/ppermute | solution.py:229
  94.5 5.0 %collective-permute-start.19 = (f32[64,512]{1,0:T(8,128)S(1)}, f32[64,512]{1,0:T(8,128)S(1)}, u32[]{:S(2)}, u32[]{:S(2)}) collective-permute-start(f32[64,512]{1,0:T(8,128)S(1)} %select_add_fusion.1), channel_id=1, source_target_pairs={{0,8},{2,10},{4,12},{6,14},{8,0},{10,2},{12,4},{14,6},{16,24},{18,... | collective-permute-start | bytes 393224 | tf_op jit(solution)/shard_map/ppermute | solution.py:229
  99.6 7.3 %collective-permute-start.22 = (f32[64,512]{1,0:T(8,128)S(1)}, f32[64,512]{1,0:T(8,128)S(1)}, u32[]{:S(2)}, u32[]{:S(2)}) collective-permute-start(f32[64,512]{1,0:T(8,128)S(1)} %add.49), channel_id=1, source_target_pairs={{0,16},{2,18},{4,20},{6,22},{8,24},{10,26},{12,28},{14,30},{16,0},... | collective-permute-start | bytes 393224 | tf_op jit(solution)/shard_map/ppermute | solution.py:229
  101.1 9.2 %collective-permute-start.20 = (f32[2,64,512]{2,1,0:T(8,128)S(1)}, f32[2,64,512]{2,1,0:T(8,128)S(1)}, u32[]{:S(2)}, u32[]{:S(2)}) collective-permute-start(f32[2,64,512]{2,1,0:T(8,128)S(1)} %pad_maximum_fusion.5), channel_id=1, source_target_pairs={{0,4},{2,6},{4,0},{6,2},{8,12},{10,14},{12,8},{14,10},{16,20},{18,... | collective-permute-start | bytes 786440 | tf_op jit(solution)/shard_map/ppermute | solution.py:229
  103.7 13.2 %collective-permute-start.9 = (f32[4,256,128]{2,1,0:T(8,128)S(1)}, f32[4,256,128]{2,1,0:T(8,128)S(1)}, u32[]{:S(2)}, u32[]{:S(2)}) collective-permute-start(f32[4,256,128]{2,1,0:T(8,128)S(1)} %pad_maximum_fusion.2), channel_id=1, source_target_pairs={{0,1},{1,0},{2,3},{3,2},{4,5},{5,4},{6,7},{7,6},{8,9},{9,8},{10,11... | collective-permute-start | bytes 1572872 | tf_op jit(solution)/shard_map/ppermute | solution.py:229
  106.9 6.4 %collective-permute-start.23 = (f32[64,512]{1,0:T(8,128)S(1)}, f32[64,512]{1,0:T(8,128)S(1)}, u32[]{:S(2)}, u32[]{:S(2)}) collective-permute-start(f32[64,512]{1,0:T(8,128)S(1)} %add.50), channel_id=1, source_target_pairs={{0,4},{2,6},{4,0},{6,2},{8,12},{10,14},{12,8},{14,10},{16,20},{18,... | collective-permute-start | bytes 393224 | tf_op jit(solution)/shard_map/ppermute | solution.py:229
  111.2 28.6 %collective-permute-start.21 = (f32[2,128,512]{2,1,0:T(8,128)}, f32[2,128,512]{2,1,0:T(8,128)}, u32[]{:S(2)}, u32[]{:S(2)}) collective-permute-start(f32[2,128,512]{2,1,0:T(8,128)} %pad_maximum_fusion.3), channel_id=1, source_target_pairs={{0,2},{2,0},{4,6},{6,4},{8,10},{10,8},{12,14},{14,12},{16,18},{18,... | collective-permute-start | bytes 1572872 | tf_op jit(solution)/shard_map/ppermute | solution.py:229
  113.3 3.5 %copy-start.8 = (f32[64,512]{1,0:T(8,128)}, f32[64,512]{1,0:T(8,128)S(1)}, u32[]{:S(2)}) copy-start(f32[64,512]{1,0:T(8,128)S(1)} %get-tuple-element.35) | copy-start | bytes 393220
  113.3 3.5 %copy-start.10 = (f32[64,512]{1,0:T(8,128)}, f32[64,512]{1,0:T(8,128)S(1)}, u32[]{:S(2)}) copy-start(f32[64,512]{1,0:T(8,128)S(1)} %get-tuple-element.36) | copy-start | bytes 393220
  114.1 21.4 %collective-permute-start.24 = (f32[128,512]{1,0:T(8,128)}, f32[128,512]{1,0:T(8,128)}, u32[]{:S(2)}, u32[]{:S(2)}) collective-permute-start(f32[128,512]{1,0:T(8,128)} %pad_maximum_fusion.6), channel_id=1, source_target_pairs={{0,2},{2,0},{4,6},{6,4},{8,10},{10,8},{12,14},{14,12},{16,18},{18,... | collective-permute-start | bytes 786440 | tf_op jit(solution)/shard_map/ppermute | solution.py:229
  117.9 17.6 %copy-start.9 = (f32[64,512]{1,0:T(8,128)S(1)}, f32[64,512]{1,0:T(8,128)}, u32[]{:S(2)}) copy-start(f32[64,512]{1,0:T(8,128)} %copy-done.8) | copy-start | bytes 393220
  117.9 17.6 %copy-start.11 = (f32[64,512]{1,0:T(8,128)S(1)}, f32[64,512]{1,0:T(8,128)}, u32[]{:S(2)}) copy-start(f32[64,512]{1,0:T(8,128)} %copy-done.10) | copy-start | bytes 393220
  135.5 2.6 %copy-start.16 = (f32[256,256]{1,0:T(8,128)S(1)}, f32[256,256]{1,0:T(8,128)}, u32[]{:S(2)}) copy-start(f32[256,256]{1,0:T(8,128)} %get-tuple-element.11) | copy-start | bytes 786436
  135.5 3.0 %copy-start.15 = (f32[256,256]{1,0:T(8,128)S(1)}, f32[256,256]{1,0:T(8,128)}, u32[]{:S(2)}) copy-start(f32[256,256]{1,0:T(8,128)} %get-tuple-element.7) | copy-start | bytes 786436
  138.4 2.6 %copy-start.14 = (f32[256,256]{1,0:T(8,128)S(1)}, f32[256,256]{1,0:T(8,128)}, u32[]{:S(2)}) copy-start(f32[256,256]{1,0:T(8,128)} %get-tuple-element.9) | copy-start | bytes 786436
  139.9 1.6 %copy-start.13 = (f32[256,256]{1,0:T(8,128)S(1)}, f32[256,256]{1,0:T(8,128)}, u32[]{:S(2)}) copy-start(f32[256,256]{1,0:T(8,128)} %get-tuple-element.10) | copy-start | bytes 786436

commit v3 on v2

--- a/solution.py
+++ b/solution.py
@@ -13,7 +13,6 @@
 WIDE = 16
 NN = ((1,), (0,))
 NT = ((1,), (1,))
-TN = ((0,), (0,))
 HIGH = lax.Precision.HIGH
 
 
@@ -118,27 +117,77 @@
         out[k][mid:end, t1 : t1 + width] = x2 - m21 if t1 == t2 else -m21
 
 
-def inverse_kernel(count, size, *refs):
-    ins, outs, work = refs[:count], refs[count : 2 * count], refs[2 * count :]
+def first_kernel(size, core_ref, gram_ref, mine_ref, other_ref, *refs):
+    count = mine_ref.shape[0] + 1
+    inverse, rest, kept = refs[:count], refs[count : 2 * count], refs[2 * count : 3 * count]
+    work = refs[3 * count :]
+    width = mine_ref.shape[2]
+    half = size // 2
+    swap = core_ref[0] == 1
     for k in range(count):
-        work[k][...] = ins[k][...]
-        for t in range(0, size, LANES):
-            outs[k][:, t : t + LANES] = jnp.zeros((size, LANES), jnp.float32)
-    node_factor(work, outs, 0, size, BASE)
-
-
-def factor_inverse(grams):
-    count, size = len(grams), grams[0].shape[0]
-    spec = pl.BlockSpec(memory_space=pltpu.VMEM)
-    return pl.pallas_call(
-        functools.partial(inverse_kernel, count, size),
-        out_shape=[jax.ShapeDtypeStruct((size, size), jnp.float32)] * count,
-        in_specs=[spec] * count,
-        out_specs=[spec] * count,
+        if k == 0:
+            work[k][...] = gram_ref[...]
+        elif width == size:
+            work[k][...] = mine_ref[k - 1]
+        else:
+            mine, other = mine_ref[k - 1], other_ref[k - 1]
+            work[k][:, :width] = jnp.where(swap, other, mine)
+            work[k][:, width:] = jnp.where(swap, mine, other)
+        for t in range(0, half, LANES):
+            inverse[k][:, t : t + LANES] = jnp.zeros((half, LANES), jnp.float32)
+    node_factor(work, inverse, 0, half, BASE)
+    for k in range(count):
+        x1 = inverse[k][...]
+        l21 = dot3(work[k][half:, :half], x1, NT)
+        rest[k][...] = work[k][half:, half:] - dot3(l21, l21, NT)
+        kept[k][...] = dot3(l21, x1, NN)
+
+
+def second_kernel(count, half, *refs):
+    inverse, rest, kept = refs[:count], refs[count : 2 * count], refs[2 * count : 3 * count]
+    out = refs[3 * count : 4 * count]
+    work, second = refs[4 * count : 5 * count], refs[5 * count :]
+    for k in range(count):
+        work[k][...] = rest[k][...]
+        for t in range(0, half, LANES):
+            second[k][:, t : t + LANES] = jnp.zeros((half, LANES), jnp.float32)
+        out[k][:half, :half] = inverse[k][...]
+        out[k][:half, half:] = jnp.zeros((half, half), jnp.float32)
+    node_factor(work, second, 0, half, BASE)
+    for k in range(count):
+        x2 = second[k][...]
+        out[k][half:, half:] = x2
+        out[k][half:, :half] = -dot3(x2, kept[k][...], NN)
+
+
+def factor_first(core, gram, mine, other):
+    count, size = mine.shape[0] + 1, gram.shape[0]
+    half = size // 2
+    vmem = pl.BlockSpec(memory_space=pltpu.VMEM)
+    smem = pl.BlockSpec(memory_space=pltpu.SMEM)
+    return pl.pallas_call(
+        functools.partial(first_kernel, size),
+        out_shape=[jax.ShapeDtypeStruct((half, half), jnp.float32)] * (3 * count),
+        in_specs=[smem, vmem, vmem, vmem],
+        out_specs=[vmem] * (3 * count),
         scratch_shapes=[pltpu.VMEM((size, size), jnp.float32)] * count,
-        cost_estimate=pl.CostEstimate(flops=15 * 10**9, bytes_accessed=8 * count * size**2, transcendentals=0),
-        name="factor_inverse",
-    )(*grams)
+        cost_estimate=pl.CostEstimate(flops=7 * 10**9, bytes_accessed=8 * count * size**2, transcendentals=0),
+        name="factor_first",
+    )(core, gram, mine, other)
+
+
+def factor_second(parts):
+    count, half = len(parts) // 3, parts[0].shape[0]
+    vmem = pl.BlockSpec(memory_space=pltpu.VMEM)
+    return pl.pallas_call(
+        functools.partial(second_kernel, count, half),
+        out_shape=[jax.ShapeDtypeStruct((2 * half, 2 * half), jnp.float32)] * count,
+        in_specs=[vmem] * (3 * count),
+        out_specs=[vmem] * count,
+        scratch_shapes=[pltpu.VMEM((half, half), jnp.float32)] * (2 * count),
+        cost_estimate=pl.CostEstimate(flops=7 * 10**9, bytes_accessed=32 * count * half**2, transcendentals=0),
+        name="factor_second",
+    )(*parts)
 
 
 def near_kernel(groups, block_count, slot_count, index_ref, count_ref, *refs):
@@ -158,14 +207,12 @@
     size = blocks_ref.shape[2]
     for b in range(block_count):
         rows = pl.ds(b * size, size)
-        out_ref[rows, :] = base_ref[rows, :]
+        total = base_ref[rows, :]
         for j in range(slot_count):
-
-            @pl.when(j < count_ref[b])
-            def _(b=b, j=j, rows=rows):
-                start = pl.multiple_of(index_ref[b, j] * size, size)
-                piece = ext[pl.ds(start, size), :]
-                out_ref[rows, :] -= dot3(blocks_ref[b, j], piece, NN)
+            start = pl.multiple_of(index_ref[b, j] * size, size)
+            piece = jnp.where(j < count_ref[b], ext[pl.ds(start, size), :], 0.0)
+            total = total - dot3(blocks_ref[b, j], piece, NN)
+        out_ref[rows, :] = total
 
 
 def near_apply(blocks, base, pieces, index, count):
@@ -193,36 +240,103 @@
     )(index, count, blocks, base, *pieces)
 
 
-def fold_kernel(index_ref, count_ref, blocks_ref, sketch_ref, out_ref):
+def leaf_kernel(core_ref, mine_ref, other_ref, sketch_ref, turned_ref, gram_ref, part_ref):
+    width = mine_ref.shape[1]
+    if width == gram_ref.shape[0]:
+        sketch = mine_ref[...]
+    else:
+        swap = core_ref[0] == 1
+        mine, other = mine_ref[...], other_ref[...]
+        sketch = jnp.concatenate([jnp.where(swap, other, mine), jnp.where(swap, mine, other)], axis=1)
+    sketch_ref[...] = sketch
+    turned = sketch.T
+    turned_ref[...] = turned
+    gram = dot3(turned, sketch, NN)
+    gram_ref[...] = gram
+    rank = gram.shape[0]
+    part_ref[...] = jnp.where(core_ref[0] == 1, gram[:, rank - width :], gram[:, :width])
+
+
+def leaf_products(core, mine, other, rank):
+    rows, width = mine.shape
+    vmem = pl.BlockSpec(memory_space=pltpu.VMEM)
+    smem = pl.BlockSpec(memory_space=pltpu.SMEM)
+    shapes = [(rows, rank), (rank, rows), (rank, rank), (rank, width)]
+    return pl.pallas_call(
+        leaf_kernel,
+        out_shape=[jax.ShapeDtypeStruct(shape, jnp.float32) for shape in shapes],
+        in_specs=[smem, vmem, vmem],
+        out_specs=[vmem] * 4,
+        cost_estimate=pl.CostEstimate(flops=6 * rows * rank * rank, bytes_accessed=16 * rows * rank, transcendentals=0),
+        name="leaf_products",
+    )(core, mine, other)
+
+
+def fold_kernel(index_ref, count_ref, blocks_ref, turned_ref, out_ref):
     block_count, slot_count, size, _ = blocks_ref.shape
     out_ref[...] = jnp.zeros(out_ref.shape, jnp.float32)
     for b in range(block_count):
+        turned = turned_ref[:, b * size : (b + 1) * size]
         for j in range(slot_count):
-
-            @pl.when(j < count_ref[b])
-            def _(b=b, j=j):
-                target = pl.ds(pl.multiple_of(index_ref[b, j] * size, size), size)
-                rows = pl.ds(b * size, size)
-                out_ref[target, :] += dot3(blocks_ref[b, j], sketch_ref[rows, :], TN)
-
-
-def near_fold(blocks, sketch, index, count, total):
+            block = jnp.where(j < count_ref[b], blocks_ref[b, j], 0.0)
+            out_ref[index_ref[b, j]] -= dot3(turned, block, NN)
+
+
+def near_fold(blocks, turned, index, count):
     block_count, slot_count, size, _ = blocks.shape
-    rank = sketch.shape[1]
+    rank = turned.shape[0]
     vmem = pl.BlockSpec(memory_space=pltpu.VMEM)
     smem = pl.BlockSpec(memory_space=pltpu.SMEM)
     return pl.pallas_call(
         fold_kernel,
-        out_shape=jax.ShapeDtypeStruct((total, rank), jnp.float32),
+        out_shape=jax.ShapeDtypeStruct((3 * block_count, rank, size), jnp.float32),
         in_specs=[smem, smem, vmem, vmem],
         out_specs=vmem,
         cost_estimate=pl.CostEstimate(
             flops=6 * block_count * slot_count * size * size * rank,
-            bytes_accessed=4 * (total * rank + sketch.size + blocks.size),
+            bytes_accessed=4 * (turned.size + blocks.size + 3 * block_count * rank * size),
             transcendentals=0,
         ),
         name="near_fold",
-    )(index, count, blocks, sketch)
+    )(index, count, blocks, turned)
+
+
+def reduce_kernel(place_ref, *refs):
+    count = LEVELS
+    inverses, first, first_other = refs[:count], refs[count], refs[count + 1]
+    early, last = refs[count + 2 : count + 6], refs[count + 6 : count + 10]
+    out_ref, stage = refs[count + 10 :]
+    rank = inverses[0].shape[0]
+    half, quarter = rank // 2, rank // 4
+    for h in range(count):
+        if h == 0:
+            parts = [(half, first[...], 0), (half, first_other[...], 1)]
+        elif h < count - 1:
+            parts = [(quarter, early[i][h - 1], 2 + i) for i in range(4)]
+        else:
+            parts = [(quarter, last[i][...], 2 + i) for i in range(4)]
+        for depth, value, at in parts:
+            stage[h, pl.ds(pl.multiple_of(place_ref[at], depth), depth), :] = value
+    for h in range(count):
+        out_ref[h, 0] = dot3(inverses[h][...], stage[h], NN)
+
+
+def reduce_all(place, inverses, first, early, last):
+    rank, width = inverses[0].shape[0], last[0].shape[1]
+    vmem = pl.BlockSpec(memory_space=pltpu.VMEM)
+    smem = pl.BlockSpec(memory_space=pltpu.SMEM)
+    args = [*inverses, *first, *early, *last]
+    return pl.pallas_call(
+        reduce_kernel,
+        out_shape=jax.ShapeDtypeStruct((LEVELS, 1, rank, width), jnp.float32),
+        in_specs=[smem] + [vmem] * len(args),
+        out_specs=vmem,
+        scratch_shapes=[pltpu.VMEM((LEVELS, rank, width), jnp.float32)],
+        cost_estimate=pl.CostEstimate(
+            flops=6 * LEVELS * rank * rank * width, bytes_accessed=8 * LEVELS * rank * (rank + width), transcendentals=0
+        ),
+        name="reduce_all",
+    )(place, *args)
 
 
 def across(value, axis, bit):
@@ -235,108 +349,104 @@
     return lax.ppermute(value, axis, [(i, t) for i, t in steps if 0 <= t < count])
 
 
-def halo(own, parts):
-    rows = own.shape[0] // parts
-    peer = [across(own[i * rows : (i + 1) * rows], "rows", 0) for i in range(parts)]
-    far = [relayed(piece, "rows") for piece in peer]
-    return far + [own] + peer
-
-
 def pick(flag, first, second):
     return jnp.where(flag, second, first)
 
 
-def shards(samples, probes, near_blocks, near_cols, near_count, sketch):
-    rows_dev, samp_dev = samples.shape
+def halves_of(value, bit):
+    half = value.shape[0] // 2
+    return pick(bit, value[:half], value[half:]), pick(bit, value[half:], value[:half])
+
+
+def leaf_and_levels(samples, probes, near_blocks, near_cols, near_count, sketch):
+    rows_dev, _ = samples.shape
     block_size = near_blocks.shape[2]
     block_count = rows_dev // block_size
     rank = sketch.shape[1]
     position = lax.axis_index("rows")
-    bits = [position >> h & 1 == 1 for h in range(LEVELS)]
+    bits = [position >> h & 1 for h in range(LEVELS)]
+    odd = bits[0] == 1
+    upper = bits[1] == 1
     halves = 2 if lax.axis_size("samp") == 2 else 1
-    core = lax.axis_index("samp") % 2 == 1
+    core = lax.axis_index("samp") % 2
+    core_flag = core.reshape(1).astype(jnp.int32)
 
     index = near_cols - (position * block_count - block_count)
-    swapped = jnp.where(index < block_count, index + 2 * block_count, jnp.where(index >= 2 * block_count, index - 2 * block_count, index))
-    index = jnp.where(bits[0], swapped, index)
+    moved = jnp.where(index < block_count, 2 * block_count, jnp.where(index >= 2 * block_count, -2 * block_count, 0))
+    index = index + jnp.where(odd, moved, 0)
+
+    blocks = [probes[i * block_size : (i + 1) * block_size] for i in range(block_count)]
+    peer = [across(blocks[i], "rows", 0) for i in range(block_count)]
+    far = [relayed(peer[i], "rows") for i in range(block_count)]
 
     if halves == 2:
         width = rank // 2
-        turned = pick(core, sketch, jnp.concatenate([sketch[:, width:], sketch[:, :width]], axis=1))
-        probe_part = jnp.dot(probes, turned, precision=HIGH)
-        sample_part = jnp.dot(samples, turned, precision=HIGH)
-        got_probe = across(probe_part[:, width:], "samp", 0)
-        got_sample = across(sample_part[:, width:], "samp", 0)
-        probe_sketch = probe_part[:, :width] + got_probe
-        sample_sketch = sample_part[:, :width] + got_sample
+        turned_sketch = pick(core == 1, sketch, jnp.concatenate([sketch[:, width:], sketch[:, :width]], axis=1))
+        probe_part = jnp.dot(probes, turned_sketch, precision=HIGH)
+        sample_part = jnp.dot(samples, turned_sketch, precision=HIGH)
+        probe_sketch = probe_part[:, :width] + across(probe_part[:, width:], "samp", 0)
+        sample_sketch = sample_part[:, :width] + across(sample_part[:, width:], "samp", 0)
     else:
-        width = rank
         probe_sketch = lax.psum(jnp.dot(probes, sketch, precision=HIGH), "samp")
         sample_sketch = lax.psum(jnp.dot(samples, sketch, precision=HIGH), "samp")
-    mine = near_apply(near_blocks, sample_sketch, halo(probe_sketch, 1), index, near_count)
-    if halves == 2:
-        other = across(mine, "samp", 0)
-        leaf_sketch = jnp.concatenate([pick(core, mine, other), pick(core, other, mine)], axis=1)
-    else:
-        leaf_sketch = mine
-
-    gram = jnp.einsum("rk,rl->kl", leaf_sketch, leaf_sketch, precision=HIGH)
-    part = pick(core, gram[:, :width], gram[:, rank - width :])
+    peer_sketch = across(probe_sketch, "rows", 0)
+    far_sketch = relayed(peer_sketch, "rows")
+    mine = near_apply(near_blocks, sample_sketch, [far_sketch, probe_sketch, peer_sketch], index, near_count)
+    other = across(mine, "samp", 0) if halves == 2 else mine
+    leaf_sketch, turned, gram, part = leaf_products(core_flag, mine, other, rank)
+
     sums = []
     for h in range(LEVELS):
         part = part + across(part, "rows", h)
         sums.append(part)
     sums = jnp.stack(sums)
-    if halves == 2:
-        other = across(sums, "samp", 0)
-        sums = jnp.concatenate([pick(core, sums, other), pick(core, other, sums)], axis=2)
-    leaf_inverse, *inverses = factor_inverse([gram] + [sums[h] for h in range(LEVELS)])
+    sums_other = across(sums, "samp", 0) if halves == 2 else sums
+    parts = factor_first(core_flag, gram, sums, sums_other)
+    leaf_inverse, *inverses = factor_second(parts)
     leaf_basis = lax.dot_general(leaf_sketch, leaf_inverse, (NT, ((), ())), precision=HIGH)
 
-    folded = near_fold(near_blocks, leaf_sketch, index, near_count, 3 * rows_dev)
-
-    def transposed(left, right):
-        return lax.dot_general(left, right, (TN, ((), ())), precision=HIGH)
-
-    pieces = halo(probes, block_count)
-    product = transposed(leaf_sketch, samples)
-    at = 0
-    terms = []
-    for piece in pieces:
-        depth = piece.shape[0]
-        terms.append(transposed(folded[at : at + depth], piece))
-        at += depth
-    parts = len(terms) // 2
-    for i in [parts] + [i for p in range(parts) for i in (parts + 1 + p, p)]:
-        product = product - terms[i]
-
-    def keep_send(value, bit):
-        half = value.shape[0] // 2
-        return pick(bit, value[:half], value[half:]), pick(bit, value[half:], value[:half])
-
-    def joined(value, bit, level):
-        other = across(value, "rows", level)
-        return jnp.concatenate([pick(bit, value, other), pick(bit, other, value)], axis=-2)
-
-    keep, send = keep_send(product, bits[0])
+    folded = near_fold(near_blocks, turned, index, near_count)
+
+    def times(left, right):
+        return jnp.dot(left, right, precision=HIGH)
+
+    product = times(turned, samples)
+    for i in range(block_count):
+        product = product + times(folded[block_count + i], blocks[i])
+    for i in range(block_count):
+        product = product + times(folded[2 * block_count + i], peer[i])
+    for i in range(block_count):
+        product = product + times(folded[i], far[i])
+
+    keep, send = halves_of(product, odd)
     first = keep + across(send, "rows", 0)
-    keep, send = keep_send(first, bits[1])
+    first_other = across(first, "rows", 0)
+    keep, send = halves_of(first, upper)
     quarter = keep + across(send, "rows", 1)
     quarters = [quarter]
     for h in range(2, LEVELS):
         quarter = quarter + across(quarter, "rows", h)
         quarters.append(quarter)
-    outputs = [joined(first, bits[0], 0)]
-    early = joined(joined(jnp.stack(quarters[:2]), bits[1], 1), bits[0], 0)
-    outputs += [early[0], early[1]]
-    outputs += [joined(joined(value, bits[1], 1), bits[0], 0) for value in quarters[2:]]
-    reduced = [jnp.dot(inverse, value, precision=HIGH) for inverse, value in zip(inverses, outputs)]
-    return (leaf_basis, jnp.stack(reduced)[:, None, :, :])
+
+    def gathered(value):
+        along = across(value, "rows", 1)
+        beside = across(value, "rows", 0)
+        diagonal = across(along, "rows", 0)
+        return [value, along, beside, diagonal]
+
+    early = gathered(jnp.stack(quarters[:-1]))
+    last = gathered(quarters[-1])
+    half = rank // 2
+    x, y = bits[0] * half, bits[1] * (half // 2)
+    fx, fy = half - x, half // 2 - y
+    place = jnp.stack([x, fx, x + y, x + fy, fx + y, fx + fy]).astype(jnp.int32)
+    reduced = reduce_all(place, inverses, [first, first_other], early, last)
+    return (leaf_basis, reduced)
 
 
 def solution(mesh):
     return jax.shard_map(
-        shards,
+        leaf_and_levels,
         mesh=mesh,
         in_specs=(
             P("rows", "samp"),

time: 144 us -> 165 us (1.15)
  waiting for transfers between devices: 26.2 us -> 52.5 us
  other arithmetic: 13.1 us -> 2.88 us
  Pallas kernels: 27.9 us -> 37.5 us
  starting transfers between devices: 48.7 us -> 44.7 us
  matrix products: 21.4 us -> 18.4 us
  local copies, waits for them, and re-layouts: 5.02 us -> 6.87 us
    ppermute x21 -> x23, waiting for transfers between devices: 21.4 us -> 41.5 us  [across(): lax.ppermute(value, axis, [(i, i ^ 1 << bit) for i in range(lax.axis_size...]
    pallas_call x2 -> x5, Pallas kernels: 22.8 us -> 32.7 us  [the longest x1 11.7 us: factor_first(): pl.pallas_call(functools.partial(first_kernel, size), out_shape=[jax.Shap...]
    ppermute x4, waiting for transfers between devices: 4.73 us -> 11 us  [relayed(): lax.ppermute(value, axis, [(i, t) for i, t in steps if 0 <= t < count])]
    select_n x10 -> x2, other arithmetic: 4.34 us -> 0.06 us  [pick(): return jnp.where(flag, second, first)]
    ppermute x4, starting transfers between devices: 18.5 us -> 15.3 us  [relayed(): lax.ppermute(value, axis, [(i, t) for i, t in steps if 0 <= t < count])]
    dot_general x16 -> x13, matrix products: 21.4 us -> 18.4 us  [the longest x10 12.8 us: times(): return jnp.dot(left, right, precision=HIGH)]
    concatenate x3 -> x0, other arithmetic: 2.61 us -> none  [the longest x2 1.61 us: joined(): jnp.concatenate([pick(bit, value, other), pick(bit, other, value)], axis=-2)]
    unnamed x36, local copies, waits for them, and re-layouts: 0.83 us -> 3.09 us
  transfers between devices with their start and end apart: 25 -> 27, of which waited for: 10 -> 12; matrix products, arithmetic and copies ran while one was open for 22% -> 13% of each run, Pallas kernels for 19% -> 20%
where the time goes in v3:
time: 165 us; the launch traced here: 164 us
  waiting for transfers between devices  52.5 us (32%)
  starting transfers between devices  44.7 us (27%)
  Pallas kernels  37.5 us (23%)
  matrix products  18.4 us (11%)
  local copies, waits for them, and re-layouts  6.87 us (4%)
  other arithmetic  2.88 us (2%)
    ppermute x23, waiting for transfers between devices, across(): lax.ppermute(value, axis, [(i, i ^ 1 << bit) for i in range(lax.axis_size...  41.5 us
    ppermute x23, starting transfers between devices, across(): lax.ppermute(value, axis, [(i, i ^ 1 << bit) for i in range(lax.axis_size...  29.3 us
    ppermute x4, starting transfers between devices, relayed(): lax.ppermute(value, axis, [(i, t) for i, t in steps if 0 <= t < count])  15.3 us
    dot_general x10, matrix products, times(): return jnp.dot(left, right, precision=HIGH)  12.8 us
    pallas_call x1, Pallas kernels, factor_first(): pl.pallas_call(functools.partial(first_kernel, size), out_shape=[jax.Shap...  11.7 us
    ppermute x4, waiting for transfers between devices, relayed(): lax.ppermute(value, axis, [(i, t) for i, t in steps if 0 <= t < count])  11 us
    pallas_call x1, Pallas kernels, factor_second(): pl.pallas_call(functools.partial(second_kernel, count, half), out_shape=[...  9.6 us
    pallas_call x1, Pallas kernels, near_apply(): pl.pallas_call(functools.partial(near_kernel, len(pieces), block_count, s...  4.81 us
  transfers between devices with their start and end apart: 27, of which 12 were waited for; matrix products, arithmetic and copies ran while one was open for 13% of the time, Pallas kernels for 20%

profile of v3, /device:TPU:0, one launch (start us, length us, event | category | flops | bytes accessed | tf_op | source)
XLA Modules:
  0.0 163.9 jit_solution(9283839102115643394)
XLA Ops:
  0.7 1.2 fusion.21
  1.9 2.4 %convolution_bitcast_fusion = f32[768,256]{1,0:T(8,128)S(1)} fusion(f32[768,512]{1,0:T(8,128)} %param.7, f32[512,256]{1,0:T(8,128)} %param.11, f32[512,128]{1,0:T(8,128)S(1)} %get-tuple-element.54, f32[512,128]{1,0:T(8,128)S(1)} %get-tuple-element.53, pred[]{:T(512)S(6)} %eq.12), kind=kOutput, calls=%fused_computation | convolution fusion | flops 604241920 | bytes 3407873 | tf_op jit(solution)/shard_map/dot_general | solution.py:385
  4.7 1.4 collective-permute-done.1
  6.2 3.0 %collective-permute-start.2 = (f32[768,128]{1,0:T(8,128)S(1)}, f32[768,128]{1,0:T(8,128)}, u32[]{:S(2)}, u32[]{:S(2)}) collective-permute-start(f32[768,128]{1,0:T(8,128)S(1)} %slice_add_fusion.refs_3_), channel_id=1, source_target_pairs={{0,2},{2,0},{4,6},{6,4},{8,10},{10,8},{12,14},{14,12},{16,18},{18,... | collective-permute-start | bytes 1179656 | tf_op jit(solution)/shard_map/ppermute | solution.py:343
  11.7 1.2 fusion.20
  13.1 1.9 %collective-permute-start.10 = (f32[256,512]{1,0:T(8,128)}, f32[256,512]{1,0:T(8,128)}, u32[]{:S(2)}, u32[]{:S(2)}) collective-permute-start(f32[256,512]{1,0:T(8,128)} %get-tuple-element.50), channel_id=1, source_target_pairs={{0,2},{2,0},{4,6},{6,4},{8,10},{10,8},{12,14},{14,12},{16,18},{18,... | collective-permute-start | bytes 1572872 | tf_op jit(solution)/shard_map/ppermute | solution.py:343
  15.1 4.2 %collective-permute-done.2.refs_4_ = f32[768,128]{1,0:T(8,128)} collective-permute-done((f32[768,128]{1,0:T(8,128)S(1)}, f32[768,128]{1,0:T(8,128)}, u32[]{:S(2)}, u32[]{:S(2)}) %collective-permute-start.2) | collective-permute-done | bytes 393248 | tf_op jit(solution)/shard_map/ppermute | solution.py:343
  19.3 4.0 %collective-permute-start.3 = (f32[768,128]{1,0:T(8,128)}, f32[768,128]{1,0:T(8,128)S(1)}, u32[]{:S(2)}, u32[]{:S(2)}) collective-permute-start(f32[768,128]{1,0:T(8,128)} %collective-permute-done.2.refs_4_), channel_id=1, source_target_pairs={{0,4},{4,8},{6,2},{8,12},{10,6},{12,16},{14,10},{16,20},{18,14},{2... | collective-permute-start | bytes 1179656 | tf_op jit(solution)/shard_map/ppermute | solution.py:349
  23.9 1.9 %slice_add_fusion.1.refs_1_ = f32[768,128]{1,0:T(8,128)} fusion(f32[768,128]{1,0:T(8,128)} %collective-permute-done, f32[768,256]{1,0:T(8,128)} %copy-done.5), kind=kLoop, calls=%fused_computation.14 | loop fusion | flops 98304 | bytes 1179648 | tf_op jit(solution)/shard_map/add | solution.py:388
  25.8 4.8 %collective-permute-done.3.refs_2_ = f32[768,128]{1,0:T(8,128)S(1)} collective-permute-done((f32[768,128]{1,0:T(8,128)}, f32[768,128]{1,0:T(8,128)S(1)}, u32[]{:S(2)}, u32[]{:S(2)}) %collective-permute-start.3) | collective-permute-done | bytes 393248 | tf_op jit(solution)/shard_map/ppermute | solution.py:349
  31.3 4.8 %near_apply.1.mine_ref = f32[768,128]{1,0:T(8,128)} custom-call(s32[3,3]{1,0:T(4,128)} %select_add_fusion.2.index_ref, s32[3]{0:T(128)} %count_ref.3, f32[3,3,256,256]{3,2,1,0:T(8,128)} %blocks_ref.1, f32[768,128]{1,0:T(8,128)} %slice_add_fusion.1.refs_1_, f32[768,128]{1,0:T(8,128)} %copy-done.12, f32[768,128]{1,0:T(8,128)} %copy-done.7, ...), custom_call_target="tpu_custom_call" | custom-call | flops 452984832 | bytes 4325376 | tf_op jit(solution)/shard_map/near_apply/pallas_call | solution.py:225
  36.2 16.3 %collective-permute-done.12 = f32[256,512]{1,0:T(8,128)} collective-permute-done((f32[256,512]{1,0:T(8,128)}, f32[256,512]{1,0:T(8,128)}, u32[]{:S(2)}, u32[]{:S(2)}) %collective-permute-start.12) | collective-permute-done | bytes 524320 | tf_op jit(solution)/shard_map/ppermute | solution.py:343
  52.5 4.5 %collective-permute-start.15 = (f32[256,512]{1,0:T(8,128)}, f32[256,512]{1,0:T(8,128)}, u32[]{:S(2)}, u32[]{:S(2)}) collective-permute-start(f32[256,512]{1,0:T(8,128)} %collective-permute-done.12), channel_id=1, source_target_pairs={{0,4},{4,8},{6,2},{8,12},{10,6},{12,16},{14,10},{16,20},{18,14},{2... | collective-permute-start | bytes 1572872 | tf_op jit(solution)/shard_map/ppermute | solution.py:349
  57.0 3.4 %collective-permute-start.14 = (f32[256,512]{1,0:T(8,128)}, f32[256,512]{1,0:T(8,128)}, u32[]{:S(2)}, u32[]{:S(2)}) collective-permute-start(f32[256,512]{1,0:T(8,128)} %collective-permute-done.11), channel_id=1, source_target_pairs={{0,4},{4,8},{6,2},{8,12},{10,6},{12,16},{14,10},{16,20},{18,14},{2... | collective-permute-start | bytes 1572872 | tf_op jit(solution)/shard_map/ppermute | solution.py:349
  60.4 3.5 %collective-permute-start.13 = (f32[256,512]{1,0:T(8,128)}, f32[256,512]{1,0:T(8,128)}, u32[]{:S(2)}, u32[]{:S(2)}) collective-permute-start(f32[256,512]{1,0:T(8,128)} %collective-permute-done.10), channel_id=1, source_target_pairs={{0,4},{4,8},{6,2},{8,12},{10,6},{12,16},{14,10},{16,20},{18,14},{2... | collective-permute-start | bytes 1572872 | tf_op jit(solution)/shard_map/ppermute | solution.py:349
  64.6 2.5 %leaf_products.1 = (f32[768,256]{1,0:T(8,128)}, f32[256,768]{1,0:T(8,128)}, f32[256,256]{1,0:T(8,128)}, f32[256,128]{1,0:T(8,128)}) custom-call(s32[1]{0:T(128)} %bitcast.core_ref, f32[768,128]{1,0:T(8,128)} %near_apply.1.mine_ref, f32[768,128]{1,0:T(8,128)} %copy-done.17), custom_call_target="tpu_custom_call" | custom-call | flops 301989888 | bytes 3145728 | tf_op jit(solution)/shard_map/leaf_products/pallas_call | solution.py:265
  67.1 4.6 %near_fold.1 = f32[9,256,256]{2,1,0:T(8,128)} custom-call(s32[3,3]{1,0:T(4,128)} %select_add_fusion.2.index_ref, s32[3]{0:T(128)} %count_ref.3, f32[3,3,256,256]{3,2,1,0:T(8,128)} %blocks_ref.1, f32[256,768]{1,0:T(8,128)} %get-tuple-element.49.turned_ref), custom_call_target="tpu_custom_call" | custom-call | flops 905969664 | bytes 5505024 | tf_op jit(solution)/shard_map/near_fold/pallas_call | solution.py:290
  71.7 1.5 fusion.12
  73.2 1.3 fusion.13
  75.0 1.4 fusion.10
  76.5 1.5 fusion.11
  78.0 1.4 fusion.9
  79.4 1.4 fusion.7
  80.8 1.4 fusion.8
  82.3 1.0 fusion.4
  83.3 6.3 %collective-permute-done.13 = f32[256,512]{1,0:T(8,128)} collective-permute-done((f32[256,512]{1,0:T(8,128)}, f32[256,512]{1,0:T(8,128)}, u32[]{:S(2)}, u32[]{:S(2)}) %collective-permute-start.13) | collective-permute-done | bytes 524320 | tf_op jit(solution)/shard_map/ppermute | solution.py:349
  89.5 1.5 fusion.6
  91.1 2.5 %collective-permute-start.16 = (f32[128,512]{1,0:T(8,128)S(1)}, f32[128,512]{1,0:T(8,128)S(1)}, u32[]{:S(2)}, u32[]{:S(2)}) collective-permute-start(f32[128,512]{1,0:T(8,128)S(1)} %slice_select_fusion), channel_id=1, source_target_pairs={{0,2},{2,0},{4,6},{6,4},{8,10},{10,8},{12,14},{14,12},{16,18},{18,... | collective-permute-start | bytes 786440 | tf_op jit(solution)/shard_map/ppermute | solution.py:343
  93.6 2.5 %collective-permute-start.6 = (f32[256,128]{1,0:T(8,128)S(1)}, f32[256,128]{1,0:T(8,128)S(1)}, u32[]{:S(2)}, u32[]{:S(2)}) collective-permute-start(f32[256,128]{1,0:T(8,128)S(1)} %add.81), channel_id=1, source_target_pairs={{0,4},{2,6},{4,0},{6,2},{8,12},{10,14},{12,8},{14,10},{16,20},{18,... | collective-permute-start | bytes 393224 | tf_op jit(solution)/shard_map/ppermute | solution.py:343
  96.1 2.9 %collective-permute-done.6 = f32[256,128]{1,0:T(8,128)S(1)} collective-permute-done((f32[256,128]{1,0:T(8,128)S(1)}, f32[256,128]{1,0:T(8,128)S(1)}, u32[]{:S(2)}, u32[]{:S(2)}) %collective-permute-start.6) | collective-permute-done | bytes 131104 | tf_op jit(solution)/shard_map/ppermute | solution.py:343
  99.1 1.6 %collective-permute-start.7 = (f32[256,128]{1,0:T(8,128)S(1)}, f32[256,128]{1,0:T(8,128)S(1)}, u32[]{:S(2)}, u32[]{:S(2)}) collective-permute-start(f32[256,128]{1,0:T(8,128)S(1)} %add.82), channel_id=1, source_target_pairs={{0,8},{2,10},{4,12},{6,14},{8,0},{10,2},{12,4},{14,6},{16,24},{18,... | collective-permute-start | bytes 393224 | tf_op jit(solution)/shard_map/ppermute | solution.py:343
  100.8 3.3 %collective-permute-done.7 = f32[256,128]{1,0:T(8,128)S(1)} collective-permute-done((f32[256,128]{1,0:T(8,128)S(1)}, f32[256,128]{1,0:T(8,128)S(1)}, u32[]{:S(2)}, u32[]{:S(2)}) %collective-permute-start.7) | collective-permute-done | bytes 131104 | tf_op jit(solution)/shard_map/ppermute | solution.py:343
  104.1 4.0 %collective-permute-start.8 = (f32[256,128]{1,0:T(8,128)S(1)}, f32[256,128]{1,0:T(8,128)S(1)}, u32[]{:S(2)}, u32[]{:S(2)}) collective-permute-start(f32[256,128]{1,0:T(8,128)S(1)} %add.83), channel_id=1, source_target_pairs={{0,16},{2,18},{4,20},{6,22},{8,24},{10,26},{12,28},{14,30},{16,0},... | collective-permute-start | bytes 393224 | tf_op jit(solution)/shard_map/ppermute | solution.py:343
  108.1 2.1 %collective-permute-start.18 = (f32[64,512]{1,0:T(8,128)S(1)}, f32[64,512]{1,0:T(8,128)S(1)}, u32[]{:S(2)}, u32[]{:S(2)}) collective-permute-start(f32[64,512]{1,0:T(8,128)S(1)} %slice_select_fusion.1), channel_id=1, source_target_pairs={{0,4},{2,6},{4,0},{6,2},{8,12},{10,14},{12,8},{14,10},{16,20},{18,... | collective-permute-start | bytes 393224 | tf_op jit(solution)/shard_map/ppermute | solution.py:343
  110.2 2.3 %collective-permute-done.8 = f32[256,128]{1,0:T(8,128)S(1)} collective-permute-done((f32[256,128]{1,0:T(8,128)S(1)}, f32[256,128]{1,0:T(8,128)S(1)}, u32[]{:S(2)}, u32[]{:S(2)}) %collective-permute-start.8) | collective-permute-done | bytes 131104 | tf_op jit(solution)/shard_map/ppermute | solution.py:343
  113.7 4.9 %collective-permute-done.19 = f32[64,512]{1,0:T(8,128)S(1)} collective-permute-done((f32[64,512]{1,0:T(8,128)S(1)}, f32[64,512]{1,0:T(8,128)S(1)}, u32[]{:S(2)}, u32[]{:S(2)}) %collective-permute-start.19) | collective-permute-done | bytes 131104 | tf_op jit(solution)/shard_map/ppermute | solution.py:343
  118.6 1.8 %collective-permute-start.23 = (f32[64,512]{1,0:T(8,128)S(1)}, f32[64,512]{1,0:T(8,128)S(1)}, u32[]{:S(2)}, u32[]{:S(2)}) collective-permute-start(f32[64,512]{1,0:T(8,128)S(1)} %add.100), channel_id=1, source_target_pairs={{0,16},{2,18},{4,20},{6,22},{8,24},{10,26},{12,28},{14,30},{16,0},... | collective-permute-start | bytes 393224 | tf_op jit(solution)/shard_map/ppermute | solution.py:343
  120.4 1.9 %collective-permute-start.20 = (f32[2,64,512]{2,1,0:T(8,128)S(1)}, f32[2,64,512]{2,1,0:T(8,128)S(1)}, u32[]{:S(2)}, u32[]{:S(2)}) collective-permute-start(f32[2,64,512]{2,1,0:T(8,128)S(1)} %pad_maximum_fusion.1.refs_6_), channel_id=1, source_target_pairs={{0,4},{2,6},{4,0},{6,2},{8,12},{10,14},{12,8},{14,10},{16,20},{18,... | collective-permute-start | bytes 786440 | tf_op jit(solution)/shard_map/ppermute | solution.py:343
  122.3 4.6 %collective-permute-done.23 = f32[64,512]{1,0:T(8,128)S(1)} collective-permute-done((f32[64,512]{1,0:T(8,128)S(1)}, f32[64,512]{1,0:T(8,128)S(1)}, u32[]{:S(2)}, u32[]{:S(2)}) %collective-permute-start.23) | collective-permute-done | bytes 131104 | tf_op jit(solution)/shard_map/ppermute | solution.py:343
  126.9 2.5 %collective-permute-start.24 = (f32[64,512]{1,0:T(8,128)S(1)}, f32[64,512]{1,0:T(8,128)}, u32[]{:S(2)}, u32[]{:S(2)}) collective-permute-start(f32[64,512]{1,0:T(8,128)S(1)} %add.101.refs_10_), channel_id=1, source_target_pairs={{0,4},{2,6},{4,0},{6,2},{8,12},{10,14},{12,8},{14,10},{16,20},{18,... | collective-permute-start | bytes 393224 | tf_op jit(solution)/shard_map/ppermute | solution.py:343
  130.0 2.0 %collective-permute-start.21 = (f32[2,64,512]{2,1,0:T(8,128)S(1)}, f32[2,64,512]{2,1,0:T(8,128)}, u32[]{:S(2)}, u32[]{:S(2)}) collective-permute-start(f32[2,64,512]{2,1,0:T(8,128)S(1)} %pad_maximum_fusion.1.refs_6_), channel_id=1, source_target_pairs={{0,2},{2,0},{4,6},{6,4},{8,10},{10,8},{12,14},{14,12},{16,18},{18,... | collective-permute-start | bytes 786440 | tf_op jit(solution)/shard_map/ppermute | solution.py:343
  132.1 1.1 collective-permute-done.24.refs_11_
  133.2 0.9 collective-permute-start.22
  134.1 1.1 collective-permute-start.26
  135.2 11.7 %factor_first.1 = (f32[128,128]{1,0:T(8,128)}, f32[128,128]{1,0:T(8,128)}, f32[128,128]{1,0:T(8,128)}, f32[128,128]{1,0:T(8,128)}, f32[128,128]{1,0:T(8,128)}, /...) custom-call(s32[1]{0:T(128)} %bitcast.core_ref, ...), custom_call_target="tpu_custom_call" | custom-call | flops 7000000000 | bytes 2621440 | tf_op jit(solution)/shard_map/factor_first/pallas_call | solution.py:168
  146.9 9.6 %factor_second.1 = (f32[256,256]{1,0:T(8,128)}, f32[256,256]{1,0:T(8,128)}, f32[256,256]{1,0:T(8,128)}, f32[256,256]{1,0:T(8,128)}, f32[256,256]{1,0:T(8,128)}) custom-call(f32[128,128]{1,0:T(8,128)} %get-tuple-element.29.refs_0_, f32[128,128]{1,0:T(8,128)} %get-tuple-element.30.refs_1_, f32[128,128]{1,0:T(8,128)} %get-tuple-element.31.refs_2_, ...), custom_call_target="tpu_custom_call" | custom-call | flops 7000000000 | bytes 2621440 | tf_op jit(solution)/shard_map/factor_second/pallas_call | solution.py:182
  156.5 2.3 %fusion.22 = f32[768,256]{1,0:T(8,128)} fusion(f32[768,256]{1,0:T(8,128)S(1)} %copy-done.9, f32[256,256]{1,0:T(8,128)} %get-tuple-element.44), kind=kOutput, calls=%fused_computation.46 | convolution fusion | flops 301989888 | bytes 1835008 | tf_op jit(solution)/shard_map/dot_general | solution.py:406
  159.6 4.3 %reduce_all.1 = f32[4,1,256,512]{3,2,1,0:T(8,128)} custom-call(s32[6]{0:T(128)} %stack.56.place_ref, f32[256,256]{1,0:T(8,128)} %get-tuple-element.45.refs_0_, f32[256,256]{1,0:T(8,128)} %get-tuple-element.46.refs_1_, f32[256,256]{1,0:T(8,128)} %get-tuple-element.47.refs_2_, f32[256,256]{1,0:T(8,128)} %get-tuple-element.48.refs_3_, f32[128,512]{1,0:T(8,128)} %copy-done.4, ...), custom_call_target="tpu_custom_call" | custom-call | flops 805306368 | bytes 6291456 | tf_op jit(solution)/shard_map/reduce_all/pallas_call | solution.py:329
  (81 shorter events, 8.8 us)
Async XLA Ops:
  0.6 8.6 %copy-start = (f32[768,512]{1,0:T(8,128)S(1)}, f32[768,512]{1,0:T(8,128)}, u32[]{:S(2)}) copy-start(f32[768,512]{1,0:T(8,128)} %param.6) | copy-start | bytes 4718596
  1.8 7.4 %copy-start.3 = (f32[512,256]{1,0:T(8,128)S(1)}, f32[512,256]{1,0:T(8,128)}, u32[]{:S(2)}) copy-start(f32[512,256]{1,0:T(8,128)} %param.11) | copy-start | bytes 1572868
  4.3 1.8 %collective-permute-start.1 = (f32[768,128]{1,0:T(8,128)S(1)}, f32[768,128]{1,0:T(8,128)S(1)}, u32[]{:S(2)}, u32[]{:S(2)}) collective-permute-start(f32[768,128]{1,0:T(8,128)S(1)} %slice.95), channel_id=1, source_target_pairs={{0,1},{1,0},{2,3},{3,2},{4,5},{5,4},{6,7},{7,6},{8,9},{9,8},{10,11... | collective-permute-start | bytes 1179656 | tf_op jit(solution)/shard_map/ppermute | solution.py:343
  6.2 6.7 %copy-start.7 = (f32[768,128]{1,0:T(8,128)}, f32[768,128]{1,0:T(8,128)S(1)}, u32[]{:S(2)}) copy-start(f32[768,128]{1,0:T(8,128)S(1)} %slice_add_fusion.refs_3_) | copy-start | bytes 1179652
  6.2 5.5 %copy-start.1 = (f32[768,512]{1,0:T(8,128)S(1)}, f32[768,512]{1,0:T(8,128)}, u32[]{:S(2)}) copy-start(f32[768,512]{1,0:T(8,128)} %param.7) | copy-start | bytes 4718596
  6.2 13.1 %collective-permute-start.2 = (f32[768,128]{1,0:T(8,128)S(1)}, f32[768,128]{1,0:T(8,128)}, u32[]{:S(2)}, u32[]{:S(2)}) collective-permute-start(f32[768,128]{1,0:T(8,128)S(1)} %slice_add_fusion.refs_3_), channel_id=1, source_target_pairs={{0,2},{2,0},{4,6},{6,4},{8,10},{10,8},{12,14},{14,12},{16,18},{18,... | collective-permute-start | bytes 1179656 | tf_op jit(solution)/shard_map/ppermute | solution.py:343
  10.1 0.9 copy-start.5
  10.9 12.3 %copy-start.16 = (s32[3,3]{1,0:T(4,128)S(1)}, s32[3,3]{1,0:T(4,128)}, u32[]{:S(2)}) copy-start(s32[3,3]{1,0:T(4,128)} %param.9) | copy-start | bytes 112
  11.7 12.2 %collective-permute-start = (f32[768,128]{1,0:T(8,128)}, f32[768,128]{1,0:T(8,128)}, u32[]{:S(2)}, u32[]{:S(2)}) collective-permute-start(f32[768,128]{1,0:T(8,128)} %slice.93), channel_id=1, source_target_pairs={{0,1},{1,0},{2,3},{3,2},{4,5},{5,4},{6,7},{7,6},{8,9},{9,8},{10,11... | collective-permute-start | bytes 1179656 | tf_op jit(solution)/shard_map/ppermute | solution.py:343
  12.9 44.0 %collective-permute-start.11 = (f32[256,512]{1,0:T(8,128)}, f32[256,512]{1,0:T(8,128)}, u32[]{:S(2)}, u32[]{:S(2)}) collective-permute-start(f32[256,512]{1,0:T(8,128)} %get-tuple-element.52), channel_id=1, source_target_pairs={{0,2},{2,0},{4,6},{6,4},{8,10},{10,8},{12,14},{14,12},{16,18},{18,... | collective-permute-start | bytes 1572872 | tf_op jit(solution)/shard_map/ppermute | solution.py:343
  13.1 47.3 %collective-permute-start.10 = (f32[256,512]{1,0:T(8,128)}, f32[256,512]{1,0:T(8,128)}, u32[]{:S(2)}, u32[]{:S(2)}) collective-permute-start(f32[256,512]{1,0:T(8,128)} %get-tuple-element.50), channel_id=1, source_target_pairs={{0,2},{2,0},{4,6},{6,4},{8,10},{10,8},{12,14},{14,12},{16,18},{18,... | collective-permute-start | bytes 1572872 | tf_op jit(solution)/shard_map/ppermute | solution.py:343
  15.0 37.5 %collective-permute-start.12 = (f32[256,512]{1,0:T(8,128)}, f32[256,512]{1,0:T(8,128)}, u32[]{:S(2)}, u32[]{:S(2)}) collective-permute-start(f32[256,512]{1,0:T(8,128)} %get-tuple-element.51), channel_id=1, source_target_pairs={{0,2},{2,0},{4,6},{6,4},{8,10},{10,8},{12,14},{14,12},{16,18},{18,... | collective-permute-start | bytes 1572872 | tf_op jit(solution)/shard_map/ppermute | solution.py:343
  19.3 11.2 %collective-permute-start.3 = (f32[768,128]{1,0:T(8,128)}, f32[768,128]{1,0:T(8,128)S(1)}, u32[]{:S(2)}, u32[]{:S(2)}) collective-permute-start(f32[768,128]{1,0:T(8,128)} %collective-permute-done.2.refs_4_), channel_id=1, source_target_pairs={{0,4},{4,8},{6,2},{8,12},{10,6},{12,16},{14,10},{16,20},{18,14},{2... | collective-permute-start | bytes 1179656 | tf_op jit(solution)/shard_map/ppermute | solution.py:349
  30.5 0.7 copy-start.12
  36.1 27.7 %collective-permute-start.4 = (f32[768,128]{1,0:T(8,128)}, f32[768,128]{1,0:T(8,128)S(1)}, u32[]{:S(2)}, u32[]{:S(2)}) collective-permute-start(f32[768,128]{1,0:T(8,128)} %near_apply.1.mine_ref), channel_id=1, source_target_pairs={{0,1},{1,0},{2,3},{3,2},{4,5},{5,4},{6,7},{7,6},{8,9},{9,8},{10,11... | collective-permute-start | bytes 1179656 | tf_op jit(solution)/shard_map/ppermute | solution.py:343
  52.5 26.9 %collective-permute-start.15 = (f32[256,512]{1,0:T(8,128)}, f32[256,512]{1,0:T(8,128)}, u32[]{:S(2)}, u32[]{:S(2)}) collective-permute-start(f32[256,512]{1,0:T(8,128)} %collective-permute-done.12), channel_id=1, source_target_pairs={{0,4},{4,8},{6,2},{8,12},{10,6},{12,16},{14,10},{16,20},{18,14},{2... | collective-permute-start | bytes 1572872 | tf_op jit(solution)/shard_map/ppermute | solution.py:349
  57.0 23.9 %collective-permute-start.14 = (f32[256,512]{1,0:T(8,128)}, f32[256,512]{1,0:T(8,128)}, u32[]{:S(2)}, u32[]{:S(2)}) collective-permute-start(f32[256,512]{1,0:T(8,128)} %collective-permute-done.11), channel_id=1, source_target_pairs={{0,4},{4,8},{6,2},{8,12},{10,6},{12,16},{14,10},{16,20},{18,14},{2... | collective-permute-start | bytes 1572872 | tf_op jit(solution)/shard_map/ppermute | solution.py:349
  60.4 29.1 %collective-permute-start.13 = (f32[256,512]{1,0:T(8,128)}, f32[256,512]{1,0:T(8,128)}, u32[]{:S(2)}, u32[]{:S(2)}) collective-permute-start(f32[256,512]{1,0:T(8,128)} %collective-permute-done.10), channel_id=1, source_target_pairs={{0,4},{4,8},{6,2},{8,12},{10,6},{12,16},{14,10},{16,20},{18,14},{2... | collective-permute-start | bytes 1572872 | tf_op jit(solution)/shard_map/ppermute | solution.py:349
  63.8 0.7 copy-start.17
  71.7 2.8 %copy-start.2 = (f32[9,256,256]{2,1,0:T(8,128)S(1)}, f32[9,256,256]{2,1,0:T(8,128)}, u32[]{:S(2)}) copy-start(f32[9,256,256]{2,1,0:T(8,128)} %near_fold.1) | copy-start | bytes 7077892
  71.7 3.2 %copy-start.15 = (f32[256,128]{1,0:T(8,128)S(1)}, f32[256,128]{1,0:T(8,128)}, u32[]{:S(2)}) copy-start(f32[256,128]{1,0:T(8,128)} %get-tuple-element.28) | copy-start | bytes 393220
  74.9 18.6 %collective-permute-start.5 = (f32[256,128]{1,0:T(8,128)S(1)}, f32[256,128]{1,0:T(8,128)S(1)}, u32[]{:S(2)}, u32[]{:S(2)}) collective-permute-start(f32[256,128]{1,0:T(8,128)S(1)} %copy-done.15), channel_id=1, source_target_pairs={{0,2},{2,0},{4,6},{6,4},{8,10},{10,8},{12,14},{14,12},{16,18},{18,... | collective-permute-start | bytes 393224 | tf_op jit(solution)/shard_map/ppermute | solution.py:343
  76.4 5.8 %copy-start.6 = (f32[256,768]{1,0:T(8,128)S(1)}, f32[256,768]{1,0:T(8,128)}, u32[]{:S(2)}) copy-start(f32[256,768]{1,0:T(8,128)} %get-tuple-element.49.turned_ref) | copy-start | bytes 2359300
  91.1 9.6 %collective-permute-start.16 = (f32[128,512]{1,0:T(8,128)S(1)}, f32[128,512]{1,0:T(8,128)S(1)}, u32[]{:S(2)}, u32[]{:S(2)}) collective-permute-start(f32[128,512]{1,0:T(8,128)S(1)} %slice_select_fusion), channel_id=1, source_target_pairs={{0,2},{2,0},{4,6},{6,4},{8,10},{10,8},{12,14},{14,12},{16,18},{18,... | collective-permute-start | bytes 786440 | tf_op jit(solution)/shard_map/ppermute | solution.py:343
  93.6 5.4 %collective-permute-start.6 = (f32[256,128]{1,0:T(8,128)S(1)}, f32[256,128]{1,0:T(8,128)S(1)}, u32[]{:S(2)}, u32[]{:S(2)}) collective-permute-start(f32[256,128]{1,0:T(8,128)S(1)} %add.81), channel_id=1, source_target_pairs={{0,4},{2,6},{4,0},{6,2},{8,12},{10,14},{12,8},{14,10},{16,20},{18,... | collective-permute-start | bytes 393224 | tf_op jit(solution)/shard_map/ppermute | solution.py:343
  99.1 5.0 %collective-permute-start.7 = (f32[256,128]{1,0:T(8,128)S(1)}, f32[256,128]{1,0:T(8,128)S(1)}, u32[]{:S(2)}, u32[]{:S(2)}) collective-permute-start(f32[256,128]{1,0:T(8,128)S(1)} %add.82), channel_id=1, source_target_pairs={{0,8},{2,10},{4,12},{6,14},{8,0},{10,2},{12,4},{14,6},{16,24},{18,... | collective-permute-start | bytes 393224 | tf_op jit(solution)/shard_map/ppermute | solution.py:343
  100.8 46.1 %copy-start.4 = (f32[128,512]{1,0:T(8,128)}, f32[128,512]{1,0:T(8,128)S(1)}, u32[]{:S(2)}) copy-start(f32[128,512]{1,0:T(8,128)S(1)} %select_add_fusion.refs_4_) | copy-start | bytes 786436
  104.1 8.3 %collective-permute-start.8 = (f32[256,128]{1,0:T(8,128)S(1)}, f32[256,128]{1,0:T(8,128)S(1)}, u32[]{:S(2)}, u32[]{:S(2)}) collective-permute-start(f32[256,128]{1,0:T(8,128)S(1)} %add.83), channel_id=1, source_target_pairs={{0,16},{2,18},{4,20},{6,22},{8,24},{10,26},{12,28},{14,30},{16,0},... | collective-permute-start | bytes 393224 | tf_op jit(solution)/shard_map/ppermute | solution.py:343
  108.1 5.0 %collective-permute-start.18 = (f32[64,512]{1,0:T(8,128)S(1)}, f32[64,512]{1,0:T(8,128)S(1)}, u32[]{:S(2)}, u32[]{:S(2)}) collective-permute-start(f32[64,512]{1,0:T(8,128)S(1)} %slice_select_fusion.1), channel_id=1, source_target_pairs={{0,4},{2,6},{4,0},{6,2},{8,12},{10,14},{12,8},{14,10},{16,20},{18,... | collective-permute-start | bytes 393224 | tf_op jit(solution)/shard_map/ppermute | solution.py:343
  112.5 22.7 %copy-start.11 = (f32[4,256,128]{2,1,0:T(8,128)}, f32[4,256,128]{2,1,0:T(8,128)S(1)}, u32[]{:S(2)}) copy-start(f32[4,256,128]{2,1,0:T(8,128)S(1)} %pad_maximum_fusion.mine_ref) | copy-start | bytes 1572868
  112.5 21.6 %collective-permute-start.9 = (f32[4,256,128]{2,1,0:T(8,128)S(1)}, f32[4,256,128]{2,1,0:T(8,128)}, u32[]{:S(2)}, u32[]{:S(2)}) collective-permute-start(f32[4,256,128]{2,1,0:T(8,128)S(1)} %pad_maximum_fusion.mine_ref), channel_id=1, source_target_pairs={{0,1},{1,0},{2,3},{3,2},{4,5},{5,4},{6,7},{7,6},{8,9},{9,8},{10,11... | collective-permute-start | bytes 1572872 | tf_op jit(solution)/shard_map/ppermute | solution.py:343
  113.2 5.4 %collective-permute-start.19 = (f32[64,512]{1,0:T(8,128)S(1)}, f32[64,512]{1,0:T(8,128)S(1)}, u32[]{:S(2)}, u32[]{:S(2)}) collective-permute-start(f32[64,512]{1,0:T(8,128)S(1)} %select_add_fusion.1), channel_id=1, source_target_pairs={{0,8},{2,10},{4,12},{6,14},{8,0},{10,2},{12,4},{14,6},{16,24},{18,... | collective-permute-start | bytes 393224 | tf_op jit(solution)/shard_map/ppermute | solution.py:343
  118.6 8.3 %collective-permute-start.23 = (f32[64,512]{1,0:T(8,128)S(1)}, f32[64,512]{1,0:T(8,128)S(1)}, u32[]{:S(2)}, u32[]{:S(2)}) collective-permute-start(f32[64,512]{1,0:T(8,128)S(1)} %add.100), channel_id=1, source_target_pairs={{0,16},{2,18},{4,20},{6,22},{8,24},{10,26},{12,28},{14,30},{16,0},... | collective-permute-start | bytes 393224 | tf_op jit(solution)/shard_map/ppermute | solution.py:343
  120.4 26.5 %copy-start.8 = (f32[2,64,512]{2,1,0:T(8,128)}, f32[2,64,512]{2,1,0:T(8,128)S(1)}, u32[]{:S(2)}) copy-start(f32[2,64,512]{2,1,0:T(8,128)S(1)} %pad_maximum_fusion.1.refs_6_) | copy-start | bytes 786436
  120.4 11.6 %collective-permute-start.20 = (f32[2,64,512]{2,1,0:T(8,128)S(1)}, f32[2,64,512]{2,1,0:T(8,128)S(1)}, u32[]{:S(2)}, u32[]{:S(2)}) collective-permute-start(f32[2,64,512]{2,1,0:T(8,128)S(1)} %pad_maximum_fusion.1.refs_6_), channel_id=1, source_target_pairs={{0,4},{2,6},{4,0},{6,2},{8,12},{10,14},{12,8},{14,10},{16,20},{18,... | collective-permute-start | bytes 786440 | tf_op jit(solution)/shard_map/ppermute | solution.py:343
  126.9 20.0 %copy-start.10 = (f32[64,512]{1,0:T(8,128)}, f32[64,512]{1,0:T(8,128)S(1)}, u32[]{:S(2)}) copy-start(f32[64,512]{1,0:T(8,128)S(1)} %add.101.refs_10_) | copy-start | bytes 393220
  126.9 6.3 %collective-permute-start.24 = (f32[64,512]{1,0:T(8,128)S(1)}, f32[64,512]{1,0:T(8,128)}, u32[]{:S(2)}, u32[]{:S(2)}) collective-permute-start(f32[64,512]{1,0:T(8,128)S(1)} %add.101.refs_10_), channel_id=1, source_target_pairs={{0,4},{2,6},{4,0},{6,2},{8,12},{10,14},{12,8},{14,10},{16,20},{18,... | collective-permute-start | bytes 393224 | tf_op jit(solution)/shard_map/ppermute | solution.py:343
  130.0 28.9 %collective-permute-start.17 = (f32[128,512]{1,0:T(8,128)S(1)}, f32[128,512]{1,0:T(8,128)S(1)}, u32[]{:S(2)}, u32[]{:S(2)}) collective-permute-start(f32[128,512]{1,0:T(8,128)S(1)} %select_add_fusion.refs_4_), channel_id=1, source_target_pairs={{0,2},{2,0},{4,6},{6,4},{8,10},{10,8},{12,14},{14,12},{16,18},{18,... | collective-permute-start | bytes 786440 | tf_op jit(solution)/shard_map/ppermute | solution.py:343
  130.0 28.9 %collective-permute-start.21 = (f32[2,64,512]{2,1,0:T(8,128)S(1)}, f32[2,64,512]{2,1,0:T(8,128)}, u32[]{:S(2)}, u32[]{:S(2)}) collective-permute-start(f32[2,64,512]{2,1,0:T(8,128)S(1)} %pad_maximum_fusion.1.refs_6_), channel_id=1, source_target_pairs={{0,2},{2,0},{4,6},{6,4},{8,10},{10,8},{12,14},{14,12},{16,18},{18,... | collective-permute-start | bytes 786440 | tf_op jit(solution)/shard_map/ppermute | solution.py:343
  132.0 14.9 %copy-start.13 = (f32[2,64,512]{2,1,0:T(8,128)}, f32[2,64,512]{2,1,0:T(8,128)S(1)}, u32[]{:S(2)}) copy-start(f32[2,64,512]{2,1,0:T(8,128)S(1)} %collective-permute-done.20.refs_7_) | copy-start | bytes 786436
  132.0 26.9 %collective-permute-start.25 = (f32[64,512]{1,0:T(8,128)S(1)}, f32[64,512]{1,0:T(8,128)}, u32[]{:S(2)}, u32[]{:S(2)}) collective-permute-start(f32[64,512]{1,0:T(8,128)S(1)} %add.101.refs_10_), channel_id=1, source_target_pairs={{0,2},{2,0},{4,6},{6,4},{8,10},{10,8},{12,14},{14,12},{16,18},{18,... | collective-permute-start | bytes 393224 | tf_op jit(solution)/shard_map/ppermute | solution.py:343
  133.2 25.7 %collective-permute-start.22 = (f32[2,64,512]{2,1,0:T(8,128)S(1)}, f32[2,64,512]{2,1,0:T(8,128)}, u32[]{:S(2)}, u32[]{:S(2)}) collective-permute-start(f32[2,64,512]{2,1,0:T(8,128)S(1)} %collective-permute-done.20.refs_7_), channel_id=1, source_target_pairs={{0,2},{2,0},{4,6},{6,4},{8,10},{10,8},{12,14},{14,12},{16,18},{18,... | collective-permute-start | bytes 786440 | tf_op jit(solution)/shard_map/ppermute | solution.py:343
  134.1 24.8 %collective-permute-start.26 = (f32[64,512]{1,0:T(8,128)}, f32[64,512]{1,0:T(8,128)}, u32[]{:S(2)}, u32[]{:S(2)}) collective-permute-start(f32[64,512]{1,0:T(8,128)} %collective-permute-done.24.refs_11_), channel_id=1, source_target_pairs={{0,2},{2,0},{4,6},{6,4},{8,10},{10,8},{12,14},{14,12},{16,18},{18,... | collective-permute-start | bytes 393224 | tf_op jit(solution)/shard_map/ppermute | solution.py:343
  146.9 9.6 %copy-start.9 = (f32[768,256]{1,0:T(8,128)S(1)}, f32[768,256]{1,0:T(8,128)}, u32[]{:S(2)}) copy-start(f32[768,256]{1,0:T(8,128)} %get-tuple-element.26) | copy-start | bytes 2359300
  158.9 0.7 copy-start.14

commit v4 on v3

--- a/solution.py
+++ b/solution.py
@@ -11,6 +11,7 @@
 LANES = 128
 BASE = 64
 WIDE = 16
+SPLIT = 2
 NN = ((1,), (0,))
 NT = ((1,), (1,))
 HIGH = lax.Precision.HIGH
@@ -117,12 +118,10 @@
         out[k][mid:end, t1 : t1 + width] = x2 - m21 if t1 == t2 else -m21
 
 
-def first_kernel(size, core_ref, gram_ref, mine_ref, other_ref, *refs):
+def inverse_kernel(size, core_ref, gram_ref, mine_ref, other_ref, *refs):
     count = mine_ref.shape[0] + 1
-    inverse, rest, kept = refs[:count], refs[count : 2 * count], refs[2 * count : 3 * count]
-    work = refs[3 * count :]
+    out, work = refs[:count], refs[count:]
     width = mine_ref.shape[2]
-    half = size // 2
     swap = core_ref[0] == 1
     for k in range(count):
         if k == 0:
@@ -133,67 +132,33 @@
             mine, other = mine_ref[k - 1], other_ref[k - 1]
             work[k][:, :width] = jnp.where(swap, other, mine)
             work[k][:, width:] = jnp.where(swap, mine, other)
-        for t in range(0, half, LANES):
-            inverse[k][:, t : t + LANES] = jnp.zeros((half, LANES), jnp.float32)
-    node_factor(work, inverse, 0, half, BASE)
-    for k in range(count):
-        x1 = inverse[k][...]
-        l21 = dot3(work[k][half:, :half], x1, NT)
-        rest[k][...] = work[k][half:, half:] - dot3(l21, l21, NT)
-        kept[k][...] = dot3(l21, x1, NN)
-
-
-def second_kernel(count, half, *refs):
-    inverse, rest, kept = refs[:count], refs[count : 2 * count], refs[2 * count : 3 * count]
-    out = refs[3 * count : 4 * count]
-    work, second = refs[4 * count : 5 * count], refs[5 * count :]
-    for k in range(count):
-        work[k][...] = rest[k][...]
-        for t in range(0, half, LANES):
-            second[k][:, t : t + LANES] = jnp.zeros((half, LANES), jnp.float32)
-        out[k][:half, :half] = inverse[k][...]
-        out[k][:half, half:] = jnp.zeros((half, half), jnp.float32)
-    node_factor(work, second, 0, half, BASE)
-    for k in range(count):
-        x2 = second[k][...]
-        out[k][half:, half:] = x2
-        out[k][half:, :half] = -dot3(x2, kept[k][...], NN)
-
-
-def factor_first(core, gram, mine, other):
+        for t in range(0, size, LANES):
+            out[k][:, t : t + LANES] = jnp.zeros((size, LANES), jnp.float32)
+    node_factor(work, out, 0, size, BASE)
+
+
+def factor_inverse(core, gram, mine, other):
     count, size = mine.shape[0] + 1, gram.shape[0]
-    half = size // 2
     vmem = pl.BlockSpec(memory_space=pltpu.VMEM)
     smem = pl.BlockSpec(memory_space=pltpu.SMEM)
     return pl.pallas_call(
-        functools.partial(first_kernel, size),
-        out_shape=[jax.ShapeDtypeStruct((half, half), jnp.float32)] * (3 * count),
+        functools.partial(inverse_kernel, size),
+        out_shape=[jax.ShapeDtypeStruct((size, size), jnp.float32)] * count,
         in_specs=[smem, vmem, vmem, vmem],
-        out_specs=[vmem] * (3 * count),
+        out_specs=[vmem] * count,
         scratch_shapes=[pltpu.VMEM((size, size), jnp.float32)] * count,
-        cost_estimate=pl.CostEstimate(flops=7 * 10**9, bytes_accessed=8 * count * size**2, transcendentals=0),
-        name="factor_first",
+        cost_estimate=pl.CostEstimate(flops=15 * 10**9, bytes_accessed=8 * count * size**2, transcendentals=0),
+        name="factor_inverse",
     )(core, gram, mine, other)
 
 
-def factor_second(parts):
-    count, half = len(parts) // 3, parts[0].shape[0]
-    vmem = pl.BlockSpec(memory_space=pltpu.VMEM)
-    return pl.pallas_call(
-        functools.partial(second_kernel, count, half),
-        out_shape=[jax.ShapeDtypeStruct((2 * half, 2 * half), jnp.float32)] * count,
-        in_specs=[vmem] * (3 * count),
-        out_specs=[vmem] * count,
-        scratch_shapes=[pltpu.VMEM((half, half), jnp.float32)] * (2 * count),
-        cost_estimate=pl.CostEstimate(flops=7 * 10**9, bytes_accessed=32 * count * half**2, transcendentals=0),
-        name="factor_second",
-    )(*parts)
-
-
-def near_kernel(groups, block_count, slot_count, index_ref, count_ref, *refs):
-    blocks_ref, base_ref = refs[0], refs[1]
-    pieces = refs[2 : 2 + groups]
-    out_ref, ext, sems = refs[2 + groups :]
+def near_kernel(groups, first_slot, spots, sketched, index_ref, count_ref, blocks_ref, base_ref, *refs):
+    pieces = refs[:groups]
+    sketch_ref = refs[groups] if sketched else None
+    rest = refs[groups + sketched :]
+    out_ref = rest[0]
+    ext, sems = rest[-2:]
+    block_count, slot_count, size, _ = blocks_ref.shape
     copies = []
     at = 0
     for g in range(groups):
@@ -202,31 +167,43 @@
         at += depth
     for copy in copies:
         copy.start()
+    out_ref[...] = base_ref[...]
     for copy in copies:
         copy.wait()
-    size = blocks_ref.shape[2]
     for b in range(block_count):
         rows = pl.ds(b * size, size)
-        total = base_ref[rows, :]
-        for j in range(slot_count):
-            start = pl.multiple_of(index_ref[b, j] * size, size)
-            piece = jnp.where(j < count_ref[b], ext[pl.ds(start, size), :], 0.0)
-            total = total - dot3(blocks_ref[b, j], piece, NN)
-        out_ref[rows, :] = total
-
-
-def near_apply(blocks, base, pieces, index, count):
+        for j in range(first_slot, slot_count):
+            spot = index_ref[b, j]
+            start = jnp.int32(0)
+            here = jnp.bool_(False)
+            for order, name in enumerate(spots):
+                same = spot == name
+                start = jnp.where(same, order * size, start)
+                here = here | same
+
+            @pl.when(here & (j < count_ref[b]))
+            def _(b=b, j=j, rows=rows, start=start):
+                piece = ext[pl.ds(pl.multiple_of(start, size), size), :]
+                out_ref[rows, :] -= dot3(blocks_ref[b, j], piece, NN)
+
+    if sketched:
+        rest[1][...] = dot3(out_ref[...], sketch_ref[...], NN)
+
+
+def near_step(blocks, base, pieces, spots, index, count, first_slot, sketch=None):
     block_count, slot_count, size, _ = blocks.shape
     rows, width = base.shape
     total = sum(piece.shape[0] for piece in pieces)
     vmem = pl.BlockSpec(memory_space=pltpu.VMEM)
     smem = pl.BlockSpec(memory_space=pltpu.SMEM)
     hbm = pl.BlockSpec(memory_space=pl.ANY)
+    extra = [] if sketch is None else [sketch]
+    shapes = [(rows, width)] + [(rows, value.shape[1]) for value in extra]
     return pl.pallas_call(
-        functools.partial(near_kernel, len(pieces), block_count, slot_count),
-        out_shape=jax.ShapeDtypeStruct((rows, width), jnp.float32),
-        in_specs=[smem, smem, vmem, vmem] + [hbm] * len(pieces),
-        out_specs=vmem,
+        functools.partial(near_kernel, len(pieces), first_slot, tuple(spots), len(extra)),
+        out_shape=[jax.ShapeDtypeStruct(shape, jnp.float32) for shape in shapes],
+        in_specs=[smem, smem, vmem, vmem] + [hbm] * len(pieces) + [vmem] * len(extra),
+        out_specs=[vmem] * len(shapes),
         scratch_shapes=[
             pltpu.VMEM((total, width), jnp.float32),
             pltpu.SemaphoreType.DMA((len(pieces),)),
@@ -236,69 +213,51 @@
             bytes_accessed=4 * (total * width + 2 * rows * width + blocks.size),
             transcendentals=0,
         ),
-        name="near_apply",
-    )(index, count, blocks, base, *pieces)
-
-
-def leaf_kernel(core_ref, mine_ref, other_ref, sketch_ref, turned_ref, gram_ref, part_ref):
-    width = mine_ref.shape[1]
-    if width == gram_ref.shape[0]:
-        sketch = mine_ref[...]
-    else:
-        swap = core_ref[0] == 1
-        mine, other = mine_ref[...], other_ref[...]
-        sketch = jnp.concatenate([jnp.where(swap, other, mine), jnp.where(swap, mine, other)], axis=1)
+        name="near_step",
+    )(index, count, blocks, base, *pieces, *extra)
+
+
+def leaf_kernel(flag_ref, half_ref, other_ref, far_ref, sketch_ref, gram_ref, part_ref, keep_ref, send_ref, product):
+    sketch = half_ref[...] + other_ref[...] if other_ref is not None else half_ref[...]
     sketch_ref[...] = sketch
     turned = sketch.T
-    turned_ref[...] = turned
     gram = dot3(turned, sketch, NN)
     gram_ref[...] = gram
     rank = gram.shape[0]
-    part_ref[...] = jnp.where(core_ref[0] == 1, gram[:, rank - width :], gram[:, :width])
-
-
-def leaf_products(core, mine, other, rank):
-    rows, width = mine.shape
+    width = part_ref.shape[1]
+    part_ref[...] = jnp.where(flag_ref[0] == 1, gram[:, rank - width :], gram[:, :width])
+    product[...] = dot3(turned, far_ref[...], NN)
+    depth = keep_ref.shape[0]
+    keep_ref[...] = product[pl.ds(pl.multiple_of(flag_ref[1], depth), depth), :]
+    send_ref[...] = product[pl.ds(pl.multiple_of(flag_ref[2], depth), depth), :]
+
+
+def leaf_products(flag, part, other, far):
+    rows, rank = part.shape
+    width = far.shape[1]
     vmem = pl.BlockSpec(memory_space=pltpu.VMEM)
     smem = pl.BlockSpec(memory_space=pltpu.SMEM)
-    shapes = [(rows, rank), (rank, rows), (rank, rank), (rank, width)]
+    half = rank // 2
+    shapes = [(rows, rank), (rank, rank), (rank, rank if other is None else half), (half, width), (half, width)]
+    kernel = leaf_kernel
+    args = [flag, part, other, far]
+    if other is None:
+        args = [flag, part, far]
+
+        def kernel(flag_ref, part_ref, far_ref, *refs):
+            leaf_kernel(flag_ref, part_ref, None, far_ref, *refs)
+
     return pl.pallas_call(
-        leaf_kernel,
+        kernel,
         out_shape=[jax.ShapeDtypeStruct(shape, jnp.float32) for shape in shapes],
-        in_specs=[smem, vmem, vmem],
-        out_specs=[vmem] * 4,
-        cost_estimate=pl.CostEstimate(flops=6 * rows * rank * rank, bytes_accessed=16 * rows * rank, transcendentals=0),
+        in_specs=[smem] + [vmem] * (len(args) - 1),
+        out_specs=[vmem] * len(shapes),
+        scratch_shapes=[pltpu.VMEM((rank, width), jnp.float32)],
+        cost_estimate=pl.CostEstimate(
+            flops=6 * rows * rank * (rank + width), bytes_accessed=4 * rows * (3 * rank + width), transcendentals=0
+        ),
         name="leaf_products",
-    )(core, mine, other)
-
-
-def fold_kernel(index_ref, count_ref, blocks_ref, turned_ref, out_ref):
-    block_count, slot_count, size, _ = blocks_ref.shape
-    out_ref[...] = jnp.zeros(out_ref.shape, jnp.float32)
-    for b in range(block_count):
-        turned = turned_ref[:, b * size : (b + 1) * size]
-        for j in range(slot_count):
-            block = jnp.where(j < count_ref[b], blocks_ref[b, j], 0.0)
-            out_ref[index_ref[b, j]] -= dot3(turned, block, NN)
-
-
-def near_fold(blocks, turned, index, count):
-    block_count, slot_count, size, _ = blocks.shape
-    rank = turned.shape[0]
-    vmem = pl.BlockSpec(memory_space=pltpu.VMEM)
-    smem = pl.BlockSpec(memory_space=pltpu.SMEM)
-    return pl.pallas_call(
-        fold_kernel,
-        out_shape=jax.ShapeDtypeStruct((3 * block_count, rank, size), jnp.float32),
-        in_specs=[smem, smem, vmem, vmem],
-        out_specs=vmem,
-        cost_estimate=pl.CostEstimate(
-            flops=6 * block_count * slot_count * size * size * rank,
-            bytes_accessed=4 * (turned.size + blocks.size + 3 * block_count * rank * size),
-            transcendentals=0,
-        ),
-        name="near_fold",
-    )(index, count, blocks, turned)
+    )(*args)
 
 
 def reduce_kernel(place_ref, *refs):
@@ -375,25 +334,25 @@
     moved = jnp.where(index < block_count, 2 * block_count, jnp.where(index >= 2 * block_count, -2 * block_count, 0))
     index = index + jnp.where(odd, moved, 0)
 
-    blocks = [probes[i * block_size : (i + 1) * block_size] for i in range(block_count)]
-    peer = [across(blocks[i], "rows", 0) for i in range(block_count)]
-    far = [relayed(peer[i], "rows") for i in range(block_count)]
-
+    parts = block_count * SPLIT
+    depth = rows_dev // parts
+    later = lax.optimization_barrier(probes)
+    pieces = [(later if i else probes)[i * depth : (i + 1) * depth] for i in range(parts)]
+    peer = [across(pieces[i], "rows", 0) for i in range(parts)]
+    far = [relayed(peer[i], "rows") for i in range(parts)]
+
+    own = range(block_count, 2 * block_count)
+    (left,) = near_step(near_blocks, samples, [probes], own, index, near_count, 0)
+    early = (block_count - 1) * SPLIT
+    spots = [*range(block_count - 1), *range(2 * block_count, 3 * block_count)]
+    (left,) = near_step(near_blocks, left, far[:early] + peer, spots, index, near_count, 1)
+    far_samples, partial = near_step(near_blocks, left, far[early:], [block_count - 1], index, near_count, 1, sketch)
     if halves == 2:
-        width = rank // 2
-        turned_sketch = pick(core == 1, sketch, jnp.concatenate([sketch[:, width:], sketch[:, :width]], axis=1))
-        probe_part = jnp.dot(probes, turned_sketch, precision=HIGH)
-        sample_part = jnp.dot(samples, turned_sketch, precision=HIGH)
-        probe_sketch = probe_part[:, :width] + across(probe_part[:, width:], "samp", 0)
-        sample_sketch = sample_part[:, :width] + across(sample_part[:, width:], "samp", 0)
+        other = across(partial, "samp", 0)
     else:
-        probe_sketch = lax.psum(jnp.dot(probes, sketch, precision=HIGH), "samp")
-        sample_sketch = lax.psum(jnp.dot(samples, sketch, precision=HIGH), "samp")
-    peer_sketch = across(probe_sketch, "rows", 0)
-    far_sketch = relayed(peer_sketch, "rows")
-    mine = near_apply(near_blocks, sample_sketch, [far_sketch, probe_sketch, peer_sketch], index, near_count)
-    other = across(mine, "samp", 0) if halves == 2 else mine
-    leaf_sketch, turned, gram, part = leaf_products(core_flag, mine, other, rank)
+        partial, other = lax.psum(partial, "samp"), None
+    flag = jnp.stack([core, bits[0] * (rank // 2), (1 - bits[0]) * (rank // 2)]).astype(jnp.int32)
+    leaf_sketch, gram, part, keep, send = leaf_products(flag, partial, other, far_samples)
 
     sums = []
     for h in range(LEVELS):
@@ -401,24 +360,9 @@
         sums.append(part)
     sums = jnp.stack(sums)
     sums_other = across(sums, "samp", 0) if halves == 2 else sums
-    parts = factor_first(core_flag, gram, sums, sums_other)
-    leaf_inverse, *inverses = factor_second(parts)
+    leaf_inverse, *inverses = factor_inverse(core_flag, gram, sums, sums_other)
     leaf_basis = lax.dot_general(leaf_sketch, leaf_inverse, (NT, ((), ())), precision=HIGH)
 
-    folded = near_fold(near_blocks, turned, index, near_count)
-
-    def times(left, right):
-        return jnp.dot(left, right, precision=HIGH)
-
-    product = times(turned, samples)
-    for i in range(block_count):
-        product = product + times(folded[block_count + i], blocks[i])
-    for i in range(block_count):
-        product = product + times(folded[2 * block_count + i], peer[i])
-    for i in range(block_count):
-        product = product + times(folded[i], far[i])
-
-    keep, send = halves_of(product, odd)
     first = keep + across(send, "rows", 0)
     first_other = across(first, "rows", 0)
     keep, send = halves_of(first, upper)

time: 165 us -> 147 us (0.89)
  waiting for transfers between devices: 52.5 us -> 33.4 us
  matrix products: 18.4 us -> 2.35 us
  starting transfers between devices: 44.7 us -> 55.6 us
  Pallas kernels: 37.5 us -> 43 us
    dot_general x12 -> x0, matrix products: 16.1 us -> none  [the longest x10 12.8 us: times(): return jnp.dot(left, right, precision=HIGH)]
    ppermute x4 -> x6, waiting for transfers between devices: 11 us -> 0.02 us  [relayed(): lax.ppermute(value, axis, [(i, t) for i, t in steps if 0 <= t < count])]
    ppermute x23, waiting for transfers between devices: 41.5 us -> 33.4 us  [across(): lax.ppermute(value, axis, [(i, i ^ 1 << bit) for i in range(lax.axis_size...]
    ppermute x4 -> x6, starting transfers between devices: 15.3 us -> 22.9 us  [relayed(): lax.ppermute(value, axis, [(i, t) for i, t in steps if 0 <= t < count])]
    pallas_call x5, Pallas kernels: 33.2 us -> 38.8 us  [the longest x1 17.6 us: factor_inverse(): pl.pallas_call(functools.partial(inverse_kernel, size), out_shape=[jax.Sh...]
    ppermute x23, starting transfers between devices: 29.3 us -> 32.7 us  [across(): lax.ppermute(value, axis, [(i, i ^ 1 << bit) for i in range(lax.axis_size...]
    add x2 -> x0, other arithmetic: 1.96 us -> none  [the longest x1 1.91 us: leaf_and_levels(): sample_part[:, :width] + across(sample_part[:, width:], 'samp', 0)]
    unnamed x36 -> x52, local copies, waits for them, and re-layouts: 3.09 us -> 4.71 us
  transfers between devices with their start and end apart: 27 -> 29, of which waited for: 12 -> 15; matrix products, arithmetic and copies ran while one was open for 13% -> 5% of each run, Pallas kernels for 20% -> 20%
where the time goes in v4:
time: 147 us; the launch traced here: 146 us
  starting transfers between devices  55.6 us (38%)
  Pallas kernels  43 us (29%)
  waiting for transfers between devices  33.4 us (23%)
  local copies, waits for them, and re-layouts  7.71 us (5%)
  other arithmetic  3.31 us (2%)
  matrix products  2.35 us (2%)
    ppermute x23, waiting for transfers between devices, across(): lax.ppermute(value, axis, [(i, i ^ 1 << bit) for i in range(lax.axis_size...  33.4 us
    ppermute x23, starting transfers between devices, across(): lax.ppermute(value, axis, [(i, i ^ 1 << bit) for i in range(lax.axis_size...  32.7 us
    ppermute x6, starting transfers between devices, relayed(): lax.ppermute(value, axis, [(i, t) for i, t in steps if 0 <= t < count])  22.9 us
    pallas_call x1, Pallas kernels, factor_inverse(): pl.pallas_call(functools.partial(inverse_kernel, size), out_shape=[jax.Sh...  17.6 us
    pallas_call x3, Pallas kernels, near_step(): pl.pallas_call(functools.partial(near_kernel, len(pieces), first_slot, tu...  17.1 us
    unnamed x52, local copies, waits for them, and re-layouts  4.71 us
    pallas_call x1, Pallas kernels, reduce_all(): pl.pallas_call(reduce_kernel, out_shape=jax.ShapeDtypeStruct((LEVELS, 1,...  4.28 us
    pallas_call x1, Pallas kernels, leaf_products(): pl.pallas_call(kernel, out_shape=[jax.ShapeDtypeStruct(shape, jnp.float32...  4.08 us
  transfers between devices with their start and end apart: 29, of which 15 were waited for; matrix products, arithmetic and copies ran while one was open for 5% of the time, Pallas kernels for 20%

profile of v4, /device:TPU:0, one launch (start us, length us, event | category | flops | bytes accessed | tf_op | source)
XLA Modules:
  0.0 146.5 jit_solution(12937648612888375241)
XLA Ops:
  0.6 1.0 slice.26
  1.6 3.0 %collective-permute-start = (f32[128,512]{1,0:T(8,128)S(1)}, f32[128,512]{1,0:T(8,128)S(1)}, u32[]{:S(2)}, u32[]{:S(2)}) collective-permute-start(f32[128,512]{1,0:T(8,128)S(1)} %slice.26), channel_id=1, source_target_pairs={{0,2},{2,0},{4,6},{6,4},{8,10},{10,8},{12,14},{14,12},{16,18},{18,... | collective-permute-start | bytes 786440 | tf_op jit(solution)/shard_map/ppermute | solution.py:302
  4.6 1.4 fusion
  6.1 2.0 %collective-permute-start.4 = (f32[128,512]{1,0:T(8,128)S(1)}, f32[128,512]{1,0:T(8,128)S(1)}, u32[]{:S(2)}, u32[]{:S(2)}) collective-permute-start(f32[128,512]{1,0:T(8,128)S(1)} %get-tuple-element.29), channel_id=1, source_target_pairs={{0,2},{2,0},{4,6},{6,4},{8,10},{10,8},{12,14},{14,12},{16,18},{18,... | collective-permute-start | bytes 786440 | tf_op jit(solution)/shard_map/ppermute | solution.py:302
  8.2 1.9 %collective-permute-start.8 = (f32[128,512]{1,0:T(8,128)S(1)}, f32[128,512]{1,0:T(8,128)S(1)}, u32[]{:S(2)}, u32[]{:S(2)}) collective-permute-start(f32[128,512]{1,0:T(8,128)S(1)} %get-tuple-element.27), channel_id=1, source_target_pairs={{0,2},{2,0},{4,6},{6,4},{8,10},{10,8},{12,14},{14,12},{16,18},{18,... | collective-permute-start | bytes 786440 | tf_op jit(solution)/shard_map/ppermute | solution.py:302
  10.1 1.7 %collective-permute-done.refs_4_ = f32[128,512]{1,0:T(8,128)S(1)} collective-permute-done((f32[128,512]{1,0:T(8,128)S(1)}, f32[128,512]{1,0:T(8,128)S(1)}, u32[]{:S(2)}, u32[]{:S(2)}) %collective-permute-start) | collective-permute-done | bytes 262176 | tf_op jit(solution)/shard_map/ppermute | solution.py:302
  11.8 2.0 %collective-permute-start.9 = (f32[128,512]{1,0:T(8,128)S(1)}, f32[128,512]{1,0:T(8,128)S(1)}, u32[]{:S(2)}, u32[]{:S(2)}) collective-permute-start(f32[128,512]{1,0:T(8,128)S(1)} %get-tuple-element.26), channel_id=1, source_target_pairs={{0,2},{2,0},{4,6},{6,4},{8,10},{10,8},{12,14},{14,12},{16,18},{18,... | collective-permute-start | bytes 786440 | tf_op jit(solution)/shard_map/ppermute | solution.py:302
  13.8 3.6 %collective-permute-done.2.refs_5_ = f32[128,512]{1,0:T(8,128)S(1)} collective-permute-done((f32[128,512]{1,0:T(8,128)S(1)}, f32[128,512]{1,0:T(8,128)S(1)}, u32[]{:S(2)}, u32[]{:S(2)}) %collective-permute-start.2) | collective-permute-done | bytes 262176 | tf_op jit(solution)/shard_map/ppermute | solution.py:302
  17.4 4.0 %collective-permute-start.1 = (f32[128,512]{1,0:T(8,128)S(1)}, f32[128,512]{1,0:T(8,128)S(1)}, u32[]{:S(2)}, u32[]{:S(2)}) collective-permute-start(f32[128,512]{1,0:T(8,128)S(1)} %collective-permute-done.refs_4_), channel_id=1, source_target_pairs={{0,4},{4,8},{6,2},{8,12},{10,6},{12,16},{14,10},{16,20},{18,14},{2... | collective-permute-start | bytes 786440 | tf_op jit(solution)/shard_map/ppermute | solution.py:308
  21.4 1.6 %collective-permute-done.4.refs_6_ = f32[128,512]{1,0:T(8,128)S(1)} collective-permute-done((f32[128,512]{1,0:T(8,128)S(1)}, f32[128,512]{1,0:T(8,128)S(1)}, u32[]{:S(2)}, u32[]{:S(2)}) %collective-permute-start.4) | collective-permute-done | bytes 262176 | tf_op jit(solution)/shard_map/ppermute | solution.py:302
  23.0 4.0 %collective-permute-start.3 = (f32[128,512]{1,0:T(8,128)S(1)}, f32[128,512]{1,0:T(8,128)S(1)}, u32[]{:S(2)}, u32[]{:S(2)}) collective-permute-start(f32[128,512]{1,0:T(8,128)S(1)} %collective-permute-done.2.refs_5_), channel_id=1, source_target_pairs={{0,4},{4,8},{6,2},{8,12},{10,6},{12,16},{14,10},{16,20},{18,14},{2... | collective-permute-start | bytes 786440 | tf_op jit(solution)/shard_map/ppermute | solution.py:308
  27.0 1.7 %collective-permute-done.6.refs_7_ = f32[128,512]{1,0:T(8,128)S(1)} collective-permute-done((f32[128,512]{1,0:T(8,128)S(1)}, f32[128,512]{1,0:T(8,128)S(1)}, u32[]{:S(2)}, u32[]{:S(2)}) %collective-permute-start.6) | collective-permute-done | bytes 262176 | tf_op jit(solution)/shard_map/ppermute | solution.py:302
  28.7 4.0 %collective-permute-start.5 = (f32[128,512]{1,0:T(8,128)S(1)}, f32[128,512]{1,0:T(8,128)S(1)}, u32[]{:S(2)}, u32[]{:S(2)}) collective-permute-start(f32[128,512]{1,0:T(8,128)S(1)} %collective-permute-done.4.refs_6_), channel_id=1, source_target_pairs={{0,4},{4,8},{6,2},{8,12},{10,6},{12,16},{14,10},{16,20},{18,14},{2... | collective-permute-start | bytes 786440 | tf_op jit(solution)/shard_map/ppermute | solution.py:308
  32.6 1.7 %collective-permute-done.8.refs_8_ = f32[128,512]{1,0:T(8,128)S(1)} collective-permute-done((f32[128,512]{1,0:T(8,128)S(1)}, f32[128,512]{1,0:T(8,128)S(1)}, u32[]{:S(2)}, u32[]{:S(2)}) %collective-permute-start.8) | collective-permute-done | bytes 262176 | tf_op jit(solution)/shard_map/ppermute | solution.py:302
  34.3 4.0 %collective-permute-start.7 = (f32[128,512]{1,0:T(8,128)S(1)}, f32[128,512]{1,0:T(8,128)S(1)}, u32[]{:S(2)}, u32[]{:S(2)}) collective-permute-start(f32[128,512]{1,0:T(8,128)S(1)} %collective-permute-done.6.refs_7_), channel_id=1, source_target_pairs={{0,4},{4,8},{6,2},{8,12},{10,6},{12,16},{14,10},{16,20},{18,14},{2... | collective-permute-start | bytes 786440 | tf_op jit(solution)/shard_map/ppermute | solution.py:308
  39.0 3.7 %collective-permute-start.10 = (f32[128,512]{1,0:T(8,128)S(1)}, f32[128,512]{1,0:T(8,128)S(1)}, u32[]{:S(2)}, u32[]{:S(2)}) collective-permute-start(f32[128,512]{1,0:T(8,128)S(1)} %collective-permute-done.8.refs_8_), channel_id=1, source_target_pairs={{0,4},{4,8},{6,2},{8,12},{10,6},{12,16},{14,10},{16,20},{18,14},{2... | collective-permute-start | bytes 786440 | tf_op jit(solution)/shard_map/ppermute | solution.py:308
  42.8 3.4 %collective-permute-start.11 = (f32[128,512]{1,0:T(8,128)S(1)}, f32[128,512]{1,0:T(8,128)S(1)}, u32[]{:S(2)}, u32[]{:S(2)}) collective-permute-start(f32[128,512]{1,0:T(8,128)S(1)} %collective-permute-done.9.refs_9_), channel_id=1, source_target_pairs={{0,4},{4,8},{6,2},{8,12},{10,6},{12,16},{14,10},{16,20},{18,14},{2... | collective-permute-start | bytes 786440 | tf_op jit(solution)/shard_map/ppermute | solution.py:308
  46.2 6.3 %near_step.3.base_ref = f32[768,512]{1,0:T(8,128)} custom-call(s32[3,3]{1,0:T(4,128)} %select_add_fusion.1.index_ref, s32[3]{0:T(128)} %count_ref.5, f32[3,3,256,256]{3,2,1,0:T(8,128)} %blocks_ref.5, f32[768,512]{1,0:T(8,128)} %base_ref.1, f32[768,512]{1,0:T(8,128)} %refs_0_.1), custom_call_target="tpu_custom_call" | custom-call | flops 1811939328 | bytes 7077888 | tf_op jit(solution)/shard_map/near_step/pallas_call | solution.py:202
  53.3 0.7 copy-done.14
  54.0 5.8 %near_step.4.base_ref = f32[768,512]{1,0:T(8,128)} custom-call(s32[3,3]{1,0:T(4,128)} %select_add_fusion.1.index_ref, s32[3]{0:T(128)} %count_ref.5, f32[3,3,256,256]{3,2,1,0:T(8,128)} %blocks_ref.5, f32[768,512]{1,0:T(8,128)} %near_step.3.base_ref, f32[128,512]{1,0:T(8,128)} %copy-done.11, f32[128,512]{1,0:T(8,128)} %copy-done.12, f32[128,512]{1,0:T(8,128)} %copy-done.13, ...), custom_call_target="tpu_custom_call" | custom-call | flops 1811939328 | bytes 8126464 | tf_op jit(solution)/shard_map/near_step/pallas_call | solution.py:202
  60.6 0.7 copy-done.25
  61.3 5.0 %near_step.5 = (f32[768,512]{1,0:T(8,128)}, f32[768,256]{1,0:T(8,128)}) custom-call(s32[3,3]{1,0:T(4,128)} %select_add_fusion.1.index_ref, s32[3]{0:T(128)} %count_ref.5, f32[3,3,256,256]{3,2,1,0:T(8,128)} %blocks_ref.5, f32[768,512]{1,0:T(8,128)} %near_step.4.base_ref, f32[128,512]{1,0:T(8,128)} %copy-done.24, f32[128,512]{1,0:T(8,128)} %copy-done.25, ...), custom_call_target="tpu_custom_call" | custom-call | flops 1811939328 | bytes 6029312 | tf_op jit(solution)/shard_map/near_step/pallas_call | solution.py:202
  67.0 1.9 %collective-permute-done.12.other_ref = f32[768,256]{1,0:T(8,128)S(1)} collective-permute-done((f32[768,256]{1,0:T(8,128)}, f32[768,256]{1,0:T(8,128)S(1)}, u32[]{:S(2)}, u32[]{:S(2)}) %collective-permute-start.12) | collective-permute-done | bytes 786464 | tf_op jit(solution)/shard_map/ppermute | solution.py:302
  68.8 0.9 copy-done.23
  69.7 4.1 %leaf_products.1 = (f32[768,256]{1,0:T(8,128)}, f32[256,256]{1,0:T(8,128)}, f32[256,128]{1,0:T(8,128)}, f32[128,512]{1,0:T(8,128)}, f32[128,512]{1,0:T(8,128)}) custom-call(s32[3]{0:T(128)} %pad_add_fusion.flag_ref, f32[768,256]{1,0:T(8,128)} %get-tuple-element.14.half_ref, f32[768,256]{1,0:T(8,128)} %copy-done.23, f32[768,512]{1,0:T(8,128)} %get-tuple-element.15.far_ref), custom_call_target="tpu_custom_call" | custom-call | flops 905969664 | bytes 3932160 | tf_op jit(solution)/shard_map/leaf_products/pallas_call | solution.py:250
  73.8 2.0 %collective-permute-start.18 = (f32[128,512]{1,0:T(8,128)}, f32[128,512]{1,0:T(8,128)S(1)}, u32[]{:S(2)}, u32[]{:S(2)}) collective-permute-start(f32[128,512]{1,0:T(8,128)} %get-tuple-element.25), channel_id=1, source_target_pairs={{0,2},{2,0},{4,6},{6,4},{8,10},{10,8},{12,14},{14,12},{16,18},{18,... | collective-permute-start | bytes 786440 | tf_op jit(solution)/shard_map/ppermute | solution.py:302
  75.8 4.6 %collective-permute-done.13 = f32[256,128]{1,0:T(8,128)S(1)} collective-permute-done((f32[256,128]{1,0:T(8,128)}, f32[256,128]{1,0:T(8,128)S(1)}, u32[]{:S(2)}, u32[]{:S(2)}) %collective-permute-start.13) | collective-permute-done | bytes 131104 | tf_op jit(solution)/shard_map/ppermute | solution.py:302
  80.4 0.9 add.46
  81.3 2.1 %collective-permute-start.14 = (f32[256,128]{1,0:T(8,128)S(1)}, f32[256,128]{1,0:T(8,128)S(1)}, u32[]{:S(2)}, u32[]{:S(2)}) collective-permute-start(f32[256,128]{1,0:T(8,128)S(1)} %add.46), channel_id=1, source_target_pairs={{0,4},{2,6},{4,0},{6,2},{8,12},{10,14},{12,8},{14,10},{16,20},{18,... | collective-permute-start | bytes 393224 | tf_op jit(solution)/shard_map/ppermute | solution.py:302
  83.4 2.9 %collective-permute-done.14 = f32[256,128]{1,0:T(8,128)S(1)} collective-permute-done((f32[256,128]{1,0:T(8,128)S(1)}, f32[256,128]{1,0:T(8,128)S(1)}, u32[]{:S(2)}, u32[]{:S(2)}) %collective-permute-start.14) | collective-permute-done | bytes 131104 | tf_op jit(solution)/shard_map/ppermute | solution.py:302
  86.4 2.2 %collective-permute-start.15 = (f32[256,128]{1,0:T(8,128)S(1)}, f32[256,128]{1,0:T(8,128)S(1)}, u32[]{:S(2)}, u32[]{:S(2)}) collective-permute-start(f32[256,128]{1,0:T(8,128)S(1)} %add.47), channel_id=1, source_target_pairs={{0,8},{2,10},{4,12},{6,14},{8,0},{10,2},{12,4},{14,6},{16,24},{18,... | collective-permute-start | bytes 393224 | tf_op jit(solution)/shard_map/ppermute | solution.py:302
  88.6 1.0 add.54.refs_4_
  89.6 1.9 %collective-permute-done.15 = f32[256,128]{1,0:T(8,128)S(1)} collective-permute-done((f32[256,128]{1,0:T(8,128)S(1)}, f32[256,128]{1,0:T(8,128)S(1)}, u32[]{:S(2)}, u32[]{:S(2)}) %collective-permute-start.15) | collective-permute-done | bytes 131104 | tf_op jit(solution)/shard_map/ppermute | solution.py:302
  91.5 3.1 %collective-permute-start.16 = (f32[256,128]{1,0:T(8,128)S(1)}, f32[256,128]{1,0:T(8,128)S(1)}, u32[]{:S(2)}, u32[]{:S(2)}) collective-permute-start(f32[256,128]{1,0:T(8,128)S(1)} %add.48), channel_id=1, source_target_pairs={{0,16},{2,18},{4,20},{6,22},{8,24},{10,26},{12,28},{14,30},{16,0},... | collective-permute-start | bytes 393224 | tf_op jit(solution)/shard_map/ppermute | solution.py:302
  94.7 2.1 %collective-permute-start.20 = (f32[64,512]{1,0:T(8,128)S(1)}, f32[64,512]{1,0:T(8,128)S(1)}, u32[]{:S(2)}, u32[]{:S(2)}) collective-permute-start(f32[64,512]{1,0:T(8,128)S(1)} %slice_select_fusion), channel_id=1, source_target_pairs={{0,4},{2,6},{4,0},{6,2},{8,12},{10,14},{12,8},{14,10},{16,20},{18,... | collective-permute-start | bytes 393224 | tf_op jit(solution)/shard_map/ppermute | solution.py:302
  96.8 0.8 collective-permute-done.16
  97.8 2.0 %collective-permute-done.20 = f32[64,512]{1,0:T(8,128)S(1)} collective-permute-done((f32[64,512]{1,0:T(8,128)S(1)}, f32[64,512]{1,0:T(8,128)S(1)}, u32[]{:S(2)}, u32[]{:S(2)}) %collective-permute-start.20) | collective-permute-done | bytes 131104 | tf_op jit(solution)/shard_map/ppermute | solution.py:302
  100.2 4.6 %collective-permute-done.21 = f32[64,512]{1,0:T(8,128)S(1)} collective-permute-done((f32[64,512]{1,0:T(8,128)S(1)}, f32[64,512]{1,0:T(8,128)S(1)}, u32[]{:S(2)}, u32[]{:S(2)}) %collective-permute-start.21) | collective-permute-done | bytes 131104 | tf_op jit(solution)/shard_map/ppermute | solution.py:302
  104.8 2.1 %collective-permute-start.25 = (f32[64,512]{1,0:T(8,128)S(1)}, f32[64,512]{1,0:T(8,128)S(1)}, u32[]{:S(2)}, u32[]{:S(2)}) collective-permute-start(f32[64,512]{1,0:T(8,128)S(1)} %add.56), channel_id=1, source_target_pairs={{0,16},{2,18},{4,20},{6,22},{8,24},{10,26},{12,28},{14,30},{16,0},... | collective-permute-start | bytes 393224 | tf_op jit(solution)/shard_map/ppermute | solution.py:302
  106.9 2.0 %collective-permute-start.22 = (f32[2,64,512]{2,1,0:T(8,128)S(1)}, f32[2,64,512]{2,1,0:T(8,128)S(1)}, u32[]{:S(2)}, u32[]{:S(2)}) collective-permute-start(f32[2,64,512]{2,1,0:T(8,128)S(1)} %pad_maximum_fusion.1.refs_6_), channel_id=1, source_target_pairs={{0,4},{2,6},{4,0},{6,2},{8,12},{10,14},{12,8},{14,10},{16,20},{18,... | collective-permute-start | bytes 786440 | tf_op jit(solution)/shard_map/ppermute | solution.py:302
  108.9 4.1 %collective-permute-done.25 = f32[64,512]{1,0:T(8,128)S(1)} collective-permute-done((f32[64,512]{1,0:T(8,128)S(1)}, f32[64,512]{1,0:T(8,128)S(1)}, u32[]{:S(2)}, u32[]{:S(2)}) %collective-permute-start.25) | collective-permute-done | bytes 131104 | tf_op jit(solution)/shard_map/ppermute | solution.py:302
  113.0 2.6 %collective-permute-start.26 = (f32[64,512]{1,0:T(8,128)S(1)}, f32[64,512]{1,0:T(8,128)S(1)}, u32[]{:S(2)}, u32[]{:S(2)}) collective-permute-start(f32[64,512]{1,0:T(8,128)S(1)} %add.57.refs_10_), channel_id=1, source_target_pairs={{0,4},{2,6},{4,0},{6,2},{8,12},{10,14},{12,8},{14,10},{16,20},{18,... | collective-permute-start | bytes 393224 | tf_op jit(solution)/shard_map/ppermute | solution.py:302
  117.0 1.3 collective-permute-start.23
  119.2 1.2 collective-permute-start.24
  120.3 0.9 collective-permute-start.28
  121.2 17.6 %factor_inverse.1 = (f32[256,256]{1,0:T(8,128)}, f32[256,256]{1,0:T(8,128)}, f32[256,256]{1,0:T(8,128)}, f32[256,256]{1,0:T(8,128)}, f32[256,256]{1,0:T(8,128)}) custom-call(s32[1]{0:T(128)} %bitcast.core_ref, f32[256,256]{1,0:T(8,128)} %get-tuple-element.17.gram_ref, f32[4,256,128]{2,1,0:T(8,128)} %copy-done.4, f32[4,256,128]{2,1,0:T(8,128)} %collective-permute-done.17.other_ref), custom_call_target="tpu_custom_call" | custom-call | flops 15000000512 | bytes 2621440 | tf_op jit(solution)/shard_map/factor_inverse/pallas_call | solution.py:144
  138.9 2.3 %fusion.1 = f32[768,256]{1,0:T(8,128)} fusion(f32[768,256]{1,0:T(8,128)S(1)} %copy-done.2, f32[256,256]{1,0:T(8,128)} %get-tuple-element.19), kind=kOutput, calls=%fused_computation.8 | convolution fusion | flops 301989888 | bytes 1835008 | tf_op jit(solution)/shard_map/dot_general | solution.py:364
  142.2 4.3 %reduce_all.1 = f32[4,1,256,512]{3,2,1,0:T(8,128)} custom-call(s32[6]{0:T(128)} %stack.69.place_ref, f32[256,256]{1,0:T(8,128)} %get-tuple-element.20.refs_0_, f32[256,256]{1,0:T(8,128)} %get-tuple-element.21.refs_1_, f32[256,256]{1,0:T(8,128)} %get-tuple-element.22.refs_2_, f32[256,256]{1,0:T(8,128)} %get-tuple-element.23.refs_3_, f32[128,512]{1,0:T(8,128)} %copy-done, ...), custom_call_target="tpu_custom_call" | custom-call | flops 805306368 | bytes 6291456 | tf_op jit(solution)/shard_map/reduce_all/pallas_call | solution.py:288
  (85 shorter events, 7.0 us)
Async XLA Ops:
  0.6 37.6 %copy-start.22 = (s32[3,3]{1,0:T(4,128)S(1)}, s32[3,3]{1,0:T(4,128)}, u32[]{:S(2)}) copy-start(s32[3,3]{1,0:T(4,128)} %param.9) | copy-start | bytes 112
  1.6 10.2 %collective-permute-start = (f32[128,512]{1,0:T(8,128)S(1)}, f32[128,512]{1,0:T(8,128)S(1)}, u32[]{:S(2)}, u32[]{:S(2)}) collective-permute-start(f32[128,512]{1,0:T(8,128)S(1)} %slice.26), channel_id=1, source_target_pairs={{0,2},{2,0},{4,6},{6,4},{8,10},{10,8},{12,14},{14,12},{16,18},{18,... | collective-permute-start | bytes 786440 | tf_op jit(solution)/shard_map/ppermute | solution.py:302
  6.0 11.4 %collective-permute-start.2 = (f32[128,512]{1,0:T(8,128)S(1)}, f32[128,512]{1,0:T(8,128)S(1)}, u32[]{:S(2)}, u32[]{:S(2)}) collective-permute-start(f32[128,512]{1,0:T(8,128)S(1)} %get-tuple-element.30), channel_id=1, source_target_pairs={{0,2},{2,0},{4,6},{6,4},{8,10},{10,8},{12,14},{14,12},{16,18},{18,... | collective-permute-start | bytes 786440 | tf_op jit(solution)/shard_map/ppermute | solution.py:302
  6.1 16.9 %collective-permute-start.4 = (f32[128,512]{1,0:T(8,128)S(1)}, f32[128,512]{1,0:T(8,128)S(1)}, u32[]{:S(2)}, u32[]{:S(2)}) collective-permute-start(f32[128,512]{1,0:T(8,128)S(1)} %get-tuple-element.29), channel_id=1, source_target_pairs={{0,2},{2,0},{4,6},{6,4},{8,10},{10,8},{12,14},{14,12},{16,18},{18,... | collective-permute-start | bytes 786440 | tf_op jit(solution)/shard_map/ppermute | solution.py:302
  8.1 20.6 %collective-permute-start.6 = (f32[128,512]{1,0:T(8,128)S(1)}, f32[128,512]{1,0:T(8,128)S(1)}, u32[]{:S(2)}, u32[]{:S(2)}) collective-permute-start(f32[128,512]{1,0:T(8,128)S(1)} %get-tuple-element.28), channel_id=1, source_target_pairs={{0,2},{2,0},{4,6},{6,4},{8,10},{10,8},{12,14},{14,12},{16,18},{18,... | collective-permute-start | bytes 786440 | tf_op jit(solution)/shard_map/ppermute | solution.py:302
  8.2 26.1 %collective-permute-start.8 = (f32[128,512]{1,0:T(8,128)S(1)}, f32[128,512]{1,0:T(8,128)S(1)}, u32[]{:S(2)}, u32[]{:S(2)}) collective-permute-start(f32[128,512]{1,0:T(8,128)S(1)} %get-tuple-element.27), channel_id=1, source_target_pairs={{0,2},{2,0},{4,6},{6,4},{8,10},{10,8},{12,14},{14,12},{16,18},{18,... | collective-permute-start | bytes 786440 | tf_op jit(solution)/shard_map/ppermute | solution.py:302
  11.8 40.7 %copy-start.5 = (f32[128,512]{1,0:T(8,128)}, f32[128,512]{1,0:T(8,128)S(1)}, u32[]{:S(2)}) copy-start(f32[128,512]{1,0:T(8,128)S(1)} %collective-permute-done.refs_4_) | copy-start | bytes 786436
  11.8 27.2 %collective-permute-start.9 = (f32[128,512]{1,0:T(8,128)S(1)}, f32[128,512]{1,0:T(8,128)S(1)}, u32[]{:S(2)}, u32[]{:S(2)}) collective-permute-start(f32[128,512]{1,0:T(8,128)S(1)} %get-tuple-element.26), channel_id=1, source_target_pairs={{0,2},{2,0},{4,6},{6,4},{8,10},{10,8},{12,14},{14,12},{16,18},{18,... | collective-permute-start | bytes 786440 | tf_op jit(solution)/shard_map/ppermute | solution.py:302
  17.4 35.1 %copy-start.6 = (f32[128,512]{1,0:T(8,128)}, f32[128,512]{1,0:T(8,128)S(1)}, u32[]{:S(2)}) copy-start(f32[128,512]{1,0:T(8,128)S(1)} %collective-permute-done.2.refs_5_) | copy-start | bytes 786436
  17.4 25.3 %collective-permute-start.1 = (f32[128,512]{1,0:T(8,128)S(1)}, f32[128,512]{1,0:T(8,128)S(1)}, u32[]{:S(2)}, u32[]{:S(2)}) collective-permute-start(f32[128,512]{1,0:T(8,128)S(1)} %collective-permute-done.refs_4_), channel_id=1, source_target_pairs={{0,4},{4,8},{6,2},{8,12},{10,6},{12,16},{14,10},{16,20},{18,14},{2... | collective-permute-start | bytes 786440 | tf_op jit(solution)/shard_map/ppermute | solution.py:308
  23.0 29.5 %copy-start.7 = (f32[128,512]{1,0:T(8,128)}, f32[128,512]{1,0:T(8,128)S(1)}, u32[]{:S(2)}) copy-start(f32[128,512]{1,0:T(8,128)S(1)} %collective-permute-done.4.refs_6_) | copy-start | bytes 786436
  23.0 29.5 %collective-permute-start.3 = (f32[128,512]{1,0:T(8,128)S(1)}, f32[128,512]{1,0:T(8,128)S(1)}, u32[]{:S(2)}, u32[]{:S(2)}) collective-permute-start(f32[128,512]{1,0:T(8,128)S(1)} %collective-permute-done.2.refs_5_), channel_id=1, source_target_pairs={{0,4},{4,8},{6,2},{8,12},{10,6},{12,16},{14,10},{16,20},{18,14},{2... | collective-permute-start | bytes 786440 | tf_op jit(solution)/shard_map/ppermute | solution.py:308
  28.7 23.8 %copy-start.9 = (f32[128,512]{1,0:T(8,128)}, f32[128,512]{1,0:T(8,128)S(1)}, u32[]{:S(2)}) copy-start(f32[128,512]{1,0:T(8,128)S(1)} %collective-permute-done.6.refs_7_) | copy-start | bytes 786436
  28.7 23.9 %collective-permute-start.5 = (f32[128,512]{1,0:T(8,128)S(1)}, f32[128,512]{1,0:T(8,128)S(1)}, u32[]{:S(2)}, u32[]{:S(2)}) collective-permute-start(f32[128,512]{1,0:T(8,128)S(1)} %collective-permute-done.4.refs_6_), channel_id=1, source_target_pairs={{0,4},{4,8},{6,2},{8,12},{10,6},{12,16},{14,10},{16,20},{18,14},{2... | collective-permute-start | bytes 786440 | tf_op jit(solution)/shard_map/ppermute | solution.py:308
  34.3 18.2 %copy-start.8 = (f32[128,512]{1,0:T(8,128)}, f32[128,512]{1,0:T(8,128)S(1)}, u32[]{:S(2)}) copy-start(f32[128,512]{1,0:T(8,128)S(1)} %collective-permute-done.8.refs_8_) | copy-start | bytes 786436
  34.3 18.3 %collective-permute-start.7 = (f32[128,512]{1,0:T(8,128)S(1)}, f32[128,512]{1,0:T(8,128)S(1)}, u32[]{:S(2)}, u32[]{:S(2)}) collective-permute-start(f32[128,512]{1,0:T(8,128)S(1)} %collective-permute-done.6.refs_7_), channel_id=1, source_target_pairs={{0,4},{4,8},{6,2},{8,12},{10,6},{12,16},{14,10},{16,20},{18,14},{2... | collective-permute-start | bytes 786440 | tf_op jit(solution)/shard_map/ppermute | solution.py:308
  39.0 13.5 %copy-start.10 = (f32[128,512]{1,0:T(8,128)}, f32[128,512]{1,0:T(8,128)S(1)}, u32[]{:S(2)}) copy-start(f32[128,512]{1,0:T(8,128)S(1)} %collective-permute-done.9.refs_9_) | copy-start | bytes 786436
  39.0 20.8 %collective-permute-start.10 = (f32[128,512]{1,0:T(8,128)S(1)}, f32[128,512]{1,0:T(8,128)S(1)}, u32[]{:S(2)}, u32[]{:S(2)}) collective-permute-start(f32[128,512]{1,0:T(8,128)S(1)} %collective-permute-done.8.refs_8_), channel_id=1, source_target_pairs={{0,4},{4,8},{6,2},{8,12},{10,6},{12,16},{14,10},{16,20},{18,14},{2... | collective-permute-start | bytes 786440 | tf_op jit(solution)/shard_map/ppermute | solution.py:308
  42.7 9.8 %copy-start.11 = (f32[128,512]{1,0:T(8,128)}, f32[128,512]{1,0:T(8,128)S(1)}, u32[]{:S(2)}) copy-start(f32[128,512]{1,0:T(8,128)S(1)} %collective-permute-done.1.refs_0_) | copy-start | bytes 786436
  42.8 17.2 %collective-permute-start.11 = (f32[128,512]{1,0:T(8,128)S(1)}, f32[128,512]{1,0:T(8,128)S(1)}, u32[]{:S(2)}, u32[]{:S(2)}) collective-permute-start(f32[128,512]{1,0:T(8,128)S(1)} %collective-permute-done.9.refs_9_), channel_id=1, source_target_pairs={{0,4},{4,8},{6,2},{8,12},{10,6},{12,16},{14,10},{16,20},{18,14},{2... | collective-permute-start | bytes 786440 | tf_op jit(solution)/shard_map/ppermute | solution.py:308
  66.3 2.6 %collective-permute-start.12 = (f32[768,256]{1,0:T(8,128)}, f32[768,256]{1,0:T(8,128)S(1)}, u32[]{:S(2)}, u32[]{:S(2)}) collective-permute-start(f32[768,256]{1,0:T(8,128)} %get-tuple-element.14.half_ref), channel_id=1, source_target_pairs={{0,1},{1,0},{2,3},{3,2},{4,5},{5,4},{6,7},{7,6},{8,9},{9,8},{10,11... | collective-permute-start | bytes 2359304 | tf_op jit(solution)/shard_map/ppermute | solution.py:302
  68.8 0.9 copy-start.23
  73.8 6.6 %collective-permute-start.13 = (f32[256,128]{1,0:T(8,128)}, f32[256,128]{1,0:T(8,128)S(1)}, u32[]{:S(2)}, u32[]{:S(2)}) collective-permute-start(f32[256,128]{1,0:T(8,128)} %get-tuple-element.18), channel_id=1, source_target_pairs={{0,2},{2,0},{4,6},{6,4},{8,10},{10,8},{12,14},{14,12},{16,18},{18,... | collective-permute-start | bytes 393224 | tf_op jit(solution)/shard_map/ppermute | solution.py:302
  73.8 14.8 %collective-permute-start.18 = (f32[128,512]{1,0:T(8,128)}, f32[128,512]{1,0:T(8,128)S(1)}, u32[]{:S(2)}, u32[]{:S(2)}) collective-permute-start(f32[128,512]{1,0:T(8,128)} %get-tuple-element.25), channel_id=1, source_target_pairs={{0,2},{2,0},{4,6},{6,4},{8,10},{10,8},{12,14},{14,12},{16,18},{18,... | collective-permute-start | bytes 786440 | tf_op jit(solution)/shard_map/ppermute | solution.py:302
  81.3 5.0 %collective-permute-start.14 = (f32[256,128]{1,0:T(8,128)S(1)}, f32[256,128]{1,0:T(8,128)S(1)}, u32[]{:S(2)}, u32[]{:S(2)}) collective-permute-start(f32[256,128]{1,0:T(8,128)S(1)} %add.46), channel_id=1, source_target_pairs={{0,4},{2,6},{4,0},{6,2},{8,12},{10,14},{12,8},{14,10},{16,20},{18,... | collective-permute-start | bytes 393224 | tf_op jit(solution)/shard_map/ppermute | solution.py:302
  86.4 5.2 %collective-permute-start.15 = (f32[256,128]{1,0:T(8,128)S(1)}, f32[256,128]{1,0:T(8,128)S(1)}, u32[]{:S(2)}, u32[]{:S(2)}) collective-permute-start(f32[256,128]{1,0:T(8,128)S(1)} %add.47), channel_id=1, source_target_pairs={{0,8},{2,10},{4,12},{6,14},{8,0},{10,2},{12,4},{14,6},{16,24},{18,... | collective-permute-start | bytes 393224 | tf_op jit(solution)/shard_map/ppermute | solution.py:302
  89.6 26.7 %copy-start = (f32[128,512]{1,0:T(8,128)}, f32[128,512]{1,0:T(8,128)S(1)}, u32[]{:S(2)}) copy-start(f32[128,512]{1,0:T(8,128)S(1)} %add.54.refs_4_) | copy-start | bytes 786436
  91.5 6.1 %collective-permute-start.16 = (f32[256,128]{1,0:T(8,128)S(1)}, f32[256,128]{1,0:T(8,128)S(1)}, u32[]{:S(2)}, u32[]{:S(2)}) collective-permute-start(f32[256,128]{1,0:T(8,128)S(1)} %add.48), channel_id=1, source_target_pairs={{0,16},{2,18},{4,20},{6,22},{8,24},{10,26},{12,28},{14,30},{16,0},... | collective-permute-start | bytes 393224 | tf_op jit(solution)/shard_map/ppermute | solution.py:302
  94.7 5.0 %collective-permute-start.20 = (f32[64,512]{1,0:T(8,128)S(1)}, f32[64,512]{1,0:T(8,128)S(1)}, u32[]{:S(2)}, u32[]{:S(2)}) collective-permute-start(f32[64,512]{1,0:T(8,128)S(1)} %slice_select_fusion), channel_id=1, source_target_pairs={{0,4},{2,6},{4,0},{6,2},{8,12},{10,14},{12,8},{14,10},{16,20},{18,... | collective-permute-start | bytes 393224 | tf_op jit(solution)/shard_map/ppermute | solution.py:302
  97.7 23.5 %copy-start.4 = (f32[4,256,128]{2,1,0:T(8,128)}, f32[4,256,128]{2,1,0:T(8,128)S(1)}, u32[]{:S(2)}) copy-start(f32[4,256,128]{2,1,0:T(8,128)S(1)} %pad_maximum_fusion.mine_ref) | copy-start | bytes 1572868
  97.7 22.6 %collective-permute-start.17 = (f32[4,256,128]{2,1,0:T(8,128)S(1)}, f32[4,256,128]{2,1,0:T(8,128)}, u32[]{:S(2)}, u32[]{:S(2)}) collective-permute-start(f32[4,256,128]{2,1,0:T(8,128)S(1)} %pad_maximum_fusion.mine_ref), channel_id=1, source_target_pairs={{0,1},{1,0},{2,3},{3,2},{4,5},{5,4},{6,7},{7,6},{8,9},{9,8},{10,11... | collective-permute-start | bytes 1572872 | tf_op jit(solution)/shard_map/ppermute | solution.py:302
  99.8 5.0 %collective-permute-start.21 = (f32[64,512]{1,0:T(8,128)S(1)}, f32[64,512]{1,0:T(8,128)S(1)}, u32[]{:S(2)}, u32[]{:S(2)}) collective-permute-start(f32[64,512]{1,0:T(8,128)S(1)} %select_add_fusion), channel_id=1, source_target_pairs={{0,8},{2,10},{4,12},{6,14},{8,0},{10,2},{12,4},{14,6},{16,24},{18,... | collective-permute-start | bytes 393224 | tf_op jit(solution)/shard_map/ppermute | solution.py:302
  104.8 8.2 %collective-permute-start.25 = (f32[64,512]{1,0:T(8,128)S(1)}, f32[64,512]{1,0:T(8,128)S(1)}, u32[]{:S(2)}, u32[]{:S(2)}) collective-permute-start(f32[64,512]{1,0:T(8,128)S(1)} %add.56), channel_id=1, source_target_pairs={{0,16},{2,18},{4,20},{6,22},{8,24},{10,26},{12,28},{14,30},{16,0},... | collective-permute-start | bytes 393224 | tf_op jit(solution)/shard_map/ppermute | solution.py:302
  106.9 31.9 %copy-start.1 = (f32[2,64,512]{2,1,0:T(8,128)}, f32[2,64,512]{2,1,0:T(8,128)S(1)}, u32[]{:S(2)}) copy-start(f32[2,64,512]{2,1,0:T(8,128)S(1)} %pad_maximum_fusion.1.refs_6_) | copy-start | bytes 786436
  106.9 11.4 %collective-permute-start.22 = (f32[2,64,512]{2,1,0:T(8,128)S(1)}, f32[2,64,512]{2,1,0:T(8,128)S(1)}, u32[]{:S(2)}, u32[]{:S(2)}) collective-permute-start(f32[2,64,512]{2,1,0:T(8,128)S(1)} %pad_maximum_fusion.1.refs_6_), channel_id=1, source_target_pairs={{0,4},{2,6},{4,0},{6,2},{8,12},{10,14},{12,8},{14,10},{16,20},{18,... | collective-permute-start | bytes 786440 | tf_op jit(solution)/shard_map/ppermute | solution.py:302
  113.0 25.8 %copy-start.3 = (f32[64,512]{1,0:T(8,128)}, f32[64,512]{1,0:T(8,128)S(1)}, u32[]{:S(2)}) copy-start(f32[64,512]{1,0:T(8,128)S(1)} %add.57.refs_10_) | copy-start | bytes 393220
  113.0 6.2 %collective-permute-start.26 = (f32[64,512]{1,0:T(8,128)S(1)}, f32[64,512]{1,0:T(8,128)S(1)}, u32[]{:S(2)}, u32[]{:S(2)}) collective-permute-start(f32[64,512]{1,0:T(8,128)S(1)} %add.57.refs_10_), channel_id=1, source_target_pairs={{0,4},{2,6},{4,0},{6,2},{8,12},{10,14},{12,8},{14,10},{16,20},{18,... | collective-permute-start | bytes 393224 | tf_op jit(solution)/shard_map/ppermute | solution.py:302
  116.3 24.9 %collective-permute-start.19 = (f32[128,512]{1,0:T(8,128)S(1)}, f32[128,512]{1,0:T(8,128)S(1)}, u32[]{:S(2)}, u32[]{:S(2)}) collective-permute-start(f32[128,512]{1,0:T(8,128)S(1)} %add.54.refs_4_), channel_id=1, source_target_pairs={{0,2},{2,0},{4,6},{6,4},{8,10},{10,8},{12,14},{14,12},{16,18},{18,... | collective-permute-start | bytes 786440 | tf_op jit(solution)/shard_map/ppermute | solution.py:302
  117.0 24.2 %collective-permute-start.23 = (f32[2,64,512]{2,1,0:T(8,128)S(1)}, f32[2,64,512]{2,1,0:T(8,128)S(1)}, u32[]{:S(2)}, u32[]{:S(2)}) collective-permute-start(f32[2,64,512]{2,1,0:T(8,128)S(1)} %pad_maximum_fusion.1.refs_6_), channel_id=1, source_target_pairs={{0,2},{2,0},{4,6},{6,4},{8,10},{10,8},{12,14},{14,12},{16,18},{18,... | collective-permute-start | bytes 786440 | tf_op jit(solution)/shard_map/ppermute | solution.py:302
  118.3 20.5 %copy-start.15 = (f32[2,64,512]{2,1,0:T(8,128)}, f32[2,64,512]{2,1,0:T(8,128)S(1)}, u32[]{:S(2)}) copy-start(f32[2,64,512]{2,1,0:T(8,128)S(1)} %collective-permute-done.22.refs_7_) | copy-start | bytes 786436
  118.3 22.9 %collective-permute-start.27 = (f32[64,512]{1,0:T(8,128)S(1)}, f32[64,512]{1,0:T(8,128)S(1)}, u32[]{:S(2)}, u32[]{:S(2)}) collective-permute-start(f32[64,512]{1,0:T(8,128)S(1)} %add.57.refs_10_), channel_id=1, source_target_pairs={{0,2},{2,0},{4,6},{6,4},{8,10},{10,8},{12,14},{14,12},{16,18},{18,... | collective-permute-start | bytes 393224 | tf_op jit(solution)/shard_map/ppermute | solution.py:302
  119.2 19.7 %copy-start.19 = (f32[64,512]{1,0:T(8,128)}, f32[64,512]{1,0:T(8,128)S(1)}, u32[]{:S(2)}) copy-start(f32[64,512]{1,0:T(8,128)S(1)} %collective-permute-done.26.refs_11_) | copy-start | bytes 393220
  119.2 22.1 %collective-permute-start.24 = (f32[2,64,512]{2,1,0:T(8,128)S(1)}, f32[2,64,512]{2,1,0:T(8,128)S(1)}, u32[]{:S(2)}, u32[]{:S(2)}) collective-permute-start(f32[2,64,512]{2,1,0:T(8,128)S(1)} %collective-permute-done.22.refs_7_), channel_id=1, source_target_pairs={{0,2},{2,0},{4,6},{6,4},{8,10},{10,8},{12,14},{14,12},{16,18},{18,... | collective-permute-start | bytes 786440 | tf_op jit(solution)/shard_map/ppermute | solution.py:302
  120.3 20.9 %collective-permute-start.28 = (f32[64,512]{1,0:T(8,128)S(1)}, f32[64,512]{1,0:T(8,128)S(1)}, u32[]{:S(2)}, u32[]{:S(2)}) collective-permute-start(f32[64,512]{1,0:T(8,128)S(1)} %collective-permute-done.26.refs_11_), channel_id=1, source_target_pairs={{0,2},{2,0},{4,6},{6,4},{8,10},{10,8},{12,14},{14,12},{16,18},{18,... | collective-permute-start | bytes 393224 | tf_op jit(solution)/shard_map/ppermute | solution.py:302
  121.2 17.6 %copy-start.2 = (f32[768,256]{1,0:T(8,128)S(1)}, f32[768,256]{1,0:T(8,128)}, u32[]{:S(2)}) copy-start(f32[768,256]{1,0:T(8,128)} %get-tuple-element.16) | copy-start | bytes 2359300
  141.2 0.8 copy-start.20
  141.3 0.9 copy-start.21
  141.3 0.9 copy-start.18
  (7 other events, 5.1 us)

commit v5 on v4

--- a/solution.py
+++ b/solution.py
@@ -143,7 +143,7 @@
     smem = pl.BlockSpec(memory_space=pltpu.SMEM)
     return pl.pallas_call(
         functools.partial(inverse_kernel, size),
-        out_shape=[jax.ShapeDtypeStruct((size, size), jnp.float32)] * count,
+        out_shape=[pltpu.VMEM((size, size), jnp.float32)] * count,
         in_specs=[smem, vmem, vmem, vmem],
         out_specs=[vmem] * count,
         scratch_shapes=[pltpu.VMEM((size, size), jnp.float32)] * count,
@@ -201,7 +201,7 @@
     shapes = [(rows, width)] + [(rows, value.shape[1]) for value in extra]
     return pl.pallas_call(
         functools.partial(near_kernel, len(pieces), first_slot, tuple(spots), len(extra)),
-        out_shape=[jax.ShapeDtypeStruct(shape, jnp.float32) for shape in shapes],
+        out_shape=[pltpu.VMEM(shape, jnp.float32) for shape in shapes],
         in_specs=[smem, smem, vmem, vmem] + [hbm] * len(pieces) + [vmem] * len(extra),
         out_specs=[vmem] * len(shapes),
         scratch_shapes=[
@@ -249,7 +249,7 @@
 
     return pl.pallas_call(
         kernel,
-        out_shape=[jax.ShapeDtypeStruct(shape, jnp.float32) for shape in shapes],
+        out_shape=[pltpu.VMEM(shape, jnp.float32) for shape in shapes],
         in_specs=[smem] + [vmem] * (len(args) - 1),
         out_specs=[vmem] * len(shapes),
         scratch_shapes=[pltpu.VMEM((rank, width), jnp.float32)],
@@ -260,46 +260,93 @@
     )(*args)
 
 
-def reduce_kernel(place_ref, *refs):
-    count = LEVELS
-    inverses, first, first_other = refs[:count], refs[count], refs[count + 1]
-    early, last = refs[count + 2 : count + 6], refs[count + 6 : count + 10]
-    out_ref, stage = refs[count + 10 :]
-    rank = inverses[0].shape[0]
-    half, quarter = rank // 2, rank // 4
+def staged(stage, place_ref, parts):
+    for value, at in parts:
+        depth = value.shape[0]
+        stage[pl.ds(pl.multiple_of(place_ref[at], depth), depth), :] = value
+    return stage[...]
+
+
+def early_kernel(place_ref, *refs):
+    count = LEVELS - 1
+    inverses, first = refs[:count], refs[count : count + 2]
+    early = refs[count + 2 : count + 6]
+    out_ref, stage, result, sems = refs[count + 6 :]
+    copies = []
     for h in range(count):
         if h == 0:
-            parts = [(half, first[...], 0), (half, first_other[...], 1)]
-        elif h < count - 1:
-            parts = [(quarter, early[i][h - 1], 2 + i) for i in range(4)]
+            parts = [(first[0][...], 0), (first[1][...], 1)]
         else:
-            parts = [(quarter, last[i][...], 2 + i) for i in range(4)]
-        for depth, value, at in parts:
-            stage[h, pl.ds(pl.multiple_of(place_ref[at], depth), depth), :] = value
-    for h in range(count):
-        out_ref[h, 0] = dot3(inverses[h][...], stage[h], NN)
-
-
-def reduce_all(place, inverses, first, early, last):
-    rank, width = inverses[0].shape[0], last[0].shape[1]
+            parts = [(early[i][h - 1], 2 + i) for i in range(4)]
+        result[h] = dot3(inverses[h][...], staged(stage.at[h], place_ref, parts), NN)
+        copies.append(pltpu.make_async_copy(result.at[h], out_ref.at[h, 0], sems.at[h]))
+        copies[-1].start()
+    for copy in copies:
+        copy.wait()
+
+
+def reduce_early(place, inverses, first, early):
+    rank, width = inverses[0].shape[0], first[0].shape[1]
     vmem = pl.BlockSpec(memory_space=pltpu.VMEM)
     smem = pl.BlockSpec(memory_space=pltpu.SMEM)
-    args = [*inverses, *first, *early, *last]
+    args = [*inverses, *first, *early]
+    count = LEVELS - 1
     return pl.pallas_call(
-        reduce_kernel,
+        early_kernel,
         out_shape=jax.ShapeDtypeStruct((LEVELS, 1, rank, width), jnp.float32),
         in_specs=[smem] + [vmem] * len(args),
-        out_specs=vmem,
-        scratch_shapes=[pltpu.VMEM((LEVELS, rank, width), jnp.float32)],
+        out_specs=pl.BlockSpec(memory_space=pl.ANY),
+        scratch_shapes=[
+            pltpu.VMEM((count, rank, width), jnp.float32),
+            pltpu.VMEM((count, rank, width), jnp.float32),
+            pltpu.SemaphoreType.DMA((count,)),
+        ],
         cost_estimate=pl.CostEstimate(
-            flops=6 * LEVELS * rank * rank * width, bytes_accessed=8 * LEVELS * rank * (rank + width), transcendentals=0
+            flops=6 * count * rank * rank * width, bytes_accessed=8 * count * rank * (rank + width), transcendentals=0
         ),
-        name="reduce_all",
+        name="reduce_early",
     )(place, *args)
+
+
+def last_kernel(place_ref, inverse_ref, *refs):
+    last = refs[:4]
+    out_ref, stage, result, sem = refs[5:]
+    value = staged(stage, place_ref, [(last[i][...], 2 + i) for i in range(4)])
+    result[...] = dot3(inverse_ref[...], value, NN)
+    copy = pltpu.make_async_copy(result, out_ref.at[LEVELS - 1, 0], sem)
+    copy.start()
+    copy.wait()
+
+
+def reduce_last(place, inverse, last, reduced):
+    rank, width = inverse.shape[0], last[0].shape[1]
+    vmem = pl.BlockSpec(memory_space=pltpu.VMEM)
+    smem = pl.BlockSpec(memory_space=pltpu.SMEM)
+    hbm = pl.BlockSpec(memory_space=pl.ANY)
+    return pl.pallas_call(
+        last_kernel,
+        out_shape=jax.ShapeDtypeStruct(reduced.shape, jnp.float32),
+        in_specs=[smem] + [vmem] * 5 + [hbm],
+        out_specs=hbm,
+        scratch_shapes=[
+            pltpu.VMEM((rank, width), jnp.float32),
+            pltpu.VMEM((rank, width), jnp.float32),
+            pltpu.SemaphoreType.DMA,
+        ],
+        input_output_aliases={6: 0},
+        cost_estimate=pl.CostEstimate(
+            flops=6 * rank * rank * width, bytes_accessed=8 * rank * (rank + width), transcendentals=0
+        ),
+        name="reduce_last",
+    )(place, inverse, *last, reduced)
 
 
 def across(value, axis, bit):
     return lax.ppermute(value, axis, [(i, i ^ 1 << bit) for i in range(lax.axis_size(axis))])
+
+
+def diagonal_of(value, axis):
+    return lax.ppermute(value, axis, [(i, i ^ 3) for i in range(lax.axis_size(axis))])
 
 
 def relayed(value, axis):
@@ -375,7 +422,7 @@
     def gathered(value):
         along = across(value, "rows", 1)
         beside = across(value, "rows", 0)
-        diagonal = across(along, "rows", 0)
+        diagonal = diagonal_of(value, "rows")
         return [value, along, beside, diagonal]
 
     early = gathered(jnp.stack(quarters[:-1]))
@@ -384,7 +431,8 @@
     x, y = bits[0] * half, bits[1] * (half // 2)
     fx, fy = half - x, half // 2 - y
     place = jnp.stack([x, fx, x + y, x + fy, fx + y, fx + fy]).astype(jnp.int32)
-    reduced = reduce_all(place, inverses, [first, first_other], early, last)
+    reduced = reduce_early(place, inverses[:-1], [first, first_other], early)
+    reduced = reduce_last(place, inverses[-1], last, reduced)
     return (leaf_basis, reduced)
 
 

time: 147 us -> 140 us (0.952)
  Pallas kernels: 43 us -> 39.3 us
  other arithmetic: 3.31 us -> 1.6 us
    ppermute x23 -> x21, starting transfers between devices: 32.7 us -> 26.8 us  [across(): lax.ppermute(value, axis, [(i, i ^ 1 << bit) for i in range(lax.axis_size...]
    pallas_call x3, Pallas kernels: 17.1 us -> 13.9 us  [near_step(): pl.pallas_call(functools.partial(near_kernel, len(pieces), first_slot, tu...]
    ppermute x0 -> x2, starting transfers between devices: none -> 3.09 us  [diagonal_of(): lax.ppermute(value, axis, [(i, i ^ 3) for i in range(lax.axis_size(axis))])]
    ppermute x6, starting transfers between devices: 22.9 us -> 25.2 us  [relayed(): lax.ppermute(value, axis, [(i, t) for i, t in steps if 0 <= t < count])]
    ppermute x23 -> x21, waiting for transfers between devices: 33.4 us -> 32.5 us  [across(): lax.ppermute(value, axis, [(i, i ^ 1 << bit) for i in range(lax.axis_size...]
    pallas_call x3 -> x4, Pallas kernels: 26 us -> 25.5 us  [the longest x1 16.6 us: factor_inverse(): pl.pallas_call(functools.partial(inverse_kernel, size), out_shape=[pltpu....]
    unnamed x52 -> x50, local copies, waits for them, and re-layouts: 4.71 us -> 5.05 us
  transfers between devices with their start and end apart: 29 -> 29, of which waited for: 15 -> 14; matrix products, arithmetic and copies ran while one was open for 5% -> 4% of each run, Pallas kernels for 20% -> 21%
where the time goes in v5:
time: 140 us
  starting transfers between devices  55.1 us (39%)
  Pallas kernels  39.3 us (28%)
  waiting for transfers between devices  33.1 us (24%)
  local copies, waits for them, and re-layouts  8.07 us (6%)
  other arithmetic  1.6 us (1%)
    ppermute x21, waiting for transfers between devices, across(): lax.ppermute(value, axis, [(i, i ^ 1 << bit) for i in range(lax.axis_size...  32.5 us
    ppermute x21, starting transfers between devices, across(): lax.ppermute(value, axis, [(i, i ^ 1 << bit) for i in range(lax.axis_size...  26.8 us
    ppermute x6, starting transfers between devices, relayed(): lax.ppermute(value, axis, [(i, t) for i, t in steps if 0 <= t < count])  25.2 us
    pallas_call x1, Pallas kernels, factor_inverse(): pl.pallas_call(functools.partial(inverse_kernel, size), out_shape=[pltpu....  16.6 us
    pallas_call x3, Pallas kernels, near_step(): pl.pallas_call(functools.partial(near_kernel, len(pieces), first_slot, tu...  13.9 us
    unnamed x50, local copies, waits for them, and re-layouts  5.05 us
    pallas_call x1, Pallas kernels, reduce_early(): pl.pallas_call(early_kernel, out_shape=jax.ShapeDtypeStruct((LEVELS, 1, r...  3.27 us
    pallas_call x1, Pallas kernels, leaf_products(): pl.pallas_call(kernel, out_shape=[pltpu.VMEM(shape, jnp.float32) for shap...  3.21 us
  transfers between devices with their start and end apart: 29, of which 14 were waited for; matrix products, arithmetic and copies ran while one was open for 4% of the time, Pallas kernels for 21%

profile of v5, /device:TPU:0, one launch (start us, length us, event | category | flops | bytes accessed | tf_op | source)
XLA Modules:
  0.0 139.9 jit_solution(9893925617679793594)
XLA Ops:
  0.6 1.0 slice.26
  1.6 3.0 %collective-permute-start = (f32[128,512]{1,0:T(8,128)S(1)}, f32[128,512]{1,0:T(8,128)S(1)}, u32[]{:S(2)}, u32[]{:S(2)}) collective-permute-start(f32[128,512]{1,0:T(8,128)S(1)} %slice.26), channel_id=1, source_target_pairs={{0,2},{2,0},{4,6},{6,4},{8,10},{10,8},{12,14},{14,12},{16,18},{18,... | collective-permute-start | bytes 786440 | tf_op jit(solution)/shard_map/ppermute | solution.py:345
  4.6 1.4 fusion
  6.1 2.0 %collective-permute-start.4 = (f32[128,512]{1,0:T(8,128)S(1)}, f32[128,512]{1,0:T(8,128)S(1)}, u32[]{:S(2)}, u32[]{:S(2)}) collective-permute-start(f32[128,512]{1,0:T(8,128)S(1)} %get-tuple-element.29), channel_id=1, source_target_pairs={{0,2},{2,0},{4,6},{6,4},{8,10},{10,8},{12,14},{14,12},{16,18},{18,... | collective-permute-start | bytes 786440 | tf_op jit(solution)/shard_map/ppermute | solution.py:345
  8.2 1.9 %collective-permute-start.8 = (f32[128,512]{1,0:T(8,128)S(1)}, f32[128,512]{1,0:T(8,128)S(1)}, u32[]{:S(2)}, u32[]{:S(2)}) collective-permute-start(f32[128,512]{1,0:T(8,128)S(1)} %get-tuple-element.27), channel_id=1, source_target_pairs={{0,2},{2,0},{4,6},{6,4},{8,10},{10,8},{12,14},{14,12},{16,18},{18,... | collective-permute-start | bytes 786440 | tf_op jit(solution)/shard_map/ppermute | solution.py:345
  10.1 1.7 %collective-permute-done.refs_4_ = f32[128,512]{1,0:T(8,128)S(1)} collective-permute-done((f32[128,512]{1,0:T(8,128)S(1)}, f32[128,512]{1,0:T(8,128)S(1)}, u32[]{:S(2)}, u32[]{:S(2)}) %collective-permute-start) | collective-permute-done | bytes 262176 | tf_op jit(solution)/shard_map/ppermute | solution.py:345
  11.8 2.0 %collective-permute-start.9 = (f32[128,512]{1,0:T(8,128)S(1)}, f32[128,512]{1,0:T(8,128)S(1)}, u32[]{:S(2)}, u32[]{:S(2)}) collective-permute-start(f32[128,512]{1,0:T(8,128)S(1)} %get-tuple-element.26), channel_id=1, source_target_pairs={{0,2},{2,0},{4,6},{6,4},{8,10},{10,8},{12,14},{14,12},{16,18},{18,... | collective-permute-start | bytes 786440 | tf_op jit(solution)/shard_map/ppermute | solution.py:345
  13.8 3.6 %collective-permute-done.2.refs_5_ = f32[128,512]{1,0:T(8,128)S(1)} collective-permute-done((f32[128,512]{1,0:T(8,128)S(1)}, f32[128,512]{1,0:T(8,128)S(1)}, u32[]{:S(2)}, u32[]{:S(2)}) %collective-permute-start.2) | collective-permute-done | bytes 262176 | tf_op jit(solution)/shard_map/ppermute | solution.py:345
  17.4 4.0 %collective-permute-start.1 = (f32[128,512]{1,0:T(8,128)S(1)}, f32[128,512]{1,0:T(8,128)S(1)}, u32[]{:S(2)}, u32[]{:S(2)}) collective-permute-start(f32[128,512]{1,0:T(8,128)S(1)} %collective-permute-done.refs_4_), channel_id=1, source_target_pairs={{0,4},{4,8},{6,2},{8,12},{10,6},{12,16},{14,10},{16,20},{18,14},{2... | collective-permute-start | bytes 786440 | tf_op jit(solution)/shard_map/ppermute | solution.py:355
  21.4 1.6 %collective-permute-done.4.refs_6_ = f32[128,512]{1,0:T(8,128)S(1)} collective-permute-done((f32[128,512]{1,0:T(8,128)S(1)}, f32[128,512]{1,0:T(8,128)S(1)}, u32[]{:S(2)}, u32[]{:S(2)}) %collective-permute-start.4) | collective-permute-done | bytes 262176 | tf_op jit(solution)/shard_map/ppermute | solution.py:345
  23.0 4.6 %collective-permute-start.3 = (f32[128,512]{1,0:T(8,128)S(1)}, f32[128,512]{1,0:T(8,128)}, u32[]{:S(2)}, u32[]{:S(2)}) collective-permute-start(f32[128,512]{1,0:T(8,128)S(1)} %collective-permute-done.2.refs_5_), channel_id=1, source_target_pairs={{0,4},{4,8},{6,2},{8,12},{10,6},{12,16},{14,10},{16,20},{18,14},{2... | collective-permute-start | bytes 786440 | tf_op jit(solution)/shard_map/ppermute | solution.py:355
  27.7 1.0 collective-permute-done.6.refs_7_
  28.7 4.7 %collective-permute-start.5 = (f32[128,512]{1,0:T(8,128)S(1)}, f32[128,512]{1,0:T(8,128)}, u32[]{:S(2)}, u32[]{:S(2)}) collective-permute-start(f32[128,512]{1,0:T(8,128)S(1)} %collective-permute-done.4.refs_6_), channel_id=1, source_target_pairs={{0,4},{4,8},{6,2},{8,12},{10,6},{12,16},{14,10},{16,20},{18,14},{2... | collective-permute-start | bytes 786440 | tf_op jit(solution)/shard_map/ppermute | solution.py:355
  33.3 1.0 collective-permute-done.8.refs_8_
  34.3 4.6 %collective-permute-start.7 = (f32[128,512]{1,0:T(8,128)S(1)}, f32[128,512]{1,0:T(8,128)}, u32[]{:S(2)}, u32[]{:S(2)}) collective-permute-start(f32[128,512]{1,0:T(8,128)S(1)} %collective-permute-done.6.refs_7_), channel_id=1, source_target_pairs={{0,4},{4,8},{6,2},{8,12},{10,6},{12,16},{14,10},{16,20},{18,14},{2... | collective-permute-start | bytes 786440 | tf_op jit(solution)/shard_map/ppermute | solution.py:355
  39.5 3.9 %collective-permute-start.10 = (f32[128,512]{1,0:T(8,128)S(1)}, f32[128,512]{1,0:T(8,128)}, u32[]{:S(2)}, u32[]{:S(2)}) collective-permute-start(f32[128,512]{1,0:T(8,128)S(1)} %collective-permute-done.8.refs_8_), channel_id=1, source_target_pairs={{0,4},{4,8},{6,2},{8,12},{10,6},{12,16},{14,10},{16,20},{18,14},{2... | collective-permute-start | bytes 786440 | tf_op jit(solution)/shard_map/ppermute | solution.py:355
  43.4 3.4 %collective-permute-start.11 = (f32[128,512]{1,0:T(8,128)S(1)}, f32[128,512]{1,0:T(8,128)}, u32[]{:S(2)}, u32[]{:S(2)}) collective-permute-start(f32[128,512]{1,0:T(8,128)S(1)} %collective-permute-done.9.refs_9_), channel_id=1, source_target_pairs={{0,4},{4,8},{6,2},{8,12},{10,6},{12,16},{14,10},{16,20},{18,14},{2... | collective-permute-start | bytes 786440 | tf_op jit(solution)/shard_map/ppermute | solution.py:355
  46.9 5.1 %near_step.3.base_ref = f32[768,512]{1,0:T(8,128)S(1)} custom-call(s32[3,3]{1,0:T(4,128)} %select_add_fusion.1.index_ref, s32[3]{0:T(128)} %count_ref.5, f32[3,3,256,256]{3,2,1,0:T(8,128)} %blocks_ref.5, f32[768,512]{1,0:T(8,128)} %base_ref.1, f32[768,512]{1,0:T(8,128)} %refs_0_.1), custom_call_target="tpu_custom_call" | custom-call | flops 1811939328 | bytes 7077888 | tf_op jit(solution)/shard_map/near_step/pallas_call | solution.py:202
  52.1 1.1 copy-done
  53.2 4.7 %near_step.4.base_ref = f32[768,512]{1,0:T(8,128)S(1)} custom-call(s32[3,3]{1,0:T(4,128)} %select_add_fusion.1.index_ref, s32[3]{0:T(128)} %count_ref.5, f32[3,3,256,256]{3,2,1,0:T(8,128)} %blocks_ref.5, f32[768,512]{1,0:T(8,128)} %copy-done, f32[128,512]{1,0:T(8,128)} %copy-done.19, f32[128,512]{1,0:T(8,128)} %collective-permute-done.3.refs_1_, ...), custom_call_target="tpu_custom_call" | custom-call | flops 1811939328 | bytes 8126464 | tf_op jit(solution)/shard_map/near_step/pallas_call | solution.py:202
  57.9 1.1 copy-done.1
  59.1 4.1 %near_step.5 = (f32[768,512]{1,0:T(8,128)S(1)}, f32[768,256]{1,0:T(8,128)S(1)}) custom-call(s32[3,3]{1,0:T(4,128)} %select_add_fusion.1.index_ref, s32[3]{0:T(128)} %count_ref.5, f32[3,3,256,256]{3,2,1,0:T(8,128)} %blocks_ref.5, f32[768,512]{1,0:T(8,128)} %copy-done.1, f32[128,512]{1,0:T(8,128)} %collective-permute-done.10.refs_0_, ...), custom_call_target="tpu_custom_call" | custom-call | flops 1811939328 | bytes 6029312 | tf_op jit(solution)/shard_map/near_step/pallas_call | solution.py:202
  63.2 1.1 copy-done.7
  65.1 1.5 %collective-permute-done.12.other_ref = f32[768,256]{1,0:T(8,128)S(1)} collective-permute-done((f32[768,256]{1,0:T(8,128)S(1)}, f32[768,256]{1,0:T(8,128)S(1)}, u32[]{:S(2)}, u32[]{:S(2)}) %collective-permute-start.12) | collective-permute-done | bytes 786464 | tf_op jit(solution)/shard_map/ppermute | solution.py:345
  66.6 0.9 copy-done.24
  67.5 3.2 %leaf_products.1 = (f32[768,256]{1,0:T(8,128)S(1)}, f32[256,256]{1,0:T(8,128)S(1)}, f32[256,128]{1,0:T(8,128)S(1)}, f32[128,512]{1,0:T(8,128)S(1)}, f32[128,512]{1,0:T(8,128)S(1)}) custom-call(s32[3]{0:T(128)} %pad_add_fusion.flag_ref, f32[768,256]{1,0:T(8,128)} %copy-done.6, f32[768,256]{1,0:T(8,128)} %copy-done.24, f32[768,512]{1,0:T(8,128)} %copy-done.7), custom_call_target="tpu_custom_call" | custom-call | flops 905969664 | bytes 3932160 | tf_op jit(solution)/shard_map/leaf_products/pallas_call | solution.py:250
  70.8 2.0 %collective-permute-start.18 = (f32[128,512]{1,0:T(8,128)S(1)}, f32[128,512]{1,0:T(8,128)S(1)}, u32[]{:S(2)}, u32[]{:S(2)}) collective-permute-start(f32[128,512]{1,0:T(8,128)S(1)} %get-tuple-element.22), channel_id=1, source_target_pairs={{0,2},{2,0},{4,6},{6,4},{8,10},{10,8},{12,14},{14,12},{16,18},{18,... | collective-permute-start | bytes 786440 | tf_op jit(solution)/shard_map/ppermute | solution.py:345
  72.8 4.3 %collective-permute-done.13 = f32[256,128]{1,0:T(8,128)S(1)} collective-permute-done((f32[256,128]{1,0:T(8,128)S(1)}, f32[256,128]{1,0:T(8,128)S(1)}, u32[]{:S(2)}, u32[]{:S(2)}) %collective-permute-start.13) | collective-permute-done | bytes 131104 | tf_op jit(solution)/shard_map/ppermute | solution.py:345
  77.2 1.4 %collective-permute-start.14 = (f32[256,128]{1,0:T(8,128)S(1)}, f32[256,128]{1,0:T(8,128)S(1)}, u32[]{:S(2)}, u32[]{:S(2)}) collective-permute-start(f32[256,128]{1,0:T(8,128)S(1)} %add.46), channel_id=1, source_target_pairs={{0,4},{2,6},{4,0},{6,2},{8,12},{10,14},{12,8},{14,10},{16,20},{18,... | collective-permute-start | bytes 393224 | tf_op jit(solution)/shard_map/ppermute | solution.py:345
  78.6 3.6 %collective-permute-done.14 = f32[256,128]{1,0:T(8,128)S(1)} collective-permute-done((f32[256,128]{1,0:T(8,128)S(1)}, f32[256,128]{1,0:T(8,128)S(1)}, u32[]{:S(2)}, u32[]{:S(2)}) %collective-permute-start.14) | collective-permute-done | bytes 131104 | tf_op jit(solution)/shard_map/ppermute | solution.py:345
  82.2 1.5 %collective-permute-start.15 = (f32[256,128]{1,0:T(8,128)S(1)}, f32[256,128]{1,0:T(8,128)S(1)}, u32[]{:S(2)}, u32[]{:S(2)}) collective-permute-start(f32[256,128]{1,0:T(8,128)S(1)} %add.47), channel_id=1, source_target_pairs={{0,8},{2,10},{4,12},{6,14},{8,0},{10,2},{12,4},{14,6},{16,24},{18,... | collective-permute-start | bytes 393224 | tf_op jit(solution)/shard_map/ppermute | solution.py:345
  83.8 3.4 %collective-permute-done.15 = f32[256,128]{1,0:T(8,128)S(1)} collective-permute-done((f32[256,128]{1,0:T(8,128)S(1)}, f32[256,128]{1,0:T(8,128)S(1)}, u32[]{:S(2)}, u32[]{:S(2)}) %collective-permute-start.15) | collective-permute-done | bytes 131104 | tf_op jit(solution)/shard_map/ppermute | solution.py:345
  87.3 2.6 %collective-permute-start.16 = (f32[256,128]{1,0:T(8,128)S(1)}, f32[256,128]{1,0:T(8,128)S(1)}, u32[]{:S(2)}, u32[]{:S(2)}) collective-permute-start(f32[256,128]{1,0:T(8,128)S(1)} %add.48), channel_id=1, source_target_pairs={{0,16},{2,18},{4,20},{6,22},{8,24},{10,26},{12,28},{14,30},{16,0},... | collective-permute-start | bytes 393224 | tf_op jit(solution)/shard_map/ppermute | solution.py:345
  89.9 2.1 %collective-permute-start.19 = (f32[64,512]{1,0:T(8,128)S(1)}, f32[64,512]{1,0:T(8,128)S(1)}, u32[]{:S(2)}, u32[]{:S(2)}) collective-permute-start(f32[64,512]{1,0:T(8,128)S(1)} %slice_select_fusion), channel_id=1, source_target_pairs={{0,4},{2,6},{4,0},{6,2},{8,12},{10,14},{12,8},{14,10},{16,20},{18,... | collective-permute-start | bytes 393224 | tf_op jit(solution)/shard_map/ppermute | solution.py:345
  92.0 2.6 %collective-permute-done.16 = f32[256,128]{1,0:T(8,128)S(1)} collective-permute-done((f32[256,128]{1,0:T(8,128)S(1)}, f32[256,128]{1,0:T(8,128)S(1)}, u32[]{:S(2)}, u32[]{:S(2)}) %collective-permute-start.16) | collective-permute-done | bytes 131104 | tf_op jit(solution)/shard_map/ppermute | solution.py:345
  95.4 5.4 %collective-permute-done.20 = f32[64,512]{1,0:T(8,128)S(1)} collective-permute-done((f32[64,512]{1,0:T(8,128)S(1)}, f32[64,512]{1,0:T(8,128)S(1)}, u32[]{:S(2)}, u32[]{:S(2)}) %collective-permute-start.20) | collective-permute-done | bytes 131104 | tf_op jit(solution)/shard_map/ppermute | solution.py:345
  100.8 1.3 collective-permute-start.21
  102.8 1.0 collective-permute-start.25
  103.9 2.1 %collective-permute-start.26 = (f32[2,64,512]{2,1,0:T(8,128)S(1)}, f32[2,64,512]{2,1,0:T(8,128)}, u32[]{:S(2)}, u32[]{:S(2)}) collective-permute-start(f32[2,64,512]{2,1,0:T(8,128)S(1)} %pad_maximum_fusion.1.refs_5_), channel_id=1, source_target_pairs={{0,4},{2,6},{4,0},{6,2},{8,12},{10,14},{12,8},{14,10},{16,20},{18,... | collective-permute-start | bytes 786440 | tf_op jit(solution)/shard_map/ppermute | solution.py:345
  105.9 0.9 collective-permute-start.27
  106.8 2.6 %collective-permute-done.21 = f32[64,512]{1,0:T(8,128)S(1)} collective-permute-done((f32[64,512]{1,0:T(8,128)S(1)}, f32[64,512]{1,0:T(8,128)S(1)}, u32[]{:S(2)}, u32[]{:S(2)}) %collective-permute-start.21) | collective-permute-done | bytes 131104 | tf_op jit(solution)/shard_map/ppermute | solution.py:345
  109.4 1.5 %collective-permute-start.28 = (f32[2,64,512]{2,1,0:T(8,128)S(1)}, f32[2,64,512]{2,1,0:T(8,128)}, u32[]{:S(2)}, u32[]{:S(2)}) collective-permute-start(f32[2,64,512]{2,1,0:T(8,128)S(1)} %pad_maximum_fusion.1.refs_5_), channel_id=1, source_target_pairs={{0,6},{2,4},{4,2},{6,0},{8,14},{10,12},{12,10},{14,8},{16,22},{18,... | collective-permute-start | bytes 786440 | tf_op jit(solution)/shard_map/ppermute | solution.py:349
  111.1 16.6 %factor_inverse.1 = (f32[256,256]{1,0:T(8,128)S(1)}, f32[256,256]{1,0:T(8,128)S(1)}, f32[256,256]{1,0:T(8,128)S(1)}, f32[256,256]{1,0:T(8,128)S(1)}, f32[256,256]{1,0:T(8,128)S(1)}) custom-call(s32[1]{0:T(128)} %bitcast.core_ref, f32[256,256]{1,0:T(8,128)} %copy-done.8, f32[4,256,128]{2,1,0:T(8,128)} %copy-done.12, ...), custom_call_target="tpu_custom_call" | custom-call | flops 15000000512 | bytes 2621440 | tf_op jit(solution)/shard_map/factor_inverse/pallas_call | solution.py:144
  127.8 2.0 %collective-permute-start.23 = (f32[64,512]{1,0:T(8,128)S(1)}, f32[64,512]{1,0:T(8,128)S(1)}, u32[]{:S(2)}, u32[]{:S(2)}) collective-permute-start(f32[64,512]{1,0:T(8,128)S(1)} %add.57.refs_0_), channel_id=1, source_target_pairs={{0,2},{2,0},{4,6},{6,4},{8,10},{10,8},{12,14},{14,12},{16,18},{18,... | collective-permute-start | bytes 393224 | tf_op jit(solution)/shard_map/ppermute | solution.py:345
  129.8 1.5 %collective-permute-start.24 = (f32[64,512]{1,0:T(8,128)S(1)}, f32[64,512]{1,0:T(8,128)S(1)}, u32[]{:S(2)}, u32[]{:S(2)}) collective-permute-start(f32[64,512]{1,0:T(8,128)S(1)} %add.57.refs_0_), channel_id=1, source_target_pairs={{0,6},{2,4},{4,2},{6,0},{8,14},{10,12},{12,10},{14,8},{16,22},{18,... | collective-permute-start | bytes 393224 | tf_op jit(solution)/shard_map/ppermute | solution.py:349
  131.3 1.4 fusion.1
  132.8 3.3 %reduce_early.1.refs_4_ = f32[4,1,256,512]{3,2,1,0:T(8,128)} custom-call(s32[6]{0:T(128)} %stack.69.place_ref, f32[256,256]{1,0:T(8,128)} %copy-done.3, f32[256,256]{1,0:T(8,128)} %copy-done.4, f32[256,256]{1,0:T(8,128)} %copy-done.5, f32[128,512]{1,0:T(8,128)} %copy-done.9, f32[128,512]{1,0:T(8,128)} %copy-done.20, f32[2,64,512]{2,1,0:T(8,128)} %copy-done.10, ...), custom_call_target="tpu_custom_call" | custom-call | flops 603979776 | bytes 4718592 | tf_op jit(solution)/shard_map/reduce_early/pallas_call | solution.py:294
  137.3 2.4 %reduce_last.1 = f32[4,1,256,512]{3,2,1,0:T(8,128)} custom-call(s32[6]{0:T(128)} %stack.69.place_ref, f32[256,256]{1,0:T(8,128)} %copy-done.2, f32[64,512]{1,0:T(8,128)} %copy-done.11, f32[64,512]{1,0:T(8,128)} %collective-permute-done.22.refs_1_, f32[64,512]{1,0:T(8,128)} %copy-done.21, f32[64,512]{1,0:T(8,128)} %copy-done.22, ...), custom_call_target="tpu_custom_call", output_to_operand_aliasing={{}: (6, {})} | custom-call | flops 201326592 | bytes 1572864 | tf_op jit(solution)/shard_map/reduce_last/pallas_call | solution.py:326
  (84 shorter events, 4.6 us)
Async XLA Ops:
  0.6 38.3 %copy-start.23 = (s32[3,3]{1,0:T(4,128)S(1)}, s32[3,3]{1,0:T(4,128)}, u32[]{:S(2)}) copy-start(s32[3,3]{1,0:T(4,128)} %param.9) | copy-start | bytes 112
  1.6 10.2 %collective-permute-start = (f32[128,512]{1,0:T(8,128)S(1)}, f32[128,512]{1,0:T(8,128)S(1)}, u32[]{:S(2)}, u32[]{:S(2)}) collective-permute-start(f32[128,512]{1,0:T(8,128)S(1)} %slice.26), channel_id=1, source_target_pairs={{0,2},{2,0},{4,6},{6,4},{8,10},{10,8},{12,14},{14,12},{16,18},{18,... | collective-permute-start | bytes 786440 | tf_op jit(solution)/shard_map/ppermute | solution.py:345
  6.0 11.4 %collective-permute-start.2 = (f32[128,512]{1,0:T(8,128)S(1)}, f32[128,512]{1,0:T(8,128)S(1)}, u32[]{:S(2)}, u32[]{:S(2)}) collective-permute-start(f32[128,512]{1,0:T(8,128)S(1)} %get-tuple-element.30), channel_id=1, source_target_pairs={{0,2},{2,0},{4,6},{6,4},{8,10},{10,8},{12,14},{14,12},{16,18},{18,... | collective-permute-start | bytes 786440 | tf_op jit(solution)/shard_map/ppermute | solution.py:345
  6.1 16.9 %collective-permute-start.4 = (f32[128,512]{1,0:T(8,128)S(1)}, f32[128,512]{1,0:T(8,128)S(1)}, u32[]{:S(2)}, u32[]{:S(2)}) collective-permute-start(f32[128,512]{1,0:T(8,128)S(1)} %get-tuple-element.29), channel_id=1, source_target_pairs={{0,2},{2,0},{4,6},{6,4},{8,10},{10,8},{12,14},{14,12},{16,18},{18,... | collective-permute-start | bytes 786440 | tf_op jit(solution)/shard_map/ppermute | solution.py:345
  8.1 20.6 %collective-permute-start.6 = (f32[128,512]{1,0:T(8,128)S(1)}, f32[128,512]{1,0:T(8,128)S(1)}, u32[]{:S(2)}, u32[]{:S(2)}) collective-permute-start(f32[128,512]{1,0:T(8,128)S(1)} %get-tuple-element.28), channel_id=1, source_target_pairs={{0,2},{2,0},{4,6},{6,4},{8,10},{10,8},{12,14},{14,12},{16,18},{18,... | collective-permute-start | bytes 786440 | tf_op jit(solution)/shard_map/ppermute | solution.py:345
  8.2 26.1 %collective-permute-start.8 = (f32[128,512]{1,0:T(8,128)S(1)}, f32[128,512]{1,0:T(8,128)S(1)}, u32[]{:S(2)}, u32[]{:S(2)}) collective-permute-start(f32[128,512]{1,0:T(8,128)S(1)} %get-tuple-element.27), channel_id=1, source_target_pairs={{0,2},{2,0},{4,6},{6,4},{8,10},{10,8},{12,14},{14,12},{16,18},{18,... | collective-permute-start | bytes 786440 | tf_op jit(solution)/shard_map/ppermute | solution.py:345
  11.8 40.2 %copy-start.13 = (f32[128,512]{1,0:T(8,128)}, f32[128,512]{1,0:T(8,128)S(1)}, u32[]{:S(2)}) copy-start(f32[128,512]{1,0:T(8,128)S(1)} %collective-permute-done.refs_4_) | copy-start | bytes 786436
  11.8 27.7 %collective-permute-start.9 = (f32[128,512]{1,0:T(8,128)S(1)}, f32[128,512]{1,0:T(8,128)S(1)}, u32[]{:S(2)}, u32[]{:S(2)}) collective-permute-start(f32[128,512]{1,0:T(8,128)S(1)} %get-tuple-element.26), channel_id=1, source_target_pairs={{0,2},{2,0},{4,6},{6,4},{8,10},{10,8},{12,14},{14,12},{16,18},{18,... | collective-permute-start | bytes 786440 | tf_op jit(solution)/shard_map/ppermute | solution.py:345
  17.4 34.6 %copy-start.14 = (f32[128,512]{1,0:T(8,128)}, f32[128,512]{1,0:T(8,128)S(1)}, u32[]{:S(2)}) copy-start(f32[128,512]{1,0:T(8,128)S(1)} %collective-permute-done.2.refs_5_) | copy-start | bytes 786436
  17.4 26.0 %collective-permute-start.1 = (f32[128,512]{1,0:T(8,128)S(1)}, f32[128,512]{1,0:T(8,128)S(1)}, u32[]{:S(2)}, u32[]{:S(2)}) collective-permute-start(f32[128,512]{1,0:T(8,128)S(1)} %collective-permute-done.refs_4_), channel_id=1, source_target_pairs={{0,4},{4,8},{6,2},{8,12},{10,6},{12,16},{14,10},{16,20},{18,14},{2... | collective-permute-start | bytes 786440 | tf_op jit(solution)/shard_map/ppermute | solution.py:355
  23.0 29.0 %copy-start.15 = (f32[128,512]{1,0:T(8,128)}, f32[128,512]{1,0:T(8,128)S(1)}, u32[]{:S(2)}) copy-start(f32[128,512]{1,0:T(8,128)S(1)} %collective-permute-done.4.refs_6_) | copy-start | bytes 786436
  23.0 30.2 %collective-permute-start.3 = (f32[128,512]{1,0:T(8,128)S(1)}, f32[128,512]{1,0:T(8,128)}, u32[]{:S(2)}, u32[]{:S(2)}) collective-permute-start(f32[128,512]{1,0:T(8,128)S(1)} %collective-permute-done.2.refs_5_), channel_id=1, source_target_pairs={{0,4},{4,8},{6,2},{8,12},{10,6},{12,16},{14,10},{16,20},{18,14},{2... | collective-permute-start | bytes 786440 | tf_op jit(solution)/shard_map/ppermute | solution.py:355
  28.7 23.4 %copy-start.17 = (f32[128,512]{1,0:T(8,128)}, f32[128,512]{1,0:T(8,128)S(1)}, u32[]{:S(2)}) copy-start(f32[128,512]{1,0:T(8,128)S(1)} %collective-permute-done.6.refs_7_) | copy-start | bytes 786436
  28.7 24.6 %collective-permute-start.5 = (f32[128,512]{1,0:T(8,128)S(1)}, f32[128,512]{1,0:T(8,128)}, u32[]{:S(2)}, u32[]{:S(2)}) collective-permute-start(f32[128,512]{1,0:T(8,128)S(1)} %collective-permute-done.4.refs_6_), channel_id=1, source_target_pairs={{0,4},{4,8},{6,2},{8,12},{10,6},{12,16},{14,10},{16,20},{18,14},{2... | collective-permute-start | bytes 786440 | tf_op jit(solution)/shard_map/ppermute | solution.py:355
  34.3 17.8 %copy-start.16 = (f32[128,512]{1,0:T(8,128)}, f32[128,512]{1,0:T(8,128)S(1)}, u32[]{:S(2)}) copy-start(f32[128,512]{1,0:T(8,128)S(1)} %collective-permute-done.8.refs_8_) | copy-start | bytes 786436
  34.3 19.0 %collective-permute-start.7 = (f32[128,512]{1,0:T(8,128)S(1)}, f32[128,512]{1,0:T(8,128)}, u32[]{:S(2)}, u32[]{:S(2)}) collective-permute-start(f32[128,512]{1,0:T(8,128)S(1)} %collective-permute-done.6.refs_7_), channel_id=1, source_target_pairs={{0,4},{4,8},{6,2},{8,12},{10,6},{12,16},{14,10},{16,20},{18,14},{2... | collective-permute-start | bytes 786440 | tf_op jit(solution)/shard_map/ppermute | solution.py:355
  39.5 12.5 %copy-start.18 = (f32[128,512]{1,0:T(8,128)}, f32[128,512]{1,0:T(8,128)S(1)}, u32[]{:S(2)}) copy-start(f32[128,512]{1,0:T(8,128)S(1)} %collective-permute-done.9.refs_9_) | copy-start | bytes 786436
  39.5 19.5 %collective-permute-start.10 = (f32[128,512]{1,0:T(8,128)S(1)}, f32[128,512]{1,0:T(8,128)}, u32[]{:S(2)}, u32[]{:S(2)}) collective-permute-start(f32[128,512]{1,0:T(8,128)S(1)} %collective-permute-done.8.refs_8_), channel_id=1, source_target_pairs={{0,4},{4,8},{6,2},{8,12},{10,6},{12,16},{14,10},{16,20},{18,14},{2... | collective-permute-start | bytes 786440 | tf_op jit(solution)/shard_map/ppermute | solution.py:355
  43.4 8.6 %copy-start.19 = (f32[128,512]{1,0:T(8,128)}, f32[128,512]{1,0:T(8,128)S(1)}, u32[]{:S(2)}) copy-start(f32[128,512]{1,0:T(8,128)S(1)} %collective-permute-done.1.refs_0_) | copy-start | bytes 786436
  43.4 15.6 %collective-permute-start.11 = (f32[128,512]{1,0:T(8,128)S(1)}, f32[128,512]{1,0:T(8,128)}, u32[]{:S(2)}, u32[]{:S(2)}) collective-permute-start(f32[128,512]{1,0:T(8,128)S(1)} %collective-permute-done.9.refs_9_), channel_id=1, source_target_pairs={{0,4},{4,8},{6,2},{8,12},{10,6},{12,16},{14,10},{16,20},{18,14},{2... | collective-permute-start | bytes 786440 | tf_op jit(solution)/shard_map/ppermute | solution.py:355
  64.3 2.3 %copy-start.6 = (f32[768,256]{1,0:T(8,128)}, f32[768,256]{1,0:T(8,128)S(1)}, u32[]{:S(2)}) copy-start(f32[768,256]{1,0:T(8,128)S(1)} %get-tuple-element.14.half_ref) | copy-start | bytes 2359300
  64.3 2.3 %collective-permute-start.12 = (f32[768,256]{1,0:T(8,128)S(1)}, f32[768,256]{1,0:T(8,128)S(1)}, u32[]{:S(2)}, u32[]{:S(2)}) collective-permute-start(f32[768,256]{1,0:T(8,128)S(1)} %get-tuple-element.14.half_ref), channel_id=1, source_target_pairs={{0,1},{1,0},{2,3},{3,2},{4,5},{5,4},{6,7},{7,6},{8,9},{9,8},{10,11... | collective-permute-start | bytes 2359304 | tf_op jit(solution)/shard_map/ppermute | solution.py:345
  70.7 24.0 %copy-start.8 = (f32[256,256]{1,0:T(8,128)}, f32[256,256]{1,0:T(8,128)S(1)}, u32[]{:S(2)}) copy-start(f32[256,256]{1,0:T(8,128)S(1)} %get-tuple-element.17.gram_ref) | copy-start | bytes 786436
  70.7 6.4 %collective-permute-start.13 = (f32[256,128]{1,0:T(8,128)S(1)}, f32[256,128]{1,0:T(8,128)S(1)}, u32[]{:S(2)}, u32[]{:S(2)}) collective-permute-start(f32[256,128]{1,0:T(8,128)S(1)} %get-tuple-element.18), channel_id=1, source_target_pairs={{0,2},{2,0},{4,6},{6,4},{8,10},{10,8},{12,14},{14,12},{16,18},{18,... | collective-permute-start | bytes 393224 | tf_op jit(solution)/shard_map/ppermute | solution.py:345
  70.8 13.0 %collective-permute-start.18 = (f32[128,512]{1,0:T(8,128)S(1)}, f32[128,512]{1,0:T(8,128)S(1)}, u32[]{:S(2)}, u32[]{:S(2)}) collective-permute-start(f32[128,512]{1,0:T(8,128)S(1)} %get-tuple-element.22), channel_id=1, source_target_pairs={{0,2},{2,0},{4,6},{6,4},{8,10},{10,8},{12,14},{14,12},{16,18},{18,... | collective-permute-start | bytes 786440 | tf_op jit(solution)/shard_map/ppermute | solution.py:345
  77.2 5.0 %collective-permute-start.14 = (f32[256,128]{1,0:T(8,128)S(1)}, f32[256,128]{1,0:T(8,128)S(1)}, u32[]{:S(2)}, u32[]{:S(2)}) collective-permute-start(f32[256,128]{1,0:T(8,128)S(1)} %add.46), channel_id=1, source_target_pairs={{0,4},{2,6},{4,0},{6,2},{8,12},{10,14},{12,8},{14,10},{16,20},{18,... | collective-permute-start | bytes 393224 | tf_op jit(solution)/shard_map/ppermute | solution.py:345
  82.2 5.0 %collective-permute-start.15 = (f32[256,128]{1,0:T(8,128)S(1)}, f32[256,128]{1,0:T(8,128)S(1)}, u32[]{:S(2)}, u32[]{:S(2)}) collective-permute-start(f32[256,128]{1,0:T(8,128)S(1)} %add.47), channel_id=1, source_target_pairs={{0,8},{2,10},{4,12},{6,14},{8,0},{10,2},{12,4},{14,6},{16,24},{18,... | collective-permute-start | bytes 393224 | tf_op jit(solution)/shard_map/ppermute | solution.py:345
  83.8 19.0 %copy-start.9 = (f32[128,512]{1,0:T(8,128)}, f32[128,512]{1,0:T(8,128)S(1)}, u32[]{:S(2)}) copy-start(f32[128,512]{1,0:T(8,128)S(1)} %add.54.refs_3_) | copy-start | bytes 786436
  87.3 7.3 %collective-permute-start.16 = (f32[256,128]{1,0:T(8,128)S(1)}, f32[256,128]{1,0:T(8,128)S(1)}, u32[]{:S(2)}, u32[]{:S(2)}) collective-permute-start(f32[256,128]{1,0:T(8,128)S(1)} %add.48), channel_id=1, source_target_pairs={{0,16},{2,18},{4,20},{6,22},{8,24},{10,26},{12,28},{14,30},{16,0},... | collective-permute-start | bytes 393224 | tf_op jit(solution)/shard_map/ppermute | solution.py:345
  89.9 5.0 %collective-permute-start.19 = (f32[64,512]{1,0:T(8,128)S(1)}, f32[64,512]{1,0:T(8,128)S(1)}, u32[]{:S(2)}, u32[]{:S(2)}) collective-permute-start(f32[64,512]{1,0:T(8,128)S(1)} %slice_select_fusion), channel_id=1, source_target_pairs={{0,4},{2,6},{4,0},{6,2},{8,12},{10,14},{12,8},{14,10},{16,20},{18,... | collective-permute-start | bytes 393224 | tf_op jit(solution)/shard_map/ppermute | solution.py:345
  94.7 16.4 %copy-start.12 = (f32[4,256,128]{2,1,0:T(8,128)}, f32[4,256,128]{2,1,0:T(8,128)S(1)}, u32[]{:S(2)}) copy-start(f32[4,256,128]{2,1,0:T(8,128)S(1)} %pad_maximum_fusion.mine_ref) | copy-start | bytes 1572868
  94.7 16.3 %collective-permute-start.17 = (f32[4,256,128]{2,1,0:T(8,128)S(1)}, f32[4,256,128]{2,1,0:T(8,128)}, u32[]{:S(2)}, u32[]{:S(2)}) collective-permute-start(f32[4,256,128]{2,1,0:T(8,128)S(1)} %pad_maximum_fusion.mine_ref), channel_id=1, source_target_pairs={{0,1},{1,0},{2,3},{3,2},{4,5},{5,4},{6,7},{7,6},{8,9},{9,8},{10,11... | collective-permute-start | bytes 1572872 | tf_op jit(solution)/shard_map/ppermute | solution.py:345
  95.0 5.8 %collective-permute-start.20 = (f32[64,512]{1,0:T(8,128)S(1)}, f32[64,512]{1,0:T(8,128)S(1)}, u32[]{:S(2)}, u32[]{:S(2)}) collective-permute-start(f32[64,512]{1,0:T(8,128)S(1)} %select_add_fusion), channel_id=1, source_target_pairs={{0,8},{2,10},{4,12},{6,14},{8,0},{10,2},{12,4},{14,6},{16,24},{18,... | collective-permute-start | bytes 393224 | tf_op jit(solution)/shard_map/ppermute | solution.py:345
  100.8 8.6 %collective-permute-start.21 = (f32[64,512]{1,0:T(8,128)S(1)}, f32[64,512]{1,0:T(8,128)S(1)}, u32[]{:S(2)}, u32[]{:S(2)}) collective-permute-start(f32[64,512]{1,0:T(8,128)S(1)} %add.56), channel_id=1, source_target_pairs={{0,16},{2,18},{4,20},{6,22},{8,24},{10,26},{12,28},{14,30},{16,0},... | collective-permute-start | bytes 393224 | tf_op jit(solution)/shard_map/ppermute | solution.py:345
  102.8 25.0 %collective-permute-start.25 = (f32[128,512]{1,0:T(8,128)S(1)}, f32[128,512]{1,0:T(8,128)S(1)}, u32[]{:S(2)}, u32[]{:S(2)}) collective-permute-start(f32[128,512]{1,0:T(8,128)S(1)} %add.54.refs_3_), channel_id=1, source_target_pairs={{0,2},{2,0},{4,6},{6,4},{8,10},{10,8},{12,14},{14,12},{16,18},{18,... | collective-permute-start | bytes 786440 | tf_op jit(solution)/shard_map/ppermute | solution.py:345
  103.9 23.9 %copy-start.10 = (f32[2,64,512]{2,1,0:T(8,128)}, f32[2,64,512]{2,1,0:T(8,128)S(1)}, u32[]{:S(2)}) copy-start(f32[2,64,512]{2,1,0:T(8,128)S(1)} %pad_maximum_fusion.1.refs_5_) | copy-start | bytes 786436
  103.9 25.9 %collective-permute-start.26 = (f32[2,64,512]{2,1,0:T(8,128)S(1)}, f32[2,64,512]{2,1,0:T(8,128)}, u32[]{:S(2)}, u32[]{:S(2)}) collective-permute-start(f32[2,64,512]{2,1,0:T(8,128)S(1)} %pad_maximum_fusion.1.refs_5_), channel_id=1, source_target_pairs={{0,4},{2,6},{4,0},{6,2},{8,12},{10,14},{12,8},{14,10},{16,20},{18,... | collective-permute-start | bytes 786440 | tf_op jit(solution)/shard_map/ppermute | solution.py:345
  105.9 26.8 %collective-permute-start.27 = (f32[2,64,512]{2,1,0:T(8,128)S(1)}, f32[2,64,512]{2,1,0:T(8,128)}, u32[]{:S(2)}, u32[]{:S(2)}) collective-permute-start(f32[2,64,512]{2,1,0:T(8,128)S(1)} %pad_maximum_fusion.1.refs_5_), channel_id=1, source_target_pairs={{0,2},{2,0},{4,6},{6,4},{8,10},{10,8},{12,14},{14,12},{16,18},{18,... | collective-permute-start | bytes 786440 | tf_op jit(solution)/shard_map/ppermute | solution.py:345
  109.4 23.3 %collective-permute-start.28 = (f32[2,64,512]{2,1,0:T(8,128)S(1)}, f32[2,64,512]{2,1,0:T(8,128)}, u32[]{:S(2)}, u32[]{:S(2)}) collective-permute-start(f32[2,64,512]{2,1,0:T(8,128)S(1)} %pad_maximum_fusion.1.refs_5_), channel_id=1, source_target_pairs={{0,6},{2,4},{4,2},{6,0},{8,14},{10,12},{12,10},{14,8},{16,22},{18,... | collective-permute-start | bytes 786440 | tf_op jit(solution)/shard_map/ppermute | solution.py:349
  111.0 18.8 %copy-start.11 = (f32[64,512]{1,0:T(8,128)}, f32[64,512]{1,0:T(8,128)S(1)}, u32[]{:S(2)}) copy-start(f32[64,512]{1,0:T(8,128)S(1)} %add.57.refs_0_) | copy-start | bytes 393220
  111.0 25.0 %collective-permute-start.22 = (f32[64,512]{1,0:T(8,128)S(1)}, f32[64,512]{1,0:T(8,128)}, u32[]{:S(2)}, u32[]{:S(2)}) collective-permute-start(f32[64,512]{1,0:T(8,128)S(1)} %add.57.refs_0_), channel_id=1, source_target_pairs={{0,4},{2,6},{4,0},{6,2},{8,12},{10,14},{12,8},{14,10},{16,20},{18,... | collective-permute-start | bytes 393224 | tf_op jit(solution)/shard_map/ppermute | solution.py:345
  127.7 5.0 %copy-start.3 = (f32[256,256]{1,0:T(8,128)}, f32[256,256]{1,0:T(8,128)S(1)}, u32[]{:S(2)}) copy-start(f32[256,256]{1,0:T(8,128)S(1)} %get-tuple-element.23.refs_0_) | copy-start | bytes 786436
  127.8 5.0 %copy-start.4 = (f32[256,256]{1,0:T(8,128)}, f32[256,256]{1,0:T(8,128)S(1)}, u32[]{:S(2)}) copy-start(f32[256,256]{1,0:T(8,128)S(1)} %get-tuple-element.24.refs_1_) | copy-start | bytes 786436
  127.8 5.0 %copy-start.5 = (f32[256,256]{1,0:T(8,128)}, f32[256,256]{1,0:T(8,128)S(1)}, u32[]{:S(2)}) copy-start(f32[256,256]{1,0:T(8,128)S(1)} %get-tuple-element.25.refs_2_) | copy-start | bytes 786436
  127.8 8.3 %copy-start.2 = (f32[256,256]{1,0:T(8,128)}, f32[256,256]{1,0:T(8,128)S(1)}, u32[]{:S(2)}) copy-start(f32[256,256]{1,0:T(8,128)S(1)} %get-tuple-element.20.inverse_ref) | copy-start | bytes 786436
  127.8 5.0 %copy-start.20 = (f32[128,512]{1,0:T(8,128)}, f32[128,512]{1,0:T(8,128)S(1)}, u32[]{:S(2)}) copy-start(f32[128,512]{1,0:T(8,128)S(1)} %collective-permute-done.25.refs_4_) | copy-start | bytes 786436
  127.8 8.3 %collective-permute-start.23 = (f32[64,512]{1,0:T(8,128)S(1)}, f32[64,512]{1,0:T(8,128)S(1)}, u32[]{:S(2)}, u32[]{:S(2)}) collective-permute-start(f32[64,512]{1,0:T(8,128)S(1)} %add.57.refs_0_), channel_id=1, source_target_pairs={{0,2},{2,0},{4,6},{6,4},{8,10},{10,8},{12,14},{14,12},{16,18},{18,... | collective-permute-start | bytes 393224 | tf_op jit(solution)/shard_map/ppermute | solution.py:345
  129.8 6.9 %collective-permute-start.24 = (f32[64,512]{1,0:T(8,128)S(1)}, f32[64,512]{1,0:T(8,128)S(1)}, u32[]{:S(2)}, u32[]{:S(2)}) collective-permute-start(f32[64,512]{1,0:T(8,128)S(1)} %add.57.refs_0_), channel_id=1, source_target_pairs={{0,6},{2,4},{4,2},{6,0},{8,14},{10,12},{12,10},{14,8},{16,22},{18,... | collective-permute-start | bytes 393224 | tf_op jit(solution)/shard_map/ppermute | solution.py:349
  (6 other events, 5.7 us)

commit v6 on v5

--- a/solution.py
+++ b/solution.py
@@ -152,24 +152,18 @@
     )(core, gram, mine, other)
 
 
-def near_kernel(groups, first_slot, spots, sketched, index_ref, count_ref, blocks_ref, base_ref, *refs):
+def near_kernel(groups, first_slot, spots, sketched, index_ref, count_ref, flag_ref, blocks_ref, base_ref, *refs):
     pieces = refs[:groups]
     sketch_ref = refs[groups] if sketched else None
     rest = refs[groups + sketched :]
-    out_ref = rest[0]
-    ext, sems = rest[-2:]
+    out_ref, ext = rest[0], rest[-1]
     block_count, slot_count, size, _ = blocks_ref.shape
-    copies = []
     at = 0
     for g in range(groups):
         depth = pieces[g].shape[0]
-        copies.append(pltpu.make_async_copy(pieces[g], ext.at[pl.ds(at, depth)], sems.at[g]))
+        ext[at : at + depth, :] = pieces[g][...]
         at += depth
-    for copy in copies:
-        copy.start()
     out_ref[...] = base_ref[...]
-    for copy in copies:
-        copy.wait()
     for b in range(block_count):
         rows = pl.ds(b * size, size)
         for j in range(first_slot, slot_count):
@@ -190,31 +184,27 @@
         rest[1][...] = dot3(out_ref[...], sketch_ref[...], NN)
 
 
-def near_step(blocks, base, pieces, spots, index, count, first_slot, sketch=None):
+def near_step(blocks, base, pieces, spots, index, count, flag, first_slot, sketch=None):
     block_count, slot_count, size, _ = blocks.shape
     rows, width = base.shape
     total = sum(piece.shape[0] for piece in pieces)
     vmem = pl.BlockSpec(memory_space=pltpu.VMEM)
     smem = pl.BlockSpec(memory_space=pltpu.SMEM)
-    hbm = pl.BlockSpec(memory_space=pl.ANY)
     extra = [] if sketch is None else [sketch]
     shapes = [(rows, width)] + [(rows, value.shape[1]) for value in extra]
     return pl.pallas_call(
         functools.partial(near_kernel, len(pieces), first_slot, tuple(spots), len(extra)),
         out_shape=[pltpu.VMEM(shape, jnp.float32) for shape in shapes],
-        in_specs=[smem, smem, vmem, vmem] + [hbm] * len(pieces) + [vmem] * len(extra),
+        in_specs=[smem] * 3 + [vmem] * (2 + len(pieces) + len(extra)),
         out_specs=[vmem] * len(shapes),
-        scratch_shapes=[
-            pltpu.VMEM((total, width), jnp.float32),
-            pltpu.SemaphoreType.DMA((len(pieces),)),
-        ],
+        scratch_shapes=[pltpu.VMEM((total, width), jnp.float32)],
         cost_estimate=pl.CostEstimate(
             flops=6 * block_count * slot_count * size * size * width,
             bytes_accessed=4 * (total * width + 2 * rows * width + blocks.size),
             transcendentals=0,
         ),
         name="near_step",
-    )(index, count, blocks, base, *pieces, *extra)
+    )(index, count, flag, blocks, base, *pieces, *extra)
 
 
 def leaf_kernel(flag_ref, half_ref, other_ref, far_ref, sketch_ref, gram_ref, part_ref, keep_ref, send_ref, product):
@@ -260,41 +250,35 @@
     )(*args)
 
 
-def staged(stage, place_ref, parts):
-    for value, at in parts:
-        depth = value.shape[0]
-        stage[pl.ds(pl.multiple_of(place_ref[at], depth), depth), :] = value
+def staged(stage, flag_ref, mine, other):
+    depth = mine.shape[0]
+    stage[pl.ds(pl.multiple_of(flag_ref[1], depth), depth), :] = mine
+    stage[pl.ds(pl.multiple_of(flag_ref[2], depth), depth), :] = other
     return stage[...]
 
 
-def early_kernel(place_ref, *refs):
+def early_kernel(flag_ref, *refs):
     count = LEVELS - 1
-    inverses, first = refs[:count], refs[count : count + 2]
-    early = refs[count + 2 : count + 6]
-    out_ref, stage, result, sems = refs[count + 6 :]
+    inverses, mine_ref, other_ref = refs[:count], refs[count], refs[count + 1]
+    out_ref, stage, result, sems = refs[count + 2 :]
     copies = []
     for h in range(count):
-        if h == 0:
-            parts = [(first[0][...], 0), (first[1][...], 1)]
-        else:
-            parts = [(early[i][h - 1], 2 + i) for i in range(4)]
-        result[h] = dot3(inverses[h][...], staged(stage.at[h], place_ref, parts), NN)
+        result[h] = dot3(inverses[h][...], staged(stage.at[h], flag_ref, mine_ref[h], other_ref[h]), NN)
         copies.append(pltpu.make_async_copy(result.at[h], out_ref.at[h, 0], sems.at[h]))
         copies[-1].start()
     for copy in copies:
         copy.wait()
 
 
-def reduce_early(place, inverses, first, early):
-    rank, width = inverses[0].shape[0], first[0].shape[1]
+def reduce_early(flag, inverses, mine, other):
+    rank, width = inverses[0].shape[0], mine.shape[2]
     vmem = pl.BlockSpec(memory_space=pltpu.VMEM)
     smem = pl.BlockSpec(memory_space=pltpu.SMEM)
-    args = [*inverses, *first, *early]
     count = LEVELS - 1
     return pl.pallas_call(
         early_kernel,
         out_shape=jax.ShapeDtypeStruct((LEVELS, 1, rank, width), jnp.float32),
-        in_specs=[smem] + [vmem] * len(args),
+        in_specs=[smem] + [vmem] * (count + 2),
         out_specs=pl.BlockSpec(memory_space=pl.ANY),
         scratch_shapes=[
             pltpu.VMEM((count, rank, width), jnp.float32),
@@ -305,63 +289,47 @@
             flops=6 * count * rank * rank * width, bytes_accessed=8 * count * rank * (rank + width), transcendentals=0
         ),
         name="reduce_early",
-    )(place, *args)
-
-
-def last_kernel(place_ref, inverse_ref, *refs):
-    last = refs[:4]
-    out_ref, stage, result, sem = refs[5:]
-    value = staged(stage, place_ref, [(last[i][...], 2 + i) for i in range(4)])
-    result[...] = dot3(inverse_ref[...], value, NN)
+    )(flag, *inverses, mine, other)
+
+
+def last_kernel(flag_ref, inverse_ref, mine_ref, other_ref, kept_ref, out_ref, stage, result, sem):
+    result[...] = dot3(inverse_ref[...], staged(stage, flag_ref, mine_ref[...], other_ref[...]), NN)
     copy = pltpu.make_async_copy(result, out_ref.at[LEVELS - 1, 0], sem)
     copy.start()
     copy.wait()
 
 
-def reduce_last(place, inverse, last, reduced):
-    rank, width = inverse.shape[0], last[0].shape[1]
+def reduce_last(flag, inverse, mine, other, reduced):
+    rank, width = inverse.shape[0], mine.shape[1]
     vmem = pl.BlockSpec(memory_space=pltpu.VMEM)
     smem = pl.BlockSpec(memory_space=pltpu.SMEM)
     hbm = pl.BlockSpec(memory_space=pl.ANY)
     return pl.pallas_call(
         last_kernel,
         out_shape=jax.ShapeDtypeStruct(reduced.shape, jnp.float32),
-        in_specs=[smem] + [vmem] * 5 + [hbm],
+        in_specs=[smem] + [vmem] * 3 + [hbm],
         out_specs=hbm,
         scratch_shapes=[
             pltpu.VMEM((rank, width), jnp.float32),
             pltpu.VMEM((rank, width), jnp.float32),
             pltpu.SemaphoreType.DMA,
         ],
-        input_output_aliases={6: 0},
+        input_output_aliases={4: 0},
         cost_estimate=pl.CostEstimate(
             flops=6 * rank * rank * width, bytes_accessed=8 * rank * (rank + width), transcendentals=0
         ),
         name="reduce_last",
-    )(place, inverse, *last, reduced)
+    )(flag, inverse, mine, other, reduced)
 
 
 def across(value, axis, bit):
     return lax.ppermute(value, axis, [(i, i ^ 1 << bit) for i in range(lax.axis_size(axis))])
-
-
-def diagonal_of(value, axis):
-    return lax.ppermute(value, axis, [(i, i ^ 3) for i in range(lax.axis_size(axis))])
 
 
 def relayed(value, axis):
     count = lax.axis_size(axis)
     steps = [(i, i + 2 if i % 2 == 0 else i - 2) for i in range(count)]
     return lax.ppermute(value, axis, [(i, t) for i, t in steps if 0 <= t < count])
-
-
-def pick(flag, first, second):
-    return jnp.where(flag, second, first)
-
-
-def halves_of(value, bit):
-    half = value.shape[0] // 2
-    return pick(bit, value[:half], value[half:]), pick(bit, value[half:], value[:half])
 
 
 def leaf_and_levels(samples, probes, near_blocks, near_cols, near_count, sketch):
@@ -372,10 +340,10 @@
     position = lax.axis_index("rows")
     bits = [position >> h & 1 for h in range(LEVELS)]
     odd = bits[0] == 1
-    upper = bits[1] == 1
     halves = 2 if lax.axis_size("samp") == 2 else 1
     core = lax.axis_index("samp") % 2
-    core_flag = core.reshape(1).astype(jnp.int32)
+    half = rank // 2
+    flag = jnp.stack([core, bits[0] * half, half - bits[0] * half]).astype(jnp.int32)
 
     index = near_cols - (position * block_count - block_count)
     moved = jnp.where(index < block_count, 2 * block_count, jnp.where(index >= 2 * block_count, -2 * block_count, 0))
@@ -388,17 +356,15 @@
     peer = [across(pieces[i], "rows", 0) for i in range(parts)]
     far = [relayed(peer[i], "rows") for i in range(parts)]
 
-    own = range(block_count, 2 * block_count)
-    (left,) = near_step(near_blocks, samples, [probes], own, index, near_count, 0)
     early = (block_count - 1) * SPLIT
-    spots = [*range(block_count - 1), *range(2 * block_count, 3 * block_count)]
-    (left,) = near_step(near_blocks, left, far[:early] + peer, spots, index, near_count, 1)
-    far_samples, partial = near_step(near_blocks, left, far[early:], [block_count - 1], index, near_count, 1, sketch)
+    spots = [*range(block_count - 1), *range(block_count, 3 * block_count)]
+    (left,) = near_step(near_blocks, samples, far[:early] + [probes] + peer, spots, index, near_count, flag, 0)
+    spots = [block_count - 1]
+    far_samples, partial = near_step(near_blocks, left, far[early:], spots, index, near_count, flag, 1, sketch)
     if halves == 2:
         other = across(partial, "samp", 0)
     else:
         partial, other = lax.psum(partial, "samp"), None
-    flag = jnp.stack([core, bits[0] * (rank // 2), (1 - bits[0]) * (rank // 2)]).astype(jnp.int32)
     leaf_sketch, gram, part, keep, send = leaf_products(flag, partial, other, far_samples)
 
     sums = []
@@ -407,32 +373,19 @@
         sums.append(part)
     sums = jnp.stack(sums)
     sums_other = across(sums, "samp", 0) if halves == 2 else sums
-    leaf_inverse, *inverses = factor_inverse(core_flag, gram, sums, sums_other)
+    leaf_inverse, *inverses = factor_inverse(flag, gram, sums, sums_other)
     leaf_basis = lax.dot_general(leaf_sketch, leaf_inverse, (NT, ((), ())), precision=HIGH)
 
-    first = keep + across(send, "rows", 0)
-    first_other = across(first, "rows", 0)
-    keep, send = halves_of(first, upper)
-    quarter = keep + across(send, "rows", 1)
-    quarters = [quarter]
-    for h in range(2, LEVELS):
-        quarter = quarter + across(quarter, "rows", h)
-        quarters.append(quarter)
-
-    def gathered(value):
-        along = across(value, "rows", 1)
-        beside = across(value, "rows", 0)
-        diagonal = diagonal_of(value, "rows")
-        return [value, along, beside, diagonal]
-
-    early = gathered(jnp.stack(quarters[:-1]))
-    last = gathered(quarters[-1])
-    half = rank // 2
-    x, y = bits[0] * half, bits[1] * (half // 2)
-    fx, fy = half - x, half // 2 - y
-    place = jnp.stack([x, fx, x + y, x + fy, fx + y, fx + fy]).astype(jnp.int32)
-    reduced = reduce_early(place, inverses[:-1], [first, first_other], early)
-    reduced = reduce_last(place, inverses[-1], last, reduced)
+    value = keep + across(send, "rows", 0)
+    values = [value]
+    for h in range(1, LEVELS):
+        value = value + across(value, "rows", h)
+        values.append(value)
+    lower = jnp.stack(values[:-1])
+    lower_other = across(lower, "rows", 0)
+    last_other = across(value, "rows", 0)
+    reduced = reduce_early(flag, inverses[:-1], lower, lower_other)
+    reduced = reduce_last(flag, inverses[-1], value, last_other, reduced)
     return (leaf_basis, reduced)
 
 

time: 140 us -> 136 us (0.971)
  starting transfers between devices: 55.1 us -> 46.5 us
  waiting for transfers between devices: 33.1 us -> 41.5 us
  Pallas kernels: 39.3 us -> 35 us
    ppermute x21 -> x18, waiting for transfers between devices: 32.5 us -> 41.5 us  [across(): lax.ppermute(value, axis, [(i, i ^ 1 << bit) for i in range(lax.axis_size...]
    pallas_call x3 -> x2, Pallas kernels: 13.9 us -> 9.56 us  [near_step(): pl.pallas_call(functools.partial(near_kernel, len(pieces), first_slot, tu...]
    ppermute x21 -> x18, starting transfers between devices: 26.8 us -> 22.6 us  [across(): lax.ppermute(value, axis, [(i, i ^ 1 << bit) for i in range(lax.axis_size...]
    ppermute x2 -> x0, starting transfers between devices: 3.09 us -> none  [diagonal_of(): lax.ppermute(value, axis, [(i, i ^ 3) for i in range(lax.axis_size(axis))])]
    unnamed x50 -> x48, local copies, waits for them, and re-layouts: 5.05 us -> 6.09 us
  transfers between devices with their start and end apart: 29 -> 24, of which waited for: 14 -> 12; matrix products, arithmetic and copies ran while one was open for 4% -> 3% of each run, Pallas kernels for 21% -> 19%
where the time goes in v6:
time: 136 us
  starting transfers between devices  46.5 us (34%)
  waiting for transfers between devices  41.5 us (31%)
  Pallas kernels  35 us (26%)
  local copies, waits for them, and re-layouts  8.43 us (6%)
  other arithmetic  1.54 us (1%)
  matrix products  1.4 us (1%)
    ppermute x18, waiting for transfers between devices, across(): lax.ppermute(value, axis, [(i, i ^ 1 << bit) for i in range(lax.axis_size...  41.5 us
    ppermute x6, starting transfers between devices, relayed(): lax.ppermute(value, axis, [(i, t) for i, t in steps if 0 <= t < count])  23.9 us
    ppermute x18, starting transfers between devices, across(): lax.ppermute(value, axis, [(i, i ^ 1 << bit) for i in range(lax.axis_size...  22.6 us
    pallas_call x1, Pallas kernels, factor_inverse(): pl.pallas_call(functools.partial(inverse_kernel, size), out_shape=[pltpu....  16.6 us
    pallas_call x2, Pallas kernels, near_step(): pl.pallas_call(functools.partial(near_kernel, len(pieces), first_slot, tu...  9.56 us
    unnamed x48, local copies, waits for them, and re-layouts  6.09 us
    pallas_call x1, Pallas kernels, reduce_early(): pl.pallas_call(early_kernel, out_shape=jax.ShapeDtypeStruct((LEVELS, 1, r...  3.3 us
    pallas_call x1, Pallas kernels, leaf_products(): pl.pallas_call(kernel, out_shape=[pltpu.VMEM(shape, jnp.float32) for shap...  3.21 us
  transfers between devices with their start and end apart: 24, of which 12 were waited for; matrix products, arithmetic and copies ran while one was open for 3% of the time, Pallas kernels for 19%

profile of v6, /device:TPU:0, one launch (start us, length us, event | category | flops | bytes accessed | tf_op | source)
XLA Modules:
  0.0 135.6 jit_solution(9049697831223804525)
XLA Ops:
  0.6 1.0 slice.18
  1.6 3.0 %collective-permute-start = (f32[128,512]{1,0:T(8,128)S(1)}, f32[128,512]{1,0:T(8,128)S(1)}, u32[]{:S(2)}, u32[]{:S(2)}) collective-permute-start(f32[128,512]{1,0:T(8,128)S(1)} %slice.18), channel_id=1, source_target_pairs={{0,2},{2,0},{4,6},{6,4},{8,10},{10,8},{12,14},{14,12},{16,18},{18,... | collective-permute-start | bytes 786440 | tf_op jit(solution)/shard_map/ppermute | solution.py:326
  4.6 1.4 %fusion = (f32[128,512]{1,0:T(8,128)S(1)}, f32[128,512]{1,0:T(8,128)S(1)}, f32[128,512]{1,0:T(8,128)S(1)}, f32[128,512]{1,0:T(8,128)S(1)}, f32[128,512]{1,0:T(8,128)S(1)}) fusion(f32[768,512]{1,0:T(8,128)} %refs_4_.1), kind=kLoop, calls=%fused_computation.5 | loop fusion | bytes 2621440 | tf_op jit(solution)/shard_map/slice | solution.py:355
  6.1 2.0 %collective-permute-start.6 = (f32[128,512]{1,0:T(8,128)S(1)}, f32[128,512]{1,0:T(8,128)S(1)}, u32[]{:S(2)}, u32[]{:S(2)}) collective-permute-start(f32[128,512]{1,0:T(8,128)S(1)} %get-tuple-element.28), channel_id=1, source_target_pairs={{0,2},{2,0},{4,6},{6,4},{8,10},{10,8},{12,14},{14,12},{16,18},{18,... | collective-permute-start | bytes 786440 | tf_op jit(solution)/shard_map/ppermute | solution.py:326
  8.2 1.9 %collective-permute-start.2 = (f32[128,512]{1,0:T(8,128)S(1)}, f32[128,512]{1,0:T(8,128)S(1)}, u32[]{:S(2)}, u32[]{:S(2)}) collective-permute-start(f32[128,512]{1,0:T(8,128)S(1)} %get-tuple-element.30), channel_id=1, source_target_pairs={{0,2},{2,0},{4,6},{6,4},{8,10},{10,8},{12,14},{14,12},{16,18},{18,... | collective-permute-start | bytes 786440 | tf_op jit(solution)/shard_map/ppermute | solution.py:326
  10.1 1.7 %collective-permute-done.refs_5_ = f32[128,512]{1,0:T(8,128)S(1)} collective-permute-done((f32[128,512]{1,0:T(8,128)S(1)}, f32[128,512]{1,0:T(8,128)S(1)}, u32[]{:S(2)}, u32[]{:S(2)}) %collective-permute-start) | collective-permute-done | bytes 262176 | tf_op jit(solution)/shard_map/ppermute | solution.py:326
  11.8 2.0 %collective-permute-start.8 = (f32[128,512]{1,0:T(8,128)S(1)}, f32[128,512]{1,0:T(8,128)S(1)}, u32[]{:S(2)}, u32[]{:S(2)}) collective-permute-start(f32[128,512]{1,0:T(8,128)S(1)} %get-tuple-element.27), channel_id=1, source_target_pairs={{0,2},{2,0},{4,6},{6,4},{8,10},{10,8},{12,14},{14,12},{16,18},{18,... | collective-permute-start | bytes 786440 | tf_op jit(solution)/shard_map/ppermute | solution.py:326
  13.8 3.6 %collective-permute-done.9.refs_10_ = f32[128,512]{1,0:T(8,128)S(1)} collective-permute-done((f32[128,512]{1,0:T(8,128)S(1)}, f32[128,512]{1,0:T(8,128)S(1)}, u32[]{:S(2)}, u32[]{:S(2)}) %collective-permute-start.9) | collective-permute-done | bytes 262176 | tf_op jit(solution)/shard_map/ppermute | solution.py:326
  17.4 4.0 %collective-permute-start.1 = (f32[128,512]{1,0:T(8,128)S(1)}, f32[128,512]{1,0:T(8,128)S(1)}, u32[]{:S(2)}, u32[]{:S(2)}) collective-permute-start(f32[128,512]{1,0:T(8,128)S(1)} %collective-permute-done.refs_5_), channel_id=1, source_target_pairs={{0,4},{4,8},{6,2},{8,12},{10,6},{12,16},{14,10},{16,20},{18,14},{2... | collective-permute-start | bytes 786440 | tf_op jit(solution)/shard_map/ppermute | solution.py:332
  21.4 1.6 %collective-permute-done.6.refs_8_ = f32[128,512]{1,0:T(8,128)S(1)} collective-permute-done((f32[128,512]{1,0:T(8,128)S(1)}, f32[128,512]{1,0:T(8,128)S(1)}, u32[]{:S(2)}, u32[]{:S(2)}) %collective-permute-start.6) | collective-permute-done | bytes 262176 | tf_op jit(solution)/shard_map/ppermute | solution.py:326
  23.0 4.0 %collective-permute-start.7 = (f32[128,512]{1,0:T(8,128)S(1)}, f32[128,512]{1,0:T(8,128)S(1)}, u32[]{:S(2)}, u32[]{:S(2)}) collective-permute-start(f32[128,512]{1,0:T(8,128)S(1)} %collective-permute-done.6.refs_8_), channel_id=1, source_target_pairs={{0,4},{4,8},{6,2},{8,12},{10,6},{12,16},{14,10},{16,20},{18,14},{2... | collective-permute-start | bytes 786440 | tf_op jit(solution)/shard_map/ppermute | solution.py:332
  27.0 1.7 %collective-permute-done.4.refs_7_ = f32[128,512]{1,0:T(8,128)S(1)} collective-permute-done((f32[128,512]{1,0:T(8,128)S(1)}, f32[128,512]{1,0:T(8,128)S(1)}, u32[]{:S(2)}, u32[]{:S(2)}) %collective-permute-start.4) | collective-permute-done | bytes 262176 | tf_op jit(solution)/shard_map/ppermute | solution.py:326
  28.7 4.0 %collective-permute-start.5 = (f32[128,512]{1,0:T(8,128)S(1)}, f32[128,512]{1,0:T(8,128)S(1)}, u32[]{:S(2)}, u32[]{:S(2)}) collective-permute-start(f32[128,512]{1,0:T(8,128)S(1)} %collective-permute-done.4.refs_7_), channel_id=1, source_target_pairs={{0,4},{4,8},{6,2},{8,12},{10,6},{12,16},{14,10},{16,20},{18,14},{2... | collective-permute-start | bytes 786440 | tf_op jit(solution)/shard_map/ppermute | solution.py:332
  32.6 1.7 %collective-permute-done.2.refs_6_ = f32[128,512]{1,0:T(8,128)S(1)} collective-permute-done((f32[128,512]{1,0:T(8,128)S(1)}, f32[128,512]{1,0:T(8,128)S(1)}, u32[]{:S(2)}, u32[]{:S(2)}) %collective-permute-start.2) | collective-permute-done | bytes 262176 | tf_op jit(solution)/shard_map/ppermute | solution.py:326
  34.3 4.7 %collective-permute-start.3 = (f32[128,512]{1,0:T(8,128)S(1)}, f32[128,512]{1,0:T(8,128)}, u32[]{:S(2)}, u32[]{:S(2)}) collective-permute-start(f32[128,512]{1,0:T(8,128)S(1)} %collective-permute-done.2.refs_6_), channel_id=1, source_target_pairs={{0,4},{4,8},{6,2},{8,12},{10,6},{12,16},{14,10},{16,20},{18,14},{2... | collective-permute-start | bytes 786440 | tf_op jit(solution)/shard_map/ppermute | solution.py:332
  38.9 0.6 select_add_fusion.index_ref
  39.5 3.9 %collective-permute-start.11 = (f32[128,512]{1,0:T(8,128)S(1)}, f32[128,512]{1,0:T(8,128)}, u32[]{:S(2)}, u32[]{:S(2)}) collective-permute-start(f32[128,512]{1,0:T(8,128)S(1)} %collective-permute-done.9.refs_10_), channel_id=1, source_target_pairs={{0,4},{4,8},{6,2},{8,12},{10,6},{12,16},{14,10},{16,20},{18,14},{2... | collective-permute-start | bytes 786440 | tf_op jit(solution)/shard_map/ppermute | solution.py:332
  43.4 3.5 %collective-permute-start.10 = (f32[128,512]{1,0:T(8,128)S(1)}, f32[128,512]{1,0:T(8,128)}, u32[]{:S(2)}, u32[]{:S(2)}) collective-permute-start(f32[128,512]{1,0:T(8,128)S(1)} %collective-permute-done.8.refs_9_), channel_id=1, source_target_pairs={{0,4},{4,8},{6,2},{8,12},{10,6},{12,16},{14,10},{16,20},{18,14},{2... | collective-permute-start | bytes 786440 | tf_op jit(solution)/shard_map/ppermute | solution.py:332
  46.9 0.7 pad_add_fusion.flag_ref.core_ref
  47.6 0.7 copy-done.18
  48.2 0.7 copy-done.19
  49.0 6.0 %near_step.2.base_ref = f32[768,512]{1,0:T(8,128)S(1)} custom-call(s32[3,3]{1,0:T(4,128)} %select_add_fusion.index_ref, s32[3]{0:T(128)} %count_ref.3, s32[3]{0:T(128)} %pad_add_fusion.flag_ref.core_ref, f32[3,3,256,256]{3,2,1,0:T(8,128)} %blocks_ref.3, f32[768,512]{1,0:T(8,128)} %base_ref.1, f32[128,512]{1,0:T(8,128)} %copy-done.17, ...), custom_call_target="tpu_custom_call" | custom-call | flops 1811939328 | bytes 9699328 | tf_op jit(solution)/shard_map/near_step/pallas_call | solution.py:195
  55.0 1.1 copy-done
  56.2 3.5 %near_step.3 = (f32[768,512]{1,0:T(8,128)S(1)}, f32[768,256]{1,0:T(8,128)S(1)}) custom-call(s32[3,3]{1,0:T(4,128)} %select_add_fusion.index_ref, s32[3]{0:T(128)} %count_ref.3, s32[3]{0:T(128)} %pad_add_fusion.flag_ref.core_ref, f32[3,3,256,256]{3,2,1,0:T(8,128)} %blocks_ref.3, f32[768,512]{1,0:T(8,128)} %copy-done, ...), custom_call_target="tpu_custom_call" | custom-call | flops 1811939328 | bytes 6029312 | tf_op jit(solution)/shard_map/near_step/pallas_call | solution.py:195
  59.7 1.1 copy-done.6
  60.9 2.3 %collective-permute-done.12.other_ref = f32[768,256]{1,0:T(8,128)S(1)} collective-permute-done((f32[768,256]{1,0:T(8,128)S(1)}, f32[768,256]{1,0:T(8,128)S(1)}, u32[]{:S(2)}, u32[]{:S(2)}) %collective-permute-start.12) | collective-permute-done | bytes 786464 | tf_op jit(solution)/shard_map/ppermute | solution.py:326
  63.2 0.9 copy-done.22
  64.0 3.2 %leaf_products.1 = (f32[768,256]{1,0:T(8,128)S(1)}, f32[256,256]{1,0:T(8,128)S(1)}, f32[256,128]{1,0:T(8,128)S(1)}, f32[128,512]{1,0:T(8,128)S(1)}, f32[128,512]{1,0:T(8,128)S(1)}) custom-call(s32[3]{0:T(128)} %pad_add_fusion.flag_ref.core_ref, f32[768,256]{1,0:T(8,128)} %copy-done.5, f32[768,256]{1,0:T(8,128)} %copy-done.22, f32[768,512]{1,0:T(8,128)} %copy-done.6), custom_call_target="tpu_custom_call" | custom-call | flops 905969664 | bytes 3932160 | tf_op jit(solution)/shard_map/leaf_products/pallas_call | solution.py:240
  67.4 2.0 %collective-permute-start.18 = (f32[128,512]{1,0:T(8,128)S(1)}, f32[128,512]{1,0:T(8,128)S(1)}, u32[]{:S(2)}, u32[]{:S(2)}) collective-permute-start(f32[128,512]{1,0:T(8,128)S(1)} %get-tuple-element.22), channel_id=1, source_target_pairs={{0,2},{2,0},{4,6},{6,4},{8,10},{10,8},{12,14},{14,12},{16,18},{18,... | collective-permute-start | bytes 786440 | tf_op jit(solution)/shard_map/ppermute | solution.py:326
  69.4 4.3 %collective-permute-done.13 = f32[256,128]{1,0:T(8,128)S(1)} collective-permute-done((f32[256,128]{1,0:T(8,128)S(1)}, f32[256,128]{1,0:T(8,128)S(1)}, u32[]{:S(2)}, u32[]{:S(2)}) %collective-permute-start.13) | collective-permute-done | bytes 131104 | tf_op jit(solution)/shard_map/ppermute | solution.py:326
  73.7 1.2 collective-permute-start.14
  75.0 3.8 %collective-permute-done.14 = f32[256,128]{1,0:T(8,128)S(1)} collective-permute-done((f32[256,128]{1,0:T(8,128)S(1)}, f32[256,128]{1,0:T(8,128)S(1)}, u32[]{:S(2)}, u32[]{:S(2)}) %collective-permute-start.14) | collective-permute-done | bytes 131104 | tf_op jit(solution)/shard_map/ppermute | solution.py:326
  78.8 1.2 collective-permute-start.19
  80.1 1.6 %collective-permute-start.15 = (f32[256,128]{1,0:T(8,128)S(1)}, f32[256,128]{1,0:T(8,128)S(1)}, u32[]{:S(2)}, u32[]{:S(2)}) collective-permute-start(f32[256,128]{1,0:T(8,128)S(1)} %add.35), channel_id=1, source_target_pairs={{0,8},{2,10},{4,12},{6,14},{8,0},{10,2},{12,4},{14,6},{16,24},{18,... | collective-permute-start | bytes 393224 | tf_op jit(solution)/shard_map/ppermute | solution.py:326
  81.7 3.4 %collective-permute-done.15 = f32[256,128]{1,0:T(8,128)S(1)} collective-permute-done((f32[256,128]{1,0:T(8,128)S(1)}, f32[256,128]{1,0:T(8,128)S(1)}, u32[]{:S(2)}, u32[]{:S(2)}) %collective-permute-start.15) | collective-permute-done | bytes 131104 | tf_op jit(solution)/shard_map/ppermute | solution.py:326
  85.1 2.7 %collective-permute-start.16 = (f32[256,128]{1,0:T(8,128)S(1)}, f32[256,128]{1,0:T(8,128)S(1)}, u32[]{:S(2)}, u32[]{:S(2)}) collective-permute-start(f32[256,128]{1,0:T(8,128)S(1)} %add.36), channel_id=1, source_target_pairs={{0,16},{2,18},{4,20},{6,22},{8,24},{10,26},{12,28},{14,30},{16,0},... | collective-permute-start | bytes 393224 | tf_op jit(solution)/shard_map/ppermute | solution.py:326
  88.3 3.1 %collective-permute-done.16 = f32[256,128]{1,0:T(8,128)S(1)} collective-permute-done((f32[256,128]{1,0:T(8,128)S(1)}, f32[256,128]{1,0:T(8,128)S(1)}, u32[]{:S(2)}, u32[]{:S(2)}) %collective-permute-start.16) | collective-permute-done | bytes 131104 | tf_op jit(solution)/shard_map/ppermute | solution.py:326
  91.6 3.7 %collective-permute-done.20 = f32[128,512]{1,0:T(8,128)S(1)} collective-permute-done((f32[128,512]{1,0:T(8,128)S(1)}, f32[128,512]{1,0:T(8,128)S(1)}, u32[]{:S(2)}, u32[]{:S(2)}) %collective-permute-start.20) | collective-permute-done | bytes 262176 | tf_op jit(solution)/shard_map/ppermute | solution.py:326
  95.3 1.3 collective-permute-start.21
  96.7 1.1 collective-permute-start.23
  97.8 10.7 %collective-permute-done.21 = f32[128,512]{1,0:T(8,128)S(1)} collective-permute-done((f32[128,512]{1,0:T(8,128)S(1)}, f32[128,512]{1,0:T(8,128)S(1)}, u32[]{:S(2)}, u32[]{:S(2)}) %collective-permute-start.21) | collective-permute-done | bytes 262176 | tf_op jit(solution)/shard_map/ppermute | solution.py:326
  108.5 1.6 %collective-permute-start.22 = (f32[128,512]{1,0:T(8,128)S(1)}, f32[128,512]{1,0:T(8,128)S(1)}, u32[]{:S(2)}, u32[]{:S(2)}) collective-permute-start(f32[128,512]{1,0:T(8,128)S(1)} %add.41.mine_ref), channel_id=1, source_target_pairs={{0,2},{2,0},{4,6},{6,4},{8,10},{10,8},{12,14},{14,12},{16,18},{18,... | collective-permute-start | bytes 786440 | tf_op jit(solution)/shard_map/ppermute | solution.py:326
  110.1 0.8 copy-done.23
  110.9 16.6 %factor_inverse.1 = (f32[256,256]{1,0:T(8,128)S(1)}, f32[256,256]{1,0:T(8,128)S(1)}, f32[256,256]{1,0:T(8,128)S(1)}, f32[256,256]{1,0:T(8,128)S(1)}, f32[256,256]{1,0:T(8,128)S(1)}) custom-call(s32[3]{0:T(128)} %pad_add_fusion.flag_ref.core_ref, f32[256,256]{1,0:T(8,128)} %copy-done.7, f32[4,256,128]{2,1,0:T(8,128)} %copy-done.10, f32[4,256,128]{2,1,0:T(8,128)} %copy-done.23), custom_call_target="tpu_custom_call" | custom-call | flops 15000000512 | bytes 2621440 | tf_op jit(solution)/shard_map/factor_inverse/pallas_call | solution.py:144
  127.6 1.4 %fusion.1 = f32[768,256]{1,0:T(8,128)} fusion(f32[768,256]{1,0:T(8,128)S(1)} %get-tuple-element.16, f32[256,256]{1,0:T(8,128)S(1)} %get-tuple-element.19), kind=kOutput, calls=%fused_computation.6 | convolution fusion | flops 301989888 | bytes 1835008 | tf_op jit(solution)/shard_map/dot_general | solution.py:377
  129.0 3.3 %reduce_early.1.kept_ref = f32[4,1,256,512]{3,2,1,0:T(8,128)} custom-call(s32[3]{0:T(128)} %pad_add_fusion.flag_ref.core_ref, f32[256,256]{1,0:T(8,128)} %copy-done.2, f32[256,256]{1,0:T(8,128)} %copy-done.3, f32[256,256]{1,0:T(8,128)} %copy-done.4, f32[3,128,512]{2,1,0:T(8,128)} %copy-done.8, f32[3,128,512]{2,1,0:T(8,128)} %collective-permute-done.23.refs_4_), custom_call_target="tpu_custom_call" | custom-call | flops 603979776 | bytes 4718592 | tf_op jit(solution)/shard_map/reduce_early/pallas_call | solution.py:278
  132.4 0.7 copy-done.20
  133.1 2.3 %reduce_last.1 = f32[4,1,256,512]{3,2,1,0:T(8,128)} custom-call(s32[3]{0:T(128)} %pad_add_fusion.flag_ref.core_ref, f32[256,256]{1,0:T(8,128)} %copy-done.1, f32[128,512]{1,0:T(8,128)} %copy-done.9, f32[128,512]{1,0:T(8,128)} %copy-done.20, f32[4,1,256,512]{3,2,1,0:T(8,128)} %reduce_early.1.kept_ref), custom_call_target="tpu_custom_call", output_to_operand_aliasing={{}: (4, {})} | custom-call | flops 201326592 | bytes 1572864 | tf_op jit(solution)/shard_map/reduce_last/pallas_call | solution.py:307
  (69 shorter events, 1.3 us)
Async XLA Ops:
  0.6 38.3 %copy-start.21 = (s32[3,3]{1,0:T(4,128)S(1)}, s32[3,3]{1,0:T(4,128)}, u32[]{:S(2)}) copy-start(s32[3,3]{1,0:T(4,128)} %param.9) | copy-start | bytes 112
  1.6 10.2 %collective-permute-start = (f32[128,512]{1,0:T(8,128)S(1)}, f32[128,512]{1,0:T(8,128)S(1)}, u32[]{:S(2)}, u32[]{:S(2)}) collective-permute-start(f32[128,512]{1,0:T(8,128)S(1)} %slice.18), channel_id=1, source_target_pairs={{0,2},{2,0},{4,6},{6,4},{8,10},{10,8},{12,14},{14,12},{16,18},{18,... | collective-permute-start | bytes 786440 | tf_op jit(solution)/shard_map/ppermute | solution.py:326
  6.0 11.4 %collective-permute-start.9 = (f32[128,512]{1,0:T(8,128)S(1)}, f32[128,512]{1,0:T(8,128)S(1)}, u32[]{:S(2)}, u32[]{:S(2)}) collective-permute-start(f32[128,512]{1,0:T(8,128)S(1)} %get-tuple-element.26), channel_id=1, source_target_pairs={{0,2},{2,0},{4,6},{6,4},{8,10},{10,8},{12,14},{14,12},{16,18},{18,... | collective-permute-start | bytes 786440 | tf_op jit(solution)/shard_map/ppermute | solution.py:326
  6.1 16.9 %collective-permute-start.6 = (f32[128,512]{1,0:T(8,128)S(1)}, f32[128,512]{1,0:T(8,128)S(1)}, u32[]{:S(2)}, u32[]{:S(2)}) collective-permute-start(f32[128,512]{1,0:T(8,128)S(1)} %get-tuple-element.28), channel_id=1, source_target_pairs={{0,2},{2,0},{4,6},{6,4},{8,10},{10,8},{12,14},{14,12},{16,18},{18,... | collective-permute-start | bytes 786440 | tf_op jit(solution)/shard_map/ppermute | solution.py:326
  8.1 20.6 %collective-permute-start.4 = (f32[128,512]{1,0:T(8,128)S(1)}, f32[128,512]{1,0:T(8,128)S(1)}, u32[]{:S(2)}, u32[]{:S(2)}) collective-permute-start(f32[128,512]{1,0:T(8,128)S(1)} %get-tuple-element.29), channel_id=1, source_target_pairs={{0,2},{2,0},{4,6},{6,4},{8,10},{10,8},{12,14},{14,12},{16,18},{18,... | collective-permute-start | bytes 786440 | tf_op jit(solution)/shard_map/ppermute | solution.py:326
  8.2 26.1 %collective-permute-start.2 = (f32[128,512]{1,0:T(8,128)S(1)}, f32[128,512]{1,0:T(8,128)S(1)}, u32[]{:S(2)}, u32[]{:S(2)}) collective-permute-start(f32[128,512]{1,0:T(8,128)S(1)} %get-tuple-element.30), channel_id=1, source_target_pairs={{0,2},{2,0},{4,6},{6,4},{8,10},{10,8},{12,14},{14,12},{16,18},{18,... | collective-permute-start | bytes 786440 | tf_op jit(solution)/shard_map/ppermute | solution.py:326
  11.8 37.1 %copy-start.11 = (f32[128,512]{1,0:T(8,128)}, f32[128,512]{1,0:T(8,128)S(1)}, u32[]{:S(2)}) copy-start(f32[128,512]{1,0:T(8,128)S(1)} %collective-permute-done.refs_5_) | copy-start | bytes 786436
  11.8 27.7 %collective-permute-start.8 = (f32[128,512]{1,0:T(8,128)S(1)}, f32[128,512]{1,0:T(8,128)S(1)}, u32[]{:S(2)}, u32[]{:S(2)}) collective-permute-start(f32[128,512]{1,0:T(8,128)S(1)} %get-tuple-element.27), channel_id=1, source_target_pairs={{0,2},{2,0},{4,6},{6,4},{8,10},{10,8},{12,14},{14,12},{16,18},{18,... | collective-permute-start | bytes 786440 | tf_op jit(solution)/shard_map/ppermute | solution.py:326
  17.4 31.5 %copy-start.12 = (f32[128,512]{1,0:T(8,128)}, f32[128,512]{1,0:T(8,128)S(1)}, u32[]{:S(2)}) copy-start(f32[128,512]{1,0:T(8,128)S(1)} %collective-permute-done.9.refs_10_) | copy-start | bytes 786436
  17.4 26.0 %collective-permute-start.1 = (f32[128,512]{1,0:T(8,128)S(1)}, f32[128,512]{1,0:T(8,128)S(1)}, u32[]{:S(2)}, u32[]{:S(2)}) collective-permute-start(f32[128,512]{1,0:T(8,128)S(1)} %collective-permute-done.refs_5_), channel_id=1, source_target_pairs={{0,4},{4,8},{6,2},{8,12},{10,6},{12,16},{14,10},{16,20},{18,14},{2... | collective-permute-start | bytes 786440 | tf_op jit(solution)/shard_map/ppermute | solution.py:332
  23.0 25.9 %copy-start.13 = (f32[128,512]{1,0:T(8,128)}, f32[128,512]{1,0:T(8,128)S(1)}, u32[]{:S(2)}) copy-start(f32[128,512]{1,0:T(8,128)S(1)} %collective-permute-done.6.refs_8_) | copy-start | bytes 786436
  23.0 24.5 %collective-permute-start.7 = (f32[128,512]{1,0:T(8,128)S(1)}, f32[128,512]{1,0:T(8,128)S(1)}, u32[]{:S(2)}, u32[]{:S(2)}) collective-permute-start(f32[128,512]{1,0:T(8,128)S(1)} %collective-permute-done.6.refs_8_), channel_id=1, source_target_pairs={{0,4},{4,8},{6,2},{8,12},{10,6},{12,16},{14,10},{16,20},{18,14},{2... | collective-permute-start | bytes 786440 | tf_op jit(solution)/shard_map/ppermute | solution.py:332
  28.7 20.3 %copy-start.14 = (f32[128,512]{1,0:T(8,128)}, f32[128,512]{1,0:T(8,128)S(1)}, u32[]{:S(2)}) copy-start(f32[128,512]{1,0:T(8,128)S(1)} %collective-permute-done.4.refs_7_) | copy-start | bytes 786436
  28.7 18.9 %collective-permute-start.5 = (f32[128,512]{1,0:T(8,128)S(1)}, f32[128,512]{1,0:T(8,128)S(1)}, u32[]{:S(2)}, u32[]{:S(2)}) collective-permute-start(f32[128,512]{1,0:T(8,128)S(1)} %collective-permute-done.4.refs_7_), channel_id=1, source_target_pairs={{0,4},{4,8},{6,2},{8,12},{10,6},{12,16},{14,10},{16,20},{18,14},{2... | collective-permute-start | bytes 786440 | tf_op jit(solution)/shard_map/ppermute | solution.py:332
  34.3 14.7 %copy-start.15 = (f32[128,512]{1,0:T(8,128)}, f32[128,512]{1,0:T(8,128)S(1)}, u32[]{:S(2)}) copy-start(f32[128,512]{1,0:T(8,128)S(1)} %collective-permute-done.2.refs_6_) | copy-start | bytes 786436
  34.3 14.7 %collective-permute-start.3 = (f32[128,512]{1,0:T(8,128)S(1)}, f32[128,512]{1,0:T(8,128)}, u32[]{:S(2)}, u32[]{:S(2)}) collective-permute-start(f32[128,512]{1,0:T(8,128)S(1)} %collective-permute-done.2.refs_6_), channel_id=1, source_target_pairs={{0,4},{4,8},{6,2},{8,12},{10,6},{12,16},{14,10},{16,20},{18,14},{2... | collective-permute-start | bytes 786440 | tf_op jit(solution)/shard_map/ppermute | solution.py:332
  39.5 9.5 %copy-start.16 = (f32[128,512]{1,0:T(8,128)}, f32[128,512]{1,0:T(8,128)S(1)}, u32[]{:S(2)}) copy-start(f32[128,512]{1,0:T(8,128)S(1)} %collective-permute-done.8.refs_9_) | copy-start | bytes 786436
  39.5 16.6 %collective-permute-start.11 = (f32[128,512]{1,0:T(8,128)S(1)}, f32[128,512]{1,0:T(8,128)}, u32[]{:S(2)}, u32[]{:S(2)}) collective-permute-start(f32[128,512]{1,0:T(8,128)S(1)} %collective-permute-done.9.refs_10_), channel_id=1, source_target_pairs={{0,4},{4,8},{6,2},{8,12},{10,6},{12,16},{14,10},{16,20},{18,14},{2... | collective-permute-start | bytes 786440 | tf_op jit(solution)/shard_map/ppermute | solution.py:332
  43.4 5.6 %copy-start.17 = (f32[128,512]{1,0:T(8,128)}, f32[128,512]{1,0:T(8,128)S(1)}, u32[]{:S(2)}) copy-start(f32[128,512]{1,0:T(8,128)S(1)} %collective-permute-done.1.refs_0_) | copy-start | bytes 786436
  43.4 12.8 %collective-permute-start.10 = (f32[128,512]{1,0:T(8,128)S(1)}, f32[128,512]{1,0:T(8,128)}, u32[]{:S(2)}, u32[]{:S(2)}) collective-permute-start(f32[128,512]{1,0:T(8,128)S(1)} %collective-permute-done.8.refs_9_), channel_id=1, source_target_pairs={{0,4},{4,8},{6,2},{8,12},{10,6},{12,16},{14,10},{16,20},{18,14},{2... | collective-permute-start | bytes 786440 | tf_op jit(solution)/shard_map/ppermute | solution.py:332
  47.5 0.7 copy-start.18
  48.2 0.7 copy-start.19
  55.0 1.1 copy-start
  59.7 1.1 copy-start.6
  60.9 2.3 %copy-start.5 = (f32[768,256]{1,0:T(8,128)}, f32[768,256]{1,0:T(8,128)S(1)}, u32[]{:S(2)}) copy-start(f32[768,256]{1,0:T(8,128)S(1)} %get-tuple-element.14.half_ref) | copy-start | bytes 2359300
  60.9 2.3 %collective-permute-start.12 = (f32[768,256]{1,0:T(8,128)S(1)}, f32[768,256]{1,0:T(8,128)S(1)}, u32[]{:S(2)}, u32[]{:S(2)}) collective-permute-start(f32[768,256]{1,0:T(8,128)S(1)} %get-tuple-element.14.half_ref), channel_id=1, source_target_pairs={{0,1},{1,0},{2,3},{3,2},{4,5},{5,4},{6,7},{7,6},{8,9},{9,8},{10,11... | collective-permute-start | bytes 2359304 | tf_op jit(solution)/shard_map/ppermute | solution.py:326
  63.2 0.9 copy-start.22
  67.3 24.2 %copy-start.7 = (f32[256,256]{1,0:T(8,128)}, f32[256,256]{1,0:T(8,128)S(1)}, u32[]{:S(2)}) copy-start(f32[256,256]{1,0:T(8,128)S(1)} %get-tuple-element.17.gram_ref) | copy-start | bytes 786436
  67.3 6.4 %collective-permute-start.13 = (f32[256,128]{1,0:T(8,128)S(1)}, f32[256,128]{1,0:T(8,128)S(1)}, u32[]{:S(2)}, u32[]{:S(2)}) collective-permute-start(f32[256,128]{1,0:T(8,128)S(1)} %get-tuple-element.18), channel_id=1, source_target_pairs={{0,2},{2,0},{4,6},{6,4},{8,10},{10,8},{12,14},{14,12},{16,18},{18,... | collective-permute-start | bytes 393224 | tf_op jit(solution)/shard_map/ppermute | solution.py:326
  67.4 11.4 %collective-permute-start.18 = (f32[128,512]{1,0:T(8,128)S(1)}, f32[128,512]{1,0:T(8,128)S(1)}, u32[]{:S(2)}, u32[]{:S(2)}) collective-permute-start(f32[128,512]{1,0:T(8,128)S(1)} %get-tuple-element.22), channel_id=1, source_target_pairs={{0,2},{2,0},{4,6},{6,4},{8,10},{10,8},{12,14},{14,12},{16,18},{18,... | collective-permute-start | bytes 786440 | tf_op jit(solution)/shard_map/ppermute | solution.py:326
  73.7 5.0 %collective-permute-start.14 = (f32[256,128]{1,0:T(8,128)S(1)}, f32[256,128]{1,0:T(8,128)S(1)}, u32[]{:S(2)}, u32[]{:S(2)}) collective-permute-start(f32[256,128]{1,0:T(8,128)S(1)} %add.34), channel_id=1, source_target_pairs={{0,4},{2,6},{4,0},{6,2},{8,12},{10,14},{12,8},{14,10},{16,20},{18,... | collective-permute-start | bytes 393224 | tf_op jit(solution)/shard_map/ppermute | solution.py:326
  78.8 8.9 %collective-permute-start.19 = (f32[128,512]{1,0:T(8,128)S(1)}, f32[128,512]{1,0:T(8,128)S(1)}, u32[]{:S(2)}, u32[]{:S(2)}) collective-permute-start(f32[128,512]{1,0:T(8,128)S(1)} %add.38), channel_id=1, source_target_pairs={{0,4},{2,6},{4,0},{6,2},{8,12},{10,14},{12,8},{14,10},{16,20},{18,... | collective-permute-start | bytes 786440 | tf_op jit(solution)/shard_map/ppermute | solution.py:326
  80.1 5.0 %collective-permute-start.15 = (f32[256,128]{1,0:T(8,128)S(1)}, f32[256,128]{1,0:T(8,128)S(1)}, u32[]{:S(2)}, u32[]{:S(2)}) collective-permute-start(f32[256,128]{1,0:T(8,128)S(1)} %add.35), channel_id=1, source_target_pairs={{0,8},{2,10},{4,12},{6,14},{8,0},{10,2},{12,4},{14,6},{16,24},{18,... | collective-permute-start | bytes 393224 | tf_op jit(solution)/shard_map/ppermute | solution.py:326
  85.1 6.3 %collective-permute-start.16 = (f32[256,128]{1,0:T(8,128)S(1)}, f32[256,128]{1,0:T(8,128)S(1)}, u32[]{:S(2)}, u32[]{:S(2)}) collective-permute-start(f32[256,128]{1,0:T(8,128)S(1)} %add.36), channel_id=1, source_target_pairs={{0,16},{2,18},{4,20},{6,22},{8,24},{10,26},{12,28},{14,30},{16,0},... | collective-permute-start | bytes 393224 | tf_op jit(solution)/shard_map/ppermute | solution.py:326
  87.8 7.5 %collective-permute-start.20 = (f32[128,512]{1,0:T(8,128)S(1)}, f32[128,512]{1,0:T(8,128)S(1)}, u32[]{:S(2)}, u32[]{:S(2)}) collective-permute-start(f32[128,512]{1,0:T(8,128)S(1)} %add.39), channel_id=1, source_target_pairs={{0,8},{2,10},{4,12},{6,14},{8,0},{10,2},{12,4},{14,6},{16,24},{18,... | collective-permute-start | bytes 786440 | tf_op jit(solution)/shard_map/ppermute | solution.py:326
  91.5 17.1 %copy-start.10 = (f32[4,256,128]{2,1,0:T(8,128)}, f32[4,256,128]{2,1,0:T(8,128)S(1)}, u32[]{:S(2)}) copy-start(f32[4,256,128]{2,1,0:T(8,128)S(1)} %pad_maximum_fusion.1.mine_ref) | copy-start | bytes 1572868
  91.5 18.7 %collective-permute-start.17 = (f32[4,256,128]{2,1,0:T(8,128)S(1)}, f32[4,256,128]{2,1,0:T(8,128)S(1)}, u32[]{:S(2)}, u32[]{:S(2)}) collective-permute-start(f32[4,256,128]{2,1,0:T(8,128)S(1)} %pad_maximum_fusion.1.mine_ref), channel_id=1, source_target_pairs={{0,1},{1,0},{2,3},{3,2},{4,5},{5,4},{6,7},{7,6},{8,9},{9,8},{10,11... | collective-permute-start | bytes 1572872 | tf_op jit(solution)/shard_map/ppermute | solution.py:326
  95.3 13.2 %collective-permute-start.21 = (f32[128,512]{1,0:T(8,128)S(1)}, f32[128,512]{1,0:T(8,128)S(1)}, u32[]{:S(2)}, u32[]{:S(2)}) collective-permute-start(f32[128,512]{1,0:T(8,128)S(1)} %add.40), channel_id=1, source_target_pairs={{0,16},{2,18},{4,20},{6,22},{8,24},{10,26},{12,28},{14,30},{16,0},... | collective-permute-start | bytes 786440 | tf_op jit(solution)/shard_map/ppermute | solution.py:326
  96.7 30.9 %copy-start.8 = (f32[3,128,512]{2,1,0:T(8,128)}, f32[3,128,512]{2,1,0:T(8,128)S(1)}, u32[]{:S(2)}) copy-start(f32[3,128,512]{2,1,0:T(8,128)S(1)} %pad_maximum_fusion.refs_3_) | copy-start | bytes 2359300
  96.7 32.3 %collective-permute-start.23 = (f32[3,128,512]{2,1,0:T(8,128)S(1)}, f32[3,128,512]{2,1,0:T(8,128)}, u32[]{:S(2)}, u32[]{:S(2)}) collective-permute-start(f32[3,128,512]{2,1,0:T(8,128)S(1)} %pad_maximum_fusion.refs_3_), channel_id=1, source_target_pairs={{0,2},{2,0},{4,6},{6,4},{8,10},{10,8},{12,14},{14,12},{16,18},{18,... | collective-permute-start | bytes 2359304 | tf_op jit(solution)/shard_map/ppermute | solution.py:326
  108.5 19.0 %copy-start.9 = (f32[128,512]{1,0:T(8,128)}, f32[128,512]{1,0:T(8,128)S(1)}, u32[]{:S(2)}) copy-start(f32[128,512]{1,0:T(8,128)S(1)} %add.41.mine_ref) | copy-start | bytes 786436
  108.5 23.8 %collective-permute-start.22 = (f32[128,512]{1,0:T(8,128)S(1)}, f32[128,512]{1,0:T(8,128)S(1)}, u32[]{:S(2)}, u32[]{:S(2)}) collective-permute-start(f32[128,512]{1,0:T(8,128)S(1)} %add.41.mine_ref), channel_id=1, source_target_pairs={{0,2},{2,0},{4,6},{6,4},{8,10},{10,8},{12,14},{14,12},{16,18},{18,... | collective-permute-start | bytes 786440 | tf_op jit(solution)/shard_map/ppermute | solution.py:326
  110.1 0.8 copy-start.23
  127.6 1.4 %copy-start.2 = (f32[256,256]{1,0:T(8,128)}, f32[256,256]{1,0:T(8,128)S(1)}, u32[]{:S(2)}) copy-start(f32[256,256]{1,0:T(8,128)S(1)} %get-tuple-element.23.refs_0_) | copy-start | bytes 786436
  127.6 1.4 %copy-start.3 = (f32[256,256]{1,0:T(8,128)}, f32[256,256]{1,0:T(8,128)S(1)}, u32[]{:S(2)}) copy-start(f32[256,256]{1,0:T(8,128)S(1)} %get-tuple-element.24.refs_1_) | copy-start | bytes 786436
  127.6 1.4 %copy-start.4 = (f32[256,256]{1,0:T(8,128)}, f32[256,256]{1,0:T(8,128)S(1)}, u32[]{:S(2)}) copy-start(f32[256,256]{1,0:T(8,128)S(1)} %get-tuple-element.25.refs_2_) | copy-start | bytes 786436
  127.6 4.7 %copy-start.1 = (f32[256,256]{1,0:T(8,128)}, f32[256,256]{1,0:T(8,128)S(1)}, u32[]{:S(2)}) copy-start(f32[256,256]{1,0:T(8,128)S(1)} %get-tuple-element.20.inverse_ref) | copy-start | bytes 786436
  132.4 0.7 copy-start.20

commit v7 on v6

--- a/solution.py
+++ b/solution.py
@@ -12,6 +12,7 @@
 BASE = 64
 WIDE = 16
 SPLIT = 2
+GRANT = 24 * 2**20
 NN = ((1,), (0,))
 NT = ((1,), (1,))
 HIGH = lax.Precision.HIGH
@@ -148,6 +149,7 @@
         out_specs=[vmem] * count,
         scratch_shapes=[pltpu.VMEM((size, size), jnp.float32)] * count,
         cost_estimate=pl.CostEstimate(flops=15 * 10**9, bytes_accessed=8 * count * size**2, transcendentals=0),
+        compiler_params=pltpu.CompilerParams(vmem_limit_bytes=GRANT),
         name="factor_inverse",
     )(core, gram, mine, other)
 
@@ -203,6 +205,7 @@
             bytes_accessed=4 * (total * width + 2 * rows * width + blocks.size),
             transcendentals=0,
         ),
+        compiler_params=pltpu.CompilerParams(vmem_limit_bytes=GRANT),
         name="near_step",
     )(index, count, flag, blocks, base, *pieces, *extra)
 
@@ -246,6 +249,7 @@
         cost_estimate=pl.CostEstimate(
             flops=6 * rows * rank * (rank + width), bytes_accessed=4 * rows * (3 * rank + width), transcendentals=0
         ),
+        compiler_params=pltpu.CompilerParams(vmem_limit_bytes=GRANT),
         name="leaf_products",
     )(*args)
 
@@ -288,6 +292,7 @@
         cost_estimate=pl.CostEstimate(
             flops=6 * count * rank * rank * width, bytes_accessed=8 * count * rank * (rank + width), transcendentals=0
         ),
+        compiler_params=pltpu.CompilerParams(vmem_limit_bytes=GRANT),
         name="reduce_early",
     )(flag, *inverses, mine, other)
 
@@ -318,6 +323,7 @@
         cost_estimate=pl.CostEstimate(
             flops=6 * rank * rank * width, bytes_accessed=8 * rank * (rank + width), transcendentals=0
         ),
+        compiler_params=pltpu.CompilerParams(vmem_limit_bytes=GRANT),
         name="reduce_last",
     )(flag, inverse, mine, other, reduced)
 
@@ -356,9 +362,11 @@
     peer = [across(pieces[i], "rows", 0) for i in range(parts)]
     far = [relayed(peer[i], "rows") for i in range(parts)]
 
+    spots = [*range(block_count, 2 * block_count)]
+    (left,) = near_step(near_blocks, samples, [probes], spots, index, near_count, near_count, 0)
     early = (block_count - 1) * SPLIT
-    spots = [*range(block_count - 1), *range(block_count, 3 * block_count)]
-    (left,) = near_step(near_blocks, samples, far[:early] + [probes] + peer, spots, index, near_count, flag, 0)
+    spots = [*range(block_count - 1), *range(2 * block_count, 3 * block_count)]
+    (left,) = near_step(near_blocks, left, far[:early] + peer, spots, index, near_count, flag, 1)
     spots = [block_count - 1]
     far_samples, partial = near_step(near_blocks, left, far[early:], spots, index, near_count, flag, 1, sketch)
     if halves == 2:

time: 136 us -> 129 us (0.949)
  Pallas kernels: 35 us -> 28.2 us
  starting transfers between devices: 46.5 us -> 48.9 us
  local copies, waits for them, and re-layouts: 8.43 us -> 7 us
    ppermute x6, waiting for transfers between devices: 0.02 us -> 3.74 us  [relayed(): lax.ppermute(value, axis, [(i, t) for i, t in steps if 0 <= t < count])]
    ppermute x18, starting transfers between devices: 22.6 us -> 25.9 us  [across(): lax.ppermute(value, axis, [(i, i ^ 1 << bit) for i in range(lax.axis_size...]
    unnamed x48 -> x12, local copies, waits for them, and re-layouts: 6.09 us -> 2.83 us
    ppermute x18, waiting for transfers between devices: 41.5 us -> 38.2 us  [across(): lax.ppermute(value, axis, [(i, i ^ 1 << bit) for i in range(lax.axis_size...]
    pallas_call x2 -> x3, Pallas kernels: 9.56 us -> 6.4 us  [near_step(): pl.pallas_call(functools.partial(near_kernel, len(pieces), first_slot, tu...]
    slice x2, local copies, waits for them, and re-layouts: 2.33 us -> 4.17 us  [leaf_and_levels(): (later if i else probes)[i * depth:(i + 1) * depth]]
  transfers between devices with their start and end apart: 24 -> 24, of which waited for: 12 -> 14; matrix products, arithmetic and copies ran while one was open for 3% -> 3% of each run, Pallas kernels for 19% -> 18%
where the time goes in v7:
time: 129 us
  starting transfers between devices  48.9 us (38%)
  waiting for transfers between devices  41.9 us (32%)
  Pallas kernels  28.2 us (22%)
  local copies, waits for them, and re-layouts  7 us (5%)
  matrix products  1.39 us (1%)
    ppermute x18, waiting for transfers between devices, across(): lax.ppermute(value, axis, [(i, i ^ 1 << bit) for i in range(lax.axis_size...  38.2 us
    ppermute x18, starting transfers between devices, across(): lax.ppermute(value, axis, [(i, i ^ 1 << bit) for i in range(lax.axis_size...  25.9 us
    ppermute x6, starting transfers between devices, relayed(): lax.ppermute(value, axis, [(i, t) for i, t in steps if 0 <= t < count])  23 us
    pallas_call x1, Pallas kernels, factor_inverse(): pl.pallas_call(functools.partial(inverse_kernel, size), out_shape=[pltpu....  15.9 us
    pallas_call x3, Pallas kernels, near_step(): pl.pallas_call(functools.partial(near_kernel, len(pieces), first_slot, tu...  6.4 us
    slice x2, local copies, waits for them, and re-layouts, leaf_and_levels(): (later if i else probes)[i * depth:(i + 1) * depth]  4.17 us
    ppermute x6, waiting for transfers between devices, relayed(): lax.ppermute(value, axis, [(i, t) for i, t in steps if 0 <= t < count])  3.74 us
    unnamed x12, local copies, waits for them, and re-layouts  2.83 us
  transfers between devices with their start and end apart: 24, of which 14 were waited for; matrix products, arithmetic and copies ran while one was open for 3% of the time, Pallas kernels for 18%

profile of v7, /device:TPU:0, one launch (start us, length us, event | category | flops | bytes accessed | tf_op | source)
XLA Modules:
  0.0 128.9 jit_solution(2835800904462896769)
XLA Ops:
  0.7 1.8 %slice.18 = f32[128,512]{1,0:T(8,128)} slice(f32[768,512]{1,0:T(8,128)} %refs_0_.1), slice={[0:128], [0:512]} | slice | bytes 524288 | tf_op jit(solution)/shard_map/slice | solution.py:361
  2.5 3.0 %collective-permute-start = (f32[128,512]{1,0:T(8,128)}, f32[128,512]{1,0:T(8,128)S(1)}, u32[]{:S(2)}, u32[]{:S(2)}) collective-permute-start(f32[128,512]{1,0:T(8,128)} %slice.18), channel_id=1, source_target_pairs={{0,2},{2,0},{4,6},{6,4},{8,10},{10,8},{12,14},{14,12},{16,18},{18,... | collective-permute-start | bytes 786440 | tf_op jit(solution)/shard_map/ppermute | solution.py:332
  5.5 2.3 %fusion = (f32[128,512]{1,0:T(8,128)}, f32[128,512]{1,0:T(8,128)}, f32[128,512]{1,0:T(8,128)}, f32[128,512]{1,0:T(8,128)}, f32[128,512]{1,0:T(8,128)}) fusion(f32[768,512]{1,0:T(8,128)} %refs_0_.1), kind=kLoop, calls=%fused_computation.5 | loop fusion | bytes 2621440 | tf_op jit(solution)/shard_map/slice | solution.py:361
  7.8 2.0 %collective-permute-start.4 = (f32[128,512]{1,0:T(8,128)}, f32[128,512]{1,0:T(8,128)S(1)}, u32[]{:S(2)}, u32[]{:S(2)}) collective-permute-start(f32[128,512]{1,0:T(8,128)} %get-tuple-element.29), channel_id=1, source_target_pairs={{0,2},{2,0},{4,6},{6,4},{8,10},{10,8},{12,14},{14,12},{16,18},{18,... | collective-permute-start | bytes 786440 | tf_op jit(solution)/shard_map/ppermute | solution.py:332
  9.9 2.0 %collective-permute-start.8 = (f32[128,512]{1,0:T(8,128)}, f32[128,512]{1,0:T(8,128)S(1)}, u32[]{:S(2)}, u32[]{:S(2)}) collective-permute-start(f32[128,512]{1,0:T(8,128)} %get-tuple-element.27), channel_id=1, source_target_pairs={{0,2},{2,0},{4,6},{6,4},{8,10},{10,8},{12,14},{14,12},{16,18},{18,... | collective-permute-start | bytes 786440 | tf_op jit(solution)/shard_map/ppermute | solution.py:332
  11.9 1.0 collective-permute-done.refs_4_
  12.8 2.0 %collective-permute-start.9 = (f32[128,512]{1,0:T(8,128)}, f32[128,512]{1,0:T(8,128)}, u32[]{:S(2)}, u32[]{:S(2)}) collective-permute-start(f32[128,512]{1,0:T(8,128)} %get-tuple-element.26), channel_id=1, source_target_pairs={{0,2},{2,0},{4,6},{6,4},{8,10},{10,8},{12,14},{14,12},{16,18},{18,... | collective-permute-start | bytes 786440 | tf_op jit(solution)/shard_map/ppermute | solution.py:332
  14.8 3.6 %collective-permute-done.2.refs_5_ = f32[128,512]{1,0:T(8,128)S(1)} collective-permute-done((f32[128,512]{1,0:T(8,128)}, f32[128,512]{1,0:T(8,128)S(1)}, u32[]{:S(2)}, u32[]{:S(2)}) %collective-permute-start.2) | collective-permute-done | bytes 262176 | tf_op jit(solution)/shard_map/ppermute | solution.py:332
  18.4 4.7 %collective-permute-start.1 = (f32[128,512]{1,0:T(8,128)S(1)}, f32[128,512]{1,0:T(8,128)}, u32[]{:S(2)}, u32[]{:S(2)}) collective-permute-start(f32[128,512]{1,0:T(8,128)S(1)} %collective-permute-done.refs_4_), channel_id=1, source_target_pairs={{0,4},{4,8},{6,2},{8,12},{10,6},{12,16},{14,10},{16,20},{18,14},{2... | collective-permute-start | bytes 786440 | tf_op jit(solution)/shard_map/ppermute | solution.py:338
  23.1 0.9 collective-permute-done.4.refs_6_
  24.1 4.0 %collective-permute-start.3 = (f32[128,512]{1,0:T(8,128)S(1)}, f32[128,512]{1,0:T(8,128)S(1)}, u32[]{:S(2)}, u32[]{:S(2)}) collective-permute-start(f32[128,512]{1,0:T(8,128)S(1)} %collective-permute-done.2.refs_5_), channel_id=1, source_target_pairs={{0,4},{4,8},{6,2},{8,12},{10,6},{12,16},{14,10},{16,20},{18,14},{2... | collective-permute-start | bytes 786440 | tf_op jit(solution)/shard_map/ppermute | solution.py:338
  28.0 1.8 %collective-permute-done.6.refs_7_ = f32[128,512]{1,0:T(8,128)} collective-permute-done((f32[128,512]{1,0:T(8,128)}, f32[128,512]{1,0:T(8,128)}, u32[]{:S(2)}, u32[]{:S(2)}) %collective-permute-start.6) | collective-permute-done | bytes 262176 | tf_op jit(solution)/shard_map/ppermute | solution.py:332
  29.8 4.0 %collective-permute-start.5 = (f32[128,512]{1,0:T(8,128)S(1)}, f32[128,512]{1,0:T(8,128)S(1)}, u32[]{:S(2)}, u32[]{:S(2)}) collective-permute-start(f32[128,512]{1,0:T(8,128)S(1)} %collective-permute-done.4.refs_6_), channel_id=1, source_target_pairs={{0,4},{4,8},{6,2},{8,12},{10,6},{12,16},{14,10},{16,20},{18,14},{2... | collective-permute-start | bytes 786440 | tf_op jit(solution)/shard_map/ppermute | solution.py:338
  33.7 1.5 %collective-permute-done.8.refs_8_ = f32[128,512]{1,0:T(8,128)S(1)} collective-permute-done((f32[128,512]{1,0:T(8,128)}, f32[128,512]{1,0:T(8,128)S(1)}, u32[]{:S(2)}, u32[]{:S(2)}) %collective-permute-start.8) | collective-permute-done | bytes 262176 | tf_op jit(solution)/shard_map/ppermute | solution.py:332
  35.3 4.0 %collective-permute-start.7 = (f32[128,512]{1,0:T(8,128)}, f32[128,512]{1,0:T(8,128)S(1)}, u32[]{:S(2)}, u32[]{:S(2)}) collective-permute-start(f32[128,512]{1,0:T(8,128)} %collective-permute-done.6.refs_7_), channel_id=1, source_target_pairs={{0,4},{4,8},{6,2},{8,12},{10,6},{12,16},{14,10},{16,20},{18,14},{2... | collective-permute-start | bytes 786440 | tf_op jit(solution)/shard_map/ppermute | solution.py:338
  39.3 1.4 %copy-done.1 = f32[768,512]{1,0:T(8,128)S(1)} copy-done((f32[768,512]{1,0:T(8,128)S(1)}, f32[768,512]{1,0:T(8,128)}, u32[]{:S(2)}) %copy-start.1) | copy-done | bytes 1572888
  40.7 1.4 %copy-done.2 = f32[768,512]{1,0:T(8,128)S(1)} copy-done((f32[768,512]{1,0:T(8,128)S(1)}, f32[768,512]{1,0:T(8,128)}, u32[]{:S(2)}) %copy-start.2) | copy-done | bytes 1572888
  42.1 2.4 %near_step.3.base_ref = f32[768,512]{1,0:T(8,128)S(1)} custom-call(s32[3,3]{1,0:T(4,128)S(1)} %select_add_fusion.index_ref, s32[3]{0:T(128)S(1)} %copy-done.3, s32[3]{0:T(128)S(1)} %copy-done.3, f32[3,3,256,256]{3,2,1,0:T(8,128)S(1)} %copy-done, f32[768,512]{1,0:T(8,128)S(1)} %copy-done.2, f32[768,512]{1,0:T(8,128)S(1)} %copy-done.1), custom_call_target="tpu_custom_call" | custom-call | flops 1811939328 | bytes 7077888 | tf_op jit(solution)/shard_map/near_step/pallas_call | solution.py:197
  44.5 3.4 %collective-permute-start.10 = (f32[128,512]{1,0:T(8,128)S(1)}, f32[128,512]{1,0:T(8,128)S(1)}, u32[]{:S(2)}, u32[]{:S(2)}) collective-permute-start(f32[128,512]{1,0:T(8,128)S(1)} %collective-permute-done.8.refs_8_), channel_id=1, source_target_pairs={{0,4},{4,8},{6,2},{8,12},{10,6},{12,16},{14,10},{16,20},{18,14},{2... | collective-permute-start | bytes 786440 | tf_op jit(solution)/shard_map/ppermute | solution.py:338
  47.9 3.1 %collective-permute-start.11 = (f32[128,512]{1,0:T(8,128)}, f32[128,512]{1,0:T(8,128)S(1)}, u32[]{:S(2)}, u32[]{:S(2)}) collective-permute-start(f32[128,512]{1,0:T(8,128)} %collective-permute-done.9.refs_9_), channel_id=1, source_target_pairs={{0,4},{4,8},{6,2},{8,12},{10,6},{12,16},{14,10},{16,20},{18,14},{2... | collective-permute-start | bytes 786440 | tf_op jit(solution)/shard_map/ppermute | solution.py:338
  51.0 0.1 pad_add_fusion.flag_ref.core_ref
  51.1 2.3 %near_step.4.base_ref = f32[768,512]{1,0:T(8,128)S(1)} custom-call(s32[3,3]{1,0:T(4,128)S(1)} %select_add_fusion.index_ref, s32[3]{0:T(128)S(1)} %copy-done.3, s32[3]{0:T(128)S(1)} %pad_add_fusion.flag_ref.core_ref, f32[3,3,256,256]{3,2,1,0:T(8,128)S(1)} %copy-done, f32[768,512]{1,0:T(8,128)S(1)} %near_step.3.base_ref, ...), custom_call_target="tpu_custom_call" | custom-call | flops 1811939328 | bytes 8126464 | tf_op jit(solution)/shard_map/near_step/pallas_call | solution.py:197
  53.4 0.8 collective-permute-done.10.refs_0_
  54.2 2.9 %collective-permute-done.11.refs_1_ = f32[128,512]{1,0:T(8,128)S(1)} collective-permute-done((f32[128,512]{1,0:T(8,128)}, f32[128,512]{1,0:T(8,128)S(1)}, u32[]{:S(2)}, u32[]{:S(2)}) %collective-permute-start.11) | collective-permute-done | bytes 262176 | tf_op jit(solution)/shard_map/ppermute | solution.py:338
  57.1 1.7 %near_step.5 = (f32[768,512]{1,0:T(8,128)S(1)}, f32[768,256]{1,0:T(8,128)S(1)}) custom-call(s32[3,3]{1,0:T(4,128)S(1)} %select_add_fusion.index_ref, s32[3]{0:T(128)S(1)} %copy-done.3, s32[3]{0:T(128)S(1)} %pad_add_fusion.flag_ref.core_ref, f32[3,3,256,256]{3,2,1,0:T(8,128)S(1)} %copy-done, f32[768,512]{1,0:T(8,128)S(1)} %near_step.4.base_ref, ...), custom_call_target="tpu_custom_call" | custom-call | flops 1811939328 | bytes 6029312 | tf_op jit(solution)/shard_map/near_step/pallas_call | solution.py:197
  58.9 0.1 collective-permute-start.12
  58.9 2.3 %collective-permute-done.12.other_ref = f32[768,256]{1,0:T(8,128)S(1)} collective-permute-done((f32[768,256]{1,0:T(8,128)S(1)}, f32[768,256]{1,0:T(8,128)S(1)}, u32[]{:S(2)}, u32[]{:S(2)}) %collective-permute-start.12) | collective-permute-done | bytes 786464 | tf_op jit(solution)/shard_map/ppermute | solution.py:332
  61.2 1.9 %leaf_products.1 = (f32[768,256]{1,0:T(8,128)S(1)}, f32[256,256]{1,0:T(8,128)S(1)}, f32[256,128]{1,0:T(8,128)S(1)}, f32[128,512]{1,0:T(8,128)S(1)}, f32[128,512]{1,0:T(8,128)S(1)}) custom-call(s32[3]{0:T(128)S(1)} %pad_add_fusion.flag_ref.core_ref, f32[768,256]{1,0:T(8,128)S(1)} %get-tuple-element.14.half_ref, ...), custom_call_target="tpu_custom_call" | custom-call | flops 905969664 | bytes 3932160 | tf_op jit(solution)/shard_map/leaf_products/pallas_call | solution.py:243
  63.1 0.6 collective-permute-start.13
  63.7 1.5 %collective-permute-start.18 = (f32[128,512]{1,0:T(8,128)S(1)}, f32[128,512]{1,0:T(8,128)S(1)}, u32[]{:S(2)}, u32[]{:S(2)}) collective-permute-start(f32[128,512]{1,0:T(8,128)S(1)} %get-tuple-element.22), channel_id=1, source_target_pairs={{0,2},{2,0},{4,6},{6,4},{8,10},{10,8},{12,14},{14,12},{16,18},{18,... | collective-permute-start | bytes 786440 | tf_op jit(solution)/shard_map/ppermute | solution.py:332
  65.2 4.3 %collective-permute-done.13 = f32[256,128]{1,0:T(8,128)S(1)} collective-permute-done((f32[256,128]{1,0:T(8,128)S(1)}, f32[256,128]{1,0:T(8,128)S(1)}, u32[]{:S(2)}, u32[]{:S(2)}) %collective-permute-start.13) | collective-permute-done | bytes 131104 | tf_op jit(solution)/shard_map/ppermute | solution.py:332
  69.6 3.2 %collective-permute-start.14 = (f32[256,128]{1,0:T(8,128)S(1)}, f32[256,128]{1,0:T(8,128)S(1)}, u32[]{:S(2)}, u32[]{:S(2)}) collective-permute-start(f32[256,128]{1,0:T(8,128)S(1)} %add.34), channel_id=1, source_target_pairs={{0,4},{2,6},{4,0},{6,2},{8,12},{10,14},{12,8},{14,10},{16,20},{18,... | collective-permute-start | bytes 393224 | tf_op jit(solution)/shard_map/ppermute | solution.py:332
  72.8 2.9 %collective-permute-done.14 = f32[256,128]{1,0:T(8,128)S(1)} collective-permute-done((f32[256,128]{1,0:T(8,128)S(1)}, f32[256,128]{1,0:T(8,128)S(1)}, u32[]{:S(2)}, u32[]{:S(2)}) %collective-permute-start.14) | collective-permute-done | bytes 131104 | tf_op jit(solution)/shard_map/ppermute | solution.py:332
  75.8 2.1 %collective-permute-start.19 = (f32[128,512]{1,0:T(8,128)S(1)}, f32[128,512]{1,0:T(8,128)S(1)}, u32[]{:S(2)}, u32[]{:S(2)}) collective-permute-start(f32[128,512]{1,0:T(8,128)S(1)} %add.38), channel_id=1, source_target_pairs={{0,4},{2,6},{4,0},{6,2},{8,12},{10,14},{12,8},{14,10},{16,20},{18,... | collective-permute-start | bytes 786440 | tf_op jit(solution)/shard_map/ppermute | solution.py:332
  77.9 1.6 %collective-permute-start.15 = (f32[256,128]{1,0:T(8,128)S(1)}, f32[256,128]{1,0:T(8,128)S(1)}, u32[]{:S(2)}, u32[]{:S(2)}) collective-permute-start(f32[256,128]{1,0:T(8,128)S(1)} %add.35), channel_id=1, source_target_pairs={{0,8},{2,10},{4,12},{6,14},{8,0},{10,2},{12,4},{14,6},{16,24},{18,... | collective-permute-start | bytes 393224 | tf_op jit(solution)/shard_map/ppermute | solution.py:332
  79.5 3.4 %collective-permute-done.15 = f32[256,128]{1,0:T(8,128)S(1)} collective-permute-done((f32[256,128]{1,0:T(8,128)S(1)}, f32[256,128]{1,0:T(8,128)S(1)}, u32[]{:S(2)}, u32[]{:S(2)}) %collective-permute-start.15) | collective-permute-done | bytes 131104 | tf_op jit(solution)/shard_map/ppermute | solution.py:332
  82.9 2.7 %collective-permute-start.16 = (f32[256,128]{1,0:T(8,128)S(1)}, f32[256,128]{1,0:T(8,128)S(1)}, u32[]{:S(2)}, u32[]{:S(2)}) collective-permute-start(f32[256,128]{1,0:T(8,128)S(1)} %add.36), channel_id=1, source_target_pairs={{0,16},{2,18},{4,20},{6,22},{8,24},{10,26},{12,28},{14,30},{16,0},... | collective-permute-start | bytes 393224 | tf_op jit(solution)/shard_map/ppermute | solution.py:332
  85.6 0.9 collective-permute-start.20
  86.5 2.7 %collective-permute-done.16 = f32[256,128]{1,0:T(8,128)S(1)} collective-permute-done((f32[256,128]{1,0:T(8,128)S(1)}, f32[256,128]{1,0:T(8,128)S(1)}, u32[]{:S(2)}, u32[]{:S(2)}) %collective-permute-start.16) | collective-permute-done | bytes 131104 | tf_op jit(solution)/shard_map/ppermute | solution.py:332
  89.3 3.9 %collective-permute-done.20 = f32[128,512]{1,0:T(8,128)S(1)} collective-permute-done((f32[128,512]{1,0:T(8,128)S(1)}, f32[128,512]{1,0:T(8,128)S(1)}, u32[]{:S(2)}, u32[]{:S(2)}) %collective-permute-start.20) | collective-permute-done | bytes 262176 | tf_op jit(solution)/shard_map/ppermute | solution.py:332
  93.2 2.1 %collective-permute-start.21 = (f32[128,512]{1,0:T(8,128)S(1)}, f32[128,512]{1,0:T(8,128)S(1)}, u32[]{:S(2)}, u32[]{:S(2)}) collective-permute-start(f32[128,512]{1,0:T(8,128)S(1)} %add.40), channel_id=1, source_target_pairs={{0,16},{2,18},{4,20},{6,22},{8,24},{10,26},{12,28},{14,30},{16,0},... | collective-permute-start | bytes 786440 | tf_op jit(solution)/shard_map/ppermute | solution.py:332
  95.4 1.2 collective-permute-start.23
  96.6 9.9 %collective-permute-done.21 = f32[128,512]{1,0:T(8,128)S(1)} collective-permute-done((f32[128,512]{1,0:T(8,128)S(1)}, f32[128,512]{1,0:T(8,128)S(1)}, u32[]{:S(2)}, u32[]{:S(2)}) %collective-permute-start.21) | collective-permute-done | bytes 262176 | tf_op jit(solution)/shard_map/ppermute | solution.py:332
  106.6 0.8 collective-permute-start.22
  107.4 15.9 %factor_inverse.1 = (f32[256,256]{1,0:T(8,128)S(1)}, f32[256,256]{1,0:T(8,128)S(1)}, f32[256,256]{1,0:T(8,128)S(1)}, f32[256,256]{1,0:T(8,128)S(1)}, f32[256,256]{1,0:T(8,128)S(1)}) custom-call(s32[3]{0:T(128)S(1)} %pad_add_fusion.flag_ref.core_ref, f32[256,256]{1,0:T(8,128)S(1)} %get-tuple-element.17.gram_ref, ...), custom_call_target="tpu_custom_call" | custom-call | flops 15000000512 | bytes 2621440 | tf_op jit(solution)/shard_map/factor_inverse/pallas_call | solution.py:145
  123.3 1.4 %fusion.1 = f32[768,256]{1,0:T(8,128)} fusion(f32[768,256]{1,0:T(8,128)S(1)} %get-tuple-element.16, f32[256,256]{1,0:T(8,128)S(1)} %get-tuple-element.19), kind=kOutput, calls=%fused_computation.6 | convolution fusion | flops 301989888 | bytes 1835008 | tf_op jit(solution)/shard_map/dot_general | solution.py:385
  124.7 2.2 %reduce_early.1.kept_ref = f32[4,1,256,512]{3,2,1,0:T(8,128)} custom-call(s32[3]{0:T(128)S(1)} %pad_add_fusion.flag_ref.core_ref, f32[256,256]{1,0:T(8,128)S(1)} %get-tuple-element.23.refs_0_, f32[256,256]{1,0:T(8,128)S(1)} %get-tuple-element.24.refs_1_, f32[256,256]{1,0:T(8,128)S(1)} %get-tuple-element.25.refs_2_, ...), custom_call_target="tpu_custom_call" | custom-call | flops 603979776 | bytes 4718592 | tf_op jit(solution)/shard_map/reduce_early/pallas_call | solution.py:282
  127.0 1.8 %reduce_last.1 = f32[4,1,256,512]{3,2,1,0:T(8,128)} custom-call(s32[3]{0:T(128)S(1)} %pad_add_fusion.flag_ref.core_ref, f32[256,256]{1,0:T(8,128)S(1)} %get-tuple-element.20.inverse_ref, f32[128,512]{1,0:T(8,128)S(1)} %add.41.mine_ref, f32[128,512]{1,0:T(8,128)S(1)} %collective-permute-done.22.other_ref, ...), custom_call_target="tpu_custom_call", output_to_operand_aliasing={{}: (4, {})} | custom-call | flops 201326592 | bytes 1572864 | tf_op jit(solution)/shard_map/reduce_last/pallas_call | solution.py:312
  (34 shorter events, 0.4 us)
Async XLA Ops:
  0.6 22.5 %copy-start.5 = (s32[3,3]{1,0:T(4,128)S(1)}, s32[3,3]{1,0:T(4,128)}, u32[]{:S(2)}) copy-start(s32[3,3]{1,0:T(4,128)} %param.9) | copy-start | bytes 112
  0.6 38.6 %copy-start.3 = (s32[3]{0:T(128)S(1)}, s32[3]{0:T(128)}, u32[]{:S(2)}) copy-start(s32[3]{0:T(128)} %count_ref.5) | copy-start | bytes 40
  0.7 38.6 %copy-start = (f32[3,3,256,256]{3,2,1,0:T(8,128)S(1)}, f32[3,3,256,256]{3,2,1,0:T(8,128)}, u32[]{:S(2)}) copy-start(f32[3,3,256,256]{3,2,1,0:T(8,128)} %blocks_ref.5) | copy-start | bytes 7077892
  2.5 10.3 %collective-permute-start = (f32[128,512]{1,0:T(8,128)}, f32[128,512]{1,0:T(8,128)S(1)}, u32[]{:S(2)}, u32[]{:S(2)}) collective-permute-start(f32[128,512]{1,0:T(8,128)} %slice.18), channel_id=1, source_target_pairs={{0,2},{2,0},{4,6},{6,4},{8,10},{10,8},{12,14},{14,12},{16,18},{18,... | collective-permute-start | bytes 786440 | tf_op jit(solution)/shard_map/ppermute | solution.py:332
  7.8 10.6 %collective-permute-start.2 = (f32[128,512]{1,0:T(8,128)}, f32[128,512]{1,0:T(8,128)S(1)}, u32[]{:S(2)}, u32[]{:S(2)}) collective-permute-start(f32[128,512]{1,0:T(8,128)} %get-tuple-element.30), channel_id=1, source_target_pairs={{0,2},{2,0},{4,6},{6,4},{8,10},{10,8},{12,14},{14,12},{16,18},{18,... | collective-permute-start | bytes 786440 | tf_op jit(solution)/shard_map/ppermute | solution.py:332
  7.8 16.2 %collective-permute-start.4 = (f32[128,512]{1,0:T(8,128)}, f32[128,512]{1,0:T(8,128)S(1)}, u32[]{:S(2)}, u32[]{:S(2)}) collective-permute-start(f32[128,512]{1,0:T(8,128)} %get-tuple-element.29), channel_id=1, source_target_pairs={{0,2},{2,0},{4,6},{6,4},{8,10},{10,8},{12,14},{14,12},{16,18},{18,... | collective-permute-start | bytes 786440 | tf_op jit(solution)/shard_map/ppermute | solution.py:332
  9.8 19.9 %collective-permute-start.6 = (f32[128,512]{1,0:T(8,128)}, f32[128,512]{1,0:T(8,128)}, u32[]{:S(2)}, u32[]{:S(2)}) collective-permute-start(f32[128,512]{1,0:T(8,128)} %get-tuple-element.28), channel_id=1, source_target_pairs={{0,2},{2,0},{4,6},{6,4},{8,10},{10,8},{12,14},{14,12},{16,18},{18,... | collective-permute-start | bytes 786440 | tf_op jit(solution)/shard_map/ppermute | solution.py:332
  9.9 25.4 %collective-permute-start.8 = (f32[128,512]{1,0:T(8,128)}, f32[128,512]{1,0:T(8,128)S(1)}, u32[]{:S(2)}, u32[]{:S(2)}) collective-permute-start(f32[128,512]{1,0:T(8,128)} %get-tuple-element.27), channel_id=1, source_target_pairs={{0,2},{2,0},{4,6},{6,4},{8,10},{10,8},{12,14},{14,12},{16,18},{18,... | collective-permute-start | bytes 786440 | tf_op jit(solution)/shard_map/ppermute | solution.py:332
  12.8 31.7 %collective-permute-start.9 = (f32[128,512]{1,0:T(8,128)}, f32[128,512]{1,0:T(8,128)}, u32[]{:S(2)}, u32[]{:S(2)}) collective-permute-start(f32[128,512]{1,0:T(8,128)} %get-tuple-element.26), channel_id=1, source_target_pairs={{0,2},{2,0},{4,6},{6,4},{8,10},{10,8},{12,14},{14,12},{16,18},{18,... | collective-permute-start | bytes 786440 | tf_op jit(solution)/shard_map/ppermute | solution.py:332
  18.4 29.5 %collective-permute-start.1 = (f32[128,512]{1,0:T(8,128)S(1)}, f32[128,512]{1,0:T(8,128)}, u32[]{:S(2)}, u32[]{:S(2)}) collective-permute-start(f32[128,512]{1,0:T(8,128)S(1)} %collective-permute-done.refs_4_), channel_id=1, source_target_pairs={{0,4},{4,8},{6,2},{8,12},{10,6},{12,16},{14,10},{16,20},{18,14},{2... | collective-permute-start | bytes 786440 | tf_op jit(solution)/shard_map/ppermute | solution.py:338
  24.1 27.0 %collective-permute-start.3 = (f32[128,512]{1,0:T(8,128)S(1)}, f32[128,512]{1,0:T(8,128)S(1)}, u32[]{:S(2)}, u32[]{:S(2)}) collective-permute-start(f32[128,512]{1,0:T(8,128)S(1)} %collective-permute-done.2.refs_5_), channel_id=1, source_target_pairs={{0,4},{4,8},{6,2},{8,12},{10,6},{12,16},{14,10},{16,20},{18,14},{2... | collective-permute-start | bytes 786440 | tf_op jit(solution)/shard_map/ppermute | solution.py:338
  29.8 21.3 %collective-permute-start.5 = (f32[128,512]{1,0:T(8,128)S(1)}, f32[128,512]{1,0:T(8,128)S(1)}, u32[]{:S(2)}, u32[]{:S(2)}) collective-permute-start(f32[128,512]{1,0:T(8,128)S(1)} %collective-permute-done.4.refs_6_), channel_id=1, source_target_pairs={{0,4},{4,8},{6,2},{8,12},{10,6},{12,16},{14,10},{16,20},{18,14},{2... | collective-permute-start | bytes 786440 | tf_op jit(solution)/shard_map/ppermute | solution.py:338
  35.3 15.8 %collective-permute-start.7 = (f32[128,512]{1,0:T(8,128)}, f32[128,512]{1,0:T(8,128)S(1)}, u32[]{:S(2)}, u32[]{:S(2)}) collective-permute-start(f32[128,512]{1,0:T(8,128)} %collective-permute-done.6.refs_7_), channel_id=1, source_target_pairs={{0,4},{4,8},{6,2},{8,12},{10,6},{12,16},{14,10},{16,20},{18,14},{2... | collective-permute-start | bytes 786440 | tf_op jit(solution)/shard_map/ppermute | solution.py:338
  39.3 1.4 %copy-start.1 = (f32[768,512]{1,0:T(8,128)S(1)}, f32[768,512]{1,0:T(8,128)}, u32[]{:S(2)}) copy-start(f32[768,512]{1,0:T(8,128)} %refs_0_.1) | copy-start | bytes 4718596
  40.7 1.4 %copy-start.2 = (f32[768,512]{1,0:T(8,128)S(1)}, f32[768,512]{1,0:T(8,128)}, u32[]{:S(2)}) copy-start(f32[768,512]{1,0:T(8,128)} %base_ref.1) | copy-start | bytes 4718596
  44.5 9.7 %collective-permute-start.10 = (f32[128,512]{1,0:T(8,128)S(1)}, f32[128,512]{1,0:T(8,128)S(1)}, u32[]{:S(2)}, u32[]{:S(2)}) collective-permute-start(f32[128,512]{1,0:T(8,128)S(1)} %collective-permute-done.8.refs_8_), channel_id=1, source_target_pairs={{0,4},{4,8},{6,2},{8,12},{10,6},{12,16},{14,10},{16,20},{18,14},{2... | collective-permute-start | bytes 786440 | tf_op jit(solution)/shard_map/ppermute | solution.py:338
  47.9 9.2 %collective-permute-start.11 = (f32[128,512]{1,0:T(8,128)}, f32[128,512]{1,0:T(8,128)S(1)}, u32[]{:S(2)}, u32[]{:S(2)}) collective-permute-start(f32[128,512]{1,0:T(8,128)} %collective-permute-done.9.refs_9_), channel_id=1, source_target_pairs={{0,4},{4,8},{6,2},{8,12},{10,6},{12,16},{14,10},{16,20},{18,14},{2... | collective-permute-start | bytes 786440 | tf_op jit(solution)/shard_map/ppermute | solution.py:338
  51.1 6.0 %copy-start.4 = (f32[512,256]{1,0:T(8,128)S(1)}, f32[512,256]{1,0:T(8,128)}, u32[]{:S(2)}) copy-start(f32[512,256]{1,0:T(8,128)} %refs_2_.1) | copy-start | bytes 1572868
  58.9 2.4 %collective-permute-start.12 = (f32[768,256]{1,0:T(8,128)S(1)}, f32[768,256]{1,0:T(8,128)S(1)}, u32[]{:S(2)}, u32[]{:S(2)}) collective-permute-start(f32[768,256]{1,0:T(8,128)S(1)} %get-tuple-element.14.half_ref), channel_id=1, source_target_pairs={{0,1},{1,0},{2,3},{3,2},{4,5},{5,4},{6,7},{7,6},{8,9},{9,8},{10,11... | collective-permute-start | bytes 2359304 | tf_op jit(solution)/shard_map/ppermute | solution.py:332
  63.1 6.4 %collective-permute-start.13 = (f32[256,128]{1,0:T(8,128)S(1)}, f32[256,128]{1,0:T(8,128)S(1)}, u32[]{:S(2)}, u32[]{:S(2)}) collective-permute-start(f32[256,128]{1,0:T(8,128)S(1)} %get-tuple-element.18), channel_id=1, source_target_pairs={{0,2},{2,0},{4,6},{6,4},{8,10},{10,8},{12,14},{14,12},{16,18},{18,... | collective-permute-start | bytes 393224 | tf_op jit(solution)/shard_map/ppermute | solution.py:332
  63.7 12.0 %collective-permute-start.18 = (f32[128,512]{1,0:T(8,128)S(1)}, f32[128,512]{1,0:T(8,128)S(1)}, u32[]{:S(2)}, u32[]{:S(2)}) collective-permute-start(f32[128,512]{1,0:T(8,128)S(1)} %get-tuple-element.22), channel_id=1, source_target_pairs={{0,2},{2,0},{4,6},{6,4},{8,10},{10,8},{12,14},{14,12},{16,18},{18,... | collective-permute-start | bytes 786440 | tf_op jit(solution)/shard_map/ppermute | solution.py:332
  69.6 6.1 %collective-permute-start.14 = (f32[256,128]{1,0:T(8,128)S(1)}, f32[256,128]{1,0:T(8,128)S(1)}, u32[]{:S(2)}, u32[]{:S(2)}) collective-permute-start(f32[256,128]{1,0:T(8,128)S(1)} %add.34), channel_id=1, source_target_pairs={{0,4},{2,6},{4,0},{6,2},{8,12},{10,14},{12,8},{14,10},{16,20},{18,... | collective-permute-start | bytes 393224 | tf_op jit(solution)/shard_map/ppermute | solution.py:332
  75.8 9.7 %collective-permute-start.19 = (f32[128,512]{1,0:T(8,128)S(1)}, f32[128,512]{1,0:T(8,128)S(1)}, u32[]{:S(2)}, u32[]{:S(2)}) collective-permute-start(f32[128,512]{1,0:T(8,128)S(1)} %add.38), channel_id=1, source_target_pairs={{0,4},{2,6},{4,0},{6,2},{8,12},{10,14},{12,8},{14,10},{16,20},{18,... | collective-permute-start | bytes 786440 | tf_op jit(solution)/shard_map/ppermute | solution.py:332
  77.9 5.0 %collective-permute-start.15 = (f32[256,128]{1,0:T(8,128)S(1)}, f32[256,128]{1,0:T(8,128)S(1)}, u32[]{:S(2)}, u32[]{:S(2)}) collective-permute-start(f32[256,128]{1,0:T(8,128)S(1)} %add.35), channel_id=1, source_target_pairs={{0,8},{2,10},{4,12},{6,14},{8,0},{10,2},{12,4},{14,6},{16,24},{18,... | collective-permute-start | bytes 393224 | tf_op jit(solution)/shard_map/ppermute | solution.py:332
  82.9 6.3 %collective-permute-start.16 = (f32[256,128]{1,0:T(8,128)S(1)}, f32[256,128]{1,0:T(8,128)S(1)}, u32[]{:S(2)}, u32[]{:S(2)}) collective-permute-start(f32[256,128]{1,0:T(8,128)S(1)} %add.36), channel_id=1, source_target_pairs={{0,16},{2,18},{4,20},{6,22},{8,24},{10,26},{12,28},{14,30},{16,0},... | collective-permute-start | bytes 393224 | tf_op jit(solution)/shard_map/ppermute | solution.py:332
  85.6 7.6 %collective-permute-start.20 = (f32[128,512]{1,0:T(8,128)S(1)}, f32[128,512]{1,0:T(8,128)S(1)}, u32[]{:S(2)}, u32[]{:S(2)}) collective-permute-start(f32[128,512]{1,0:T(8,128)S(1)} %add.39), channel_id=1, source_target_pairs={{0,8},{2,10},{4,12},{6,14},{8,0},{10,2},{12,4},{14,6},{16,24},{18,... | collective-permute-start | bytes 786440 | tf_op jit(solution)/shard_map/ppermute | solution.py:332
  89.2 18.2 %collective-permute-start.17 = (f32[4,256,128]{2,1,0:T(8,128)S(1)}, f32[4,256,128]{2,1,0:T(8,128)S(1)}, u32[]{:S(2)}, u32[]{:S(2)}) collective-permute-start(f32[4,256,128]{2,1,0:T(8,128)S(1)} %pad_maximum_fusion.1.mine_ref), channel_id=1, source_target_pairs={{0,1},{1,0},{2,3},{3,2},{4,5},{5,4},{6,7},{7,6},{8,9},{9,8},{10,11... | collective-permute-start | bytes 1572872 | tf_op jit(solution)/shard_map/ppermute | solution.py:332
  93.2 13.3 %collective-permute-start.21 = (f32[128,512]{1,0:T(8,128)S(1)}, f32[128,512]{1,0:T(8,128)S(1)}, u32[]{:S(2)}, u32[]{:S(2)}) collective-permute-start(f32[128,512]{1,0:T(8,128)S(1)} %add.40), channel_id=1, source_target_pairs={{0,16},{2,18},{4,20},{6,22},{8,24},{10,26},{12,28},{14,30},{16,0},... | collective-permute-start | bytes 786440 | tf_op jit(solution)/shard_map/ppermute | solution.py:332
  95.4 29.3 %collective-permute-start.23 = (f32[3,128,512]{2,1,0:T(8,128)S(1)}, f32[3,128,512]{2,1,0:T(8,128)S(1)}, u32[]{:S(2)}, u32[]{:S(2)}) collective-permute-start(f32[3,128,512]{2,1,0:T(8,128)S(1)} %pad_maximum_fusion.refs_3_), channel_id=1, source_target_pairs={{0,2},{2,0},{4,6},{6,4},{8,10},{10,8},{12,14},{14,12},{16,18},{18,... | collective-permute-start | bytes 2359304 | tf_op jit(solution)/shard_map/ppermute | solution.py:332
  106.6 20.4 %collective-permute-start.22 = (f32[128,512]{1,0:T(8,128)S(1)}, f32[128,512]{1,0:T(8,128)S(1)}, u32[]{:S(2)}, u32[]{:S(2)}) collective-permute-start(f32[128,512]{1,0:T(8,128)S(1)} %add.41.mine_ref), channel_id=1, source_target_pairs={{0,2},{2,0},{4,6},{6,4},{8,10},{10,8},{12,14},{14,12},{16,18},{18,... | collective-permute-start | bytes 786440 | tf_op jit(solution)/shard_map/ppermute | solution.py:332

commit v8 on v6

--- a/solution.py
+++ b/solution.py
@@ -12,6 +12,7 @@
 BASE = 64
 WIDE = 16
 SPLIT = 2
+GRANT = 16 * 2**20
 NN = ((1,), (0,))
 NT = ((1,), (1,))
 HIGH = lax.Precision.HIGH
@@ -148,6 +149,7 @@
         out_specs=[vmem] * count,
         scratch_shapes=[pltpu.VMEM((size, size), jnp.float32)] * count,
         cost_estimate=pl.CostEstimate(flops=15 * 10**9, bytes_accessed=8 * count * size**2, transcendentals=0),
+        compiler_params=pltpu.CompilerParams(vmem_limit_bytes=GRANT),
         name="factor_inverse",
     )(core, gram, mine, other)
 
@@ -203,6 +205,7 @@
             bytes_accessed=4 * (total * width + 2 * rows * width + blocks.size),
             transcendentals=0,
         ),
+        compiler_params=pltpu.CompilerParams(vmem_limit_bytes=GRANT),
         name="near_step",
     )(index, count, flag, blocks, base, *pieces, *extra)
 
@@ -246,6 +249,7 @@
         cost_estimate=pl.CostEstimate(
             flops=6 * rows * rank * (rank + width), bytes_accessed=4 * rows * (3 * rank + width), transcendentals=0
         ),
+        compiler_params=pltpu.CompilerParams(vmem_limit_bytes=GRANT),
         name="leaf_products",
     )(*args)
 
@@ -288,6 +292,7 @@
         cost_estimate=pl.CostEstimate(
             flops=6 * count * rank * rank * width, bytes_accessed=8 * count * rank * (rank + width), transcendentals=0
         ),
+        compiler_params=pltpu.CompilerParams(vmem_limit_bytes=GRANT),
         name="reduce_early",
     )(flag, *inverses, mine, other)
 
@@ -318,6 +323,7 @@
         cost_estimate=pl.CostEstimate(
             flops=6 * rank * rank * width, bytes_accessed=8 * rank * (rank + width), transcendentals=0
         ),
+        compiler_params=pltpu.CompilerParams(vmem_limit_bytes=GRANT),
         name="reduce_last",
     )(flag, inverse, mine, other, reduced)
 

time: 136 us -> 127 us (0.934)
  Pallas kernels: 35 us -> 27.7 us
  local copies, waits for them, and re-layouts: 8.43 us -> 5.06 us
  starting transfers between devices: 46.5 us -> 48.3 us
    unnamed x48 -> x12, local copies, waits for them, and re-layouts: 6.09 us -> 1.68 us
    pallas_call x2, Pallas kernels: 9.56 us -> 5.9 us  [near_step(): pl.pallas_call(functools.partial(near_kernel, len(pieces), first_slot, tu...]
    ppermute x18, starting transfers between devices: 22.6 us -> 24.7 us  [across(): lax.ppermute(value, axis, [(i, i ^ 1 << bit) for i in range(lax.axis_size...]
    ppermute x6, waiting for transfers between devices: 0.02 us -> 1.5 us  [relayed(): lax.ppermute(value, axis, [(i, t) for i, t in steps if 0 <= t < count])]
  transfers between devices with their start and end apart: 24 -> 24, of which waited for: 12 -> 14; matrix products, arithmetic and copies ran while one was open for 3% -> 3% of each run, Pallas kernels for 19% -> 18%
where the time goes in v8:
time: 127 us
  starting transfers between devices  48.3 us (38%)
  waiting for transfers between devices  42.7 us (34%)
  Pallas kernels  27.7 us (22%)
  local copies, waits for them, and re-layouts  5.06 us (4%)
  matrix products  1.39 us (1%)
    ppermute x18, waiting for transfers between devices, across(): lax.ppermute(value, axis, [(i, i ^ 1 << bit) for i in range(lax.axis_size...  41.2 us
    ppermute x18, starting transfers between devices, across(): lax.ppermute(value, axis, [(i, i ^ 1 << bit) for i in range(lax.axis_size...  24.7 us
    ppermute x6, starting transfers between devices, relayed(): lax.ppermute(value, axis, [(i, t) for i, t in steps if 0 <= t < count])  23.6 us
    pallas_call x1, Pallas kernels, factor_inverse(): pl.pallas_call(functools.partial(inverse_kernel, size), out_shape=[pltpu....  15.9 us
    pallas_call x2, Pallas kernels, near_step(): pl.pallas_call(functools.partial(near_kernel, len(pieces), first_slot, tu...  5.9 us
    slice x2, local copies, waits for them, and re-layouts, leaf_and_levels(): (later if i else probes)[i * depth:(i + 1) * depth]  3.37 us
  transfers between devices with their start and end apart: 24, of which 14 were waited for; matrix products, arithmetic and copies ran while one was open for 3% of the time, Pallas kernels for 18%

profile of v8, /device:TPU:0, one launch (start us, length us, event | category | flops | bytes accessed | tf_op | source)
XLA Modules:
  0.0 126.6 jit_solution(10051337840391806682)
XLA Ops:
  0.7 1.1 slice.18
  1.8 3.0 %collective-permute-start = (f32[128,512]{1,0:T(8,128)S(1)}, f32[128,512]{1,0:T(8,128)S(1)}, u32[]{:S(2)}, u32[]{:S(2)}) collective-permute-start(f32[128,512]{1,0:T(8,128)S(1)} %slice.18), channel_id=1, source_target_pairs={{0,2},{2,0},{4,6},{6,4},{8,10},{10,8},{12,14},{14,12},{16,18},{18,... | collective-permute-start | bytes 786440 | tf_op jit(solution)/shard_map/ppermute | solution.py:332
  4.8 2.3 %fusion = (f32[128,512]{1,0:T(8,128)S(1)}, f32[128,512]{1,0:T(8,128)}, f32[128,512]{1,0:T(8,128)}, f32[128,512]{1,0:T(8,128)}, f32[128,512]{1,0:T(8,128)}) fusion(f32[768,512]{1,0:T(8,128)} %refs_4_.1), kind=kLoop, calls=%fused_computation.5 | loop fusion | bytes 2621440 | tf_op jit(solution)/shard_map/slice | solution.py:361
  7.1 2.0 %collective-permute-start.6 = (f32[128,512]{1,0:T(8,128)}, f32[128,512]{1,0:T(8,128)}, u32[]{:S(2)}, u32[]{:S(2)}) collective-permute-start(f32[128,512]{1,0:T(8,128)} %get-tuple-element.28), channel_id=1, source_target_pairs={{0,2},{2,0},{4,6},{6,4},{8,10},{10,8},{12,14},{14,12},{16,18},{18,... | collective-permute-start | bytes 786440 | tf_op jit(solution)/shard_map/ppermute | solution.py:332
  9.1 2.0 %collective-permute-start.2 = (f32[128,512]{1,0:T(8,128)}, f32[128,512]{1,0:T(8,128)}, u32[]{:S(2)}, u32[]{:S(2)}) collective-permute-start(f32[128,512]{1,0:T(8,128)} %get-tuple-element.30), channel_id=1, source_target_pairs={{0,2},{2,0},{4,6},{6,4},{8,10},{10,8},{12,14},{14,12},{16,18},{18,... | collective-permute-start | bytes 786440 | tf_op jit(solution)/shard_map/ppermute | solution.py:332
  11.1 0.8 collective-permute-done.refs_5_
  12.0 2.0 %collective-permute-start.8 = (f32[128,512]{1,0:T(8,128)}, f32[128,512]{1,0:T(8,128)}, u32[]{:S(2)}, u32[]{:S(2)}) collective-permute-start(f32[128,512]{1,0:T(8,128)} %get-tuple-element.27), channel_id=1, source_target_pairs={{0,2},{2,0},{4,6},{6,4},{8,10},{10,8},{12,14},{14,12},{16,18},{18,... | collective-permute-start | bytes 786440 | tf_op jit(solution)/shard_map/ppermute | solution.py:332
  14.0 3.7 %collective-permute-done.9.refs_10_ = f32[128,512]{1,0:T(8,128)} collective-permute-done((f32[128,512]{1,0:T(8,128)S(1)}, f32[128,512]{1,0:T(8,128)}, u32[]{:S(2)}, u32[]{:S(2)}) %collective-permute-start.9) | collective-permute-done | bytes 262176 | tf_op jit(solution)/shard_map/ppermute | solution.py:332
  17.7 4.7 %collective-permute-start.1 = (f32[128,512]{1,0:T(8,128)S(1)}, f32[128,512]{1,0:T(8,128)}, u32[]{:S(2)}, u32[]{:S(2)}) collective-permute-start(f32[128,512]{1,0:T(8,128)S(1)} %collective-permute-done.refs_5_), channel_id=1, source_target_pairs={{0,4},{4,8},{6,2},{8,12},{10,6},{12,16},{14,10},{16,20},{18,14},{2... | collective-permute-start | bytes 786440 | tf_op jit(solution)/shard_map/ppermute | solution.py:338
  22.4 1.0 collective-permute-done.6.refs_8_
  23.3 4.0 %collective-permute-start.7 = (f32[128,512]{1,0:T(8,128)}, f32[128,512]{1,0:T(8,128)S(1)}, u32[]{:S(2)}, u32[]{:S(2)}) collective-permute-start(f32[128,512]{1,0:T(8,128)} %collective-permute-done.6.refs_8_), channel_id=1, source_target_pairs={{0,4},{4,8},{6,2},{8,12},{10,6},{12,16},{14,10},{16,20},{18,14},{2... | collective-permute-start | bytes 786440 | tf_op jit(solution)/shard_map/ppermute | solution.py:338
  27.3 1.7 %collective-permute-done.4.refs_7_ = f32[128,512]{1,0:T(8,128)} collective-permute-done((f32[128,512]{1,0:T(8,128)}, f32[128,512]{1,0:T(8,128)}, u32[]{:S(2)}, u32[]{:S(2)}) %collective-permute-start.4) | collective-permute-done | bytes 262176 | tf_op jit(solution)/shard_map/ppermute | solution.py:332
  28.9 4.0 %collective-permute-start.5 = (f32[128,512]{1,0:T(8,128)}, f32[128,512]{1,0:T(8,128)S(1)}, u32[]{:S(2)}, u32[]{:S(2)}) collective-permute-start(f32[128,512]{1,0:T(8,128)} %collective-permute-done.4.refs_7_), channel_id=1, source_target_pairs={{0,4},{4,8},{6,2},{8,12},{10,6},{12,16},{14,10},{16,20},{18,14},{2... | collective-permute-start | bytes 786440 | tf_op jit(solution)/shard_map/ppermute | solution.py:338
  32.9 1.7 %collective-permute-done.2.refs_6_ = f32[128,512]{1,0:T(8,128)} collective-permute-done((f32[128,512]{1,0:T(8,128)}, f32[128,512]{1,0:T(8,128)}, u32[]{:S(2)}, u32[]{:S(2)}) %collective-permute-start.2) | collective-permute-done | bytes 262176 | tf_op jit(solution)/shard_map/ppermute | solution.py:332
  34.6 4.0 %collective-permute-start.3 = (f32[128,512]{1,0:T(8,128)}, f32[128,512]{1,0:T(8,128)S(1)}, u32[]{:S(2)}, u32[]{:S(2)}) collective-permute-start(f32[128,512]{1,0:T(8,128)} %collective-permute-done.2.refs_6_), channel_id=1, source_target_pairs={{0,4},{4,8},{6,2},{8,12},{10,6},{12,16},{14,10},{16,20},{18,14},{2... | collective-permute-start | bytes 786440 | tf_op jit(solution)/shard_map/ppermute | solution.py:338
  38.5 0.8 collective-permute-done.8.refs_9_
  39.3 3.7 %collective-permute-start.11 = (f32[128,512]{1,0:T(8,128)}, f32[128,512]{1,0:T(8,128)S(1)}, u32[]{:S(2)}, u32[]{:S(2)}) collective-permute-start(f32[128,512]{1,0:T(8,128)} %collective-permute-done.9.refs_10_), channel_id=1, source_target_pairs={{0,4},{4,8},{6,2},{8,12},{10,6},{12,16},{14,10},{16,20},{18,14},{2... | collective-permute-start | bytes 786440 | tf_op jit(solution)/shard_map/ppermute | solution.py:338
  43.0 3.4 %collective-permute-start.10 = (f32[128,512]{1,0:T(8,128)}, f32[128,512]{1,0:T(8,128)S(1)}, u32[]{:S(2)}, u32[]{:S(2)}) collective-permute-start(f32[128,512]{1,0:T(8,128)} %collective-permute-done.8.refs_9_), channel_id=1, source_target_pairs={{0,4},{4,8},{6,2},{8,12},{10,6},{12,16},{14,10},{16,20},{18,14},{2... | collective-permute-start | bytes 786440 | tf_op jit(solution)/shard_map/ppermute | solution.py:338
  46.5 0.1 pad_add_fusion.flag_ref.core_ref
  46.6 1.7 %copy-done.1 = f32[3,3,256,256]{3,2,1,0:T(8,128)S(1)} copy-done((f32[3,3,256,256]{3,2,1,0:T(8,128)S(1)}, f32[3,3,256,256]{3,2,1,0:T(8,128)}, u32[]{:S(2)}) %copy-start.1) | copy-done | bytes 2359320
  48.3 4.2 %near_step.2.base_ref = f32[768,512]{1,0:T(8,128)S(1)} custom-call(s32[3,3]{1,0:T(4,128)S(1)} %select_add_fusion.index_ref, s32[3]{0:T(128)S(1)} %copy-done.3, s32[3]{0:T(128)S(1)} %pad_add_fusion.flag_ref.core_ref, f32[3,3,256,256]{3,2,1,0:T(8,128)S(1)} %copy-done.1, f32[768,512]{1,0:T(8,128)S(1)} %copy-done.2, f32[128,512]{1,0:T(8,128)} %collective-permute-done.1.refs_0_, ...), custom_call_target="tpu_custom_call" | custom-call | flops 1811939328 | bytes 9699328 | tf_op jit(solution)/shard_map/near_step/pallas_call | solution.py:197
  52.4 1.5 %collective-permute-done.10.refs_0_ = f32[128,512]{1,0:T(8,128)S(1)} collective-permute-done((f32[128,512]{1,0:T(8,128)}, f32[128,512]{1,0:T(8,128)S(1)}, u32[]{:S(2)}, u32[]{:S(2)}) %collective-permute-start.10) | collective-permute-done | bytes 262176 | tf_op jit(solution)/shard_map/ppermute | solution.py:338
  53.9 1.7 %near_step.3 = (f32[768,512]{1,0:T(8,128)S(1)}, f32[768,256]{1,0:T(8,128)S(1)}) custom-call(s32[3,3]{1,0:T(4,128)S(1)} %select_add_fusion.index_ref, s32[3]{0:T(128)S(1)} %copy-done.3, s32[3]{0:T(128)S(1)} %pad_add_fusion.flag_ref.core_ref, f32[3,3,256,256]{3,2,1,0:T(8,128)S(1)} %copy-done.1, f32[768,512]{1,0:T(8,128)S(1)} %near_step.2.base_ref, ...), custom_call_target="tpu_custom_call" | custom-call | flops 1811939328 | bytes 6029312 | tf_op jit(solution)/shard_map/near_step/pallas_call | solution.py:197
  55.7 0.1 collective-permute-start.12
  55.7 2.3 %collective-permute-done.12.other_ref = f32[768,256]{1,0:T(8,128)S(1)} collective-permute-done((f32[768,256]{1,0:T(8,128)S(1)}, f32[768,256]{1,0:T(8,128)S(1)}, u32[]{:S(2)}, u32[]{:S(2)}) %collective-permute-start.12) | collective-permute-done | bytes 786464 | tf_op jit(solution)/shard_map/ppermute | solution.py:332
  58.0 1.9 %leaf_products.1 = (f32[768,256]{1,0:T(8,128)S(1)}, f32[256,256]{1,0:T(8,128)S(1)}, f32[256,128]{1,0:T(8,128)S(1)}, f32[128,512]{1,0:T(8,128)S(1)}, f32[128,512]{1,0:T(8,128)S(1)}) custom-call(s32[3]{0:T(128)S(1)} %pad_add_fusion.flag_ref.core_ref, f32[768,256]{1,0:T(8,128)S(1)} %get-tuple-element.14.half_ref, ...), custom_call_target="tpu_custom_call" | custom-call | flops 905969664 | bytes 3932160 | tf_op jit(solution)/shard_map/leaf_products/pallas_call | solution.py:243
  59.9 2.4 %collective-permute-start.13 = (f32[256,128]{1,0:T(8,128)S(1)}, f32[256,128]{1,0:T(8,128)S(1)}, u32[]{:S(2)}, u32[]{:S(2)}) collective-permute-start(f32[256,128]{1,0:T(8,128)S(1)} %get-tuple-element.18), channel_id=1, source_target_pairs={{0,2},{2,0},{4,6},{6,4},{8,10},{10,8},{12,14},{14,12},{16,18},{18,... | collective-permute-start | bytes 393224 | tf_op jit(solution)/shard_map/ppermute | solution.py:332
  62.3 0.1 collective-permute-start.18
  62.4 4.3 %collective-permute-done.13 = f32[256,128]{1,0:T(8,128)S(1)} collective-permute-done((f32[256,128]{1,0:T(8,128)S(1)}, f32[256,128]{1,0:T(8,128)S(1)}, u32[]{:S(2)}, u32[]{:S(2)}) %collective-permute-start.13) | collective-permute-done | bytes 131104 | tf_op jit(solution)/shard_map/ppermute | solution.py:332
  66.7 2.9 %collective-permute-start.14 = (f32[256,128]{1,0:T(8,128)S(1)}, f32[256,128]{1,0:T(8,128)S(1)}, u32[]{:S(2)}, u32[]{:S(2)}) collective-permute-start(f32[256,128]{1,0:T(8,128)S(1)} %add.34), channel_id=1, source_target_pairs={{0,4},{2,6},{4,0},{6,2},{8,12},{10,14},{12,8},{14,10},{16,20},{18,... | collective-permute-start | bytes 393224 | tf_op jit(solution)/shard_map/ppermute | solution.py:332
  69.6 2.9 %collective-permute-done.14 = f32[256,128]{1,0:T(8,128)S(1)} collective-permute-done((f32[256,128]{1,0:T(8,128)S(1)}, f32[256,128]{1,0:T(8,128)S(1)}, u32[]{:S(2)}, u32[]{:S(2)}) %collective-permute-start.14) | collective-permute-done | bytes 131104 | tf_op jit(solution)/shard_map/ppermute | solution.py:332
  72.6 2.1 %collective-permute-start.19 = (f32[128,512]{1,0:T(8,128)S(1)}, f32[128,512]{1,0:T(8,128)S(1)}, u32[]{:S(2)}, u32[]{:S(2)}) collective-permute-start(f32[128,512]{1,0:T(8,128)S(1)} %add.38), channel_id=1, source_target_pairs={{0,4},{2,6},{4,0},{6,2},{8,12},{10,14},{12,8},{14,10},{16,20},{18,... | collective-permute-start | bytes 786440 | tf_op jit(solution)/shard_map/ppermute | solution.py:332
  74.7 1.2 collective-permute-start.15
  75.9 3.8 %collective-permute-done.15 = f32[256,128]{1,0:T(8,128)S(1)} collective-permute-done((f32[256,128]{1,0:T(8,128)S(1)}, f32[256,128]{1,0:T(8,128)S(1)}, u32[]{:S(2)}, u32[]{:S(2)}) %collective-permute-start.15) | collective-permute-done | bytes 131104 | tf_op jit(solution)/shard_map/ppermute | solution.py:332
  79.7 2.7 %collective-permute-start.16 = (f32[256,128]{1,0:T(8,128)S(1)}, f32[256,128]{1,0:T(8,128)S(1)}, u32[]{:S(2)}, u32[]{:S(2)}) collective-permute-start(f32[256,128]{1,0:T(8,128)S(1)} %add.36), channel_id=1, source_target_pairs={{0,16},{2,18},{4,20},{6,22},{8,24},{10,26},{12,28},{14,30},{16,0},... | collective-permute-start | bytes 393224 | tf_op jit(solution)/shard_map/ppermute | solution.py:332
  82.4 1.3 %collective-permute-start.20 = (f32[128,512]{1,0:T(8,128)S(1)}, f32[128,512]{1,0:T(8,128)S(1)}, u32[]{:S(2)}, u32[]{:S(2)}) collective-permute-start(f32[128,512]{1,0:T(8,128)S(1)} %add.39), channel_id=1, source_target_pairs={{0,8},{2,10},{4,12},{6,14},{8,0},{10,2},{12,4},{14,6},{16,24},{18,... | collective-permute-start | bytes 786440 | tf_op jit(solution)/shard_map/ppermute | solution.py:332
  83.6 3.2 %collective-permute-done.16 = f32[256,128]{1,0:T(8,128)S(1)} collective-permute-done((f32[256,128]{1,0:T(8,128)S(1)}, f32[256,128]{1,0:T(8,128)S(1)}, u32[]{:S(2)}, u32[]{:S(2)}) %collective-permute-start.16) | collective-permute-done | bytes 131104 | tf_op jit(solution)/shard_map/ppermute | solution.py:332
  86.9 0.1 collective-permute-start.17
  87.0 4.1 %collective-permute-done.20 = f32[128,512]{1,0:T(8,128)S(1)} collective-permute-done((f32[128,512]{1,0:T(8,128)S(1)}, f32[128,512]{1,0:T(8,128)S(1)}, u32[]{:S(2)}, u32[]{:S(2)}) %collective-permute-start.20) | collective-permute-done | bytes 262176 | tf_op jit(solution)/shard_map/ppermute | solution.py:332
  91.1 0.3 collective-permute-start.21
  91.4 0.1 pad_maximum_fusion.refs_3_
  91.5 1.6 %collective-permute-start.23 = (f32[3,128,512]{2,1,0:T(8,128)S(1)}, f32[3,128,512]{2,1,0:T(8,128)S(1)}, u32[]{:S(2)}, u32[]{:S(2)}) collective-permute-start(f32[3,128,512]{2,1,0:T(8,128)S(1)} %pad_maximum_fusion.refs_3_), channel_id=1, source_target_pairs={{0,2},{2,0},{4,6},{6,4},{8,10},{10,8},{12,14},{14,12},{16,18},{18,... | collective-permute-start | bytes 2359304 | tf_op jit(solution)/shard_map/ppermute | solution.py:332
  93.1 11.0 %collective-permute-done.21 = f32[128,512]{1,0:T(8,128)S(1)} collective-permute-done((f32[128,512]{1,0:T(8,128)S(1)}, f32[128,512]{1,0:T(8,128)S(1)}, u32[]{:S(2)}, u32[]{:S(2)}) %collective-permute-start.21) | collective-permute-done | bytes 262176 | tf_op jit(solution)/shard_map/ppermute | solution.py:332
  104.1 1.0 collective-permute-start.22
  105.1 15.9 %factor_inverse.1 = (f32[256,256]{1,0:T(8,128)S(1)}, f32[256,256]{1,0:T(8,128)S(1)}, f32[256,256]{1,0:T(8,128)S(1)}, f32[256,256]{1,0:T(8,128)S(1)}, f32[256,256]{1,0:T(8,128)S(1)}) custom-call(s32[3]{0:T(128)S(1)} %pad_add_fusion.flag_ref.core_ref, f32[256,256]{1,0:T(8,128)S(1)} %get-tuple-element.17.gram_ref, ...), custom_call_target="tpu_custom_call" | custom-call | flops 15000000512 | bytes 2621440 | tf_op jit(solution)/shard_map/factor_inverse/pallas_call | solution.py:145
  121.0 1.4 %fusion.1 = f32[768,256]{1,0:T(8,128)} fusion(f32[768,256]{1,0:T(8,128)S(1)} %get-tuple-element.16, f32[256,256]{1,0:T(8,128)S(1)} %get-tuple-element.19), kind=kOutput, calls=%fused_computation.6 | convolution fusion | flops 301989888 | bytes 1835008 | tf_op jit(solution)/shard_map/dot_general | solution.py:383
  122.4 2.2 %reduce_early.1.kept_ref = f32[4,1,256,512]{3,2,1,0:T(8,128)} custom-call(s32[3]{0:T(128)S(1)} %pad_add_fusion.flag_ref.core_ref, f32[256,256]{1,0:T(8,128)S(1)} %get-tuple-element.23.refs_0_, f32[256,256]{1,0:T(8,128)S(1)} %get-tuple-element.24.refs_1_, f32[256,256]{1,0:T(8,128)S(1)} %get-tuple-element.25.refs_2_, ...), custom_call_target="tpu_custom_call" | custom-call | flops 603979776 | bytes 4718592 | tf_op jit(solution)/shard_map/reduce_early/pallas_call | solution.py:282
  124.6 1.8 %reduce_last.1 = f32[4,1,256,512]{3,2,1,0:T(8,128)} custom-call(s32[3]{0:T(128)S(1)} %pad_add_fusion.flag_ref.core_ref, f32[256,256]{1,0:T(8,128)S(1)} %get-tuple-element.20.inverse_ref, f32[128,512]{1,0:T(8,128)S(1)} %add.41.mine_ref, f32[128,512]{1,0:T(8,128)S(1)} %collective-permute-done.22.other_ref, ...), custom_call_target="tpu_custom_call", output_to_operand_aliasing={{}: (4, {})} | custom-call | flops 201326592 | bytes 1572864 | tf_op jit(solution)/shard_map/reduce_last/pallas_call | solution.py:312
  (33 shorter events, 0.4 us)
Async XLA Ops:
  0.6 45.9 %copy-start = (f32[768,512]{1,0:T(8,128)S(1)}, f32[768,512]{1,0:T(8,128)}, u32[]{:S(2)}) copy-start(f32[768,512]{1,0:T(8,128)} %refs_4_.1) | copy-start | bytes 4718596
  0.6 37.9 %copy-start.5 = (s32[3,3]{1,0:T(4,128)S(1)}, s32[3,3]{1,0:T(4,128)}, u32[]{:S(2)}) copy-start(s32[3,3]{1,0:T(4,128)} %param.9) | copy-start | bytes 112
  0.7 45.9 %copy-start.3 = (s32[3]{0:T(128)S(1)}, s32[3]{0:T(128)}, u32[]{:S(2)}) copy-start(s32[3]{0:T(128)} %count_ref.3) | copy-start | bytes 40
  0.7 45.9 %copy-start.2 = (f32[768,512]{1,0:T(8,128)S(1)}, f32[768,512]{1,0:T(8,128)}, u32[]{:S(2)}) copy-start(f32[768,512]{1,0:T(8,128)} %base_ref.1) | copy-start | bytes 4718596
  1.8 10.2 %collective-permute-start = (f32[128,512]{1,0:T(8,128)S(1)}, f32[128,512]{1,0:T(8,128)S(1)}, u32[]{:S(2)}, u32[]{:S(2)}) collective-permute-start(f32[128,512]{1,0:T(8,128)S(1)} %slice.18), channel_id=1, source_target_pairs={{0,2},{2,0},{4,6},{6,4},{8,10},{10,8},{12,14},{14,12},{16,18},{18,... | collective-permute-start | bytes 786440 | tf_op jit(solution)/shard_map/ppermute | solution.py:332
  7.1 10.6 %collective-permute-start.9 = (f32[128,512]{1,0:T(8,128)S(1)}, f32[128,512]{1,0:T(8,128)}, u32[]{:S(2)}, u32[]{:S(2)}) collective-permute-start(f32[128,512]{1,0:T(8,128)S(1)} %get-tuple-element.26), channel_id=1, source_target_pairs={{0,2},{2,0},{4,6},{6,4},{8,10},{10,8},{12,14},{14,12},{16,18},{18,... | collective-permute-start | bytes 786440 | tf_op jit(solution)/shard_map/ppermute | solution.py:332
  7.1 16.2 %collective-permute-start.6 = (f32[128,512]{1,0:T(8,128)}, f32[128,512]{1,0:T(8,128)}, u32[]{:S(2)}, u32[]{:S(2)}) collective-permute-start(f32[128,512]{1,0:T(8,128)} %get-tuple-element.28), channel_id=1, source_target_pairs={{0,2},{2,0},{4,6},{6,4},{8,10},{10,8},{12,14},{14,12},{16,18},{18,... | collective-permute-start | bytes 786440 | tf_op jit(solution)/shard_map/ppermute | solution.py:332
  9.1 19.8 %collective-permute-start.4 = (f32[128,512]{1,0:T(8,128)}, f32[128,512]{1,0:T(8,128)}, u32[]{:S(2)}, u32[]{:S(2)}) collective-permute-start(f32[128,512]{1,0:T(8,128)} %get-tuple-element.29), channel_id=1, source_target_pairs={{0,2},{2,0},{4,6},{6,4},{8,10},{10,8},{12,14},{14,12},{16,18},{18,... | collective-permute-start | bytes 786440 | tf_op jit(solution)/shard_map/ppermute | solution.py:332
  9.1 25.4 %collective-permute-start.2 = (f32[128,512]{1,0:T(8,128)}, f32[128,512]{1,0:T(8,128)}, u32[]{:S(2)}, u32[]{:S(2)}) collective-permute-start(f32[128,512]{1,0:T(8,128)} %get-tuple-element.30), channel_id=1, source_target_pairs={{0,2},{2,0},{4,6},{6,4},{8,10},{10,8},{12,14},{14,12},{16,18},{18,... | collective-permute-start | bytes 786440 | tf_op jit(solution)/shard_map/ppermute | solution.py:332
  12.0 27.3 %collective-permute-start.8 = (f32[128,512]{1,0:T(8,128)}, f32[128,512]{1,0:T(8,128)}, u32[]{:S(2)}, u32[]{:S(2)}) collective-permute-start(f32[128,512]{1,0:T(8,128)} %get-tuple-element.27), channel_id=1, source_target_pairs={{0,2},{2,0},{4,6},{6,4},{8,10},{10,8},{12,14},{14,12},{16,18},{18,... | collective-permute-start | bytes 786440 | tf_op jit(solution)/shard_map/ppermute | solution.py:332
  17.7 25.3 %collective-permute-start.1 = (f32[128,512]{1,0:T(8,128)S(1)}, f32[128,512]{1,0:T(8,128)}, u32[]{:S(2)}, u32[]{:S(2)}) collective-permute-start(f32[128,512]{1,0:T(8,128)S(1)} %collective-permute-done.refs_5_), channel_id=1, source_target_pairs={{0,4},{4,8},{6,2},{8,12},{10,6},{12,16},{14,10},{16,20},{18,14},{2... | collective-permute-start | bytes 786440 | tf_op jit(solution)/shard_map/ppermute | solution.py:338
  23.3 23.2 %collective-permute-start.7 = (f32[128,512]{1,0:T(8,128)}, f32[128,512]{1,0:T(8,128)S(1)}, u32[]{:S(2)}, u32[]{:S(2)}) collective-permute-start(f32[128,512]{1,0:T(8,128)} %collective-permute-done.6.refs_8_), channel_id=1, source_target_pairs={{0,4},{4,8},{6,2},{8,12},{10,6},{12,16},{14,10},{16,20},{18,14},{2... | collective-permute-start | bytes 786440 | tf_op jit(solution)/shard_map/ppermute | solution.py:338
  28.9 17.6 %collective-permute-start.5 = (f32[128,512]{1,0:T(8,128)}, f32[128,512]{1,0:T(8,128)S(1)}, u32[]{:S(2)}, u32[]{:S(2)}) collective-permute-start(f32[128,512]{1,0:T(8,128)} %collective-permute-done.4.refs_7_), channel_id=1, source_target_pairs={{0,4},{4,8},{6,2},{8,12},{10,6},{12,16},{14,10},{16,20},{18,14},{2... | collective-permute-start | bytes 786440 | tf_op jit(solution)/shard_map/ppermute | solution.py:338
  34.6 12.0 %collective-permute-start.3 = (f32[128,512]{1,0:T(8,128)}, f32[128,512]{1,0:T(8,128)S(1)}, u32[]{:S(2)}, u32[]{:S(2)}) collective-permute-start(f32[128,512]{1,0:T(8,128)} %collective-permute-done.2.refs_6_), channel_id=1, source_target_pairs={{0,4},{4,8},{6,2},{8,12},{10,6},{12,16},{14,10},{16,20},{18,14},{2... | collective-permute-start | bytes 786440 | tf_op jit(solution)/shard_map/ppermute | solution.py:338
  39.3 13.1 %collective-permute-start.11 = (f32[128,512]{1,0:T(8,128)}, f32[128,512]{1,0:T(8,128)S(1)}, u32[]{:S(2)}, u32[]{:S(2)}) collective-permute-start(f32[128,512]{1,0:T(8,128)} %collective-permute-done.9.refs_10_), channel_id=1, source_target_pairs={{0,4},{4,8},{6,2},{8,12},{10,6},{12,16},{14,10},{16,20},{18,14},{2... | collective-permute-start | bytes 786440 | tf_op jit(solution)/shard_map/ppermute | solution.py:338
  43.0 10.9 %collective-permute-start.10 = (f32[128,512]{1,0:T(8,128)}, f32[128,512]{1,0:T(8,128)S(1)}, u32[]{:S(2)}, u32[]{:S(2)}) collective-permute-start(f32[128,512]{1,0:T(8,128)} %collective-permute-done.8.refs_9_), channel_id=1, source_target_pairs={{0,4},{4,8},{6,2},{8,12},{10,6},{12,16},{14,10},{16,20},{18,14},{2... | collective-permute-start | bytes 786440 | tf_op jit(solution)/shard_map/ppermute | solution.py:338
  46.6 1.7 %copy-start.1 = (f32[3,3,256,256]{3,2,1,0:T(8,128)S(1)}, f32[3,3,256,256]{3,2,1,0:T(8,128)}, u32[]{:S(2)}) copy-start(f32[3,3,256,256]{3,2,1,0:T(8,128)} %blocks_ref.3) | copy-start | bytes 7077892
  48.2 5.7 %copy-start.4 = (f32[512,256]{1,0:T(8,128)S(1)}, f32[512,256]{1,0:T(8,128)}, u32[]{:S(2)}) copy-start(f32[512,256]{1,0:T(8,128)} %refs_2_.1) | copy-start | bytes 1572868
  55.7 2.4 %collective-permute-start.12 = (f32[768,256]{1,0:T(8,128)S(1)}, f32[768,256]{1,0:T(8,128)S(1)}, u32[]{:S(2)}, u32[]{:S(2)}) collective-permute-start(f32[768,256]{1,0:T(8,128)S(1)} %get-tuple-element.14.half_ref), channel_id=1, source_target_pairs={{0,1},{1,0},{2,3},{3,2},{4,5},{5,4},{6,7},{7,6},{8,9},{9,8},{10,11... | collective-permute-start | bytes 2359304 | tf_op jit(solution)/shard_map/ppermute | solution.py:332
  59.9 6.8 %collective-permute-start.13 = (f32[256,128]{1,0:T(8,128)S(1)}, f32[256,128]{1,0:T(8,128)S(1)}, u32[]{:S(2)}, u32[]{:S(2)}) collective-permute-start(f32[256,128]{1,0:T(8,128)S(1)} %get-tuple-element.18), channel_id=1, source_target_pairs={{0,2},{2,0},{4,6},{6,4},{8,10},{10,8},{12,14},{14,12},{16,18},{18,... | collective-permute-start | bytes 393224 | tf_op jit(solution)/shard_map/ppermute | solution.py:332
  62.3 10.2 %collective-permute-start.18 = (f32[128,512]{1,0:T(8,128)S(1)}, f32[128,512]{1,0:T(8,128)S(1)}, u32[]{:S(2)}, u32[]{:S(2)}) collective-permute-start(f32[128,512]{1,0:T(8,128)S(1)} %get-tuple-element.22), channel_id=1, source_target_pairs={{0,2},{2,0},{4,6},{6,4},{8,10},{10,8},{12,14},{14,12},{16,18},{18,... | collective-permute-start | bytes 786440 | tf_op jit(solution)/shard_map/ppermute | solution.py:332
  66.7 5.8 %collective-permute-start.14 = (f32[256,128]{1,0:T(8,128)S(1)}, f32[256,128]{1,0:T(8,128)S(1)}, u32[]{:S(2)}, u32[]{:S(2)}) collective-permute-start(f32[256,128]{1,0:T(8,128)S(1)} %add.34), channel_id=1, source_target_pairs={{0,4},{2,6},{4,0},{6,2},{8,12},{10,14},{12,8},{14,10},{16,20},{18,... | collective-permute-start | bytes 393224 | tf_op jit(solution)/shard_map/ppermute | solution.py:332
  72.6 9.7 %collective-permute-start.19 = (f32[128,512]{1,0:T(8,128)S(1)}, f32[128,512]{1,0:T(8,128)S(1)}, u32[]{:S(2)}, u32[]{:S(2)}) collective-permute-start(f32[128,512]{1,0:T(8,128)S(1)} %add.38), channel_id=1, source_target_pairs={{0,4},{2,6},{4,0},{6,2},{8,12},{10,14},{12,8},{14,10},{16,20},{18,... | collective-permute-start | bytes 786440 | tf_op jit(solution)/shard_map/ppermute | solution.py:332
  74.7 5.0 %collective-permute-start.15 = (f32[256,128]{1,0:T(8,128)S(1)}, f32[256,128]{1,0:T(8,128)S(1)}, u32[]{:S(2)}, u32[]{:S(2)}) collective-permute-start(f32[256,128]{1,0:T(8,128)S(1)} %add.35), channel_id=1, source_target_pairs={{0,8},{2,10},{4,12},{6,14},{8,0},{10,2},{12,4},{14,6},{16,24},{18,... | collective-permute-start | bytes 393224 | tf_op jit(solution)/shard_map/ppermute | solution.py:332
  79.7 7.2 %collective-permute-start.16 = (f32[256,128]{1,0:T(8,128)S(1)}, f32[256,128]{1,0:T(8,128)S(1)}, u32[]{:S(2)}, u32[]{:S(2)}) collective-permute-start(f32[256,128]{1,0:T(8,128)S(1)} %add.36), channel_id=1, source_target_pairs={{0,16},{2,18},{4,20},{6,22},{8,24},{10,26},{12,28},{14,30},{16,0},... | collective-permute-start | bytes 393224 | tf_op jit(solution)/shard_map/ppermute | solution.py:332
  82.4 8.7 %collective-permute-start.20 = (f32[128,512]{1,0:T(8,128)S(1)}, f32[128,512]{1,0:T(8,128)S(1)}, u32[]{:S(2)}, u32[]{:S(2)}) collective-permute-start(f32[128,512]{1,0:T(8,128)S(1)} %add.39), channel_id=1, source_target_pairs={{0,8},{2,10},{4,12},{6,14},{8,0},{10,2},{12,4},{14,6},{16,24},{18,... | collective-permute-start | bytes 786440 | tf_op jit(solution)/shard_map/ppermute | solution.py:332
  86.9 18.2 %collective-permute-start.17 = (f32[4,256,128]{2,1,0:T(8,128)S(1)}, f32[4,256,128]{2,1,0:T(8,128)S(1)}, u32[]{:S(2)}, u32[]{:S(2)}) collective-permute-start(f32[4,256,128]{2,1,0:T(8,128)S(1)} %pad_maximum_fusion.1.mine_ref), channel_id=1, source_target_pairs={{0,1},{1,0},{2,3},{3,2},{4,5},{5,4},{6,7},{7,6},{8,9},{9,8},{10,11... | collective-permute-start | bytes 1572872 | tf_op jit(solution)/shard_map/ppermute | solution.py:332
  91.1 12.9 %collective-permute-start.21 = (f32[128,512]{1,0:T(8,128)S(1)}, f32[128,512]{1,0:T(8,128)S(1)}, u32[]{:S(2)}, u32[]{:S(2)}) collective-permute-start(f32[128,512]{1,0:T(8,128)S(1)} %add.40), channel_id=1, source_target_pairs={{0,16},{2,18},{4,20},{6,22},{8,24},{10,26},{12,28},{14,30},{16,0},... | collective-permute-start | bytes 786440 | tf_op jit(solution)/shard_map/ppermute | solution.py:332
  91.5 30.9 %collective-permute-start.23 = (f32[3,128,512]{2,1,0:T(8,128)S(1)}, f32[3,128,512]{2,1,0:T(8,128)S(1)}, u32[]{:S(2)}, u32[]{:S(2)}) collective-permute-start(f32[3,128,512]{2,1,0:T(8,128)S(1)} %pad_maximum_fusion.refs_3_), channel_id=1, source_target_pairs={{0,2},{2,0},{4,6},{6,4},{8,10},{10,8},{12,14},{14,12},{16,18},{18,... | collective-permute-start | bytes 2359304 | tf_op jit(solution)/shard_map/ppermute | solution.py:332
  104.1 20.5 %collective-permute-start.22 = (f32[128,512]{1,0:T(8,128)S(1)}, f32[128,512]{1,0:T(8,128)S(1)}, u32[]{:S(2)}, u32[]{:S(2)}) collective-permute-start(f32[128,512]{1,0:T(8,128)S(1)} %add.41.mine_ref), channel_id=1, source_target_pairs={{0,2},{2,0},{4,6},{6,4},{8,10},{10,8},{12,14},{14,12},{16,18},{18,... | collective-permute-start | bytes 786440 | tf_op jit(solution)/shard_map/ppermute | solution.py:332

commit v9 on v8

--- a/solution.py
+++ b/solution.py
@@ -154,21 +154,30 @@
     )(core, gram, mine, other)
 
 
-def near_kernel(groups, first_slot, spots, sketched, index_ref, count_ref, flag_ref, blocks_ref, base_ref, *refs):
+def near_kernel(groups, first_slot, spots, sketched, loads, index_ref, count_ref, flag_ref, blocks_ref, base_ref, *refs):
     pieces = refs[:groups]
     sketch_ref = refs[groups] if sketched else None
     rest = refs[groups + sketched :]
-    out_ref, ext = rest[0], rest[-1]
+    out_ref, ext = rest[0], rest[-2] if loads else rest[-1]
     block_count, slot_count, size, _ = blocks_ref.shape
+    held = rest[1] if loads else blocks_ref
+    copies = {}
+    if loads:
+        for j in range(slot_count):
+            for b in range(block_count):
+                copies[b, j] = pltpu.make_async_copy(blocks_ref.at[b, j], held.at[b, j], rest[-1].at[b, j])
+                copies[b, j].start()
     at = 0
     for g in range(groups):
         depth = pieces[g].shape[0]
         ext[at : at + depth, :] = pieces[g][...]
         at += depth
     out_ref[...] = base_ref[...]
-    for b in range(block_count):
-        rows = pl.ds(b * size, size)
-        for j in range(first_slot, slot_count):
+    for j in range(first_slot, slot_count):
+        for b in range(block_count):
+            rows = pl.ds(b * size, size)
+            if loads:
+                copies[b, j].wait()
             spot = index_ref[b, j]
             start = jnp.int32(0)
             here = jnp.bool_(False)
@@ -180,26 +189,30 @@
             @pl.when(here & (j < count_ref[b]))
             def _(b=b, j=j, rows=rows, start=start):
                 piece = ext[pl.ds(pl.multiple_of(start, size), size), :]
-                out_ref[rows, :] -= dot3(blocks_ref[b, j], piece, NN)
+                out_ref[rows, :] -= dot3(held[b, j], piece, NN)
 
     if sketched:
         rest[1][...] = dot3(out_ref[...], sketch_ref[...], NN)
 
 
-def near_step(blocks, base, pieces, spots, index, count, flag, first_slot, sketch=None):
+def near_step(blocks, base, pieces, spots, index, count, flag, first_slot, sketch=None, loads=False):
     block_count, slot_count, size, _ = blocks.shape
     rows, width = base.shape
     total = sum(piece.shape[0] for piece in pieces)
     vmem = pl.BlockSpec(memory_space=pltpu.VMEM)
     smem = pl.BlockSpec(memory_space=pltpu.SMEM)
     extra = [] if sketch is None else [sketch]
-    shapes = [(rows, width)] + [(rows, value.shape[1]) for value in extra]
+    shapes = [(rows, width)] + [(rows, value.shape[1]) for value in extra] + [blocks.shape] * loads
+    source = pl.BlockSpec(memory_space=pltpu.HBM) if loads else vmem
+    scratch = [pltpu.VMEM((total, width), jnp.float32)]
+    if loads:
+        scratch.append(pltpu.SemaphoreType.DMA((block_count, slot_count)))
     return pl.pallas_call(
-        functools.partial(near_kernel, len(pieces), first_slot, tuple(spots), len(extra)),
+        functools.partial(near_kernel, len(pieces), first_slot, tuple(spots), len(extra), loads),
         out_shape=[pltpu.VMEM(shape, jnp.float32) for shape in shapes],
-        in_specs=[smem] * 3 + [vmem] * (2 + len(pieces) + len(extra)),
+        in_specs=[smem] * 3 + [source] + [vmem] * (1 + len(pieces) + len(extra)),
         out_specs=[vmem] * len(shapes),
-        scratch_shapes=[pltpu.VMEM((total, width), jnp.float32)],
+        scratch_shapes=scratch,
         cost_estimate=pl.CostEstimate(
             flops=6 * block_count * slot_count * size * size * width,
             bytes_accessed=4 * (total * width + 2 * rows * width + blocks.size),
@@ -364,9 +377,11 @@
 
     early = (block_count - 1) * SPLIT
     spots = [*range(block_count - 1), *range(block_count, 3 * block_count)]
-    (left,) = near_step(near_blocks, samples, far[:early] + [probes] + peer, spots, index, near_count, flag, 0)
+    pieces = far[:early] + [probes] + peer
+    stored = pltpu.with_memory_space_constraint(near_blocks, pltpu.HBM)
+    left, held = near_step(stored, samples, pieces, spots, index, near_count, flag, 0, loads=True)
     spots = [block_count - 1]
-    far_samples, partial = near_step(near_blocks, left, far[early:], spots, index, near_count, flag, 1, sketch)
+    far_samples, partial = near_step(held, left, far[early:], spots, index, near_count, flag, 1, sketch)
     if halves == 2:
         other = across(partial, "samp", 0)
     else:

time: 127 us -> 128 us (level)
  waiting for transfers between devices: 42.7 us -> 45.2 us
  local copies, waits for them, and re-layouts: 5.06 us -> 3.08 us
    unnamed x12 -> x10, local copies, waits for them, and re-layouts: 1.68 us -> 0.02 us
    ppermute x18, waiting for transfers between devices: 41.2 us -> 42.7 us  [across(): lax.ppermute(value, axis, [(i, i ^ 1 << bit) for i in range(lax.axis_size...]
  transfers between devices with their start and end apart: 24 -> 24, of which waited for: 14 -> 14; matrix products, arithmetic and copies ran while one was open for 3% -> 2% of each run, Pallas kernels for 18% -> 18%
where the time goes in v9:
time: 128 us
  starting transfers between devices  48.3 us (38%)
  waiting for transfers between devices  45.2 us (35%)
  Pallas kernels  28.3 us (22%)
  local copies, waits for them, and re-layouts  3.08 us (2%)
  matrix products  1.39 us (1%)
    ppermute x18, waiting for transfers between devices, across(): lax.ppermute(value, axis, [(i, i ^ 1 << bit) for i in range(lax.axis_size...  42.7 us
    ppermute x18, starting transfers between devices, across(): lax.ppermute(value, axis, [(i, i ^ 1 << bit) for i in range(lax.axis_size...  24.6 us
    ppermute x6, starting transfers between devices, relayed(): lax.ppermute(value, axis, [(i, t) for i, t in steps if 0 <= t < count])  23.6 us
    pallas_call x1, Pallas kernels, factor_inverse(): pl.pallas_call(functools.partial(inverse_kernel, size), out_shape=[pltpu....  15.9 us
    pallas_call x2, Pallas kernels, near_step(): pl.pallas_call(functools.partial(near_kernel, len(pieces), first_slot, tu...  6.56 us
    slice x2, local copies, waits for them, and re-layouts, leaf_and_levels(): (later if i else probes)[i * depth:(i + 1) * depth]  3.06 us
  transfers between devices with their start and end apart: 24, of which 14 were waited for; matrix products, arithmetic and copies ran while one was open for 2% of the time, Pallas kernels for 18%

profile of v9, /device:TPU:0, one launch (start us, length us, event | category | flops | bytes accessed | tf_op | source)
XLA Modules:
  0.0 127.7 jit_solution(11181323252351821548)
XLA Ops:
  0.7 2.3 %fusion = (f32[128,512]{1,0:T(8,128)}, f32[128,512]{1,0:T(8,128)}, f32[128,512]{1,0:T(8,128)}, f32[128,512]{1,0:T(8,128)S(1)}, f32[128,512]{1,0:T(8,128)S(1)}) fusion(f32[768,512]{1,0:T(8,128)} %refs_4_.1), kind=kLoop, calls=%fused_computation.5 | loop fusion | bytes 2621440 | tf_op jit(solution)/shard_map/slice | solution.py:374
  3.0 3.0 %collective-permute-start.2 = (f32[128,512]{1,0:T(8,128)S(1)}, f32[128,512]{1,0:T(8,128)S(1)}, u32[]{:S(2)}, u32[]{:S(2)}) collective-permute-start(f32[128,512]{1,0:T(8,128)S(1)} %get-tuple-element.34), channel_id=1, source_target_pairs={{0,2},{2,0},{4,6},{6,4},{8,10},{10,8},{12,14},{14,12},{16,18},{18,... | collective-permute-start | bytes 786440 | tf_op jit(solution)/shard_map/ppermute | solution.py:345
  6.0 0.0 collective-permute-start.4
  6.0 2.0 %collective-permute-start.6 = (f32[128,512]{1,0:T(8,128)}, f32[128,512]{1,0:T(8,128)}, u32[]{:S(2)}, u32[]{:S(2)}) collective-permute-start(f32[128,512]{1,0:T(8,128)} %get-tuple-element.32), channel_id=1, source_target_pairs={{0,2},{2,0},{4,6},{6,4},{8,10},{10,8},{12,14},{14,12},{16,18},{18,... | collective-permute-start | bytes 786440 | tf_op jit(solution)/shard_map/ppermute | solution.py:345
  8.0 0.7 slice.18
  8.8 2.0 %collective-permute-start = (f32[128,512]{1,0:T(8,128)}, f32[128,512]{1,0:T(8,128)}, u32[]{:S(2)}, u32[]{:S(2)}) collective-permute-start(f32[128,512]{1,0:T(8,128)} %slice.18), channel_id=1, source_target_pairs={{0,2},{2,0},{4,6},{6,4},{8,10},{10,8},{12,14},{14,12},{16,18},{18,... | collective-permute-start | bytes 786440 | tf_op jit(solution)/shard_map/ppermute | solution.py:345
  10.8 2.4 %collective-permute-done.2.refs_6_ = f32[128,512]{1,0:T(8,128)S(1)} collective-permute-done((f32[128,512]{1,0:T(8,128)S(1)}, f32[128,512]{1,0:T(8,128)S(1)}, u32[]{:S(2)}, u32[]{:S(2)}) %collective-permute-start.2) | collective-permute-done | bytes 262176 | tf_op jit(solution)/shard_map/ppermute | solution.py:345
  13.1 2.0 %collective-permute-start.9 = (f32[128,512]{1,0:T(8,128)}, f32[128,512]{1,0:T(8,128)}, u32[]{:S(2)}, u32[]{:S(2)}) collective-permute-start(f32[128,512]{1,0:T(8,128)} %get-tuple-element.30), channel_id=1, source_target_pairs={{0,2},{2,0},{4,6},{6,4},{8,10},{10,8},{12,14},{14,12},{16,18},{18,... | collective-permute-start | bytes 786440 | tf_op jit(solution)/shard_map/ppermute | solution.py:345
  15.2 3.7 %collective-permute-done.4.refs_7_ = f32[128,512]{1,0:T(8,128)} collective-permute-done((f32[128,512]{1,0:T(8,128)S(1)}, f32[128,512]{1,0:T(8,128)}, u32[]{:S(2)}, u32[]{:S(2)}) %collective-permute-start.4) | collective-permute-done | bytes 262176 | tf_op jit(solution)/shard_map/ppermute | solution.py:345
  18.9 4.7 %collective-permute-start.3 = (f32[128,512]{1,0:T(8,128)S(1)}, f32[128,512]{1,0:T(8,128)}, u32[]{:S(2)}, u32[]{:S(2)}) collective-permute-start(f32[128,512]{1,0:T(8,128)S(1)} %collective-permute-done.2.refs_6_), channel_id=1, source_target_pairs={{0,4},{4,8},{6,2},{8,12},{10,6},{12,16},{14,10},{16,20},{18,14},{2... | collective-permute-start | bytes 786440 | tf_op jit(solution)/shard_map/ppermute | solution.py:351
  23.5 1.0 collective-permute-done.6.refs_8_
  24.5 4.0 %collective-permute-start.5 = (f32[128,512]{1,0:T(8,128)}, f32[128,512]{1,0:T(8,128)S(1)}, u32[]{:S(2)}, u32[]{:S(2)}) collective-permute-start(f32[128,512]{1,0:T(8,128)} %collective-permute-done.4.refs_7_), channel_id=1, source_target_pairs={{0,4},{4,8},{6,2},{8,12},{10,6},{12,16},{14,10},{16,20},{18,14},{2... | collective-permute-start | bytes 786440 | tf_op jit(solution)/shard_map/ppermute | solution.py:351
  28.4 1.6 %collective-permute-done.8.refs_9_ = f32[128,512]{1,0:T(8,128)} collective-permute-done((f32[128,512]{1,0:T(8,128)}, f32[128,512]{1,0:T(8,128)}, u32[]{:S(2)}, u32[]{:S(2)}) %collective-permute-start.8) | collective-permute-done | bytes 262176 | tf_op jit(solution)/shard_map/ppermute | solution.py:345
  30.1 4.0 %collective-permute-start.7 = (f32[128,512]{1,0:T(8,128)}, f32[128,512]{1,0:T(8,128)S(1)}, u32[]{:S(2)}, u32[]{:S(2)}) collective-permute-start(f32[128,512]{1,0:T(8,128)} %collective-permute-done.6.refs_8_), channel_id=1, source_target_pairs={{0,4},{4,8},{6,2},{8,12},{10,6},{12,16},{14,10},{16,20},{18,14},{2... | collective-permute-start | bytes 786440 | tf_op jit(solution)/shard_map/ppermute | solution.py:351
  34.1 1.6 %collective-permute-done.refs_5_ = f32[128,512]{1,0:T(8,128)} collective-permute-done((f32[128,512]{1,0:T(8,128)}, f32[128,512]{1,0:T(8,128)}, u32[]{:S(2)}, u32[]{:S(2)}) %collective-permute-start) | collective-permute-done | bytes 262176 | tf_op jit(solution)/shard_map/ppermute | solution.py:345
  35.7 4.0 %collective-permute-start.1 = (f32[128,512]{1,0:T(8,128)}, f32[128,512]{1,0:T(8,128)S(1)}, u32[]{:S(2)}, u32[]{:S(2)}) collective-permute-start(f32[128,512]{1,0:T(8,128)} %collective-permute-done.refs_5_), channel_id=1, source_target_pairs={{0,4},{4,8},{6,2},{8,12},{10,6},{12,16},{14,10},{16,20},{18,14},{2... | collective-permute-start | bytes 786440 | tf_op jit(solution)/shard_map/ppermute | solution.py:351
  39.7 0.8 collective-permute-done.9.refs_10_
  40.5 3.7 %collective-permute-start.10 = (f32[128,512]{1,0:T(8,128)}, f32[128,512]{1,0:T(8,128)S(1)}, u32[]{:S(2)}, u32[]{:S(2)}) collective-permute-start(f32[128,512]{1,0:T(8,128)} %collective-permute-done.8.refs_9_), channel_id=1, source_target_pairs={{0,4},{4,8},{6,2},{8,12},{10,6},{12,16},{14,10},{16,20},{18,14},{2... | collective-permute-start | bytes 786440 | tf_op jit(solution)/shard_map/ppermute | solution.py:351
  44.2 3.4 %collective-permute-start.11 = (f32[128,512]{1,0:T(8,128)}, f32[128,512]{1,0:T(8,128)S(1)}, u32[]{:S(2)}, u32[]{:S(2)}) collective-permute-start(f32[128,512]{1,0:T(8,128)} %collective-permute-done.9.refs_10_), channel_id=1, source_target_pairs={{0,4},{4,8},{6,2},{8,12},{10,6},{12,16},{14,10},{16,20},{18,14},{2... | collective-permute-start | bytes 786440 | tf_op jit(solution)/shard_map/ppermute | solution.py:351
  47.6 0.1 pad_add_fusion.flag_ref.core_ref
  47.7 4.8 %near_step.2 = (f32[768,512]{1,0:T(8,128)S(1)}, f32[3,3,256,256]{3,2,1,0:T(8,128)S(1)}) custom-call(s32[3,3]{1,0:T(4,128)S(1)} %select_add_fusion.index_ref, s32[3]{0:T(128)S(1)} %copy-done.2, s32[3]{0:T(128)S(1)} %pad_add_fusion.flag_ref.core_ref, f32[3,3,256,256]{3,2,1,0:T(8,128)} %blocks_ref.1, f32[768,512]{1,0:T(8,128)S(1)} %copy-done.1, ...), custom_call_target="tpu_custom_call" | custom-call | flops 1811939328 | bytes 9699328 | tf_op jit(solution)/shard_map/near_step/pallas_call | solution.py:210
  52.6 2.5 %collective-permute-done.11.refs_1_ = f32[128,512]{1,0:T(8,128)S(1)} collective-permute-done((f32[128,512]{1,0:T(8,128)}, f32[128,512]{1,0:T(8,128)S(1)}, u32[]{:S(2)}, u32[]{:S(2)}) %collective-permute-start.11) | collective-permute-done | bytes 262176 | tf_op jit(solution)/shard_map/ppermute | solution.py:351
  55.1 1.7 %near_step.3 = (f32[768,512]{1,0:T(8,128)S(1)}, f32[768,256]{1,0:T(8,128)S(1)}) custom-call(s32[3,3]{1,0:T(4,128)S(1)} %select_add_fusion.index_ref, s32[3]{0:T(128)S(1)} %copy-done.2, s32[3]{0:T(128)S(1)} %pad_add_fusion.flag_ref.core_ref, f32[3,3,256,256]{3,2,1,0:T(8,128)S(1)} %get-tuple-element.16.blocks_ref, f32[768,512]{1,0:T(8,128)S(1)} %get-tuple-element.17.base_ref, ...), custom_call_target="tpu_custom_call" | custom-call | flops 1811939328 | bytes 6029312 | tf_op jit(solution)/shard_map/near_step/pallas_call | solution.py:210
  56.8 0.1 collective-permute-start.12
  56.9 2.3 %collective-permute-done.12.other_ref = f32[768,256]{1,0:T(8,128)S(1)} collective-permute-done((f32[768,256]{1,0:T(8,128)S(1)}, f32[768,256]{1,0:T(8,128)S(1)}, u32[]{:S(2)}, u32[]{:S(2)}) %collective-permute-start.12) | collective-permute-done | bytes 786464 | tf_op jit(solution)/shard_map/ppermute | solution.py:345
  59.2 1.9 %leaf_products.1 = (f32[768,256]{1,0:T(8,128)S(1)}, f32[256,256]{1,0:T(8,128)S(1)}, f32[256,128]{1,0:T(8,128)S(1)}, f32[128,512]{1,0:T(8,128)S(1)}, f32[128,512]{1,0:T(8,128)S(1)}) custom-call(s32[3]{0:T(128)S(1)} %pad_add_fusion.flag_ref.core_ref, f32[768,256]{1,0:T(8,128)S(1)} %get-tuple-element.18.half_ref, ...), custom_call_target="tpu_custom_call" | custom-call | flops 905969664 | bytes 3932160 | tf_op jit(solution)/shard_map/leaf_products/pallas_call | solution.py:256
  61.1 2.4 %collective-permute-start.13 = (f32[256,128]{1,0:T(8,128)S(1)}, f32[256,128]{1,0:T(8,128)S(1)}, u32[]{:S(2)}, u32[]{:S(2)}) collective-permute-start(f32[256,128]{1,0:T(8,128)S(1)} %get-tuple-element.22), channel_id=1, source_target_pairs={{0,2},{2,0},{4,6},{6,4},{8,10},{10,8},{12,14},{14,12},{16,18},{18,... | collective-permute-start | bytes 393224 | tf_op jit(solution)/shard_map/ppermute | solution.py:345
  63.5 0.1 collective-permute-start.18
  63.6 4.3 %collective-permute-done.13 = f32[256,128]{1,0:T(8,128)S(1)} collective-permute-done((f32[256,128]{1,0:T(8,128)S(1)}, f32[256,128]{1,0:T(8,128)S(1)}, u32[]{:S(2)}, u32[]{:S(2)}) %collective-permute-start.13) | collective-permute-done | bytes 131104 | tf_op jit(solution)/shard_map/ppermute | solution.py:345
  67.9 2.9 %collective-permute-start.14 = (f32[256,128]{1,0:T(8,128)S(1)}, f32[256,128]{1,0:T(8,128)S(1)}, u32[]{:S(2)}, u32[]{:S(2)}) collective-permute-start(f32[256,128]{1,0:T(8,128)S(1)} %add.34), channel_id=1, source_target_pairs={{0,4},{2,6},{4,0},{6,2},{8,12},{10,14},{12,8},{14,10},{16,20},{18,... | collective-permute-start | bytes 393224 | tf_op jit(solution)/shard_map/ppermute | solution.py:345
  70.7 2.9 %collective-permute-done.14 = f32[256,128]{1,0:T(8,128)S(1)} collective-permute-done((f32[256,128]{1,0:T(8,128)S(1)}, f32[256,128]{1,0:T(8,128)S(1)}, u32[]{:S(2)}, u32[]{:S(2)}) %collective-permute-start.14) | collective-permute-done | bytes 131104 | tf_op jit(solution)/shard_map/ppermute | solution.py:345
  73.8 2.1 %collective-permute-start.19 = (f32[128,512]{1,0:T(8,128)S(1)}, f32[128,512]{1,0:T(8,128)S(1)}, u32[]{:S(2)}, u32[]{:S(2)}) collective-permute-start(f32[128,512]{1,0:T(8,128)S(1)} %add.38), channel_id=1, source_target_pairs={{0,4},{2,6},{4,0},{6,2},{8,12},{10,14},{12,8},{14,10},{16,20},{18,... | collective-permute-start | bytes 786440 | tf_op jit(solution)/shard_map/ppermute | solution.py:345
  75.8 1.2 collective-permute-start.15
  77.0 3.8 %collective-permute-done.15 = f32[256,128]{1,0:T(8,128)S(1)} collective-permute-done((f32[256,128]{1,0:T(8,128)S(1)}, f32[256,128]{1,0:T(8,128)S(1)}, u32[]{:S(2)}, u32[]{:S(2)}) %collective-permute-start.15) | collective-permute-done | bytes 131104 | tf_op jit(solution)/shard_map/ppermute | solution.py:345
  80.8 2.6 %collective-permute-start.16 = (f32[256,128]{1,0:T(8,128)S(1)}, f32[256,128]{1,0:T(8,128)S(1)}, u32[]{:S(2)}, u32[]{:S(2)}) collective-permute-start(f32[256,128]{1,0:T(8,128)S(1)} %add.36), channel_id=1, source_target_pairs={{0,16},{2,18},{4,20},{6,22},{8,24},{10,26},{12,28},{14,30},{16,0},... | collective-permute-start | bytes 393224 | tf_op jit(solution)/shard_map/ppermute | solution.py:345
  83.5 1.3 collective-permute-start.20
  84.8 3.2 %collective-permute-done.16 = f32[256,128]{1,0:T(8,128)S(1)} collective-permute-done((f32[256,128]{1,0:T(8,128)S(1)}, f32[256,128]{1,0:T(8,128)S(1)}, u32[]{:S(2)}, u32[]{:S(2)}) %collective-permute-start.16) | collective-permute-done | bytes 131104 | tf_op jit(solution)/shard_map/ppermute | solution.py:345
  88.0 0.1 collective-permute-start.17
  88.1 4.1 %collective-permute-done.20 = f32[128,512]{1,0:T(8,128)S(1)} collective-permute-done((f32[128,512]{1,0:T(8,128)S(1)}, f32[128,512]{1,0:T(8,128)S(1)}, u32[]{:S(2)}, u32[]{:S(2)}) %collective-permute-start.20) | collective-permute-done | bytes 262176 | tf_op jit(solution)/shard_map/ppermute | solution.py:345
  92.3 0.3 collective-permute-start.21
  92.6 0.1 pad_maximum_fusion.refs_3_
  92.6 1.6 %collective-permute-start.23 = (f32[3,128,512]{2,1,0:T(8,128)S(1)}, f32[3,128,512]{2,1,0:T(8,128)S(1)}, u32[]{:S(2)}, u32[]{:S(2)}) collective-permute-start(f32[3,128,512]{2,1,0:T(8,128)S(1)} %pad_maximum_fusion.refs_3_), channel_id=1, source_target_pairs={{0,2},{2,0},{4,6},{6,4},{8,10},{10,8},{12,14},{14,12},{16,18},{18,... | collective-permute-start | bytes 2359304 | tf_op jit(solution)/shard_map/ppermute | solution.py:345
  94.2 11.0 %collective-permute-done.21 = f32[128,512]{1,0:T(8,128)S(1)} collective-permute-done((f32[128,512]{1,0:T(8,128)S(1)}, f32[128,512]{1,0:T(8,128)S(1)}, u32[]{:S(2)}, u32[]{:S(2)}) %collective-permute-start.21) | collective-permute-done | bytes 262176 | tf_op jit(solution)/shard_map/ppermute | solution.py:345
  105.3 1.0 collective-permute-start.22
  106.2 15.9 %factor_inverse.1 = (f32[256,256]{1,0:T(8,128)S(1)}, f32[256,256]{1,0:T(8,128)S(1)}, f32[256,256]{1,0:T(8,128)S(1)}, f32[256,256]{1,0:T(8,128)S(1)}, f32[256,256]{1,0:T(8,128)S(1)}) custom-call(s32[3]{0:T(128)S(1)} %pad_add_fusion.flag_ref.core_ref, f32[256,256]{1,0:T(8,128)S(1)} %get-tuple-element.21.gram_ref, ...), custom_call_target="tpu_custom_call" | custom-call | flops 15000000512 | bytes 2621440 | tf_op jit(solution)/shard_map/factor_inverse/pallas_call | solution.py:145
  122.1 1.4 %fusion.1 = f32[768,256]{1,0:T(8,128)} fusion(f32[768,256]{1,0:T(8,128)S(1)} %get-tuple-element.20, f32[256,256]{1,0:T(8,128)S(1)} %get-tuple-element.23), kind=kOutput, calls=%fused_computation.6 | convolution fusion | flops 301989888 | bytes 1835008 | tf_op jit(solution)/shard_map/dot_general | solution.py:398
  123.5 2.2 %reduce_early.1.kept_ref = f32[4,1,256,512]{3,2,1,0:T(8,128)} custom-call(s32[3]{0:T(128)S(1)} %pad_add_fusion.flag_ref.core_ref, f32[256,256]{1,0:T(8,128)S(1)} %get-tuple-element.27.refs_0_, f32[256,256]{1,0:T(8,128)S(1)} %get-tuple-element.28.refs_1_, f32[256,256]{1,0:T(8,128)S(1)} %get-tuple-element.29.refs_2_, ...), custom_call_target="tpu_custom_call" | custom-call | flops 603979776 | bytes 4718592 | tf_op jit(solution)/shard_map/reduce_early/pallas_call | solution.py:295
  125.8 1.8 %reduce_last.1 = f32[4,1,256,512]{3,2,1,0:T(8,128)} custom-call(s32[3]{0:T(128)S(1)} %pad_add_fusion.flag_ref.core_ref, f32[256,256]{1,0:T(8,128)S(1)} %get-tuple-element.24.inverse_ref, f32[128,512]{1,0:T(8,128)S(1)} %add.41.mine_ref, f32[128,512]{1,0:T(8,128)S(1)} %collective-permute-done.22.other_ref, ...), custom_call_target="tpu_custom_call", output_to_operand_aliasing={{}: (4, {})} | custom-call | flops 201326592 | bytes 1572864 | tf_op jit(solution)/shard_map/reduce_last/pallas_call | solution.py:325
  (31 shorter events, 0.3 us)
Async XLA Ops:
  0.6 7.4 %copy-start = (f32[768,512]{1,0:T(8,128)S(1)}, f32[768,512]{1,0:T(8,128)}, u32[]{:S(2)}) copy-start(f32[768,512]{1,0:T(8,128)} %refs_4_.1) | copy-start | bytes 4718596
  0.6 39.0 %copy-start.4 = (s32[3,3]{1,0:T(4,128)S(1)}, s32[3,3]{1,0:T(4,128)}, u32[]{:S(2)}) copy-start(s32[3,3]{1,0:T(4,128)} %param.9) | copy-start | bytes 112
  0.7 47.1 %copy-start.2 = (s32[3]{0:T(128)S(1)}, s32[3]{0:T(128)}, u32[]{:S(2)}) copy-start(s32[3]{0:T(128)} %count_ref.3) | copy-start | bytes 40
  0.7 47.1 %copy-start.1 = (f32[768,512]{1,0:T(8,128)S(1)}, f32[768,512]{1,0:T(8,128)}, u32[]{:S(2)}) copy-start(f32[768,512]{1,0:T(8,128)} %base_ref.1) | copy-start | bytes 4718596
  3.0 10.1 %collective-permute-start.2 = (f32[128,512]{1,0:T(8,128)S(1)}, f32[128,512]{1,0:T(8,128)S(1)}, u32[]{:S(2)}, u32[]{:S(2)}) collective-permute-start(f32[128,512]{1,0:T(8,128)S(1)} %get-tuple-element.34), channel_id=1, source_target_pairs={{0,2},{2,0},{4,6},{6,4},{8,10},{10,8},{12,14},{14,12},{16,18},{18,... | collective-permute-start | bytes 786440 | tf_op jit(solution)/shard_map/ppermute | solution.py:345
  6.0 12.9 %collective-permute-start.4 = (f32[128,512]{1,0:T(8,128)S(1)}, f32[128,512]{1,0:T(8,128)}, u32[]{:S(2)}, u32[]{:S(2)}) collective-permute-start(f32[128,512]{1,0:T(8,128)S(1)} %get-tuple-element.33), channel_id=1, source_target_pairs={{0,2},{2,0},{4,6},{6,4},{8,10},{10,8},{12,14},{14,12},{16,18},{18,... | collective-permute-start | bytes 786440 | tf_op jit(solution)/shard_map/ppermute | solution.py:345
  6.0 18.5 %collective-permute-start.6 = (f32[128,512]{1,0:T(8,128)}, f32[128,512]{1,0:T(8,128)}, u32[]{:S(2)}, u32[]{:S(2)}) collective-permute-start(f32[128,512]{1,0:T(8,128)} %get-tuple-element.32), channel_id=1, source_target_pairs={{0,2},{2,0},{4,6},{6,4},{8,10},{10,8},{12,14},{14,12},{16,18},{18,... | collective-permute-start | bytes 786440 | tf_op jit(solution)/shard_map/ppermute | solution.py:345
  8.0 22.1 %collective-permute-start.8 = (f32[128,512]{1,0:T(8,128)}, f32[128,512]{1,0:T(8,128)}, u32[]{:S(2)}, u32[]{:S(2)}) collective-permute-start(f32[128,512]{1,0:T(8,128)} %get-tuple-element.31), channel_id=1, source_target_pairs={{0,2},{2,0},{4,6},{6,4},{8,10},{10,8},{12,14},{14,12},{16,18},{18,... | collective-permute-start | bytes 786440 | tf_op jit(solution)/shard_map/ppermute | solution.py:345
  8.8 27.0 %collective-permute-start = (f32[128,512]{1,0:T(8,128)}, f32[128,512]{1,0:T(8,128)}, u32[]{:S(2)}, u32[]{:S(2)}) collective-permute-start(f32[128,512]{1,0:T(8,128)} %slice.18), channel_id=1, source_target_pairs={{0,2},{2,0},{4,6},{6,4},{8,10},{10,8},{12,14},{14,12},{16,18},{18,... | collective-permute-start | bytes 786440 | tf_op jit(solution)/shard_map/ppermute | solution.py:345
  13.1 27.3 %collective-permute-start.9 = (f32[128,512]{1,0:T(8,128)}, f32[128,512]{1,0:T(8,128)}, u32[]{:S(2)}, u32[]{:S(2)}) collective-permute-start(f32[128,512]{1,0:T(8,128)} %get-tuple-element.30), channel_id=1, source_target_pairs={{0,2},{2,0},{4,6},{6,4},{8,10},{10,8},{12,14},{14,12},{16,18},{18,... | collective-permute-start | bytes 786440 | tf_op jit(solution)/shard_map/ppermute | solution.py:345
  18.9 25.3 %collective-permute-start.3 = (f32[128,512]{1,0:T(8,128)S(1)}, f32[128,512]{1,0:T(8,128)}, u32[]{:S(2)}, u32[]{:S(2)}) collective-permute-start(f32[128,512]{1,0:T(8,128)S(1)} %collective-permute-done.2.refs_6_), channel_id=1, source_target_pairs={{0,4},{4,8},{6,2},{8,12},{10,6},{12,16},{14,10},{16,20},{18,14},{2... | collective-permute-start | bytes 786440 | tf_op jit(solution)/shard_map/ppermute | solution.py:351
  24.5 23.2 %collective-permute-start.5 = (f32[128,512]{1,0:T(8,128)}, f32[128,512]{1,0:T(8,128)S(1)}, u32[]{:S(2)}, u32[]{:S(2)}) collective-permute-start(f32[128,512]{1,0:T(8,128)} %collective-permute-done.4.refs_7_), channel_id=1, source_target_pairs={{0,4},{4,8},{6,2},{8,12},{10,6},{12,16},{14,10},{16,20},{18,14},{2... | collective-permute-start | bytes 786440 | tf_op jit(solution)/shard_map/ppermute | solution.py:351
  30.1 17.6 %collective-permute-start.7 = (f32[128,512]{1,0:T(8,128)}, f32[128,512]{1,0:T(8,128)S(1)}, u32[]{:S(2)}, u32[]{:S(2)}) collective-permute-start(f32[128,512]{1,0:T(8,128)} %collective-permute-done.6.refs_8_), channel_id=1, source_target_pairs={{0,4},{4,8},{6,2},{8,12},{10,6},{12,16},{14,10},{16,20},{18,14},{2... | collective-permute-start | bytes 786440 | tf_op jit(solution)/shard_map/ppermute | solution.py:351
  35.7 12.0 %collective-permute-start.1 = (f32[128,512]{1,0:T(8,128)}, f32[128,512]{1,0:T(8,128)S(1)}, u32[]{:S(2)}, u32[]{:S(2)}) collective-permute-start(f32[128,512]{1,0:T(8,128)} %collective-permute-done.refs_5_), channel_id=1, source_target_pairs={{0,4},{4,8},{6,2},{8,12},{10,6},{12,16},{14,10},{16,20},{18,14},{2... | collective-permute-start | bytes 786440 | tf_op jit(solution)/shard_map/ppermute | solution.py:351
  40.5 12.1 %collective-permute-start.10 = (f32[128,512]{1,0:T(8,128)}, f32[128,512]{1,0:T(8,128)S(1)}, u32[]{:S(2)}, u32[]{:S(2)}) collective-permute-start(f32[128,512]{1,0:T(8,128)} %collective-permute-done.8.refs_9_), channel_id=1, source_target_pairs={{0,4},{4,8},{6,2},{8,12},{10,6},{12,16},{14,10},{16,20},{18,14},{2... | collective-permute-start | bytes 786440 | tf_op jit(solution)/shard_map/ppermute | solution.py:351
  44.2 10.9 %collective-permute-start.11 = (f32[128,512]{1,0:T(8,128)}, f32[128,512]{1,0:T(8,128)S(1)}, u32[]{:S(2)}, u32[]{:S(2)}) collective-permute-start(f32[128,512]{1,0:T(8,128)} %collective-permute-done.9.refs_10_), channel_id=1, source_target_pairs={{0,4},{4,8},{6,2},{8,12},{10,6},{12,16},{14,10},{16,20},{18,14},{2... | collective-permute-start | bytes 786440 | tf_op jit(solution)/shard_map/ppermute | solution.py:351
  47.7 7.4 %copy-start.3 = (f32[512,256]{1,0:T(8,128)S(1)}, f32[512,256]{1,0:T(8,128)}, u32[]{:S(2)}) copy-start(f32[512,256]{1,0:T(8,128)} %refs_2_.1) | copy-start | bytes 1572868
  56.8 2.4 %collective-permute-start.12 = (f32[768,256]{1,0:T(8,128)S(1)}, f32[768,256]{1,0:T(8,128)S(1)}, u32[]{:S(2)}, u32[]{:S(2)}) collective-permute-start(f32[768,256]{1,0:T(8,128)S(1)} %get-tuple-element.18.half_ref), channel_id=1, source_target_pairs={{0,1},{1,0},{2,3},{3,2},{4,5},{5,4},{6,7},{7,6},{8,9},{9,8},{10,11... | collective-permute-start | bytes 2359304 | tf_op jit(solution)/shard_map/ppermute | solution.py:345
  61.1 6.8 %collective-permute-start.13 = (f32[256,128]{1,0:T(8,128)S(1)}, f32[256,128]{1,0:T(8,128)S(1)}, u32[]{:S(2)}, u32[]{:S(2)}) collective-permute-start(f32[256,128]{1,0:T(8,128)S(1)} %get-tuple-element.22), channel_id=1, source_target_pairs={{0,2},{2,0},{4,6},{6,4},{8,10},{10,8},{12,14},{14,12},{16,18},{18,... | collective-permute-start | bytes 393224 | tf_op jit(solution)/shard_map/ppermute | solution.py:345
  63.5 10.2 %collective-permute-start.18 = (f32[128,512]{1,0:T(8,128)S(1)}, f32[128,512]{1,0:T(8,128)S(1)}, u32[]{:S(2)}, u32[]{:S(2)}) collective-permute-start(f32[128,512]{1,0:T(8,128)S(1)} %get-tuple-element.26), channel_id=1, source_target_pairs={{0,2},{2,0},{4,6},{6,4},{8,10},{10,8},{12,14},{14,12},{16,18},{18,... | collective-permute-start | bytes 786440 | tf_op jit(solution)/shard_map/ppermute | solution.py:345
  67.9 5.8 %collective-permute-start.14 = (f32[256,128]{1,0:T(8,128)S(1)}, f32[256,128]{1,0:T(8,128)S(1)}, u32[]{:S(2)}, u32[]{:S(2)}) collective-permute-start(f32[256,128]{1,0:T(8,128)S(1)} %add.34), channel_id=1, source_target_pairs={{0,4},{2,6},{4,0},{6,2},{8,12},{10,14},{12,8},{14,10},{16,20},{18,... | collective-permute-start | bytes 393224 | tf_op jit(solution)/shard_map/ppermute | solution.py:345
  73.8 9.7 %collective-permute-start.19 = (f32[128,512]{1,0:T(8,128)S(1)}, f32[128,512]{1,0:T(8,128)S(1)}, u32[]{:S(2)}, u32[]{:S(2)}) collective-permute-start(f32[128,512]{1,0:T(8,128)S(1)} %add.38), channel_id=1, source_target_pairs={{0,4},{2,6},{4,0},{6,2},{8,12},{10,14},{12,8},{14,10},{16,20},{18,... | collective-permute-start | bytes 786440 | tf_op jit(solution)/shard_map/ppermute | solution.py:345
  75.8 5.0 %collective-permute-start.15 = (f32[256,128]{1,0:T(8,128)S(1)}, f32[256,128]{1,0:T(8,128)S(1)}, u32[]{:S(2)}, u32[]{:S(2)}) collective-permute-start(f32[256,128]{1,0:T(8,128)S(1)} %add.35), channel_id=1, source_target_pairs={{0,8},{2,10},{4,12},{6,14},{8,0},{10,2},{12,4},{14,6},{16,24},{18,... | collective-permute-start | bytes 393224 | tf_op jit(solution)/shard_map/ppermute | solution.py:345
  80.8 7.2 %collective-permute-start.16 = (f32[256,128]{1,0:T(8,128)S(1)}, f32[256,128]{1,0:T(8,128)S(1)}, u32[]{:S(2)}, u32[]{:S(2)}) collective-permute-start(f32[256,128]{1,0:T(8,128)S(1)} %add.36), channel_id=1, source_target_pairs={{0,16},{2,18},{4,20},{6,22},{8,24},{10,26},{12,28},{14,30},{16,0},... | collective-permute-start | bytes 393224 | tf_op jit(solution)/shard_map/ppermute | solution.py:345
  83.5 8.7 %collective-permute-start.20 = (f32[128,512]{1,0:T(8,128)S(1)}, f32[128,512]{1,0:T(8,128)S(1)}, u32[]{:S(2)}, u32[]{:S(2)}) collective-permute-start(f32[128,512]{1,0:T(8,128)S(1)} %add.39), channel_id=1, source_target_pairs={{0,8},{2,10},{4,12},{6,14},{8,0},{10,2},{12,4},{14,6},{16,24},{18,... | collective-permute-start | bytes 786440 | tf_op jit(solution)/shard_map/ppermute | solution.py:345
  88.0 18.2 %collective-permute-start.17 = (f32[4,256,128]{2,1,0:T(8,128)S(1)}, f32[4,256,128]{2,1,0:T(8,128)S(1)}, u32[]{:S(2)}, u32[]{:S(2)}) collective-permute-start(f32[4,256,128]{2,1,0:T(8,128)S(1)} %pad_maximum_fusion.1.mine_ref), channel_id=1, source_target_pairs={{0,1},{1,0},{2,3},{3,2},{4,5},{5,4},{6,7},{7,6},{8,9},{9,8},{10,11... | collective-permute-start | bytes 1572872 | tf_op jit(solution)/shard_map/ppermute | solution.py:345
  92.3 12.9 %collective-permute-start.21 = (f32[128,512]{1,0:T(8,128)S(1)}, f32[128,512]{1,0:T(8,128)S(1)}, u32[]{:S(2)}, u32[]{:S(2)}) collective-permute-start(f32[128,512]{1,0:T(8,128)S(1)} %add.40), channel_id=1, source_target_pairs={{0,16},{2,18},{4,20},{6,22},{8,24},{10,26},{12,28},{14,30},{16,0},... | collective-permute-start | bytes 786440 | tf_op jit(solution)/shard_map/ppermute | solution.py:345
  92.6 30.9 %collective-permute-start.23 = (f32[3,128,512]{2,1,0:T(8,128)S(1)}, f32[3,128,512]{2,1,0:T(8,128)S(1)}, u32[]{:S(2)}, u32[]{:S(2)}) collective-permute-start(f32[3,128,512]{2,1,0:T(8,128)S(1)} %pad_maximum_fusion.refs_3_), channel_id=1, source_target_pairs={{0,2},{2,0},{4,6},{6,4},{8,10},{10,8},{12,14},{14,12},{16,18},{18,... | collective-permute-start | bytes 2359304 | tf_op jit(solution)/shard_map/ppermute | solution.py:345
  105.3 20.5 %collective-permute-start.22 = (f32[128,512]{1,0:T(8,128)S(1)}, f32[128,512]{1,0:T(8,128)S(1)}, u32[]{:S(2)}, u32[]{:S(2)}) collective-permute-start(f32[128,512]{1,0:T(8,128)S(1)} %add.41.mine_ref), channel_id=1, source_target_pairs={{0,2},{2,0},{4,6},{6,4},{8,10},{10,8},{12,14},{14,12},{16,18},{18,... | collective-permute-start | bytes 786440 | tf_op jit(solution)/shard_map/ppermute | solution.py:345

commit v10 on v8

--- a/solution.py
+++ b/solution.py
@@ -298,10 +298,16 @@
 
 
 def last_kernel(flag_ref, inverse_ref, mine_ref, other_ref, kept_ref, out_ref, stage, result, sem):
-    result[...] = dot3(inverse_ref[...], staged(stage, flag_ref, mine_ref[...], other_ref[...]), NN)
-    copy = pltpu.make_async_copy(result, out_ref.at[LEVELS - 1, 0], sem)
-    copy.start()
-    copy.wait()
+    value = staged(stage, flag_ref, mine_ref[...], other_ref[...])
+    half = result.shape[0] // 2
+    copies = []
+    for part in range(2):
+        rows = pl.ds(part * half, half)
+        result[rows, :] = dot3(inverse_ref[rows, :], value, NN)
+        copies.append(pltpu.make_async_copy(result.at[rows], out_ref.at[LEVELS - 1, 0, rows], sem.at[part]))
+        copies[-1].start()
+    for copy in copies:
+        copy.wait()
 
 
 def reduce_last(flag, inverse, mine, other, reduced):
@@ -317,7 +323,7 @@
         scratch_shapes=[
             pltpu.VMEM((rank, width), jnp.float32),
             pltpu.VMEM((rank, width), jnp.float32),
-            pltpu.SemaphoreType.DMA,
+            pltpu.SemaphoreType.DMA((2,)),
         ],
         input_output_aliases={4: 0},
         cost_estimate=pl.CostEstimate(
@@ -364,7 +370,9 @@
 
     early = (block_count - 1) * SPLIT
     spots = [*range(block_count - 1), *range(block_count, 3 * block_count)]
-    (left,) = near_step(near_blocks, samples, far[:early] + [probes] + peer, spots, index, near_count, flag, 0)
+    oldest = pltpu.with_memory_space_constraint(peer[0], pltpu.HBM)
+    landed = far[:early] + [probes, oldest] + peer[1:]
+    (left,) = near_step(near_blocks, samples, landed, spots, index, near_count, flag, 0)
     spots = [block_count - 1]
     far_samples, partial = near_step(near_blocks, left, far[early:], spots, index, near_count, flag, 1, sketch)
     if halves == 2:

time: 127 us -> 127 us (level)
  no operation moved by 1% of the time
where the time goes in v10:
time: 127 us; the launch traced here: 126 us
  starting transfers between devices  48.3 us (38%)
  waiting for transfers between devices  42.7 us (34%)
  Pallas kernels  27.6 us (22%)
  local copies, waits for them, and re-layouts  5.06 us (4%)
  matrix products  1.39 us (1%)
    ppermute x18, waiting for transfers between devices, across(): lax.ppermute(value, axis, [(i, i ^ 1 << bit) for i in range(lax.axis_size...  41.2 us
    ppermute x18, starting transfers between devices, across(): lax.ppermute(value, axis, [(i, i ^ 1 << bit) for i in range(lax.axis_size...  24.7 us
    ppermute x6, starting transfers between devices, relayed(): lax.ppermute(value, axis, [(i, t) for i, t in steps if 0 <= t < count])  23.6 us
    pallas_call x1, Pallas kernels, factor_inverse(): pl.pallas_call(functools.partial(inverse_kernel, size), out_shape=[pltpu....  15.9 us
    pallas_call x2, Pallas kernels, near_step(): pl.pallas_call(functools.partial(near_kernel, len(pieces), first_slot, tu...  5.89 us
    slice x2, local copies, waits for them, and re-layouts, leaf_and_levels(): (later if i else probes)[i * depth:(i + 1) * depth]  3.37 us
  transfers between devices with their start and end apart: 24, of which 14 were waited for; matrix products, arithmetic and copies ran while one was open for 3% of the time, Pallas kernels for 18%

profile of v10, /device:TPU:0, one launch (start us, length us, event | category | flops | bytes accessed | tf_op | source)
XLA Modules:
  0.0 126.5 jit_solution(4992878333086104055)
XLA Ops:
  0.7 1.1 slice.18
  1.8 3.0 %collective-permute-start = (f32[128,512]{1,0:T(8,128)S(1)}, f32[128,512]{1,0:T(8,128)}, u32[]{:S(2)}, u32[]{:S(2)}) collective-permute-start(f32[128,512]{1,0:T(8,128)S(1)} %slice.18), channel_id=1, source_target_pairs={{0,2},{2,0},{4,6},{6,4},{8,10},{10,8},{12,14},{14,12},{16,18},{18,... | collective-permute-start | bytes 786440 | tf_op jit(solution)/shard_map/ppermute | solution.py:338
  4.8 2.3 %fusion = (f32[128,512]{1,0:T(8,128)S(1)}, f32[128,512]{1,0:T(8,128)}, f32[128,512]{1,0:T(8,128)}, f32[128,512]{1,0:T(8,128)}, f32[128,512]{1,0:T(8,128)}) fusion(f32[768,512]{1,0:T(8,128)} %refs_4_.1), kind=kLoop, calls=%fused_computation.5 | loop fusion | bytes 2621440 | tf_op jit(solution)/shard_map/slice | solution.py:367
  7.1 2.0 %collective-permute-start.6 = (f32[128,512]{1,0:T(8,128)}, f32[128,512]{1,0:T(8,128)}, u32[]{:S(2)}, u32[]{:S(2)}) collective-permute-start(f32[128,512]{1,0:T(8,128)} %get-tuple-element.28), channel_id=1, source_target_pairs={{0,2},{2,0},{4,6},{6,4},{8,10},{10,8},{12,14},{14,12},{16,18},{18,... | collective-permute-start | bytes 786440 | tf_op jit(solution)/shard_map/ppermute | solution.py:338
  9.1 2.0 %collective-permute-start.2 = (f32[128,512]{1,0:T(8,128)}, f32[128,512]{1,0:T(8,128)}, u32[]{:S(2)}, u32[]{:S(2)}) collective-permute-start(f32[128,512]{1,0:T(8,128)} %get-tuple-element.30), channel_id=1, source_target_pairs={{0,2},{2,0},{4,6},{6,4},{8,10},{10,8},{12,14},{14,12},{16,18},{18,... | collective-permute-start | bytes 786440 | tf_op jit(solution)/shard_map/ppermute | solution.py:338
  11.1 1.0 collective-permute-done.refs_5_
  12.1 2.0 %collective-permute-start.8 = (f32[128,512]{1,0:T(8,128)}, f32[128,512]{1,0:T(8,128)}, u32[]{:S(2)}, u32[]{:S(2)}) collective-permute-start(f32[128,512]{1,0:T(8,128)} %get-tuple-element.27), channel_id=1, source_target_pairs={{0,2},{2,0},{4,6},{6,4},{8,10},{10,8},{12,14},{14,12},{16,18},{18,... | collective-permute-start | bytes 786440 | tf_op jit(solution)/shard_map/ppermute | solution.py:338
  14.1 3.5 %collective-permute-done.9.refs_10_ = f32[128,512]{1,0:T(8,128)S(1)} collective-permute-done((f32[128,512]{1,0:T(8,128)S(1)}, f32[128,512]{1,0:T(8,128)S(1)}, u32[]{:S(2)}, u32[]{:S(2)}) %collective-permute-start.9) | collective-permute-done | bytes 262176 | tf_op jit(solution)/shard_map/ppermute | solution.py:338
  17.6 4.7 %collective-permute-start.1 = (f32[128,512]{1,0:T(8,128)}, f32[128,512]{1,0:T(8,128)}, u32[]{:S(2)}, u32[]{:S(2)}) collective-permute-start(f32[128,512]{1,0:T(8,128)} %collective-permute-done.refs_5_), channel_id=1, source_target_pairs={{0,4},{4,8},{6,2},{8,12},{10,6},{12,16},{14,10},{16,20},{18,14},{2... | collective-permute-start | bytes 786440 | tf_op jit(solution)/shard_map/ppermute | solution.py:344
  22.3 1.1 collective-permute-done.6.refs_8_
  23.3 4.0 %collective-permute-start.7 = (f32[128,512]{1,0:T(8,128)}, f32[128,512]{1,0:T(8,128)S(1)}, u32[]{:S(2)}, u32[]{:S(2)}) collective-permute-start(f32[128,512]{1,0:T(8,128)} %collective-permute-done.6.refs_8_), channel_id=1, source_target_pairs={{0,4},{4,8},{6,2},{8,12},{10,6},{12,16},{14,10},{16,20},{18,14},{2... | collective-permute-start | bytes 786440 | tf_op jit(solution)/shard_map/ppermute | solution.py:344
  27.3 1.7 %collective-permute-done.4.refs_7_ = f32[128,512]{1,0:T(8,128)} collective-permute-done((f32[128,512]{1,0:T(8,128)}, f32[128,512]{1,0:T(8,128)}, u32[]{:S(2)}, u32[]{:S(2)}) %collective-permute-start.4) | collective-permute-done | bytes 262176 | tf_op jit(solution)/shard_map/ppermute | solution.py:338
  28.9 4.0 %collective-permute-start.5 = (f32[128,512]{1,0:T(8,128)}, f32[128,512]{1,0:T(8,128)S(1)}, u32[]{:S(2)}, u32[]{:S(2)}) collective-permute-start(f32[128,512]{1,0:T(8,128)} %collective-permute-done.4.refs_7_), channel_id=1, source_target_pairs={{0,4},{4,8},{6,2},{8,12},{10,6},{12,16},{14,10},{16,20},{18,14},{2... | collective-permute-start | bytes 786440 | tf_op jit(solution)/shard_map/ppermute | solution.py:344
  32.9 1.7 %collective-permute-done.2.refs_6_ = f32[128,512]{1,0:T(8,128)} collective-permute-done((f32[128,512]{1,0:T(8,128)}, f32[128,512]{1,0:T(8,128)}, u32[]{:S(2)}, u32[]{:S(2)}) %collective-permute-start.2) | collective-permute-done | bytes 262176 | tf_op jit(solution)/shard_map/ppermute | solution.py:338
  34.6 4.0 %collective-permute-start.3 = (f32[128,512]{1,0:T(8,128)}, f32[128,512]{1,0:T(8,128)S(1)}, u32[]{:S(2)}, u32[]{:S(2)}) collective-permute-start(f32[128,512]{1,0:T(8,128)} %collective-permute-done.2.refs_6_), channel_id=1, source_target_pairs={{0,4},{4,8},{6,2},{8,12},{10,6},{12,16},{14,10},{16,20},{18,14},{2... | collective-permute-start | bytes 786440 | tf_op jit(solution)/shard_map/ppermute | solution.py:344
  38.5 0.8 collective-permute-done.8.refs_9_
  39.3 3.7 %collective-permute-start.11 = (f32[128,512]{1,0:T(8,128)S(1)}, f32[128,512]{1,0:T(8,128)S(1)}, u32[]{:S(2)}, u32[]{:S(2)}) collective-permute-start(f32[128,512]{1,0:T(8,128)S(1)} %collective-permute-done.9.refs_10_), channel_id=1, source_target_pairs={{0,4},{4,8},{6,2},{8,12},{10,6},{12,16},{14,10},{16,20},{18,14},{2... | collective-permute-start | bytes 786440 | tf_op jit(solution)/shard_map/ppermute | solution.py:344
  43.0 3.4 %collective-permute-start.10 = (f32[128,512]{1,0:T(8,128)}, f32[128,512]{1,0:T(8,128)S(1)}, u32[]{:S(2)}, u32[]{:S(2)}) collective-permute-start(f32[128,512]{1,0:T(8,128)} %collective-permute-done.8.refs_9_), channel_id=1, source_target_pairs={{0,4},{4,8},{6,2},{8,12},{10,6},{12,16},{14,10},{16,20},{18,14},{2... | collective-permute-start | bytes 786440 | tf_op jit(solution)/shard_map/ppermute | solution.py:344
  46.5 0.1 pad_add_fusion.flag_ref.core_ref
  46.6 1.7 %copy-done.1 = f32[3,3,256,256]{3,2,1,0:T(8,128)S(1)} copy-done((f32[3,3,256,256]{3,2,1,0:T(8,128)S(1)}, f32[3,3,256,256]{3,2,1,0:T(8,128)}, u32[]{:S(2)}) %copy-start.1) | copy-done | bytes 2359320
  48.3 4.2 %near_step.2.base_ref = f32[768,512]{1,0:T(8,128)S(1)} custom-call(s32[3,3]{1,0:T(4,128)S(1)} %select_add_fusion.index_ref, s32[3]{0:T(128)S(1)} %copy-done.3, s32[3]{0:T(128)S(1)} %pad_add_fusion.flag_ref.core_ref, f32[3,3,256,256]{3,2,1,0:T(8,128)S(1)} %copy-done.1, f32[768,512]{1,0:T(8,128)S(1)} %copy-done.2, f32[128,512]{1,0:T(8,128)} %collective-permute-done.1.refs_0_, ...), custom_call_target="tpu_custom_call" | custom-call | flops 1811939328 | bytes 9699328 | tf_op jit(solution)/shard_map/near_step/pallas_call | solution.py:197
  52.4 1.5 %collective-permute-done.10.refs_0_ = f32[128,512]{1,0:T(8,128)S(1)} collective-permute-done((f32[128,512]{1,0:T(8,128)}, f32[128,512]{1,0:T(8,128)S(1)}, u32[]{:S(2)}, u32[]{:S(2)}) %collective-permute-start.10) | collective-permute-done | bytes 262176 | tf_op jit(solution)/shard_map/ppermute | solution.py:344
  53.9 1.7 %near_step.3 = (f32[768,512]{1,0:T(8,128)S(1)}, f32[768,256]{1,0:T(8,128)S(1)}) custom-call(s32[3,3]{1,0:T(4,128)S(1)} %select_add_fusion.index_ref, s32[3]{0:T(128)S(1)} %copy-done.3, s32[3]{0:T(128)S(1)} %pad_add_fusion.flag_ref.core_ref, f32[3,3,256,256]{3,2,1,0:T(8,128)S(1)} %copy-done.1, f32[768,512]{1,0:T(8,128)S(1)} %near_step.2.base_ref, ...), custom_call_target="tpu_custom_call" | custom-call | flops 1811939328 | bytes 6029312 | tf_op jit(solution)/shard_map/near_step/pallas_call | solution.py:197
  55.7 0.1 collective-permute-start.12
  55.7 2.3 %collective-permute-done.12.other_ref = f32[768,256]{1,0:T(8,128)S(1)} collective-permute-done((f32[768,256]{1,0:T(8,128)S(1)}, f32[768,256]{1,0:T(8,128)S(1)}, u32[]{:S(2)}, u32[]{:S(2)}) %collective-permute-start.12) | collective-permute-done | bytes 786464 | tf_op jit(solution)/shard_map/ppermute | solution.py:338
  58.0 1.9 %leaf_products.1 = (f32[768,256]{1,0:T(8,128)S(1)}, f32[256,256]{1,0:T(8,128)S(1)}, f32[256,128]{1,0:T(8,128)S(1)}, f32[128,512]{1,0:T(8,128)S(1)}, f32[128,512]{1,0:T(8,128)S(1)}) custom-call(s32[3]{0:T(128)S(1)} %pad_add_fusion.flag_ref.core_ref, f32[768,256]{1,0:T(8,128)S(1)} %get-tuple-element.14.half_ref, ...), custom_call_target="tpu_custom_call" | custom-call | flops 905969664 | bytes 3932160 | tf_op jit(solution)/shard_map/leaf_products/pallas_call | solution.py:243
  59.9 2.4 %collective-permute-start.13 = (f32[256,128]{1,0:T(8,128)S(1)}, f32[256,128]{1,0:T(8,128)S(1)}, u32[]{:S(2)}, u32[]{:S(2)}) collective-permute-start(f32[256,128]{1,0:T(8,128)S(1)} %get-tuple-element.18), channel_id=1, source_target_pairs={{0,2},{2,0},{4,6},{6,4},{8,10},{10,8},{12,14},{14,12},{16,18},{18,... | collective-permute-start | bytes 393224 | tf_op jit(solution)/shard_map/ppermute | solution.py:338
  62.3 0.1 collective-permute-start.18
  62.4 4.3 %collective-permute-done.13 = f32[256,128]{1,0:T(8,128)S(1)} collective-permute-done((f32[256,128]{1,0:T(8,128)S(1)}, f32[256,128]{1,0:T(8,128)S(1)}, u32[]{:S(2)}, u32[]{:S(2)}) %collective-permute-start.13) | collective-permute-done | bytes 131104 | tf_op jit(solution)/shard_map/ppermute | solution.py:338
  66.7 2.9 %collective-permute-start.14 = (f32[256,128]{1,0:T(8,128)S(1)}, f32[256,128]{1,0:T(8,128)S(1)}, u32[]{:S(2)}, u32[]{:S(2)}) collective-permute-start(f32[256,128]{1,0:T(8,128)S(1)} %add.34), channel_id=1, source_target_pairs={{0,4},{2,6},{4,0},{6,2},{8,12},{10,14},{12,8},{14,10},{16,20},{18,... | collective-permute-start | bytes 393224 | tf_op jit(solution)/shard_map/ppermute | solution.py:338
  69.6 2.9 %collective-permute-done.14 = f32[256,128]{1,0:T(8,128)S(1)} collective-permute-done((f32[256,128]{1,0:T(8,128)S(1)}, f32[256,128]{1,0:T(8,128)S(1)}, u32[]{:S(2)}, u32[]{:S(2)}) %collective-permute-start.14) | collective-permute-done | bytes 131104 | tf_op jit(solution)/shard_map/ppermute | solution.py:338
  72.6 2.1 %collective-permute-start.19 = (f32[128,512]{1,0:T(8,128)S(1)}, f32[128,512]{1,0:T(8,128)S(1)}, u32[]{:S(2)}, u32[]{:S(2)}) collective-permute-start(f32[128,512]{1,0:T(8,128)S(1)} %add.38), channel_id=1, source_target_pairs={{0,4},{2,6},{4,0},{6,2},{8,12},{10,14},{12,8},{14,10},{16,20},{18,... | collective-permute-start | bytes 786440 | tf_op jit(solution)/shard_map/ppermute | solution.py:338
  74.7 1.2 collective-permute-start.15
  75.9 3.8 %collective-permute-done.15 = f32[256,128]{1,0:T(8,128)S(1)} collective-permute-done((f32[256,128]{1,0:T(8,128)S(1)}, f32[256,128]{1,0:T(8,128)S(1)}, u32[]{:S(2)}, u32[]{:S(2)}) %collective-permute-start.15) | collective-permute-done | bytes 131104 | tf_op jit(solution)/shard_map/ppermute | solution.py:338
  79.7 2.7 %collective-permute-start.16 = (f32[256,128]{1,0:T(8,128)S(1)}, f32[256,128]{1,0:T(8,128)S(1)}, u32[]{:S(2)}, u32[]{:S(2)}) collective-permute-start(f32[256,128]{1,0:T(8,128)S(1)} %add.36), channel_id=1, source_target_pairs={{0,16},{2,18},{4,20},{6,22},{8,24},{10,26},{12,28},{14,30},{16,0},... | collective-permute-start | bytes 393224 | tf_op jit(solution)/shard_map/ppermute | solution.py:338
  82.4 1.3 %collective-permute-start.20 = (f32[128,512]{1,0:T(8,128)S(1)}, f32[128,512]{1,0:T(8,128)S(1)}, u32[]{:S(2)}, u32[]{:S(2)}) collective-permute-start(f32[128,512]{1,0:T(8,128)S(1)} %add.39), channel_id=1, source_target_pairs={{0,8},{2,10},{4,12},{6,14},{8,0},{10,2},{12,4},{14,6},{16,24},{18,... | collective-permute-start | bytes 786440 | tf_op jit(solution)/shard_map/ppermute | solution.py:338
  83.6 3.2 %collective-permute-done.16 = f32[256,128]{1,0:T(8,128)S(1)} collective-permute-done((f32[256,128]{1,0:T(8,128)S(1)}, f32[256,128]{1,0:T(8,128)S(1)}, u32[]{:S(2)}, u32[]{:S(2)}) %collective-permute-start.16) | collective-permute-done | bytes 131104 | tf_op jit(solution)/shard_map/ppermute | solution.py:338
  86.9 0.1 collective-permute-start.17
  87.0 4.1 %collective-permute-done.20 = f32[128,512]{1,0:T(8,128)S(1)} collective-permute-done((f32[128,512]{1,0:T(8,128)S(1)}, f32[128,512]{1,0:T(8,128)S(1)}, u32[]{:S(2)}, u32[]{:S(2)}) %collective-permute-start.20) | collective-permute-done | bytes 262176 | tf_op jit(solution)/shard_map/ppermute | solution.py:338
  91.1 0.3 collective-permute-start.21
  91.4 0.1 pad_maximum_fusion.refs_3_
  91.5 1.6 %collective-permute-start.23 = (f32[3,128,512]{2,1,0:T(8,128)S(1)}, f32[3,128,512]{2,1,0:T(8,128)S(1)}, u32[]{:S(2)}, u32[]{:S(2)}) collective-permute-start(f32[3,128,512]{2,1,0:T(8,128)S(1)} %pad_maximum_fusion.refs_3_), channel_id=1, source_target_pairs={{0,2},{2,0},{4,6},{6,4},{8,10},{10,8},{12,14},{14,12},{16,18},{18,... | collective-permute-start | bytes 2359304 | tf_op jit(solution)/shard_map/ppermute | solution.py:338
  93.1 11.0 %collective-permute-done.21 = f32[128,512]{1,0:T(8,128)S(1)} collective-permute-done((f32[128,512]{1,0:T(8,128)S(1)}, f32[128,512]{1,0:T(8,128)S(1)}, u32[]{:S(2)}, u32[]{:S(2)}) %collective-permute-start.21) | collective-permute-done | bytes 262176 | tf_op jit(solution)/shard_map/ppermute | solution.py:338
  104.1 1.0 collective-permute-start.22
  105.1 15.9 %factor_inverse.1 = (f32[256,256]{1,0:T(8,128)S(1)}, f32[256,256]{1,0:T(8,128)S(1)}, f32[256,256]{1,0:T(8,128)S(1)}, f32[256,256]{1,0:T(8,128)S(1)}, f32[256,256]{1,0:T(8,128)S(1)}) custom-call(s32[3]{0:T(128)S(1)} %pad_add_fusion.flag_ref.core_ref, f32[256,256]{1,0:T(8,128)S(1)} %get-tuple-element.17.gram_ref, ...), custom_call_target="tpu_custom_call" | custom-call | flops 15000000512 | bytes 2621440 | tf_op jit(solution)/shard_map/factor_inverse/pallas_call | solution.py:145
  121.0 1.4 %fusion.1 = f32[768,256]{1,0:T(8,128)} fusion(f32[768,256]{1,0:T(8,128)S(1)} %get-tuple-element.16, f32[256,256]{1,0:T(8,128)S(1)} %get-tuple-element.19), kind=kOutput, calls=%fused_computation.6 | convolution fusion | flops 301989888 | bytes 1835008 | tf_op jit(solution)/shard_map/dot_general | solution.py:391
  122.4 2.2 %reduce_early.1.kept_ref = f32[4,1,256,512]{3,2,1,0:T(8,128)} custom-call(s32[3]{0:T(128)S(1)} %pad_add_fusion.flag_ref.core_ref, f32[256,256]{1,0:T(8,128)S(1)} %get-tuple-element.23.refs_0_, f32[256,256]{1,0:T(8,128)S(1)} %get-tuple-element.24.refs_1_, f32[256,256]{1,0:T(8,128)S(1)} %get-tuple-element.25.refs_2_, ...), custom_call_target="tpu_custom_call" | custom-call | flops 603979776 | bytes 4718592 | tf_op jit(solution)/shard_map/reduce_early/pallas_call | solution.py:282
  124.6 1.7 %reduce_last.1 = f32[4,1,256,512]{3,2,1,0:T(8,128)} custom-call(s32[3]{0:T(128)S(1)} %pad_add_fusion.flag_ref.core_ref, f32[256,256]{1,0:T(8,128)S(1)} %get-tuple-element.20.inverse_ref, f32[128,512]{1,0:T(8,128)S(1)} %add.41.mine_ref, f32[128,512]{1,0:T(8,128)S(1)} %collective-permute-done.22.other_ref, ...), custom_call_target="tpu_custom_call", output_to_operand_aliasing={{}: (4, {})} | custom-call | flops 201326592 | bytes 1572864 | tf_op jit(solution)/shard_map/reduce_last/pallas_call | solution.py:318
  (33 shorter events, 0.3 us)
Async XLA Ops:
  0.6 45.9 %copy-start = (f32[768,512]{1,0:T(8,128)S(1)}, f32[768,512]{1,0:T(8,128)}, u32[]{:S(2)}) copy-start(f32[768,512]{1,0:T(8,128)} %refs_4_.1) | copy-start | bytes 4718596
  0.6 37.9 %copy-start.5 = (s32[3,3]{1,0:T(4,128)S(1)}, s32[3,3]{1,0:T(4,128)}, u32[]{:S(2)}) copy-start(s32[3,3]{1,0:T(4,128)} %param.9) | copy-start | bytes 112
  0.7 45.9 %copy-start.3 = (s32[3]{0:T(128)S(1)}, s32[3]{0:T(128)}, u32[]{:S(2)}) copy-start(s32[3]{0:T(128)} %count_ref.3) | copy-start | bytes 40
  0.7 45.9 %copy-start.2 = (f32[768,512]{1,0:T(8,128)S(1)}, f32[768,512]{1,0:T(8,128)}, u32[]{:S(2)}) copy-start(f32[768,512]{1,0:T(8,128)} %base_ref.1) | copy-start | bytes 4718596
  1.8 10.3 %collective-permute-start = (f32[128,512]{1,0:T(8,128)S(1)}, f32[128,512]{1,0:T(8,128)}, u32[]{:S(2)}, u32[]{:S(2)}) collective-permute-start(f32[128,512]{1,0:T(8,128)S(1)} %slice.18), channel_id=1, source_target_pairs={{0,2},{2,0},{4,6},{6,4},{8,10},{10,8},{12,14},{14,12},{16,18},{18,... | collective-permute-start | bytes 786440 | tf_op jit(solution)/shard_map/ppermute | solution.py:338
  7.1 10.5 %collective-permute-start.9 = (f32[128,512]{1,0:T(8,128)S(1)}, f32[128,512]{1,0:T(8,128)S(1)}, u32[]{:S(2)}, u32[]{:S(2)}) collective-permute-start(f32[128,512]{1,0:T(8,128)S(1)} %get-tuple-element.26), channel_id=1, source_target_pairs={{0,2},{2,0},{4,6},{6,4},{8,10},{10,8},{12,14},{14,12},{16,18},{18,... | collective-permute-start | bytes 786440 | tf_op jit(solution)/shard_map/ppermute | solution.py:338
  7.1 16.2 %collective-permute-start.6 = (f32[128,512]{1,0:T(8,128)}, f32[128,512]{1,0:T(8,128)}, u32[]{:S(2)}, u32[]{:S(2)}) collective-permute-start(f32[128,512]{1,0:T(8,128)} %get-tuple-element.28), channel_id=1, source_target_pairs={{0,2},{2,0},{4,6},{6,4},{8,10},{10,8},{12,14},{14,12},{16,18},{18,... | collective-permute-start | bytes 786440 | tf_op jit(solution)/shard_map/ppermute | solution.py:338
  9.1 19.8 %collective-permute-start.4 = (f32[128,512]{1,0:T(8,128)}, f32[128,512]{1,0:T(8,128)}, u32[]{:S(2)}, u32[]{:S(2)}) collective-permute-start(f32[128,512]{1,0:T(8,128)} %get-tuple-element.29), channel_id=1, source_target_pairs={{0,2},{2,0},{4,6},{6,4},{8,10},{10,8},{12,14},{14,12},{16,18},{18,... | collective-permute-start | bytes 786440 | tf_op jit(solution)/shard_map/ppermute | solution.py:338
  9.1 25.4 %collective-permute-start.2 = (f32[128,512]{1,0:T(8,128)}, f32[128,512]{1,0:T(8,128)}, u32[]{:S(2)}, u32[]{:S(2)}) collective-permute-start(f32[128,512]{1,0:T(8,128)} %get-tuple-element.30), channel_id=1, source_target_pairs={{0,2},{2,0},{4,6},{6,4},{8,10},{10,8},{12,14},{14,12},{16,18},{18,... | collective-permute-start | bytes 786440 | tf_op jit(solution)/shard_map/ppermute | solution.py:338
  12.1 27.2 %collective-permute-start.8 = (f32[128,512]{1,0:T(8,128)}, f32[128,512]{1,0:T(8,128)}, u32[]{:S(2)}, u32[]{:S(2)}) collective-permute-start(f32[128,512]{1,0:T(8,128)} %get-tuple-element.27), channel_id=1, source_target_pairs={{0,2},{2,0},{4,6},{6,4},{8,10},{10,8},{12,14},{14,12},{16,18},{18,... | collective-permute-start | bytes 786440 | tf_op jit(solution)/shard_map/ppermute | solution.py:338
  17.6 25.4 %collective-permute-start.1 = (f32[128,512]{1,0:T(8,128)}, f32[128,512]{1,0:T(8,128)}, u32[]{:S(2)}, u32[]{:S(2)}) collective-permute-start(f32[128,512]{1,0:T(8,128)} %collective-permute-done.refs_5_), channel_id=1, source_target_pairs={{0,4},{4,8},{6,2},{8,12},{10,6},{12,16},{14,10},{16,20},{18,14},{2... | collective-permute-start | bytes 786440 | tf_op jit(solution)/shard_map/ppermute | solution.py:344
  23.3 23.2 %collective-permute-start.7 = (f32[128,512]{1,0:T(8,128)}, f32[128,512]{1,0:T(8,128)S(1)}, u32[]{:S(2)}, u32[]{:S(2)}) collective-permute-start(f32[128,512]{1,0:T(8,128)} %collective-permute-done.6.refs_8_), channel_id=1, source_target_pairs={{0,4},{4,8},{6,2},{8,12},{10,6},{12,16},{14,10},{16,20},{18,14},{2... | collective-permute-start | bytes 786440 | tf_op jit(solution)/shard_map/ppermute | solution.py:344
  28.9 17.6 %collective-permute-start.5 = (f32[128,512]{1,0:T(8,128)}, f32[128,512]{1,0:T(8,128)S(1)}, u32[]{:S(2)}, u32[]{:S(2)}) collective-permute-start(f32[128,512]{1,0:T(8,128)} %collective-permute-done.4.refs_7_), channel_id=1, source_target_pairs={{0,4},{4,8},{6,2},{8,12},{10,6},{12,16},{14,10},{16,20},{18,14},{2... | collective-permute-start | bytes 786440 | tf_op jit(solution)/shard_map/ppermute | solution.py:344
  34.6 12.0 %collective-permute-start.3 = (f32[128,512]{1,0:T(8,128)}, f32[128,512]{1,0:T(8,128)S(1)}, u32[]{:S(2)}, u32[]{:S(2)}) collective-permute-start(f32[128,512]{1,0:T(8,128)} %collective-permute-done.2.refs_6_), channel_id=1, source_target_pairs={{0,4},{4,8},{6,2},{8,12},{10,6},{12,16},{14,10},{16,20},{18,14},{2... | collective-permute-start | bytes 786440 | tf_op jit(solution)/shard_map/ppermute | solution.py:344
  39.3 13.1 %collective-permute-start.11 = (f32[128,512]{1,0:T(8,128)S(1)}, f32[128,512]{1,0:T(8,128)S(1)}, u32[]{:S(2)}, u32[]{:S(2)}) collective-permute-start(f32[128,512]{1,0:T(8,128)S(1)} %collective-permute-done.9.refs_10_), channel_id=1, source_target_pairs={{0,4},{4,8},{6,2},{8,12},{10,6},{12,16},{14,10},{16,20},{18,14},{2... | collective-permute-start | bytes 786440 | tf_op jit(solution)/shard_map/ppermute | solution.py:344
  43.0 10.9 %collective-permute-start.10 = (f32[128,512]{1,0:T(8,128)}, f32[128,512]{1,0:T(8,128)S(1)}, u32[]{:S(2)}, u32[]{:S(2)}) collective-permute-start(f32[128,512]{1,0:T(8,128)} %collective-permute-done.8.refs_9_), channel_id=1, source_target_pairs={{0,4},{4,8},{6,2},{8,12},{10,6},{12,16},{14,10},{16,20},{18,14},{2... | collective-permute-start | bytes 786440 | tf_op jit(solution)/shard_map/ppermute | solution.py:344
  46.6 1.7 %copy-start.1 = (f32[3,3,256,256]{3,2,1,0:T(8,128)S(1)}, f32[3,3,256,256]{3,2,1,0:T(8,128)}, u32[]{:S(2)}) copy-start(f32[3,3,256,256]{3,2,1,0:T(8,128)} %blocks_ref.3) | copy-start | bytes 7077892
  48.2 5.7 %copy-start.4 = (f32[512,256]{1,0:T(8,128)S(1)}, f32[512,256]{1,0:T(8,128)}, u32[]{:S(2)}) copy-start(f32[512,256]{1,0:T(8,128)} %refs_2_.1) | copy-start | bytes 1572868
  55.7 2.4 %collective-permute-start.12 = (f32[768,256]{1,0:T(8,128)S(1)}, f32[768,256]{1,0:T(8,128)S(1)}, u32[]{:S(2)}, u32[]{:S(2)}) collective-permute-start(f32[768,256]{1,0:T(8,128)S(1)} %get-tuple-element.14.half_ref), channel_id=1, source_target_pairs={{0,1},{1,0},{2,3},{3,2},{4,5},{5,4},{6,7},{7,6},{8,9},{9,8},{10,11... | collective-permute-start | bytes 2359304 | tf_op jit(solution)/shard_map/ppermute | solution.py:338
  59.9 6.8 %collective-permute-start.13 = (f32[256,128]{1,0:T(8,128)S(1)}, f32[256,128]{1,0:T(8,128)S(1)}, u32[]{:S(2)}, u32[]{:S(2)}) collective-permute-start(f32[256,128]{1,0:T(8,128)S(1)} %get-tuple-element.18), channel_id=1, source_target_pairs={{0,2},{2,0},{4,6},{6,4},{8,10},{10,8},{12,14},{14,12},{16,18},{18,... | collective-permute-start | bytes 393224 | tf_op jit(solution)/shard_map/ppermute | solution.py:338
  62.3 10.2 %collective-permute-start.18 = (f32[128,512]{1,0:T(8,128)S(1)}, f32[128,512]{1,0:T(8,128)S(1)}, u32[]{:S(2)}, u32[]{:S(2)}) collective-permute-start(f32[128,512]{1,0:T(8,128)S(1)} %get-tuple-element.22), channel_id=1, source_target_pairs={{0,2},{2,0},{4,6},{6,4},{8,10},{10,8},{12,14},{14,12},{16,18},{18,... | collective-permute-start | bytes 786440 | tf_op jit(solution)/shard_map/ppermute | solution.py:338
  66.7 5.8 %collective-permute-start.14 = (f32[256,128]{1,0:T(8,128)S(1)}, f32[256,128]{1,0:T(8,128)S(1)}, u32[]{:S(2)}, u32[]{:S(2)}) collective-permute-start(f32[256,128]{1,0:T(8,128)S(1)} %add.34), channel_id=1, source_target_pairs={{0,4},{2,6},{4,0},{6,2},{8,12},{10,14},{12,8},{14,10},{16,20},{18,... | collective-permute-start | bytes 393224 | tf_op jit(solution)/shard_map/ppermute | solution.py:338
  72.6 9.7 %collective-permute-start.19 = (f32[128,512]{1,0:T(8,128)S(1)}, f32[128,512]{1,0:T(8,128)S(1)}, u32[]{:S(2)}, u32[]{:S(2)}) collective-permute-start(f32[128,512]{1,0:T(8,128)S(1)} %add.38), channel_id=1, source_target_pairs={{0,4},{2,6},{4,0},{6,2},{8,12},{10,14},{12,8},{14,10},{16,20},{18,... | collective-permute-start | bytes 786440 | tf_op jit(solution)/shard_map/ppermute | solution.py:338
  74.7 5.0 %collective-permute-start.15 = (f32[256,128]{1,0:T(8,128)S(1)}, f32[256,128]{1,0:T(8,128)S(1)}, u32[]{:S(2)}, u32[]{:S(2)}) collective-permute-start(f32[256,128]{1,0:T(8,128)S(1)} %add.35), channel_id=1, source_target_pairs={{0,8},{2,10},{4,12},{6,14},{8,0},{10,2},{12,4},{14,6},{16,24},{18,... | collective-permute-start | bytes 393224 | tf_op jit(solution)/shard_map/ppermute | solution.py:338
  79.7 7.2 %collective-permute-start.16 = (f32[256,128]{1,0:T(8,128)S(1)}, f32[256,128]{1,0:T(8,128)S(1)}, u32[]{:S(2)}, u32[]{:S(2)}) collective-permute-start(f32[256,128]{1,0:T(8,128)S(1)} %add.36), channel_id=1, source_target_pairs={{0,16},{2,18},{4,20},{6,22},{8,24},{10,26},{12,28},{14,30},{16,0},... | collective-permute-start | bytes 393224 | tf_op jit(solution)/shard_map/ppermute | solution.py:338
  82.4 8.7 %collective-permute-start.20 = (f32[128,512]{1,0:T(8,128)S(1)}, f32[128,512]{1,0:T(8,128)S(1)}, u32[]{:S(2)}, u32[]{:S(2)}) collective-permute-start(f32[128,512]{1,0:T(8,128)S(1)} %add.39), channel_id=1, source_target_pairs={{0,8},{2,10},{4,12},{6,14},{8,0},{10,2},{12,4},{14,6},{16,24},{18,... | collective-permute-start | bytes 786440 | tf_op jit(solution)/shard_map/ppermute | solution.py:338
  86.9 18.2 %collective-permute-start.17 = (f32[4,256,128]{2,1,0:T(8,128)S(1)}, f32[4,256,128]{2,1,0:T(8,128)S(1)}, u32[]{:S(2)}, u32[]{:S(2)}) collective-permute-start(f32[4,256,128]{2,1,0:T(8,128)S(1)} %pad_maximum_fusion.1.mine_ref), channel_id=1, source_target_pairs={{0,1},{1,0},{2,3},{3,2},{4,5},{5,4},{6,7},{7,6},{8,9},{9,8},{10,11... | collective-permute-start | bytes 1572872 | tf_op jit(solution)/shard_map/ppermute | solution.py:338
  91.1 12.9 %collective-permute-start.21 = (f32[128,512]{1,0:T(8,128)S(1)}, f32[128,512]{1,0:T(8,128)S(1)}, u32[]{:S(2)}, u32[]{:S(2)}) collective-permute-start(f32[128,512]{1,0:T(8,128)S(1)} %add.40), channel_id=1, source_target_pairs={{0,16},{2,18},{4,20},{6,22},{8,24},{10,26},{12,28},{14,30},{16,0},... | collective-permute-start | bytes 786440 | tf_op jit(solution)/shard_map/ppermute | solution.py:338
  91.5 30.9 %collective-permute-start.23 = (f32[3,128,512]{2,1,0:T(8,128)S(1)}, f32[3,128,512]{2,1,0:T(8,128)S(1)}, u32[]{:S(2)}, u32[]{:S(2)}) collective-permute-start(f32[3,128,512]{2,1,0:T(8,128)S(1)} %pad_maximum_fusion.refs_3_), channel_id=1, source_target_pairs={{0,2},{2,0},{4,6},{6,4},{8,10},{10,8},{12,14},{14,12},{16,18},{18,... | collective-permute-start | bytes 2359304 | tf_op jit(solution)/shard_map/ppermute | solution.py:338
  104.1 20.5 %collective-permute-start.22 = (f32[128,512]{1,0:T(8,128)S(1)}, f32[128,512]{1,0:T(8,128)S(1)}, u32[]{:S(2)}, u32[]{:S(2)}) collective-permute-start(f32[128,512]{1,0:T(8,128)S(1)} %add.41.mine_ref), channel_id=1, source_target_pairs={{0,2},{2,0},{4,6},{6,4},{8,10},{10,8},{12,14},{14,12},{16,18},{18,... | collective-permute-start | bytes 786440 | tf_op jit(solution)/shard_map/ppermute | solution.py:338
